TPU v7x, 32 devices: a whole 2x2x4 slice. The times are simulated.
32 devices in a mesh: fsdp: 16 (over z, x, core), tp: 2 (over y).
Axes of the slice: x: 2, y: 2, z: 4, core: 2. Of those that a mesh axis runs over, the one named last changes fastest.
Arguments:
- hidden_in: bfloat16 [1024, 2, 768], P(('fsdp', 'tp')), may hold values from -6 to 6
- cotangent: bfloat16 [1024, 2, 768], P(('fsdp', 'tp')), may hold values from -6 to 6
- lengths: int32 [2], replicated, may hold values from 256 to 1024, as said below
- w_query: bfloat16 [768, 768], P('fsdp', 'tp'), may hold values from -0.21875 to 0.21875
- b_query: bfloat16 [768], P('fsdp'), may hold values from -1.796875 to 1.796875
- w_key: bfloat16 [768, 768], P('fsdp', 'tp'), may hold values from -0.3125 to 0.3125
- w_value: bfloat16 [768, 768], P('fsdp', 'tp'), may hold values from -0.21875 to 0.21875
- b_value: bfloat16 [768], P('fsdp'), may hold values from -0.1796875 to 0.1796875
- w_out: bfloat16 [768, 768], P('tp', 'fsdp'), may hold values from -4 to 4
- b_out: bfloat16 [768], P('fsdp'), may hold values from -0.8984375 to 0.8984375
- first_gain: bfloat16 [768], P('fsdp'), may hold values from 0.099609375 to 1.8984375
- first_shift: bfloat16 [768], P('fsdp'), may hold values from -0.8984375 to 0.8984375
- w_up: bfloat16 [768, 3072], P('fsdp', 'tp'), may hold values from -0.21875 to 0.21875
- b_up: bfloat16 [3072], P('fsdp'), may hold values from -1.796875 to 1.796875
- w_down: bfloat16 [3072, 768], P('tp', 'fsdp'), may hold values from -0.109375 to 0.109375
- b_down: bfloat16 [768], P('fsdp'), may hold values from -0.8984375 to 0.8984375
- second_gain: bfloat16 [768], P('fsdp'), may hold values from 0.099609375 to 1.8984375
- second_shift: bfloat16 [768], P('fsdp'), may hold values from -0.8984375 to 0.8984375
Outputs:
- output: bfloat16 [1024, 2, 768], P(('fsdp', 'tp'))
- grad_hidden: float32 [1024, 2, 768], P(('fsdp', 'tp'))
- grad_w_query: float32 [768, 768], P('fsdp', 'tp')
- grad_b_query: float32 [768], P('fsdp')
- grad_w_key: float32 [768, 768], P('fsdp', 'tp')
- grad_w_value: float32 [768, 768], P('fsdp', 'tp')
- grad_b_value: float32 [768], P('fsdp')
- grad_w_out: float32 [768, 768], P('tp', 'fsdp')
- grad_b_out: float32 [768], P('fsdp')
- grad_first_gain: float32 [768], P('fsdp')
- grad_first_shift: float32 [768], P('fsdp')
- grad_w_up: float32 [768, 3072], P('fsdp', 'tp')
- grad_b_up: float32 [3072], P('fsdp')
- grad_w_down: float32 [3072, 768], P('tp', 'fsdp')
- grad_b_down: float32 [768], P('fsdp')
- grad_second_gain: float32 [768], P('fsdp')
- grad_second_shift: float32 [768], P('fsdp')
Inputs may be any that keep to these rules, and one draw needn't show every extreme that they name: `lengths`: every slot's valid tokens stand at its start; in every draw one slot, drawn from the seed, is full.
All inputs are finite; a program needn't handle non-finite values.
Results may differ from a plain program's by a relative error of at most 0.019.
Values may be sent and summed in bfloat16 or wider, within the bound.
No kernel may reach another device: no remote copies, remote signals or barrier semaphores. Data moves between devices by JAX's collectives and lax.ppermute only.
A program may use at most 192 MiB of HBM per device.

v0:
```python
import math

import jax
import jax.numpy as jnp
from jax import lax
from jax.sharding import PartitionSpec as P

HD = 64


layer_eps = 1e-12
masked_score = -1e30


def layer_norm(values, gain_vector, shift_vector):
    centre = values - jnp.mean(values, axis=-1, keepdims=True)
    spread = jnp.mean(centre * centre, axis=-1, keepdims=True)
    return centre * lax.rsqrt(spread + layer_eps) * gain_vector + shift_vector


def exact_gelu(values):
    return jax.nn.gelu(values, approximate=False)


def gather_rows(values):
    return lax.all_gather(values, "tp", axis=0, tiled=True)


def sum_rows(term_fn, local_rows):
    return lax.psum_scatter(
        term_fn(jnp.int32(0), local_rows * lax.axis_size("tp")).astype(jnp.bfloat16),
        "tp",
        scatter_dimension=0,
        tiled=True,
    ).astype(jnp.float32)


def live_rows(positions, lengths):
    return positions[:, None] < lengths[None, :]


def over_blocks(carry, pieces, step_fn):
    total_rows = pieces[0].shape[0]
    step_rows = math.gcd(total_rows, 256)

    def one_step(block_index, running):
        first_row = block_index * step_rows
        sliced = tuple(
            (lax.dynamic_slice_in_dim(member, first_row, step_rows, 0) for member in pieces)
        )
        return step_fn(running, sliced, first_row + jnp.arange(step_rows))

    return lax.fori_loop(0, total_rows // step_rows, one_step, carry)


def local(
    hidden_in,
    cotangent,
    lengths,
    w_query,
    b_query,
    w_key,
    w_value,
    b_value,
    w_out,
    b_out,
    first_gain,
    first_shift,
    w_up,
    b_up,
    w_down,
    b_down,
    second_gain,
    second_shift,
):
    gathered_weights = (
        lax.all_gather(w_query, "fsdp", axis=0, tiled=True),
        lax.all_gather(b_query, "fsdp", axis=0, tiled=True),
        lax.all_gather(w_key, "fsdp", axis=0, tiled=True),
        lax.all_gather(w_value, "fsdp", axis=0, tiled=True),
        lax.all_gather(b_value, "fsdp", axis=0, tiled=True),
        lax.all_gather(w_out, "fsdp", axis=1, tiled=True),
        lax.all_gather(b_out, "fsdp", axis=0, tiled=True),
        lax.all_gather(first_gain, "fsdp", axis=0, tiled=True),
        lax.all_gather(first_shift, "fsdp", axis=0, tiled=True),
        lax.all_gather(w_up, "fsdp", axis=0, tiled=True),
        lax.all_gather(b_up, "fsdp", axis=0, tiled=True),
        lax.all_gather(w_down, "fsdp", axis=1, tiled=True),
        lax.all_gather(b_down, "fsdp", axis=0, tiled=True),
        lax.all_gather(second_gain, "fsdp", axis=0, tiled=True),
        lax.all_gather(second_shift, "fsdp", axis=0, tiled=True),
    )
    (
        query_weight,
        query_bias_all,
        key_weight,
        value_weight,
        value_bias_all,
        out_weight,
        out_bias,
        gain_one,
        shift_one,
        up_weight,
        up_bias_all,
        down_weight,
        down_bias,
        gain_two,
        shift_two,
    ) = gathered_weights
    tp_index = lax.axis_index("tp")
    tp_count = lax.axis_size("tp")
    fsdp_index = lax.axis_index("fsdp")
    shard_pos, seq_count, model_width = hidden_in.shape
    local_rows = shard_pos * seq_count
    block_pos = shard_pos * tp_count
    tok_dev = block_pos * seq_count
    head_width = query_weight.shape[1]
    heads_local = head_width // HD
    unit_width = up_weight.shape[1]
    score_scale = HD ** (-0.5)
    own_live = live_rows(fsdp_index * block_pos + jnp.arange(block_pos), lengths)
    own_keep = jnp.transpose(own_live)[:, None, None, :]
    query_bias = lax.dynamic_slice_in_dim(
        query_bias_all, tp_index * head_width, head_width, 0
    ).astype(jnp.float32)
    value_bias = lax.dynamic_slice_in_dim(
        value_bias_all, tp_index * head_width, head_width, 0
    ).astype(jnp.float32)
    up_bias = lax.dynamic_slice_in_dim(up_bias_all, tp_index * unit_width, unit_width, 0).astype(
        jnp.float32
    )
    hidden_flat = hidden_in.reshape(local_rows, model_width)
    inputs = gather_rows(hidden_flat)
    queries = (
        jnp.dot(inputs, query_weight, preferred_element_type=jnp.float32) + query_bias
    ).astype(jnp.bfloat16)
    keys_own = jnp.dot(inputs, key_weight, preferred_element_type=jnp.float32).astype(jnp.bfloat16)
    values_own = (
        jnp.dot(inputs, value_weight, preferred_element_type=jnp.float32) + value_bias
    ).astype(jnp.bfloat16)
    head_shape = (block_pos, seq_count, heads_local, HD)
    query_heads = queries.reshape(head_shape)
    key_rows_own = keys_own.reshape(block_pos, seq_count, head_width)
    value_rows_own = values_own.reshape(block_pos, seq_count, head_width)
    key_heads_own = keys_own.reshape(head_shape)
    value_heads_own = values_own.reshape(head_shape)
    pair_own = jnp.concatenate([key_rows_own, value_rows_own], axis=2)

    def split_heads(rows):
        return rows.reshape(rows.shape[0], seq_count, heads_local, HD)

    def stats_step(current, parts, positions):
        keep = jnp.transpose(live_rows(positions, lengths))[:, None, None, :]
        row_max, row_total = current
        scores = (
            jnp.einsum(
                "qshd,kshd->shqk",
                query_heads,
                split_heads(parts[0]),
                preferred_element_type=jnp.float32,
            )
            * score_scale
        )
        masked = jnp.where(keep, scores, masked_score)
        new_max = jnp.maximum(row_max, jnp.max(masked, axis=3))
        grown = jnp.where(keep, jnp.exp(masked - new_max[..., None]), 0.0)
        return (new_max, row_total * jnp.exp(row_max - new_max) + jnp.sum(grown, axis=3))

    stat_shape = (seq_count, heads_local, block_pos)
    row_max, row_total = over_blocks(
        (jnp.full(stat_shape, masked_score, jnp.float32), jnp.zeros(stat_shape, jnp.float32)),
        (lax.all_gather(key_rows_own, "fsdp", axis=0, tiled=True),),
        stats_step,
    )
    log_total = row_max + jnp.log(row_total)

    def value_step(running, parts, positions):
        pair_rows = parts[0]
        keep = jnp.transpose(live_rows(positions, lengths))[:, None, None, :]
        scores = (
            jnp.einsum(
                "qshd,kshd->shqk",
                query_heads,
                split_heads(pair_rows[:, :, :head_width]),
                preferred_element_type=jnp.float32,
            )
            * score_scale
        )
        probs = jnp.where(keep, jnp.exp(scores - log_total[..., None]), 0.0).astype(jnp.bfloat16)
        return running + jnp.einsum(
            "shqk,kshd->qshd",
            probs,
            split_heads(pair_rows[:, :, head_width:]),
            preferred_element_type=jnp.float32,
        )

    zero_heads = jnp.zeros(head_shape, jnp.float32)
    attended = over_blocks(
        zero_heads, (lax.all_gather(pair_own, "fsdp", axis=0, tiled=True),), value_step
    )
    attended_low = attended.reshape(tok_dev, head_width).astype(jnp.bfloat16)

    def out_term(first_row, row_count):
        return jnp.dot(attended_low, out_weight, preferred_element_type=jnp.float32)

    branch_one = sum_rows(out_term, local_rows) + out_bias.astype(jnp.float32)
    first_sum = hidden_flat.astype(jnp.float32) + branch_one
    first_out, first_back = jax.vjp(
        layer_norm, first_sum, gain_one.astype(jnp.float32), shift_one.astype(jnp.float32)
    )
    normed_rows = gather_rows(first_out.astype(jnp.bfloat16))
    preact = jnp.dot(normed_rows, up_weight, preferred_element_type=jnp.float32) + up_bias
    active, gelu_back = jax.vjp(exact_gelu, preact)
    active_low = active.astype(jnp.bfloat16)

    def down_term(first_row, row_count):
        return jnp.dot(active_low, down_weight, preferred_element_type=jnp.float32)

    branch_two = sum_rows(down_term, local_rows) + down_bias.astype(jnp.float32)
    second_sum = first_out + branch_two
    output, second_back = jax.vjp(
        layer_norm, second_sum, gain_two.astype(jnp.float32), shift_two.astype(jnp.float32)
    )
    local_positions = (fsdp_index * tp_count + tp_index) * shard_pos + jnp.arange(shard_pos)
    row_live = live_rows(local_positions, lengths).reshape(local_rows)
    grad_out = cotangent.reshape(local_rows, model_width).astype(jnp.float32) * row_live[
        :, None
    ].astype(jnp.float32)
    second_grad, gain_two_grad, shift_two_grad = second_back(grad_out)
    branch_two_grad = second_grad.astype(jnp.bfloat16)
    down_bias_grad = jnp.sum(branch_two_grad.astype(jnp.float32), axis=0)
    rows_two_grad = gather_rows(branch_two_grad)
    active_grad = jnp.einsum(
        "td,fd->tf", rows_two_grad, down_weight, preferred_element_type=jnp.float32
    )
    down_weight_grad = jnp.einsum(
        "tf,td->fd", active_low, rows_two_grad, preferred_element_type=jnp.float32
    )
    preact_grad = gelu_back(active_grad)[0].astype(jnp.bfloat16)
    up_bias_grad = jnp.sum(preact_grad.astype(jnp.float32), axis=0)
    up_weight_grad = jnp.einsum(
        "td,tf->df", normed_rows, preact_grad, preferred_element_type=jnp.float32
    )

    def up_back_term(first_row, row_count):
        return jnp.einsum("tf,df->td", preact_grad, up_weight, preferred_element_type=jnp.float32)

    first_out_grad = second_grad + sum_rows(up_back_term, local_rows)
    first_grad, gain_one_grad, shift_one_grad = first_back(first_out_grad)
    branch_one_grad = first_grad.astype(jnp.bfloat16)
    out_bias_grad = jnp.sum(branch_one_grad.astype(jnp.float32), axis=0)
    rows_one_grad = gather_rows(branch_one_grad)
    attended_grad = jnp.einsum(
        "td,hd->th", rows_one_grad, out_weight, preferred_element_type=jnp.float32
    ).astype(jnp.bfloat16)
    out_weight_grad = jnp.einsum(
        "th,td->hd", attended_low, rows_one_grad, preferred_element_type=jnp.float32
    )
    grad_heads = attended_grad.reshape(head_shape)
    delta_rows = jnp.sum(grad_heads.astype(jnp.float32) * attended, axis=3)
    row_delta = jnp.transpose(delta_rows, (1, 2, 0))
    lse_rows = jnp.transpose(log_total, (2, 0, 1))
    whole_lse, whole_delta = (
        lax.all_gather(lse_rows, "fsdp", axis=0, tiled=True),
        lax.all_gather(delta_rows, "fsdp", axis=0, tiled=True),
    )
    query_rows_own = queries.reshape(block_pos, seq_count, head_width)
    grad_rows_own = attended_grad.reshape(block_pos, seq_count, head_width)

    def query_grad_step(running, parts, positions):
        pair_rows = parts[0]
        keep = jnp.transpose(live_rows(positions, lengths))[:, None, None, :]
        key_heads = split_heads(pair_rows[:, :, :head_width])
        value_heads = split_heads(pair_rows[:, :, head_width:])
        scores = (
            jnp.einsum(
                "qshd,kshd->shqk", query_heads, key_heads, preferred_element_type=jnp.float32
            )
            * score_scale
        )
        weights = jnp.where(keep, jnp.exp(scores - log_total[..., None]), 0.0)
        weight_grad = jnp.einsum(
            "qshd,kshd->shqk", grad_heads, value_heads, preferred_element_type=jnp.float32
        )
        score_grad = (weights * (weight_grad - row_delta[..., None])).astype(jnp.bfloat16)
        return (
            running
            + jnp.einsum(
                "shqk,kshd->qshd", score_grad, key_heads, preferred_element_type=jnp.float32
            )
            * score_scale
        )

    def key_grad_step(running, parts, positions):
        query_rows, grad_rows = parts
        row_count = query_rows.shape[0]
        query_part = split_heads(query_rows)
        grad_part = split_heads(grad_rows)
        lse_part = jnp.transpose(
            lax.dynamic_slice_in_dim(whole_lse, positions[0], row_count, 0), (1, 2, 0)
        )
        delta_part = jnp.transpose(
            lax.dynamic_slice_in_dim(whole_delta, positions[0], row_count, 0), (1, 2, 0)
        )
        scores = (
            jnp.einsum(
                "qshd,kshd->shqk", query_part, key_heads_own, preferred_element_type=jnp.float32
            )
            * score_scale
        )
        weights = jnp.where(own_keep, jnp.exp(scores - lse_part[..., None]), 0.0)
        weight_grad = jnp.einsum(
            "qshd,kshd->shqk", grad_part, value_heads_own, preferred_element_type=jnp.float32
        )
        score_grad = (weights * (weight_grad - delta_part[..., None])).astype(jnp.bfloat16)
        key_acc, value_acc = running
        key_acc = (
            key_acc
            + jnp.einsum(
                "shqk,qshd->kshd", score_grad, query_part, preferred_element_type=jnp.float32
            )
            * score_scale
        )
        value_acc = value_acc + jnp.einsum(
            "shqk,qshd->kshd",
            weights.astype(jnp.bfloat16),
            grad_part,
            preferred_element_type=jnp.float32,
        )
        return (key_acc, value_acc)

    query_grad = over_blocks(
        zero_heads, (lax.all_gather(pair_own, "fsdp", axis=0, tiled=True),), query_grad_step
    )
    key_grad, value_grad = over_blocks(
        (zero_heads, zero_heads),
        (
            lax.all_gather(query_rows_own, "fsdp", axis=0, tiled=True),
            lax.all_gather(grad_rows_own, "fsdp", axis=0, tiled=True),
        ),
        key_grad_step,
    )
    query_grad_low = query_grad.reshape(tok_dev, head_width).astype(jnp.bfloat16)
    key_grad_low = key_grad.reshape(tok_dev, head_width).astype(jnp.bfloat16)
    value_grad_low = value_grad.reshape(tok_dev, head_width).astype(jnp.bfloat16)
    query_weight_grad = jnp.einsum(
        "td,th->dh", inputs, query_grad_low, preferred_element_type=jnp.float32
    )
    key_weight_grad = jnp.einsum(
        "td,th->dh", inputs, key_grad_low, preferred_element_type=jnp.float32
    )
    value_weight_grad = jnp.einsum(
        "td,th->dh", inputs, value_grad_low, preferred_element_type=jnp.float32
    )
    query_bias_grad = jnp.sum(query_grad_low.astype(jnp.float32), axis=0)
    value_bias_grad = jnp.sum(value_grad_low.astype(jnp.float32), axis=0)

    def input_back_term(first_row, row_count):
        summed_term = jnp.einsum(
            "th,dh->td", query_grad_low, query_weight, preferred_element_type=jnp.float32
        )
        summed_term = summed_term + jnp.einsum(
            "th,dh->td", key_grad_low, key_weight, preferred_element_type=jnp.float32
        )
        return summed_term + jnp.einsum(
            "th,dh->td", value_grad_low, value_weight, preferred_element_type=jnp.float32
        )

    hidden_grad = first_grad + sum_rows(input_back_term, local_rows)

    def widen_half(half_part, full_width):
        return lax.dynamic_update_slice_in_dim(
            jnp.zeros((full_width,), jnp.float32), half_part, tp_index * half_part.shape[0], 0
        )

    summed = (
        lax.psum_scatter(query_weight_grad, "fsdp", scatter_dimension=0, tiled=True),
        lax.psum_scatter(
            widen_half(query_bias_grad, model_width), "fsdp", scatter_dimension=0, tiled=True
        ),
        lax.psum_scatter(key_weight_grad, "fsdp", scatter_dimension=0, tiled=True),
        lax.psum_scatter(value_weight_grad, "fsdp", scatter_dimension=0, tiled=True),
        lax.psum_scatter(
            widen_half(value_bias_grad, model_width), "fsdp", scatter_dimension=0, tiled=True
        ),
        lax.psum_scatter(out_weight_grad, "fsdp", scatter_dimension=1, tiled=True),
        lax.psum_scatter(out_bias_grad, "fsdp", scatter_dimension=0, tiled=True),
        lax.psum_scatter(gain_one_grad, "fsdp", scatter_dimension=0, tiled=True),
        lax.psum_scatter(shift_one_grad, "fsdp", scatter_dimension=0, tiled=True),
        lax.psum_scatter(up_weight_grad, "fsdp", scatter_dimension=0, tiled=True),
        lax.psum_scatter(
            widen_half(up_bias_grad, up_bias_all.shape[0]), "fsdp", scatter_dimension=0, tiled=True
        ),
        lax.psum_scatter(down_weight_grad, "fsdp", scatter_dimension=1, tiled=True),
        lax.psum_scatter(down_bias_grad, "fsdp", scatter_dimension=0, tiled=True),
        lax.psum_scatter(gain_two_grad, "fsdp", scatter_dimension=0, tiled=True),
        lax.psum_scatter(shift_two_grad, "fsdp", scatter_dimension=0, tiled=True),
    )
    vectors = lax.psum(
        (
            summed[1],
            summed[4],
            summed[6],
            summed[7],
            summed[8],
            summed[10],
            summed[12],
            summed[13],
            summed[14],
        ),
        "tp",
    )
    out_shape = (shard_pos, seq_count, model_width)
    return (
        output.reshape(out_shape).astype(jnp.bfloat16),
        hidden_grad.reshape(out_shape),
        summed[0],
        vectors[0],
        summed[2],
        summed[3],
        vectors[1],
        summed[5],
        vectors[2],
        vectors[3],
        vectors[4],
        summed[9],
        vectors[5],
        summed[11],
        vectors[6],
        vectors[7],
        vectors[8],
    )


def solution(mesh):
    in_specs = (
        P(("fsdp", "tp"), None, None),
        P(("fsdp", "tp"), None, None),
        P(),
        P("fsdp", "tp"),
        P("fsdp"),
        P("fsdp", "tp"),
        P("fsdp", "tp"),
        P("fsdp"),
        P("tp", "fsdp"),
        P("fsdp"),
        P("fsdp"),
        P("fsdp"),
        P("fsdp", "tp"),
        P("fsdp"),
        P("tp", "fsdp"),
        P("fsdp"),
        P("fsdp"),
        P("fsdp"),
    )
    out_specs = (
        P(("fsdp", "tp"), None, None),
        P(("fsdp", "tp"), None, None),
        P("fsdp", "tp"),
        P("fsdp"),
        P("fsdp", "tp"),
        P("fsdp", "tp"),
        P("fsdp"),
        P("tp", "fsdp"),
        P("fsdp"),
        P("fsdp"),
        P("fsdp"),
        P("fsdp", "tp"),
        P("fsdp"),
        P("tp", "fsdp"),
        P("fsdp"),
        P("fsdp"),
        P("fsdp"),
    )
    return jax.shard_map(local, mesh=mesh, in_specs=in_specs, out_specs=out_specs, check_vma=False)
```

profile of v0, /device:TPU:0, one launch (start us, length us, event | category | flops | bytes accessed | tf_op | source)
XLA Modules:
  0.0 868.4 jit_solution(256764183834318346)
XLA Ops:
  8.3 6.4 all_gather.76
  14.7 24.0 %all_gather.77 = bf16[768,384]{1,0:T(8,128)(2,1)S(1)} all-gather(bf16[48,384]{1,0:T(8,128)(2,1)} %param.31), channel_id=1, replica_groups=mesh['fsdp'=16,'tp'=2] {'fsdp'}, dimensions={0}, use_global_device_ids=true | all-gather | bytes 626688 | tf_op jit(solution)/shard_map/all_gather | solution.py:79
  43.9 58.1 %all-reduce.20 = (bf16[768]{0:T(1024)(128)(2,1)S(1)}, bf16[768]{0:T(1024)(128)(2,1)S(1)}, bf16[768]{0:T(1024)(128)(2,1)S(1)}, bf16[768]{0:T(1024)(128)(2,1)S(1)}...) all-reduce(bf16[768]{0:T(1024)(128)(2,1)S(1)} %dynamic-update-slice, ...), channel_id=1, replica_groups=mesh['fsdp'=16,'tp'=2] {'fsdp'}, use_global_device_ids=true, to_apply=%add.4 | all-reduce | flops 9216 | bytes 36864
  102.1 18.9 %all_gather.78 = bf16[768,384]{1,0:T(8,128)(2,1)S(1)} all-gather(bf16[48,384]{1,0:T(8,128)(2,1)S(1)} %copy-done.45), channel_id=1, replica_groups=mesh['fsdp'=16,'tp'=2] {'fsdp'}, dimensions={0}, use_global_device_ids=true | all-gather | bytes 626688 | tf_op jit(solution)/shard_map/all_gather | solution.py:80
  121.3 1.8 pad_maximum_fusion
  123.2 21.9 %all_gather.81 = bf16[768,384]{1,0:T(8,128)(2,1)S(1)} all-gather(bf16[48,384]{1,0:T(8,128)(2,1)S(1)} %copy-done.46), channel_id=1, replica_groups=mesh['fsdp'=16,'tp'=2] {'fsdp'}, dimensions={0}, use_global_device_ids=true | all-gather | bytes 626688 | tf_op jit(solution)/shard_map/all_gather | solution.py:77
  145.7 21.5 %all_gather.84 = bf16[384,768]{0,1:T(8,128)(2,1)} all-gather(bf16[384,48]{0,1:T(8,128)(2,1)S(1)} %copy-done.47), channel_id=1, replica_groups=mesh['fsdp'=16,'tp'=2] {'fsdp'}, dimensions={1}, use_global_device_ids=true | all-gather | bytes 626688 | tf_op jit(solution)/shard_map/all_gather | solution.py:82
  167.2 10.4 %while.60 = (s32[]{:T(128)}, f32[2,6,64]{2,1,0:T(8,128)S(1)}, f32[2,6,64]{2,1,0:T(8,128)S(1)}, s32[2]{0:T(128)S(1)}, bf16[1024,2,384]{2,1,0:T(2,128)(2,1)}, /*in...) while((s32[]{:T(128)}, f32[2,6,64]{2,1,0:T(8,128)S(1)}, ...), condition=%wide.region_3.4_spmd.clone, body=%wide.region_0.3_spmd.clone.sunk | while | flops 26350084 | bytes 3680950 | solution.py:53
  167.2 1.3 constant_dynamic-slice_fusion.11
  169.8 1.3 constant_dynamic-slice_fusion.11
  172.4 1.3 constant_dynamic-slice_fusion.11
  175.0 1.3 constant_dynamic-slice_fusion.11
  178.6 8.7 %copy.65 = bf16[1024,2,768]{0,2,1:T(8,128)(2,1)} copy(bf16[1024,2,768]{2,1,0:T(2,128)(2,1)} %all-gather.7.cloned.1.call-done) | data formatting | bytes 6291456
  187.4 7.2 while.61
  187.4 1.2 constant_dynamic-slice_fusion.12
  189.2 1.2 constant_dynamic-slice_fusion.12
  191.0 1.2 constant_dynamic-slice_fusion.12
  192.8 1.2 constant_dynamic-slice_fusion.12
  197.5 8.7 reduce-scatter.17.cloned.1.call-done
  207.2 1.1 multiply_reduce_fusion.7
  209.8 5.3 all_gather.88
  215.1 35.5 %all-gather.11.cloned.1.call-done = bf16[768,1536]{1,0:T(8,128)(2,1)} async-done(((bf16[48,1536]{1,0:T(8,128)(2,1)}), bf16[768,1536]{1,0:T(8,128)(2,1)}) %all-gather.11.cloned.1.call-update) | async-done | bytes 2359312 | tf_op jit(solution)/shard_map/all_gather | solution.py:86
  250.7 4.8 multiply_convert_fusion
  255.6 38.4 %all-gather.13.cloned.1.call-done = bf16[1536,768]{0,1:T(8,128)(2,1)} async-done(((bf16[1536,48]{0,1:T(8,128)(2,1)}), bf16[1536,768]{0,1:T(8,128)(2,1)}) %all-gather.13.cloned.1.call-update) | async-done | bytes 2359312 | tf_op jit(solution)/shard_map/all_gather | solution.py:88
  293.9 3.2 convolution_convert_fusion.1
  297.5 9.5 %reduce-scatter.19.cloned.1.call-done = bf16[64,768]{1,0:T(8,128)(2,1)} async-done(((bf16[128,768]{1,0:T(8,128)(2,1)}), bf16[64,768]{1,0:T(8,128)(2,1)}) %reduce-scatter.19.cloned.1.call-update) | async-done | bytes 98320 | tf_op jit(solution)/shard_map/reduce_scatter | solution.py:30
  307.1 1.3 fusion.55
  310.9 5.5 all_gather.95
  317.1 2.8 convert_reduce_fusion
  319.9 1.6 convolution_convert_fusion
  325.1 1.7 copy.80
  327.3 26.8 %all_gather.98 = f32[1024,2,6]{2,1,0:T(2,128)} all-gather(f32[64,2,6]{2,1,0:T(2,128)S(1)} %bitcast.168), channel_id=1, replica_groups=mesh['fsdp'=16,'tp'=2] {'fsdp'}, dimensions={0}, use_global_device_ids=true | all-gather | bytes 52224 | tf_op jit(solution)/shard_map/all_gather | solution.py:264
  354.1 2.0 copy.78
  357.2 1.6 multiply_reduce_fusion.3
  358.9 1.1 fusion.53
  360.7 5.7 all_gather.96
  367.4 1.1 reshape.366
  368.5 1.6 reshape.369
  371.0 11.0 %while.62 = (s32[]{:T(128)}, f32[64,2,6,64]{0,3,2,1:T(8,128)S(1)}, bf16[1024,2,768]{0,2,1:T(8,128)(2,1)}, s32[2]{0:T(128)}, bf16[64,2,6,64]{3,0,2,1:T(8,128)(2,1...) while((s32[]{:T(128)}, f32[64,2,6,64]{0,3,2,1:T(8,128)S(1)}, ...), condition=%wide.region_19.20_spmd.clone, body=%wide.region_18.19_spmd.clone.sunk | while | flops 76825352 | bytes 4924637 | solution.py:53
  371.0 1.2 constant_dynamic-slice_fusion.13
  373.7 1.2 constant_dynamic-slice_fusion.13
  376.5 1.2 constant_dynamic-slice_fusion.13
  379.2 1.2 constant_dynamic-slice_fusion.13
  382.6 22.9 %all_gather.100 = f32[1024,2,6]{2,1,0:T(2,128)S(1)} all-gather(f32[64,2,6]{2,1,0:T(2,128)} %copy-done.36), channel_id=1, replica_groups=mesh['fsdp'=16,'tp'=2] {'fsdp'}, dimensions={0}, use_global_device_ids=true | all-gather | bytes 52224 | tf_op jit(solution)/shard_map/all_gather | solution.py:265
  406.0 1.1 fusion.59
  407.0 9.5 %all-gather.17.cloned.1.call-done = bf16[1024,2,384]{2,1,0:T(2,128)(2,1)} async-done(((bf16[64,2,384]{2,1,0:T(2,128)(2,1)}), bf16[1024,2,384]{2,1,0:T(2,128)(2,1)}) %all-gather.17.cloned.1.call-update) | async-done | bytes 1572880 | tf_op jit(solution)/shard_map/all_gather | solution.py:339
  416.5 28.4 %while.63 = (s32[]{:T(128)}, f32[64,2,6,64]{0,3,2,1:T(8,128)S(1)}, f32[64,2,6,64]{0,3,2,1:T(8,128)S(1)}, bf16[1024,2,384]{2,1,0:T(2,128)(2,1)}, bf16[64,2,6,64]{...) while((s32[]{:T(128)}, f32[64,2,6,64]{0,3,2,1:T(8,128)S(1)}, ...), condition=%wide.region_21.22_spmd.clone, body=%wide.region_20.21_spmd.clone.sunk | while | flops 102285704 | bytes 8136460 | solution.py:53
  416.6 1.7 constant_dynamic-slice_fusion.14
  423.7 1.7 constant_dynamic-slice_fusion.14
  430.8 1.7 constant_dynamic-slice_fusion.14
  437.9 1.7 constant_dynamic-slice_fusion.14
  447.9 1.4 copy.87
  449.4 1.4 fusion.60
  451.2 1.4 copy.89
  453.0 1.5 copy.91
  454.6 3.0 fusion.61
  458.6 3.0 fusion.62
  464.8 59.9 %all-reduce.18 = (f32[768]{0:T(1024)S(1)}, f32[768]{0:T(1024)S(1)}, f32[768]{0:T(1024)S(1)}, f32[768]{0:T(1024)S(1)}, f32[768]{0:T(1024)S(1)}, /*index=5*/f32[30...) all-reduce(f32[768]{0:T(1024)S(1)} %dynamic_update_slice.9, ...), channel_id=7, replica_groups=mesh['fsdp'=16,'tp'=2] {'fsdp'}, use_global_device_ids=true, to_apply=%region_25.26.clone | all-reduce | flops 9216 | bytes 73728
  525.4 5.5 all-reduce.19
  532.8 48.2 %reduce-scatter.25.cloned.1.call-done = f32[384,48]{0,1:T(8,128)} async-done(((f32[384,768]{0,1:T(8,128)}), f32[384,48]{0,1:T(8,128)}) %reduce-scatter.25.cloned.1.call-update) | async-done | bytes 73744 | tf_op jit(solution)/shard_map/reduce_scatter | solution.py:386
  581.0 61.3 %reduce-scatter.33.cloned.1.call-done = f32[48,384]{1,0:T(8,128)} async-done(((f32[768,384]{1,0:T(8,128)}), f32[48,384]{1,0:T(8,128)}) %reduce-scatter.33.cloned.1.call-update) | async-done | bytes 73744
  642.3 61.2 %reduce-scatter.35.cloned.1.call-done = f32[48,384]{1,0:T(8,128)} async-done(((f32[768,384]{1,0:T(8,128)}), f32[48,384]{1,0:T(8,128)}) %reduce-scatter.35.cloned.1.call-update) | async-done | bytes 73744
  703.5 78.9 %reduce-scatter.27.cloned.1.call-done = f32[48,1536]{1,0:T(8,128)} async-done(((f32[768,1536]{1,0:T(8,128)}), f32[48,1536]{1,0:T(8,128)}) %reduce-scatter.27.cloned.1.call-update) | async-done | bytes 294928 | tf_op jit(solution)/shard_map/reduce_scatter | solution.py:390
  782.4 79.4 %reduce-scatter.29.cloned.1.call-done = f32[1536,48]{0,1:T(8,128)} async-done(((f32[1536,768]{0,1:T(8,128)}), f32[1536,48]{0,1:T(8,128)}) %reduce-scatter.29.cloned.1.call-update) | async-done | bytes 294928 | tf_op jit(solution)/shard_map/reduce_scatter | solution.py:394
  (408 shorter events, 60.2 us)
Async XLA Ops:
  7.2 32.6 %copy-start.66 = (u32[32]{0:T(128)S(1)}, u32[32]{0:T(128)}, u32[]{:S(2)}) copy-start(u32[32]{0:T(128)} %constant.283) | copy-start | bytes 388
  7.2 34.5 %copy-start.69 = (bf16[48]{0:T(256)(128)(2,1)S(1)}, bf16[48]{0:T(256)(128)(2,1)}, u32[]{:S(2)}) copy-start(bf16[48]{0:T(256)(128)(2,1)} %param.37) | copy-start | bytes 292
  7.2 34.7 %copy-start.70 = (bf16[48]{0:T(256)(128)(2,1)S(1)}, bf16[48]{0:T(256)(128)(2,1)}, u32[]{:S(2)}) copy-start(bf16[48]{0:T(256)(128)(2,1)} %param.36) | copy-start | bytes 292
  7.2 35.0 %copy-start.71 = (bf16[48]{0:T(256)(128)(2,1)S(1)}, bf16[48]{0:T(256)(128)(2,1)}, u32[]{:S(2)}) copy-start(bf16[48]{0:T(256)(128)(2,1)} %param.33) | copy-start | bytes 292
  7.2 35.2 %copy-start.72 = (bf16[48]{0:T(256)(128)(2,1)S(1)}, bf16[48]{0:T(256)(128)(2,1)}, u32[]{:S(2)}) copy-start(bf16[48]{0:T(256)(128)(2,1)} %param.30) | copy-start | bytes 292
  7.2 35.4 %copy-start.73 = (bf16[48]{0:T(256)(128)(2,1)S(1)}, bf16[48]{0:T(256)(128)(2,1)}, u32[]{:S(2)}) copy-start(bf16[48]{0:T(256)(128)(2,1)} %param.35) | copy-start | bytes 292
  7.3 35.6 %copy-start.74 = (bf16[48]{0:T(256)(128)(2,1)S(1)}, bf16[48]{0:T(256)(128)(2,1)}, u32[]{:S(2)}) copy-start(bf16[48]{0:T(256)(128)(2,1)} %param.41) | copy-start | bytes 292
  7.3 35.9 %copy-start.75 = (bf16[48]{0:T(256)(128)(2,1)S(1)}, bf16[48]{0:T(256)(128)(2,1)}, u32[]{:S(2)}) copy-start(bf16[48]{0:T(256)(128)(2,1)} %param.43) | copy-start | bytes 292
  7.3 36.1 %copy-start.76 = (bf16[48]{0:T(256)(128)(2,1)S(1)}, bf16[48]{0:T(256)(128)(2,1)}, u32[]{:S(2)}) copy-start(bf16[48]{0:T(256)(128)(2,1)} %param.42) | copy-start | bytes 292
  7.3 36.3 %copy-start.77 = (bf16[192]{0:T(256)(128)(2,1)S(1)}, bf16[192]{0:T(256)(128)(2,1)}, u32[]{:S(2)}) copy-start(bf16[192]{0:T(256)(128)(2,1)} %param.39) | copy-start | bytes 1156
  7.3 94.8 %copy-start.45 = (bf16[48,384]{1,0:T(8,128)(2,1)S(1)}, bf16[48,384]{1,0:T(8,128)(2,1)}, u32[]{:S(2)}) copy-start(bf16[48,384]{1,0:T(8,128)(2,1)} %param.32) | copy-start | bytes 110596
  7.3 115.9 %copy-start.46 = (bf16[48,384]{1,0:T(8,128)(2,1)S(1)}, bf16[48,384]{1,0:T(8,128)(2,1)}, u32[]{:S(2)}) copy-start(bf16[48,384]{1,0:T(8,128)(2,1)} %param.29) | copy-start | bytes 110596
  7.3 159.9 %all-gather.9.cloned.1.call-start = ((), (), s32[]{:S(2)}) async-start(), calls=%async_computation.11 | async-start | bytes 1671168 | tf_op jit(solution)/shard_map/all_gather | solution.py:172
  38.7 63.3 %copy-start.6 = (bf16[768,384]{1,0:T(8,128)(2,1)}, bf16[768,384]{1,0:T(8,128)(2,1)S(1)}, u32[]{:S(2)}) copy-start(bf16[768,384]{1,0:T(8,128)(2,1)S(1)} %all_gather.77) | copy-start | bytes 1769476
  39.7 138.9 %all-gather.7.cloned.1.call-start = ((), (), s32[]{:S(2)}) async-start(), calls=%async_computation.10 | async-start | bytes 3342336 | tf_op jit(solution)/shard_map/all_gather | solution.py:199
  42.2 103.5 %copy-start.47 = (bf16[384,48]{0,1:T(8,128)(2,1)S(1)}, bf16[384,48]{0,1:T(8,128)(2,1)}, u32[]{:S(2)}) copy-start(bf16[384,48]{0,1:T(8,128)(2,1)} %param.34) | copy-start | bytes 110596
  121.0 46.2 %copy-start.1 = (bf16[768,384]{1,0:T(8,128)(2,1)}, bf16[768,384]{1,0:T(8,128)(2,1)S(1)}, u32[]{:S(2)}) copy-start(bf16[768,384]{1,0:T(8,128)(2,1)S(1)} %all_gather.78) | copy-start | bytes 1769476
  121.0 46.2 %copy-start.42 = (s32[2]{0:T(128)S(1)}, s32[2]{0:T(128)}, u32[]{:S(2)}) copy-start(s32[2]{0:T(128)} %param.28) | copy-start | bytes 28
  123.1 83.1 %reduce-scatter.17.cloned.1.call-start = ((), (), s32[]{:S(2)}) async-start(), calls=%async_computation.12 | async-start | bytes 294912 | tf_op jit(solution)/shard_map/reduce_scatter | solution.py:30
  145.1 22.1 %copy-start.3 = (bf16[768,384]{1,0:T(8,128)(2,1)}, bf16[768,384]{1,0:T(8,128)(2,1)S(1)}, u32[]{:S(2)}) copy-start(bf16[768,384]{1,0:T(8,128)(2,1)S(1)} %all_gather.81) | copy-start | bytes 1769476
  145.4 21.8 %copy-start.28 = (bf16[128,384]{1,0:T(8,128)(2,1)}, bf16[128,384]{1,0:T(8,128)(2,1)S(1)}, u32[]{:S(2)}) copy-start(bf16[128,384]{1,0:T(8,128)(2,1)S(1)} %fusion.40) | copy-start | bytes 294916
  178.6 8.8 %copy-start.18 = (f32[64,2,6,64]{0,3,2,1:T(8,128)S(1)}, f32[64,2,6,64]{0,3,2,1:T(8,128)}, u32[]{:S(2)}) copy-start(f32[64,2,6,64]{0,3,2,1:T(8,128)} %custom-call.2) | copy-start | bytes 589828
  187.4 7.7 copy-start.5
  194.6 56.1 %copy-start.19 = (f32[64,2,6,64]{0,3,2,1:T(8,128)}, f32[64,2,6,64]{0,3,2,1:T(8,128)S(1)}, u32[]{:S(2)}) copy-start(f32[64,2,6,64]{0,3,2,1:T(8,128)S(1)} %get-tuple-element.547) | copy-start | bytes 589828
  194.6 102.7 %copy-start.43 = (s32[2]{0:T(128)}, s32[2]{0:T(128)S(1)}, u32[]{:S(2)}) copy-start(s32[2]{0:T(128)S(1)} %get-tuple-element.1319) | copy-start | bytes 28
  195.1 60.4 %copy-start.24 = (bf16[128,384]{1,0:T(8,128)(2,1)}, bf16[128,384]{1,0:T(8,128)(2,1)S(1)}, u32[]{:S(2)}) copy-start(bf16[128,384]{1,0:T(8,128)(2,1)S(1)} %convert_element_type.189) | copy-start | bytes 294916
  196.1 54.5 %all-gather.11.cloned.1.call-start = ((), (), s32[]{:S(2)}) async-start(), calls=%async_computation.13 | async-start | bytes 2506752 | tf_op jit(solution)/shard_map/all_gather | solution.py:86
  196.7 97.2 %all-gather.13.cloned.1.call-start = ((), (), s32[]{:S(2)}) async-start(), calls=%async_computation.14 | async-start | bytes 2506752 | tf_op jit(solution)/shard_map/all_gather | solution.py:88
  197.3 109.7 %reduce-scatter.19.cloned.1.call-start = ((), (), s32[]{:S(2)}) async-start(), calls=%async_computation.15 | async-start | bytes 294912 | tf_op jit(solution)/shard_map/reduce_scatter | solution.py:30
  207.2 99.8 %copy-start.53 = (f32[64]{0:T(128)}, f32[64]{0:T(128)S(1)}, u32[]{:S(2)}) copy-start(f32[64]{0:T(128)S(1)} %broadcast_multiply_fusion.1) | copy-start | bytes 772
  208.8 98.2 %copy-start.56 = (f32[64]{0:T(128)}, f32[64]{0:T(128)S(1)}, u32[]{:S(2)}) copy-start(f32[64]{0:T(128)S(1)} %fusion.50) | copy-start | bytes 772
  215.1 40.4 %copy-start.30 = (bf16[128,768]{1,0:T(8,128)(2,1)}, bf16[128,768]{1,0:T(8,128)(2,1)S(1)}, u32[]{:S(2)}) copy-start(bf16[128,768]{1,0:T(8,128)(2,1)S(1)} %all_gather.88) | copy-start | bytes 589828
  255.5 54.7 %copy-start.9 = (bf16[128,1536]{1,0:T(8,128)(2,1)}, bf16[128,1536]{1,0:T(8,128)(2,1)S(1)}, u32[]{:S(2)}) copy-start(bf16[128,1536]{1,0:T(8,128)(2,1)S(1)} %get-tuple-element.886) | copy-start | bytes 1179652
  255.5 41.7 %copy-start.38 = (bf16[32,2,768]{2,1,0:T(2,128)(2,1)S(1)}, bf16[32,2,768]{2,1,0:T(2,128)(2,1)}, u32[]{:S(2)}) copy-start(bf16[32,2,768]{2,1,0:T(2,128)(2,1)} %param.27) | copy-start | bytes 294916
  255.5 41.8 %copy-start.64 = (bf16[768]{0:T(1024)(128)(2,1)S(1)}, bf16[768]{0:T(1024)(128)(2,1)}, u32[]{:S(2)}) copy-start(bf16[768]{0:T(1024)(128)(2,1)} %get-tuple-element.867) | copy-start | bytes 4612
  255.5 42.0 %copy-start.63 = (bf16[768]{0:T(1024)(128)(2,1)S(1)}, bf16[768]{0:T(1024)(128)(2,1)}, u32[]{:S(2)}) copy-start(bf16[768]{0:T(1024)(128)(2,1)} %get-tuple-element.869) | copy-start | bytes 4612
  255.5 42.0 %copy-start.62 = (bf16[768]{0:T(1024)(128)(2,1)S(1)}, bf16[768]{0:T(1024)(128)(2,1)}, u32[]{:S(2)}) copy-start(bf16[768]{0:T(1024)(128)(2,1)} %get-tuple-element.868) | copy-start | bytes 4612
  255.5 51.5 %copy-start.8 = (bf16[64,768]{1,0:T(8,128)(2,1)S(1)}, bf16[64,768]{1,0:T(8,128)(2,1)}, u32[]{:S(2)}) copy-start(bf16[64,768]{1,0:T(8,128)(2,1)} %reduce-scatter.17.cloned.1.call-done) | copy-start | bytes 294916
  297.2 60.0 %reduce-scatter.21.cloned.1.call-start = ((), (), s32[]{:S(2)}) async-start(), calls=%async_computation.16 | async-start | bytes 294912 | tf_op jit(solution)/shard_map/reduce_scatter | solution.py:30
  297.4 11.9 %copy-start.40 = (f32[32,2]{1,0:T(8,128)}, f32[32,2]{1,0:T(8,128)S(1)}, u32[]{:S(2)}) copy-start(f32[32,2]{1,0:T(8,128)S(1)} %compare_convert_fusion) | copy-start | bytes 772
  307.1 10.0 %copy-start.12 = (bf16[1536,768]{0,1:T(8,128)(2,1)S(1)}, bf16[1536,768]{0,1:T(8,128)(2,1)}, u32[]{:S(2)}) copy-start(bf16[1536,768]{0,1:T(8,128)(2,1)} %all-gather.13.cloned.1.call-done) | copy-start | bytes 7077892
  310.2 47.0 %copy-start.58 = (f32[64]{0:T(128)}, f32[64]{0:T(128)S(1)}, u32[]{:S(2)}) copy-start(f32[64]{0:T(128)S(1)} %negate_multiply_fusion.2) | copy-start | bytes 772
  321.4 34.7 %copy-start.20 = (f32[64,2,6,64]{0,3,2,1:T(8,128)S(1)}, f32[64,2,6,64]{0,3,2,1:T(8,128)}, u32[]{:S(2)}) copy-start(f32[64,2,6,64]{0,3,2,1:T(8,128)} %copy-done.19) | copy-start | bytes 589828
  321.4 85.6 %all-gather.15.cloned.1.call-start = ((), (), s32[]{:S(2)}) async-start(), calls=%async_computation.17 | async-start | bytes 1671168 | tf_op jit(solution)/shard_map/all_gather | solution.py:338
  322.2 94.3 %all-gather.17.cloned.1.call-start = ((), (), s32[]{:S(2)}) async-start(), calls=%async_computation.18 | async-start | bytes 1671168 | tf_op jit(solution)/shard_map/all_gather | solution.py:339
  322.3 34.9 %copy-start.54 = (f32[64]{0:T(128)S(1)}, f32[64]{0:T(128)}, u32[]{:S(2)}) copy-start(f32[64]{0:T(128)} %copy-done.53) | copy-start | bytes 772
  322.3 34.9 %copy-start.57 = (f32[64]{0:T(128)S(1)}, f32[64]{0:T(128)}, u32[]{:S(2)}) copy-start(f32[64]{0:T(128)} %copy-done.56) | copy-start | bytes 772
  324.1 34.8 %copy-start.68 = (f32[64]{0:T(128)S(1)}, f32[64]{0:T(128)}, u32[]{:S(2)}) copy-start(f32[64]{0:T(128)} %copy-done.67) | copy-start | bytes 772
  360.0 10.5 %copy-start.14 = (f32[64,768]{1,0:T(8,128)}, f32[64,768]{1,0:T(8,128)S(1)}, u32[]{:S(2)}) copy-start(f32[64,768]{1,0:T(8,128)S(1)} %get-tuple-element.881) | copy-start | bytes 589828
  360.0 10.1 %copy-start.13 = (f32[64,2,6,64]{3,2,1,0:T(8,128)S(1)}, f32[64,2,6,64]{3,2,1,0:T(8,128)}, u32[]{:S(2)}) copy-start(f32[64,2,6,64]{3,2,1,0:T(8,128)} %copy.69) | copy-start | bytes 589828
  370.5 160.5 %reduce-scatter.23.cloned.1.call-start = ((), (), s32[]{:S(2)}) async-start(), calls=%async_computation.19 | async-start | bytes 294912 | tf_op jit(solution)/shard_map/reduce_scatter | solution.py:30
  382.0 24.0 %copy-start.4 = (bf16[768,384]{1,0:T(8,128)(2,1)S(1)}, bf16[768,384]{1,0:T(8,128)(2,1)}, u32[]{:S(2)}) copy-start(bf16[768,384]{1,0:T(8,128)(2,1)} %copy-done.3) | copy-start | bytes 1769476
  382.0 34.5 %copy-start.44 = (s32[2]{0:T(128)S(1)}, s32[2]{0:T(128)}, u32[]{:S(2)}) copy-start(s32[2]{0:T(128)} %get-tuple-element.1320) | copy-start | bytes 28
  382.0 34.5 %copy-start.78 = (s32[64]{0:T(128)S(1)}, s32[64]{0:T(128)}, u32[]{:S(2)}) copy-start(s32[64]{0:T(128)} %iota_add_fusion.4) | copy-start | bytes 772
  382.1 34.4 %copy-start = (bf16[64,2,6,64]{3,0,2,1:T(8,128)(2,1)S(1)}, bf16[64,2,6,64]{3,0,2,1:T(8,128)(2,1)}, u32[]{:S(2)}) copy-start(bf16[64,2,6,64]{3,0,2,1:T(8,128)(2,1)} %copy.80) | copy-start | bytes 294916
  382.6 33.9 %copy-start.26 = (bf16[128,384]{1,0:T(8,128)(2,1)}, bf16[128,384]{1,0:T(8,128)(2,1)S(1)}, u32[]{:S(2)}) copy-start(bf16[128,384]{1,0:T(8,128)(2,1)S(1)} %convert_element_type.217) | copy-start | bytes 294916
  447.5 85.3 %reduce-scatter.31.cloned.1.call-start = ((), (), s32[]{:S(2)}) async-start(), calls=%async_computation.23 | async-start | bytes 1253376
  449.3 131.7 %reduce-scatter.25.cloned.1.call-start = ((), (), s32[]{:S(2)}) async-start(), calls=%async_computation.20 | async-start | bytes 1253376 | tf_op jit(solution)/shard_map/reduce_scatter | solution.py:386
  450.8 191.6 %reduce-scatter.33.cloned.1.call-start = ((), (), s32[]{:S(2)}) async-start(), calls=%async_computation.24 | async-start | bytes 1253376
  452.6 250.9 %reduce-scatter.35.cloned.1.call-start = ((), (), s32[]{:S(2)}) async-start(), calls=%async_computation.25 | async-start | bytes 1253376
  454.5 327.9 %reduce-scatter.27.cloned.1.call-start = ((), (), s32[]{:S(2)}) async-start(), calls=%async_computation.21 | async-start | bytes 5013504 | tf_op jit(solution)/shard_map/reduce_scatter | solution.py:390
  457.6 404.3 %reduce-scatter.29.cloned.1.call-start = ((), (), s32[]{:S(2)}) async-start(), calls=%async_computation.22 | async-start | bytes 5013504 | tf_op jit(solution)/shard_map/reduce_scatter | solution.py:394
  461.6 69.3 %copy-start.15 = (f32[64,768]{1,0:T(8,128)S(1)}, f32[64,768]{1,0:T(8,128)}, u32[]{:S(2)}) copy-start(f32[64,768]{1,0:T(8,128)} %copy-done.14) | copy-start | bytes 589828
  461.6 69.3 %copy-start.61 = (f32[64]{0:T(128)S(1)}, f32[64]{0:T(128)}, u32[]{:S(2)}) copy-start(f32[64]{0:T(128)} %copy-done.60) | copy-start | bytes 772
  (31 other events, 65.7 us)
Sparse Core Ops, SparseCore 0:
  39.8 37.1 all-gather.8
  123.2 48.4 all-gather.6
  196.3 9.8 reduce-scatter.16
  208.3 42.2 all-gather.10
  252.8 41.0 all-gather.12
  297.3 9.7 reduce-scatter.18
  321.6 10.9 reduce-scatter.20
  334.8 39.9 all-gather.14
  377.1 39.3 all-gather.16
  447.6 9.8 reduce-scatter.22
  461.7 58.0 reduce-scatter.30
  523.9 57.1 reduce-scatter.24
  585.2 57.1 reduce-scatter.32
  646.4 57.0 reduce-scatter.34
  707.8 74.5 reduce-scatter.26
  787.2 74.5 reduce-scatter.28
where the time goes:
time: 870 us; the launch traced here: 868 us
  waiting for transfers between devices  432 us (50%)
  blocking collectives  283 us (33%)
  local copies, waits for them, and re-layouts  70.2 us (8%)
  matrix products  36.2 us (4%)
  other arithmetic  20.1 us (2%)
  between operations  17.9 us (2%)
    unnamed x19, waiting for transfers between devices  124 us
    unnamed x2, blocking collectives  118 us
    reduce_scatter x1, waiting for transfers between devices, local(): lax.psum_scatter(down_weight_grad, 'fsdp', scatter_dimension=1, tiled=True)  79.4 us
    reduce_scatter x1, waiting for transfers between devices, local(): lax.psum_scatter(up_weight_grad, 'fsdp', scatter_dimension=0, tiled=True)  78.9 us
    reduce_scatter x1, waiting for transfers between devices, local(): lax.psum_scatter(out_weight_grad, 'fsdp', scatter_dimension=1, tiled=True)  48.2 us
    all_gather x1, waiting for transfers between devices, local(): lax.all_gather(w_down, 'fsdp', axis=1, tiled=True)  38.4 us
    all_gather x1, waiting for transfers between devices, local(): lax.all_gather(w_up, 'fsdp', axis=0, tiled=True)  35.5 us
    all_gather x1, blocking collectives, local(): lax.all_gather(lse_rows, 'fsdp', axis=0, tiled=True)  26.8 us
  transfers between devices with their start and end apart: 16, of which 10 were waited for; matrix products, arithmetic and copies ran while one was open for 8% of the time, Pallas kernels for 0%

commit v1 on v0

v1 whole, which is shorter than its diff:
```python
import jax
import jax.numpy as jnp
from jax import lax
from jax.sharding import PartitionSpec as P

HD = 64
layer_eps = 1e-12
masked_score = -1e30
AXES = ("fsdp", "tp")
low_type = jnp.bfloat16
wide = jnp.float32

TP_BIT, CORE_BIT, SLOT_BIT, GROUP = 1, 2, 4, 8


def device_count():
    return lax.axis_size("fsdp") * lax.axis_size("tp")


def swap(values, bit):
    return lax.ppermute(values, AXES, [(i, i ^ bit) for i in range(device_count())])


def over_blocks(values):
    total = device_count()
    groups = [list(range(first, total, GROUP)) for first in range(GROUP)]
    return lax.all_to_all(values, AXES, 0, 0, axis_index_groups=groups)


def gather_blocks(values):
    blocks = device_count() // GROUP
    return over_blocks(jnp.broadcast_to(values[None], (blocks,) + values.shape))


def in_order(first_bit, own, other, axis):
    return jnp.where(
        first_bit == 0, jnp.stack([own, other], axis), jnp.stack([other, own], axis)
    )


def gather_group(rows):
    pair = jnp.concatenate([rows, swap(rows, TP_BIT)], 0)
    return jnp.concatenate([pair, swap(pair, CORE_BIT)], 0)


def sum_group(partial):
    half = partial.shape[0] // 2
    kept = partial[:half] + swap(partial[half:].astype(low_type), CORE_BIT).astype(wide)
    quarter = half // 2
    return kept[:quarter] + swap(kept[quarter:].astype(low_type), TP_BIT).astype(wide)


def norm_parts(values):
    centre = values - jnp.mean(values, axis=-1, keepdims=True)
    spread = jnp.mean(centre * centre, axis=-1, keepdims=True)
    scale = lax.rsqrt(spread + layer_eps)
    return centre * scale, scale


def norm_back(grad, normed, scale, gain):
    scaled = grad * gain
    mean_one = jnp.mean(scaled, axis=-1, keepdims=True)
    mean_two = jnp.mean(scaled * normed, axis=-1, keepdims=True)
    return scale * (scaled - mean_one - normed * mean_two)


def local(
    hidden_in,
    cotangent,
    lengths,
    w_query,
    b_query,
    w_key,
    w_value,
    b_value,
    w_out,
    b_out,
    first_gain,
    first_shift,
    w_up,
    b_up,
    w_down,
    b_down,
    second_gain,
    second_shift,
):
    fsdp_index = lax.axis_index("fsdp")
    tp_bit = lax.axis_index("tp")
    core_bit = fsdp_index % 2
    slot_bit = (fsdp_index // 2) % 2
    block = fsdp_index // 4
    blocks = lax.axis_size("fsdp") // 4
    shard_pos, seq_count, width = hidden_in.shape
    rows_here = 2 * shard_pos
    shard_rows = w_query.shape[0]
    head_cols = w_query.shape[1] // 2
    unit_cols = w_up.shape[1] // 2
    heads = head_cols // HD
    score_scale = HD ** (-0.5)

    def halves(weight):
        return weight.reshape(shard_rows, 2, weight.shape[1] // 2)

    def for_core(parts, which):
        return jnp.concatenate(
            [lax.dynamic_index_in_dim(part, which, 1, keepdims=False) for part in parts], 1
        )

    vectors = jnp.concatenate(
        [
            vector.reshape(shard_rows, -1)
            for vector in (
                b_query,
                b_value,
                b_out,
                first_gain,
                first_shift,
                b_down,
                second_gain,
                second_shift,
                b_up,
            )
        ],
        1,
    )
    vectors = jnp.pad(vectors, ((0, 0), (0, 128 - vectors.shape[1])))
    first_parts = [halves(w_query), halves(w_key), halves(w_value)]
    later_parts = [halves(jnp.transpose(w_out)), halves(w_up), halves(jnp.transpose(w_down))]

    def to_core(parts, shared):
        own, other = for_core(parts, core_bit), for_core(parts, 1 - core_bit)
        if shared is not None:
            own = jnp.concatenate([own, shared], 1)
            other = jnp.concatenate([other, shared], 1)
        return in_order(core_bit, own, swap(other, CORE_BIT), 0)

    def full_rows(pieces):
        stacked = in_order(slot_bit, pieces, swap(pieces, SLOT_BIT), 1)
        return stacked.reshape(width, pieces.shape[-1])

    def to_slot(values):
        own = lax.dynamic_index_in_dim(values, slot_bit, 1, keepdims=False)
        other = lax.dynamic_index_in_dim(values, 1 - slot_bit, 1, keepdims=False)
        return jnp.concatenate([own, swap(other, SLOT_BIT)], 0)

    def from_slot(rows):
        returned = swap(rows[shard_pos:], SLOT_BIT)
        return in_order(slot_bit, rows[:shard_pos], returned, 1)

    rows_low = to_slot(hidden_in)
    first_pack = to_core(first_parts, vectors)
    gathered_rows = gather_blocks(rows_low)
    gathered_first = gather_blocks(first_pack.reshape(2 * shard_rows, -1))
    pair_rows = jnp.stack([gathered_rows, swap(gathered_rows, TP_BIT)], 1)
    slot_rows = jnp.stack([pair_rows, swap(pair_rows, CORE_BIT)], 1)
    slot_rows = slot_rows.reshape(-1, width)
    first_full = full_rows(gathered_first)
    later_pack = to_core(later_parts, None).reshape(2 * shard_rows, -1)
    out_piece = gather_blocks(later_pack[:, :head_cols])
    up_piece = gather_blocks(later_pack[:, head_cols : head_cols + unit_cols])
    down_piece = gather_blocks(later_pack[:, head_cols + unit_cols :])
    out_weight = full_rows(out_piece)
    up_weight = full_rows(up_piece)
    down_weight = full_rows(down_piece)
    qkv_weight = first_full[:, : 3 * head_cols]
    vector_cols = first_full[:, 3 * head_cols :].astype(wide)
    (
        query_bias_all,
        value_bias_all,
        out_bias,
        gain_one,
        shift_one,
        down_bias,
        gain_two,
        shift_two,
    ) = [vector_cols[:, i] for i in range(8)]
    up_bias_all = vector_cols[:, 8 : 8 + b_up.shape[0] // shard_rows].reshape(-1)
    quarter = 2 * tp_bit + core_bit
    query_bias = lax.dynamic_slice_in_dim(query_bias_all, quarter * head_cols, head_cols)
    value_bias = lax.dynamic_slice_in_dim(value_bias_all, quarter * head_cols, head_cols)
    up_bias = lax.dynamic_slice_in_dim(up_bias_all, quarter * unit_cols, unit_cols)

    def positions_of(block_ids):
        shape = (block_ids.shape[0], 2, 2, 2, shard_pos)
        iota = lambda dim: lax.broadcasted_iota(jnp.int32, shape, dim)
        place = block_ids.reshape(-1, 1, 1, 1, 1) * 2 + (iota(3) ^ slot_bit)
        place = (place * 2 + (iota(1) ^ core_bit)) * 2 + (iota(2) ^ tp_bit)
        return (place * shard_pos + iota(4)).reshape(-1)

    length = lax.dynamic_index_in_dim(lengths, slot_bit, 0, keepdims=False)
    slot_live = positions_of(jnp.arange(blocks)) < length
    group_live = positions_of(block.reshape(1)) < length
    row_live = group_live[:rows_here]

    group_count = 4 * rows_here
    own_rows = lax.dynamic_slice_in_dim(slot_rows, block * group_count, group_count, 0)

    def as_heads(values):
        return values.reshape(values.shape[0], heads, HD)

    queries = (
        jnp.dot(slot_rows, qkv_weight[:, :head_cols], preferred_element_type=wide) + query_bias
    ).astype(low_type)
    keys = jnp.dot(
        slot_rows, qkv_weight[:, head_cols : 2 * head_cols], preferred_element_type=wide
    ).astype(low_type)
    values = (
        jnp.dot(slot_rows, qkv_weight[:, 2 * head_cols :], preferred_element_type=wide)
        + value_bias
    ).astype(low_type)
    query_all, key_all, value_all = as_heads(queries), as_heads(keys), as_heads(values)

    def own_of(array):
        return lax.dynamic_slice_in_dim(array, block * group_count, group_count, 0)

    query_own, key_own, value_own = own_of(query_all), own_of(key_all), own_of(value_all)
    scores = (
        jnp.einsum("qhd,khd->hqk", query_own, key_all, preferred_element_type=wide) * score_scale
    )
    masked = jnp.where(slot_live[None, None, :], scores, masked_score)
    top = jnp.max(masked, axis=2, keepdims=True)
    total = jnp.sum(jnp.exp(masked - top), axis=2, keepdims=True)
    log_total = top + jnp.log(total)
    weights = jnp.exp(masked - log_total)
    attended = jnp.einsum(
        "hqk,khd->qhd", weights.astype(low_type), value_all, preferred_element_type=wide
    )
    attended_low = attended.reshape(group_count, head_cols).astype(low_type)

    branch_one = sum_group(
        jnp.einsum("th,dh->td", attended_low, out_weight, preferred_element_type=wide)
    )
    first_sum = rows_low.astype(wide) + branch_one + out_bias
    normed_one, scale_one = norm_parts(first_sum)
    first_out = normed_one * gain_one + shift_one
    group_first = gather_group(first_out.astype(low_type))
    preact = jnp.dot(group_first, up_weight, preferred_element_type=wide) + up_bias
    spread = 0.5 * (1.0 + lax.erf(preact * (0.5**0.5)))
    active_low = (preact * spread).astype(low_type)
    branch_two = sum_group(
        jnp.einsum("tf,df->td", active_low, down_weight, preferred_element_type=wide)
    )
    normed_two, scale_two = norm_parts(first_out + branch_two + down_bias)
    output = normed_two * gain_two + shift_two
    grad_out = to_slot(cotangent).astype(wide) * row_live[:, None].astype(wide)
    second_grad = norm_back(grad_out, normed_two, scale_two, gain_two)
    gain_two_grad = jnp.sum(grad_out * normed_two, axis=0)
    shift_two_grad = jnp.sum(grad_out, axis=0)
    branch_two_grad = second_grad.astype(low_type)
    down_bias_grad = jnp.sum(branch_two_grad.astype(wide), axis=0)
    group_two = gather_group(branch_two_grad)
    active_grad = jnp.einsum("td,df->tf", group_two, down_weight, preferred_element_type=wide)
    slope = spread + preact * jnp.exp(-0.5 * preact * preact) * (2.0 * jnp.pi) ** (-0.5)
    preact_grad = (active_grad * slope).astype(low_type)
    up_bias_grad = jnp.sum(preact_grad.astype(wide), axis=0)
    first_out_grad = second_grad + sum_group(
        jnp.einsum("tf,df->td", preact_grad, up_weight, preferred_element_type=wide)
    )

    def sum_weight(partial):
        cols = partial.shape[1]
        split = partial.astype(low_type).reshape(blocks, 2, 2 * shard_rows, cols)
        own = lax.dynamic_index_in_dim(split, slot_bit, 1, keepdims=False)
        other = lax.dynamic_index_in_dim(split, 1 - slot_bit, 1, keepdims=False)
        half = own.astype(wide) + swap(other, SLOT_BIT).astype(wide)
        pieces = over_blocks(half.astype(low_type))
        summed = jnp.sum(pieces.astype(wide), axis=0).reshape(2, shard_rows, cols)
        mine = lax.dynamic_index_in_dim(summed, core_bit, 0, keepdims=False)
        theirs = lax.dynamic_index_in_dim(summed, 1 - core_bit, 0, keepdims=False)
        return in_order(core_bit, mine, swap(theirs, CORE_BIT), 1)

    up_grad = sum_weight(
        jnp.einsum("td,tf->df", group_first, preact_grad, preferred_element_type=wide)
    )
    down_grad = sum_weight(
        jnp.einsum("td,tf->df", group_two, active_low, preferred_element_type=wide)
    )
    gain_one_grad = jnp.sum(first_out_grad * normed_one, axis=0)
    shift_one_grad = jnp.sum(first_out_grad, axis=0)
    first_grad = norm_back(first_out_grad, normed_one, scale_one, gain_one)
    branch_one_grad = first_grad.astype(low_type)
    out_bias_grad = jnp.sum(branch_one_grad.astype(wide), axis=0)
    group_one = gather_group(branch_one_grad)
    attended_grad = jnp.dot(group_one, out_weight, preferred_element_type=wide).astype(low_type)
    grad_all = as_heads(gather_blocks(attended_grad).reshape(-1, head_cols))
    grad_own = as_heads(attended_grad)
    delta = jnp.einsum("qhd,qhd->hq", grad_own.astype(wide), attended)
    row_stats = gather_blocks(jnp.stack([log_total[:, :, 0], delta]))
    row_stats = jnp.moveaxis(row_stats, 0, 2).reshape(2, heads, -1)
    out_grad = sum_weight(
        jnp.einsum("td,th->dh", group_one, attended_low, preferred_element_type=wide)
    )

    weight_grad = jnp.einsum("qhd,khd->hqk", grad_own, value_all, preferred_element_type=wide)
    score_grad = (weights * (weight_grad - delta[:, :, None])).astype(low_type)
    query_grad = (
        jnp.einsum("hqk,khd->qhd", score_grad, key_all, preferred_element_type=wide) * score_scale
    )
    scores_back = (
        jnp.einsum("qhd,khd->hqk", query_all, key_own, preferred_element_type=wide) * score_scale
    )
    weights_back = jnp.where(
        group_live[None, None, :], jnp.exp(scores_back - row_stats[0][:, :, None]), 0.0
    )
    value_grad = jnp.einsum(
        "hqk,qhd->khd", weights_back.astype(low_type), grad_all, preferred_element_type=wide
    )
    back_grad = jnp.einsum("qhd,khd->hqk", grad_all, value_own, preferred_element_type=wide)
    back_score = (weights_back * (back_grad - row_stats[1][:, :, None])).astype(low_type)
    key_grad = (
        jnp.einsum("hqk,qhd->khd", back_score, query_all, preferred_element_type=wide)
        * score_scale
    )
    qkv_grad = jnp.concatenate(
        [
            grad.reshape(group_count, head_cols).astype(low_type)
            for grad in (query_grad, key_grad, value_grad)
        ],
        1,
    )
    qkv_sums = sum_weight(
        jnp.einsum("td,te->de", own_rows, qkv_grad, preferred_element_type=wide)
    )
    hidden_grad = first_grad + sum_group(
        jnp.einsum("te,de->td", qkv_grad, qkv_weight, preferred_element_type=wide)
    )
    bias_sums = jnp.sum(qkv_grad.astype(wide), axis=0)

    def widen(part):
        full = jnp.zeros((4 * part.shape[0],), wide)
        return lax.dynamic_update_slice_in_dim(full, part, quarter * part.shape[0], 0)

    fsdp_count = lax.axis_size("fsdp")
    all_vectors = jnp.concatenate(
        [
            vector.reshape(fsdp_count, -1)
            for vector in (
                widen(bias_sums[:head_cols]),
                widen(bias_sums[2 * head_cols :]),
                out_bias_grad,
                gain_one_grad,
                shift_one_grad,
                down_bias_grad,
                gain_two_grad,
                shift_two_grad,
                widen(up_bias_grad),
            )
        ],
        1,
    )
    vector_sum = jnp.sum(lax.all_to_all(all_vectors, "fsdp", 0, 0, tiled=True), axis=0)
    vector_sum = vector_sum + swap(vector_sum, TP_BIT)
    vector_grads = [
        vector_sum[i * shard_rows : (i + 1) * shard_rows] for i in range(8)
    ] + [vector_sum[8 * shard_rows :]]

    def columns(array):
        return array.reshape(shard_rows, -1)

    query_sum, key_sum, value_sum = [
        columns(qkv_sums[:, :, i * head_cols : (i + 1) * head_cols]) for i in range(3)
    ]
    return (
        from_slot(output.astype(low_type)),
        from_slot(hidden_grad),
        query_sum,
        vector_grads[0],
        key_sum,
        value_sum,
        vector_grads[1],
        jnp.transpose(columns(out_grad)),
        vector_grads[2],
        vector_grads[3],
        vector_grads[4],
        columns(up_grad),
        vector_grads[8],
        jnp.transpose(columns(down_grad)),
        vector_grads[5],
        vector_grads[6],
        vector_grads[7],
    )


def solution(mesh):
    in_specs = (
        P(("fsdp", "tp"), None, None),
        P(("fsdp", "tp"), None, None),
        P(),
        P("fsdp", "tp"),
        P("fsdp"),
        P("fsdp", "tp"),
        P("fsdp", "tp"),
        P("fsdp"),
        P("tp", "fsdp"),
        P("fsdp"),
        P("fsdp"),
        P("fsdp"),
        P("fsdp", "tp"),
        P("fsdp"),
        P("tp", "fsdp"),
        P("fsdp"),
        P("fsdp"),
        P("fsdp"),
    )
    out_specs = (
        P(("fsdp", "tp"), None, None),
        P(("fsdp", "tp"), None, None),
        P("fsdp", "tp"),
        P("fsdp"),
        P("fsdp", "tp"),
        P("fsdp", "tp"),
        P("fsdp"),
        P("tp", "fsdp"),
        P("fsdp"),
        P("fsdp"),
        P("fsdp"),
        P("fsdp", "tp"),
        P("fsdp"),
        P("tp", "fsdp"),
        P("fsdp"),
        P("fsdp"),
        P("fsdp"),
    )
    return jax.shard_map(local, mesh=mesh, in_specs=in_specs, out_specs=out_specs, check_vma=False)
```

time: 870 us -> 316 us (0.36)
  waiting for transfers between devices: 432 us -> 101 us
  blocking collectives: 283 us -> 0 us
  starting transfers between devices: 0.88 us -> 72.8 us
  other arithmetic: 20.1 us -> 36.8 us
  between operations: 17.9 us -> 2.37 us
    reduce_scatter x7 -> x0, waiting for transfers between devices: 225 us -> none  [the longest x1 79.4 us: local(): lax.psum_scatter(down_weight_grad, 'fsdp', scatter_dimension=1, tiled=True)]
    all_gather x10 -> x0, blocking collectives: 159 us -> none  [the longest x1 26.8 us: local(): lax.all_gather(lse_rows, 'fsdp', axis=0, tiled=True)]
    unnamed x19 -> x0, waiting for transfers between devices: 124 us -> none
    unnamed x2 -> x0, blocking collectives: 118 us -> none
    all_gather x6 -> x0, waiting for transfers between devices: 83.4 us -> none  [the longest x1 38.4 us: local(): lax.all_gather(w_down, 'fsdp', axis=1, tiled=True)]
    all_to_all x0 -> x12, waiting for transfers between devices: none -> 71.6 us  [the longest x11 65 us: over_blocks(): return lax.all_to_all(values, AXES, 0, 0, axis_index_groups=groups)]
    all_to_all x0 -> x12, starting transfers between devices: none -> 47.8 us  [the longest x11 44 us: over_blocks(): return lax.all_to_all(values, AXES, 0, 0, axis_index_groups=groups)]
    ppermute x0 -> x35, waiting for transfers between devices: none -> 29.8 us  [swap(): lax.ppermute(values, AXES, [(i, i ^ bit) for i in range(device_count())])]
  transfers between devices with their start and end apart: 16 -> 47, of which waited for: 10 -> 22; matrix products, arithmetic and copies ran while one was open for 8% -> 34% of each run, Pallas kernels for 0% -> 0%
where the time goes in v1:
time: 316 us; the launch traced here: 314 us
  waiting for transfers between devices  101 us (32%)
  starting transfers between devices  72.8 us (23%)
  local copies, waits for them, and re-layouts  64.3 us (20%)
  other arithmetic  36.8 us (12%)
  matrix products  36.1 us (11%)
    all_to_all x11, waiting for transfers between devices, over_blocks(): return lax.all_to_all(values, AXES, 0, 0, axis_index_groups=groups)  65 us
    all_to_all x11, starting transfers between devices, over_blocks(): return lax.all_to_all(values, AXES, 0, 0, axis_index_groups=groups)  44 us
    ppermute x35, waiting for transfers between devices, swap(): lax.ppermute(values, AXES, [(i, i ^ bit) for i in range(device_count())])  29.8 us
    ppermute x35, starting transfers between devices, swap(): lax.ppermute(values, AXES, [(i, i ^ bit) for i in range(device_count())])  25.1 us
    unnamed x174, local copies, waits for them, and re-layouts  13.5 us
    convert_element_type x4, other arithmetic, sum_weight(): pieces = over_blocks(half.astype(low_type))  7.97 us
    select_n x12, other arithmetic, in_order(): jnp.where(first_bit == 0, jnp.stack([own, other], axis), jnp.stack([other...  7.9 us
    reshape x9, local copies, waits for them, and re-layouts, local(): vector.reshape(shard_rows, -1)  6.82 us
  transfers between devices with their start and end apart: 47, of which 22 were waited for; matrix products, arithmetic and copies ran while one was open for 34% of the time, Pallas kernels for 0%

profile of v1, /device:TPU:0, one launch (start us, length us, event | category | flops | bytes accessed | tf_op | source)
XLA Modules:
  0.0 313.9 jit_solution(6611233610843147672)
XLA Ops:
  0.7 2.1 constant_dynamic-slice_fusion.3
  2.9 3.0 collective-permute-start
  14.4 4.9 %all-to-all-start = ((bf16[4,64,768]{2,1,0:T(8,128)(2,1)}), bf16[4,64,768]{2,1,0:T(8,128)(2,1)S(1)}, u32[]{:S(2)}, u32[]{:S(2)}) async-start(bf16[4,64,768]{2,1,0:T(8,128)(2,1)} %broadcast_in_dim.36), calls=%async_computation | async-start | bytes 786432 | tf_op jit(solution)/shard_map/all_to_all | solution.py:27
  21.6 9.1 %all-to-all-done = bf16[4,64,768]{2,1,0:T(8,128)(2,1)S(1)} async-done(((bf16[4,64,768]{2,1,0:T(8,128)(2,1)}), bf16[4,64,768]{2,1,0:T(8,128)(2,1)S(1)}, u32[]{:S(2)}, u32[]{:S(2)}) %all-to-all-start) | async-done | bytes 393248 | tf_op jit(solution)/shard_map/all_to_all | solution.py:27
  31.6 3.5 %all-to-all-start.1 = ((bf16[4,96,704]{2,1,0:T(8,128)(2,1)}), bf16[4,96,704]{2,1,0:T(8,128)(2,1)S(1)}, u32[]{:S(2)}, u32[]{:S(2)}) async-start(bf16[4,96,704]{2,1,0:T(8,128)(2,1)} %broadcast_in_dim.37), calls=%async_computation.1 | async-start | bytes 1179648 | tf_op jit(solution)/shard_map/all_to_all | solution.py:27
  37.6 1.5 collective-permute-start.1
  39.2 9.9 %all-to-all-done.1 = bf16[4,96,704]{2,1,0:T(8,128)(2,1)S(1)} async-done(((bf16[4,96,704]{2,1,0:T(8,128)(2,1)}), bf16[4,96,704]{2,1,0:T(8,128)(2,1)S(1)}, u32[]{:S(2)}, u32[]{:S(2)}) %all-to-all-start.1) | async-done | bytes 540704 | tf_op jit(solution)/shard_map/all_to_all | solution.py:27
  49.8 3.4 %all-to-all-start.2 = ((bf16[4,96,192]{2,1,0:T(8,128)(2,1)}), bf16[4,96,192]{2,1,0:T(8,128)(2,1)S(1)}, u32[]{:S(2)}, u32[]{:S(2)}) async-start(bf16[4,96,192]{2,1,0:T(8,128)(2,1)} %broadcast_in_dim.40), calls=%async_computation.2 | async-start | bytes 393216 | tf_op jit(solution)/shard_map/all_to_all | solution.py:27
  55.2 4.2 %all-to-all-done.2 = bf16[4,96,192]{2,1,0:T(8,128)(2,1)S(1)} async-done(((bf16[4,96,192]{2,1,0:T(8,128)(2,1)}), bf16[4,96,192]{2,1,0:T(8,128)(2,1)S(1)}, u32[]{:S(2)}, u32[]{:S(2)}) %all-to-all-start.2) | async-done | bytes 147488 | tf_op jit(solution)/shard_map/all_to_all | solution.py:27
  62.2 4.1 %all-to-all-start.3 = ((bf16[4,96,768]{2,1,0:T(8,128)(2,1)}), bf16[4,96,768]{2,1,0:T(8,128)(2,1)}, u32[]{:S(2)}, u32[]{:S(2)}) async-start(bf16[4,96,768]{2,1,0:T(8,128)(2,1)} %broadcast_in_dim.41), calls=%async_computation.3 | async-start | bytes 1179648 | tf_op jit(solution)/shard_map/all_to_all | solution.py:27
  66.4 4.4 %collective-permute-done.6 = bf16[4,96,192]{2,1,0:T(8,128)(2,1)S(1)} collective-permute-done((bf16[4,96,192]{2,1,0:T(8,128)(2,1)S(1)}, bf16[4,96,192]{2,1,0:T(8,128)(2,1)S(1)}, u32[]{:S(2)}, u32[]{:S(2)}) %collective-permute-start.6) | collective-permute-done | bytes 147488 | tf_op jit(solution)/shard_map/ppermute | solution.py:21
  72.1 2.0 slice_reduce_fusion.1
  80.9 2.3 all-to-all-done.3
  84.2 4.3 %all-to-all-start.4 = ((bf16[4,96,768]{2,1,0:T(8,128)(2,1)}), bf16[4,96,768]{2,1,0:T(8,128)(2,1)}, u32[]{:S(2)}, u32[]{:S(2)}) async-start(bf16[4,96,768]{2,1,0:T(8,128)(2,1)} %broadcast_in_dim.42), calls=%async_computation.4 | async-start | bytes 1179648 | tf_op jit(solution)/shard_map/all_to_all | solution.py:27
  88.5 3.5 %bitcast_convert_fusion = (bf16[256,3,64]{0,2,1:T(8,128)(2,1)S(1)}, f32[3,64,256]{2,1,0:T(8,128)}) fusion(bf16[1024,3,64]{0,2,1:T(8,128)(2,1)} %bitcast.262, f32[3,256,1024]{2,1,0:T(8,128)} %copy-done, f32[3,256]{1,0:T(4,128)S(1)} %log_add_fusion, pred[1024]{0:T(1024)(128)(4,1)S(1)} %copy-done.59), kind=kOutput, calls=%fused_computation.116 | convolution fusion | flops 103858176 | bytes 3837952 | tf_op jit(solution)/shard_map/hqk,khd->qhd/dot_general | solution.py:225
  95.4 1.6 collective-permute-start.8
  97.0 1.5 collective-permute-start.11
  98.5 6.0 %all-to-all-done.4 = bf16[4,96,768]{2,1,0:T(8,128)(2,1)} async-done(((bf16[4,96,768]{2,1,0:T(8,128)(2,1)}), bf16[4,96,768]{2,1,0:T(8,128)(2,1)}, u32[]{:S(2)}, u32[]{:S(2)}) %all-to-all-start.4) | async-done | bytes 589856 | tf_op jit(solution)/shard_map/all_to_all | solution.py:27
  104.5 1.5 collective-permute-start.12
  108.1 1.6 collective-permute-start.9
  114.1 1.8 maximum_select_fusion.1
  115.9 9.7 %collective-permute-done.12 = bf16[4,96,768]{2,1,0:T(8,128)(2,1)} collective-permute-done((bf16[4,96,768]{2,1,0:T(8,128)(2,1)}, bf16[4,96,768]{2,1,0:T(8,128)(2,1)}, u32[]{:S(2)}, u32[]{:S(2)}) %collective-permute-start.12) | collective-permute-done | bytes 589856 | tf_op jit(solution)/shard_map/ppermute | solution.py:21
  125.6 1.9 maximum_select_fusion.2
  127.5 2.4 multiply_convert_fusion.2
  136.2 3.7 %collective-permute-done.14 = bf16[64,768]{1,0:T(8,128)(2,1)S(1)} collective-permute-done((bf16[64,768]{1,0:T(8,128)(2,1)S(1)}, bf16[64,768]{1,0:T(8,128)(2,1)S(1)}, u32[]{:S(2)}, u32[]{:S(2)}) %collective-permute-start.14) | collective-permute-done | bytes 98336 | tf_op jit(solution)/shard_map/ppermute | solution.py:21
  142.2 1.5 convert_reduce_fusion.6
  144.2 4.1 %collective-permute-done.17 = bf16[64,768]{1,0:T(8,128)(2,1)S(1)} collective-permute-done((bf16[64,768]{1,0:T(8,128)(2,1)S(1)}, bf16[64,768]{1,0:T(8,128)(2,1)S(1)}, u32[]{:S(2)}, u32[]{:S(2)}) %collective-permute-start.17) | collective-permute-done | bytes 98336 | tf_op jit(solution)/shard_map/ppermute | solution.py:21
  149.2 2.3 fusion.49
  154.2 2.3 convert_reduce_fusion.3
  160.0 1.5 collective-permute-start.31
  163.5 2.5 convolution_convert_fusion
  169.4 1.5 multiply_reduce_fusion.1
  170.9 1.5 convert_reduce_fusion.7
  172.4 1.5 collective-permute-start.21
  174.5 2.5 collective-permute-done.21
  182.8 1.5 convolution_convert_fusion.5
  185.7 4.9 %all-to-all-start.5 = ((f32[4,2,3,256]{3,1,2,0:T(2,128)}), f32[4,2,3,256]{3,1,2,0:T(2,128)}, u32[]{:S(2)}, u32[]{:S(2)}) async-start(f32[4,2,3,256]{3,1,2,0:T(2,128)} %broadcast_in_dim.44), calls=%async_computation.5 | async-start | bytes 49152 | tf_op jit(solution)/shard_map/all_to_all | solution.py:27
  190.5 2.0 convolution_convert_fusion.4
  194.0 1.8 constant_dynamic-slice_fusion.1
  195.7 1.8 copy.249
  197.5 1.5 collective-permute-start.29
  199.0 4.1 %fusion.18 = bf16[3,64,256]{2,1,0:T(8,128)(2,1)} fusion(bf16[1024,3,64]{0,2,1:T(8,128)(2,1)S(1)} %bitcast.229, f32[3,256,1024]{2,1,0:T(8,128)} %copy-done, bf16[256,3,64]{0,2,1:T(8,128)(2,1)} %bitcast.261, bf16[1024,3,64]{0,2,1:T(8,128)(2,1)} %bitcast.263, f32[3,256]{1,0:T(4,128)S(1)} %fusion.41, f32[3,256]{1,0:T(4,128)S(1)} %copy-done.57, ...), kind=kOutput, calls=%fused_computation.40 | convolution fusion | flops 206143488 | bytes 4135936 | tf_op jit(solution)/shard_map/hqk,khd->qhd/dot_general | solution.py:297
  204.6 1.6 fusion.33
  206.2 4.8 %all-to-all-start.9 = ((bf16[4,96,192]{2,1,0:T(8,128)(2,1)}), bf16[4,96,192]{2,1,0:T(8,128)(2,1)S(1)}, u32[]{:S(2)}, u32[]{:S(2)}) async-start(bf16[4,96,192]{2,1,0:T(8,128)(2,1)} %fusion.33), calls=%async_computation.9 | async-start | bytes 393216 | tf_op jit(solution)/shard_map/all_to_all | solution.py:27
  211.1 2.2 fusion.15
  213.3 4.0 %all-to-all-done.9 = bf16[4,96,192]{2,1,0:T(8,128)(2,1)S(1)} async-done(((bf16[4,96,192]{2,1,0:T(8,128)(2,1)}), bf16[4,96,192]{2,1,0:T(8,128)(2,1)S(1)}, u32[]{:S(2)}, u32[]{:S(2)}) %all-to-all-start.9) | async-done | bytes 147488 | tf_op jit(solution)/shard_map/all_to_all | solution.py:27
  218.1 3.5 %all-to-all-start.6 = ((bf16[4,256,192]{1,2,0:T(8,128)(2,1)}), bf16[4,256,192]{1,2,0:T(8,128)(2,1)S(1)}, u32[]{:S(2)}, u32[]{:S(2)}) async-start(bf16[4,256,192]{1,2,0:T(8,128)(2,1)} %broadcast_in_dim.46), calls=%async_computation.6 | async-start | bytes 786432 | tf_op jit(solution)/shard_map/all_to_all | solution.py:27
  221.6 2.2 fusion.14
  227.4 3.6 %all-to-all-done.6 = bf16[4,256,192]{1,2,0:T(8,128)(2,1)S(1)} async-done(((bf16[4,256,192]{1,2,0:T(8,128)(2,1)}), bf16[4,256,192]{1,2,0:T(8,128)(2,1)S(1)}, u32[]{:S(2)}, u32[]{:S(2)}) %all-to-all-start.6) | async-done | bytes 393248 | tf_op jit(solution)/shard_map/all_to_all | solution.py:27
  232.3 2.7 fusion.20
  235.1 3.5 %fusion.19 = bf16[3,64,256]{2,1,0:T(8,128)(2,1)S(1)} fusion(bf16[1024,3,64]{0,2,1:T(8,128)(2,1)S(1)} %bitcast.232, f32[3,1024,256]{2,1,0:T(8,128)} %fusion.49, bf16[1024,3,64]{0,2,1:T(8,128)(2,1)} %reshape_reshape.4, f32[3,1024]{1,0:T(4,128)} %bitcast.303, f32[3,1024]{1,0:T(4,128)} %bitcast.302, pred[256]{0:T(512)(128)(4,1)} %reshape.486, ...), kind=kOutput, calls=%fused_computation.41 | convolution fusion | flops 206143488 | bytes 4162052 | tf_op jit(solution)/shard_map/hqk,qhd->khd/dot_general | solution.py:311
  240.7 3.8 %all-to-all-start.8 = ((f32[16,1,576]{2,1,0:T(1,128)}), f32[16,1,576]{2,1,0:T(1,128)S(1)}, u32[]{:S(2)}, u32[]{:S(2)}) async-start(f32[16,1,576]{2,1,0:T(1,128)} %all_to_all.47), calls=%async_computation.8 | async-start | bytes 81920 | tf_op jit(solution)/shard_map/all_to_all | solution.py:351
  244.5 6.7 %all-to-all-done.8 = f32[16,1,576]{2,1,0:T(1,128)S(1)} async-done(((f32[16,1,576]{2,1,0:T(1,128)}), f32[16,1,576]{2,1,0:T(1,128)S(1)}, u32[]{:S(2)}, u32[]{:S(2)}) %all-to-all-start.8) | async-done | bytes 36896 | tf_op jit(solution)/shard_map/all_to_all | solution.py:351
  251.8 3.5 %all-to-all-start.10 = ((bf16[4,96,768]{2,1,0:T(8,128)(2,1)}), bf16[4,96,768]{2,1,0:T(8,128)(2,1)S(1)}, u32[]{:S(2)}, u32[]{:S(2)}) async-start(bf16[4,96,768]{2,1,0:T(8,128)(2,1)} %fusion.15), calls=%async_computation.10 | async-start | bytes 1179648 | tf_op jit(solution)/shard_map/all_to_all | solution.py:27
  257.0 1.6 fusion.23
  260.9 1.5 copy.209
  263.3 1.6 collective-permute-start.28
  268.0 1.6 collective-permute-start.24
  269.6 1.7 all-to-all-done.10
  271.3 3.5 %all-to-all-start.11 = ((bf16[4,96,768]{2,1,0:T(8,128)(2,1)}), bf16[4,96,768]{2,1,0:T(8,128)(2,1)S(1)}, u32[]{:S(2)}, u32[]{:S(2)}) async-start(bf16[4,96,768]{2,1,0:T(8,128)(2,1)} %fusion.14), calls=%async_computation.11 | async-start | bytes 1179648 | tf_op jit(solution)/shard_map/all_to_all | solution.py:27
  277.0 13.1 %all-to-all-done.11 = bf16[4,96,768]{2,1,0:T(8,128)(2,1)S(1)} async-done(((bf16[4,96,768]{2,1,0:T(8,128)(2,1)}), bf16[4,96,768]{2,1,0:T(8,128)(2,1)S(1)}, u32[]{:S(2)}, u32[]{:S(2)}) %all-to-all-start.11) | async-done | bytes 589856 | tf_op jit(solution)/shard_map/all_to_all | solution.py:27
  290.2 1.9 fusion.25
  292.1 3.7 %all-to-all-start.7 = ((bf16[4,96,576]{2,1,0:T(8,128)(2,1)}), bf16[4,96,576]{2,1,0:T(8,128)(2,1)S(1)}, u32[]{:S(2)}, u32[]{:S(2)}) async-start(bf16[4,96,576]{2,1,0:T(8,128)(2,1)} %fusion.25), calls=%async_computation.7 | async-start | bytes 983040 | tf_op jit(solution)/shard_map/all_to_all | solution.py:27
  297.9 10.9 %all-to-all-done.7 = bf16[4,96,576]{2,1,0:T(8,128)(2,1)S(1)} async-done(((bf16[4,96,576]{2,1,0:T(8,128)(2,1)}), bf16[4,96,576]{2,1,0:T(8,128)(2,1)S(1)}, u32[]{:S(2)}, u32[]{:S(2)}) %all-to-all-start.7) | async-done | bytes 442400 | tf_op jit(solution)/shard_map/all_to_all | solution.py:27
  (389 shorter events, 95.6 us)
Async XLA Ops:
  0.7 18.8 %copy-start.52 = (bf16[48,384]{1,0:T(8,128)(2,1)S(1)}, bf16[48,384]{1,0:T(8,128)(2,1)}, u32[]{:S(2)}) copy-start(bf16[48,384]{1,0:T(8,128)(2,1)} %param.23) | copy-start | bytes 110596
  0.7 19.0 %copy-start.53 = (bf16[48,384]{1,0:T(8,128)(2,1)S(1)}, bf16[48,384]{1,0:T(8,128)(2,1)}, u32[]{:S(2)}) copy-start(bf16[48,384]{1,0:T(8,128)(2,1)} %param.21) | copy-start | bytes 110596
  2.9 10.8 %collective-permute-start = (bf16[32,768]{1,0:T(8,128)(2,1)S(1)}, bf16[32,768]{1,0:T(8,128)(2,1)S(1)}, u32[]{:S(2)}, u32[]{:S(2)}) collective-permute-start(bf16[32,768]{1,0:T(8,128)(2,1)S(1)} %bitcast.298), channel_id=1, source_target_pairs={{0,4},{1,5},{2,6},{3,7},{4,0},{5,1},{6,2},{7,3},{8,12},{9,13},{10,... | collective-permute-start | bytes 147464 | tf_op jit(solution)/shard_map/ppermute | solution.py:21
  14.4 16.3 %all-to-all-start = ((bf16[4,64,768]{2,1,0:T(8,128)(2,1)}), bf16[4,64,768]{2,1,0:T(8,128)(2,1)S(1)}, u32[]{:S(2)}, u32[]{:S(2)}) async-start(bf16[4,64,768]{2,1,0:T(8,128)(2,1)} %broadcast_in_dim.36), calls=%async_computation | async-start | bytes 786432 | tf_op jit(solution)/shard_map/all_to_all | solution.py:27
  19.9 15.3 %copy-start.38 = (bf16[1536,48]{0,1:T(8,128)(2,1)S(1)}, bf16[1536,48]{0,1:T(8,128)(2,1)}, u32[]{:S(2)}) copy-start(bf16[1536,48]{0,1:T(8,128)(2,1)} %param.32) | copy-start | bytes 442372
  20.1 15.2 %copy-start.39 = (bf16[48,1536]{1,0:T(8,128)(2,1)S(1)}, bf16[48,1536]{1,0:T(8,128)(2,1)}, u32[]{:S(2)}) copy-start(bf16[48,1536]{1,0:T(8,128)(2,1)} %param.30) | copy-start | bytes 442372
  20.2 1.3 collective-permute-start.3
  31.6 17.5 %all-to-all-start.1 = ((bf16[4,96,704]{2,1,0:T(8,128)(2,1)}), bf16[4,96,704]{2,1,0:T(8,128)(2,1)S(1)}, u32[]{:S(2)}, u32[]{:S(2)}) async-start(bf16[4,96,704]{2,1,0:T(8,128)(2,1)} %broadcast_in_dim.37), calls=%async_computation.1 | async-start | bytes 1179648 | tf_op jit(solution)/shard_map/all_to_all | solution.py:27
  36.1 3.0 collective-permute-start.5
  36.2 25.0 %copy-start.65 = (s32[2]{0:T(128)}, s32[2]{0:T(128)S(1)}, u32[]{:S(2)}) copy-start(s32[2]{0:T(128)S(1)} %get-tuple-element.230) | copy-start | bytes 28
  36.2 25.0 %copy-start.67 = (s32[2]{0:T(128)}, s32[2]{0:T(128)S(1)}, u32[]{:S(2)}) copy-start(s32[2]{0:T(128)S(1)} %get-tuple-element.231) | copy-start | bytes 28
  37.6 22.3 %collective-permute-start.1 = (bf16[4,64,768]{2,1,0:T(8,128)(2,1)S(1)}, bf16[4,64,768]{2,1,0:T(8,128)(2,1)S(1)}, u32[]{:S(2)}, u32[]{:S(2)}) collective-permute-start(bf16[4,64,768]{2,1,0:T(8,128)(2,1)S(1)} %all-to-all-done), channel_id=1, source_target_pairs={{0,1},{1,0},{2,3},{3,2},{4,5},{5,4},{6,7},{7,6},{8,9},{9,8},{10,11... | collective-permute-start | bytes 1179656 | tf_op jit(solution)/shard_map/ppermute | solution.py:21
  49.8 9.6 %all-to-all-start.2 = ((bf16[4,96,192]{2,1,0:T(8,128)(2,1)}), bf16[4,96,192]{2,1,0:T(8,128)(2,1)S(1)}, u32[]{:S(2)}, u32[]{:S(2)}) async-start(bf16[4,96,192]{2,1,0:T(8,128)(2,1)} %broadcast_in_dim.40), calls=%async_computation.2 | async-start | bytes 393216 | tf_op jit(solution)/shard_map/all_to_all | solution.py:27
  53.2 18.5 %collective-permute-start.4 = (bf16[4,96,704]{2,1,0:T(8,128)(2,1)S(1)}, bf16[4,96,704]{2,1,0:T(8,128)(2,1)S(1)}, u32[]{:S(2)}, u32[]{:S(2)}) collective-permute-start(bf16[4,96,704]{2,1,0:T(8,128)(2,1)S(1)} %all-to-all-done.1), channel_id=1, source_target_pairs={{0,4},{1,5},{2,6},{3,7},{4,0},{5,1},{6,2},{7,3},{8,12},{9,13},{10,... | collective-permute-start | bytes 1622024 | tf_op jit(solution)/shard_map/ppermute | solution.py:21
  59.4 11.4 %collective-permute-start.6 = (bf16[4,96,192]{2,1,0:T(8,128)(2,1)S(1)}, bf16[4,96,192]{2,1,0:T(8,128)(2,1)S(1)}, u32[]{:S(2)}, u32[]{:S(2)}) collective-permute-start(bf16[4,96,192]{2,1,0:T(8,128)(2,1)S(1)} %all-to-all-done.2), channel_id=1, source_target_pairs={{0,4},{1,5},{2,6},{3,7},{4,0},{5,1},{6,2},{7,3},{8,12},{9,13},{10,... | collective-permute-start | bytes 442376 | tf_op jit(solution)/shard_map/ppermute | solution.py:21
  61.2 13.1 %collective-permute-start.2 = (bf16[4,2,64,768]{3,2,1,0:T(8,128)(2,1)}, bf16[4,2,64,768]{3,2,1,0:T(8,128)(2,1)}, u32[]{:S(2)}, u32[]{:S(2)}) collective-permute-start(bf16[4,2,64,768]{3,2,1,0:T(8,128)(2,1)} %get-tuple-element.161), channel_id=1, source_target_pairs={{0,2},{1,3},{2,0},{3,1},{4,6},{5,7},{6,4},{7,5},{8,10},{9,11},{10,... | collective-permute-start | bytes 2359304 | tf_op jit(solution)/shard_map/ppermute | solution.py:21
  62.2 21.1 %all-to-all-start.3 = ((bf16[4,96,768]{2,1,0:T(8,128)(2,1)}), bf16[4,96,768]{2,1,0:T(8,128)(2,1)}, u32[]{:S(2)}, u32[]{:S(2)}) async-start(bf16[4,96,768]{2,1,0:T(8,128)(2,1)} %broadcast_in_dim.41), calls=%async_computation.3 | async-start | bytes 1179648 | tf_op jit(solution)/shard_map/all_to_all | solution.py:27
  84.2 20.3 %all-to-all-start.4 = ((bf16[4,96,768]{2,1,0:T(8,128)(2,1)}), bf16[4,96,768]{2,1,0:T(8,128)(2,1)}, u32[]{:S(2)}, u32[]{:S(2)}) async-start(bf16[4,96,768]{2,1,0:T(8,128)(2,1)} %broadcast_in_dim.42), calls=%async_computation.4 | async-start | bytes 1179648 | tf_op jit(solution)/shard_map/all_to_all | solution.py:27
  92.1 14.5 %copy-start.36 = (bf16[32,768]{1,0:T(8,128)(2,1)S(1)}, bf16[32,768]{1,0:T(8,128)(2,1)}, u32[]{:S(2)}) copy-start(bf16[32,768]{1,0:T(8,128)(2,1)} %copy-done.35) | copy-start | bytes 147460
  93.0 16.6 %copy-start.25 = (bf16[32,1,768]{2,1,0:T(2,128)(2,1)S(1)}, bf16[32,1,768]{2,1,0:T(2,128)(2,1)}, u32[]{:S(2)}) copy-start(bf16[32,1,768]{2,1,0:T(2,128)(2,1)} %get-tuple-element.189) | copy-start | bytes 147460
  93.1 1.5 collective-permute-start.7
  95.4 10.6 %collective-permute-start.8 = (bf16[64,768]{1,0:T(8,128)(2,1)S(1)}, bf16[64,768]{1,0:T(8,128)(2,1)S(1)}, u32[]{:S(2)}, u32[]{:S(2)}) collective-permute-start(bf16[64,768]{1,0:T(8,128)(2,1)S(1)} %slice.326), channel_id=1, source_target_pairs={{0,1},{1,0},{2,3},{3,2},{4,5},{5,4},{6,7},{7,6},{8,9},{9,8},{10,11... | collective-permute-start | bytes 294920 | tf_op jit(solution)/shard_map/ppermute | solution.py:21
  97.0 17.1 %collective-permute-start.11 = (bf16[4,96,768]{2,1,0:T(8,128)(2,1)}, bf16[4,96,768]{2,1,0:T(8,128)(2,1)}, u32[]{:S(2)}, u32[]{:S(2)}) collective-permute-start(bf16[4,96,768]{2,1,0:T(8,128)(2,1)} %all-to-all-done.3), channel_id=1, source_target_pairs={{0,4},{1,5},{2,6},{3,7},{4,0},{5,1},{6,2},{7,3},{8,12},{9,13},{10,... | collective-permute-start | bytes 1769480 | tf_op jit(solution)/shard_map/ppermute | solution.py:21
  104.5 21.1 %collective-permute-start.12 = (bf16[4,96,768]{2,1,0:T(8,128)(2,1)}, bf16[4,96,768]{2,1,0:T(8,128)(2,1)}, u32[]{:S(2)}, u32[]{:S(2)}) collective-permute-start(bf16[4,96,768]{2,1,0:T(8,128)(2,1)} %all-to-all-done.4), channel_id=1, source_target_pairs={{0,4},{1,5},{2,6},{3,7},{4,0},{5,1},{6,2},{7,3},{8,12},{9,13},{10,... | collective-permute-start | bytes 1769480 | tf_op jit(solution)/shard_map/ppermute | solution.py:21
  108.1 19.4 %copy-start.26 = (bf16[64,768]{1,0:T(8,128)(2,1)}, bf16[64,768]{1,0:T(8,128)(2,1)S(1)}, u32[]{:S(2)}) copy-start(bf16[64,768]{1,0:T(8,128)(2,1)S(1)} %fusion.45) | copy-start | bytes 294916
  108.1 5.0 %collective-permute-start.9 = (bf16[64,768]{1,0:T(8,128)(2,1)S(1)}, bf16[64,768]{1,0:T(8,128)(2,1)}, u32[]{:S(2)}, u32[]{:S(2)}) collective-permute-start(bf16[64,768]{1,0:T(8,128)(2,1)S(1)} %fusion.45), channel_id=1, source_target_pairs={{0,1},{1,0},{2,3},{3,2},{4,5},{5,4},{6,7},{7,6},{8,9},{9,8},{10,11... | collective-permute-start | bytes 294920 | tf_op jit(solution)/shard_map/ppermute | solution.py:21
  110.3 30.8 %collective-permute-start.16 = (bf16[32,768]{1,0:T(8,128)(2,1)}, bf16[32,768]{1,0:T(8,128)(2,1)}, u32[]{:S(2)}, u32[]{:S(2)}) collective-permute-start(bf16[32,768]{1,0:T(8,128)(2,1)} %bitcast.197), channel_id=1, source_target_pairs={{0,4},{1,5},{2,6},{3,7},{4,0},{5,1},{6,2},{7,3},{8,12},{9,13},{10,... | collective-permute-start | bytes 147464 | tf_op jit(solution)/shard_map/ppermute | solution.py:21
  114.0 13.5 %collective-permute-start.10 = (bf16[128,768]{1,0:T(8,128)(2,1)S(1)}, bf16[128,768]{1,0:T(8,128)(2,1)S(1)}, u32[]{:S(2)}, u32[]{:S(2)}) collective-permute-start(bf16[128,768]{1,0:T(8,128)(2,1)S(1)} %pad_maximum_fusion.10), channel_id=1, source_target_pairs={{0,2},{1,3},{2,0},{3,1},{4,6},{5,7},{6,4},{7,5},{8,10},{9,11},{10,... | collective-permute-start | bytes 589832 | tf_op jit(solution)/shard_map/ppermute | solution.py:21
  115.9 14.0 %copy-start.1 = (bf16[4,2,96,768]{3,2,1,0:T(8,128)(2,1)}, bf16[4,2,96,768]{3,2,1,0:T(8,128)(2,1)S(1)}, u32[]{:S(2)}) copy-start(bf16[4,2,96,768]{3,2,1,0:T(8,128)(2,1)S(1)} %maximum_select_fusion.1) | copy-start | bytes 3538948
  132.1 1.8 collective-permute-start.13
  133.4 15.7 %copy-start.7 = (bf16[1024,192]{0,1:T(8,128)(2,1)S(1)}, bf16[1024,192]{0,1:T(8,128)(2,1)}, u32[]{:S(2)}) copy-start(bf16[1024,192]{0,1:T(8,128)(2,1)} %copy-done.6) | copy-start | bytes 1179652
  133.4 15.7 %copy-start.9 = (bf16[1024,192]{0,1:T(8,128)(2,1)S(1)}, bf16[1024,192]{0,1:T(8,128)(2,1)}, u32[]{:S(2)}) copy-start(bf16[1024,192]{0,1:T(8,128)(2,1)} %copy-done.8) | copy-start | bytes 1179652
  135.0 5.0 %collective-permute-start.14 = (bf16[64,768]{1,0:T(8,128)(2,1)S(1)}, bf16[64,768]{1,0:T(8,128)(2,1)S(1)}, u32[]{:S(2)}, u32[]{:S(2)}) collective-permute-start(bf16[64,768]{1,0:T(8,128)(2,1)S(1)} %slice.325), channel_id=1, source_target_pairs={{0,1},{1,0},{2,3},{3,2},{4,5},{5,4},{6,7},{7,6},{8,9},{9,8},{10,11... | collective-permute-start | bytes 294920 | tf_op jit(solution)/shard_map/ppermute | solution.py:21
  136.2 12.9 %copy-start.63 = (f32[64]{0:T(128)}, f32[64]{0:T(128)S(1)}, u32[]{:S(2)}) copy-start(f32[64]{0:T(128)S(1)} %slice_convert_fusion.9) | copy-start | bytes 772
  143.7 4.6 %collective-permute-start.17 = (bf16[64,768]{1,0:T(8,128)(2,1)S(1)}, bf16[64,768]{1,0:T(8,128)(2,1)S(1)}, u32[]{:S(2)}, u32[]{:S(2)}) collective-permute-start(bf16[64,768]{1,0:T(8,128)(2,1)S(1)} %get-tuple-element.151), channel_id=1, source_target_pairs={{0,1},{1,0},{2,3},{3,2},{4,5},{5,4},{6,7},{7,6},{8,9},{9,8},{10,11... | collective-permute-start | bytes 294920 | tf_op jit(solution)/shard_map/ppermute | solution.py:21
  149.1 5.1 %collective-permute-start.18 = (bf16[128,768]{1,0:T(8,128)(2,1)}, bf16[128,768]{1,0:T(8,128)(2,1)}, u32[]{:S(2)}, u32[]{:S(2)}) collective-permute-start(bf16[128,768]{1,0:T(8,128)(2,1)} %pad_maximum_fusion.11), channel_id=1, source_target_pairs={{0,2},{1,3},{2,0},{3,1},{4,6},{5,7},{6,4},{7,5},{8,10},{9,11},{10,... | collective-permute-start | bytes 589832 | tf_op jit(solution)/shard_map/ppermute | solution.py:21
  157.1 4.4 %collective-permute-start.19 = (bf16[128,768]{1,0:T(8,128)(2,1)S(1)}, bf16[128,768]{1,0:T(8,128)(2,1)S(1)}, u32[]{:S(2)}, u32[]{:S(2)}) collective-permute-start(bf16[128,768]{1,0:T(8,128)(2,1)S(1)} %slice.320), channel_id=1, source_target_pairs={{0,2},{1,3},{2,0},{3,1},{4,6},{5,7},{6,4},{7,5},{8,10},{9,11},{10,... | collective-permute-start | bytes 589832 | tf_op jit(solution)/shard_map/ppermute | solution.py:21
  160.0 51.0 %collective-permute-start.31 = (bf16[4,96,768]{2,1,0:T(8,128)(2,1)}, bf16[4,96,768]{2,1,0:T(8,128)(2,1)}, u32[]{:S(2)}, u32[]{:S(2)}) collective-permute-start(bf16[4,96,768]{2,1,0:T(8,128)(2,1)} %dynamic-slice_bitcast_fusion.1), channel_id=1, source_target_pairs={{0,4},{1,5},{2,6},{3,7},{4,0},{5,1},{6,2},{7,3},{8,12},{9,13},{10,... | collective-permute-start | bytes 1769480 | tf_op jit(solution)/shard_map/ppermute | solution.py:21
  163.0 6.5 %collective-permute-start.20 = (bf16[64,768]{1,0:T(8,128)(2,1)}, bf16[64,768]{1,0:T(8,128)(2,1)}, u32[]{:S(2)}, u32[]{:S(2)}) collective-permute-start(bf16[64,768]{1,0:T(8,128)(2,1)} %slice.324), channel_id=1, source_target_pairs={{0,1},{1,0},{2,3},{3,2},{4,5},{5,4},{6,7},{7,6},{8,9},{9,8},{10,11... | collective-permute-start | bytes 294920 | tf_op jit(solution)/shard_map/ppermute | solution.py:21
  172.4 4.6 %collective-permute-start.21 = (bf16[64,768]{1,0:T(8,128)(2,1)S(1)}, bf16[64,768]{1,0:T(8,128)(2,1)S(1)}, u32[]{:S(2)}, u32[]{:S(2)}) collective-permute-start(bf16[64,768]{1,0:T(8,128)(2,1)S(1)} %get-tuple-element.153), channel_id=1, source_target_pairs={{0,1},{1,0},{2,3},{3,2},{4,5},{5,4},{6,7},{7,6},{8,9},{9,8},{10,11... | collective-permute-start | bytes 294920 | tf_op jit(solution)/shard_map/ppermute | solution.py:21
  174.0 7.2 %collective-permute-start.15 = (bf16[32,768]{1,0:T(8,128)(2,1)S(1)}, bf16[32,768]{1,0:T(8,128)(2,1)}, u32[]{:S(2)}, u32[]{:S(2)}) collective-permute-start(bf16[32,768]{1,0:T(8,128)(2,1)S(1)} %get-tuple-element.191), channel_id=1, source_target_pairs={{0,4},{1,5},{2,6},{3,7},{4,0},{5,1},{6,2},{7,3},{8,12},{9,13},{10,... | collective-permute-start | bytes 147464 | tf_op jit(solution)/shard_map/ppermute | solution.py:21
  177.7 5.1 %collective-permute-start.22 = (bf16[128,768]{1,0:T(8,128)(2,1)}, bf16[128,768]{1,0:T(8,128)(2,1)}, u32[]{:S(2)}, u32[]{:S(2)}) collective-permute-start(bf16[128,768]{1,0:T(8,128)(2,1)} %pad_maximum_fusion.12), channel_id=1, source_target_pairs={{0,2},{1,3},{2,0},{3,1},{4,6},{5,7},{6,4},{7,5},{8,10},{9,11},{10,... | collective-permute-start | bytes 589832 | tf_op jit(solution)/shard_map/ppermute | solution.py:21
  178.6 42.9 %collective-permute-start.33 = (bf16[4,96,768]{2,1,0:T(8,128)(2,1)}, bf16[4,96,768]{2,1,0:T(8,128)(2,1)}, u32[]{:S(2)}, u32[]{:S(2)}) collective-permute-start(bf16[4,96,768]{2,1,0:T(8,128)(2,1)} %dynamic-slice_bitcast_fusion), channel_id=1, source_target_pairs={{0,4},{1,5},{2,6},{3,7},{4,0},{5,1},{6,2},{7,3},{8,12},{9,13},{10,... | collective-permute-start | bytes 1769480 | tf_op jit(solution)/shard_map/ppermute | solution.py:21
  185.7 20.6 %all-to-all-start.5 = ((f32[4,2,3,256]{3,1,2,0:T(2,128)}), f32[4,2,3,256]{3,1,2,0:T(2,128)}, u32[]{:S(2)}, u32[]{:S(2)}) async-start(f32[4,2,3,256]{3,1,2,0:T(2,128)} %broadcast_in_dim.44), calls=%async_computation.5 | async-start | bytes 49152 | tf_op jit(solution)/shard_map/all_to_all | solution.py:27
  197.5 7.1 %collective-permute-start.29 = (bf16[4,96,192]{2,1,0:T(8,128)(2,1)}, bf16[4,96,192]{2,1,0:T(8,128)(2,1)}, u32[]{:S(2)}, u32[]{:S(2)}) collective-permute-start(bf16[4,96,192]{2,1,0:T(8,128)(2,1)} %bitcast.71), channel_id=1, source_target_pairs={{0,4},{1,5},{2,6},{3,7},{4,0},{5,1},{6,2},{7,3},{8,12},{9,13},{10,... | collective-permute-start | bytes 442376 | tf_op jit(solution)/shard_map/ppermute | solution.py:21
  203.1 14.2 %copy-start.31 = (bf16[256,192]{0,1:T(8,128)(2,1)S(1)}, bf16[256,192]{0,1:T(8,128)(2,1)}, u32[]{:S(2)}) copy-start(bf16[256,192]{0,1:T(8,128)(2,1)} %copy-done.30) | copy-start | bytes 294916
  206.2 11.1 %all-to-all-start.9 = ((bf16[4,96,192]{2,1,0:T(8,128)(2,1)}), bf16[4,96,192]{2,1,0:T(8,128)(2,1)S(1)}, u32[]{:S(2)}, u32[]{:S(2)}) async-start(bf16[4,96,192]{2,1,0:T(8,128)(2,1)} %fusion.33), calls=%async_computation.9 | async-start | bytes 393216 | tf_op jit(solution)/shard_map/all_to_all | solution.py:27
  218.1 12.9 %all-to-all-start.6 = ((bf16[4,256,192]{1,2,0:T(8,128)(2,1)}), bf16[4,256,192]{1,2,0:T(8,128)(2,1)S(1)}, u32[]{:S(2)}, u32[]{:S(2)}) async-start(bf16[4,256,192]{1,2,0:T(8,128)(2,1)} %broadcast_in_dim.46), calls=%async_computation.6 | async-start | bytes 786432 | tf_op jit(solution)/shard_map/all_to_all | solution.py:27
  223.8 2.3 collective-permute-start.30
  224.8 10.3 %copy-start.55 = (f32[1,3,4,256]{3,1,2,0:T(4,128)}, f32[1,3,4,256]{3,1,2,0:T(4,128)S(1)}, u32[]{:S(2)}) copy-start(f32[1,3,4,256]{3,1,2,0:T(4,128)S(1)} %copy.250) | copy-start | bytes 36868
  238.6 13.2 %copy-start.45 = (bf16[3,64,256]{2,1,0:T(8,128)(2,1)}, bf16[3,64,256]{2,1,0:T(8,128)(2,1)S(1)}, u32[]{:S(2)}) copy-start(bf16[3,64,256]{2,1,0:T(8,128)(2,1)S(1)} %fusion.19) | copy-start | bytes 294916
  240.7 10.5 %all-to-all-start.8 = ((f32[16,1,576]{2,1,0:T(1,128)}), f32[16,1,576]{2,1,0:T(1,128)S(1)}, u32[]{:S(2)}, u32[]{:S(2)}) async-start(f32[16,1,576]{2,1,0:T(1,128)} %all_to_all.47), calls=%async_computation.8 | async-start | bytes 81920 | tf_op jit(solution)/shard_map/all_to_all | solution.py:351
  251.8 19.4 %all-to-all-start.10 = ((bf16[4,96,768]{2,1,0:T(8,128)(2,1)}), bf16[4,96,768]{2,1,0:T(8,128)(2,1)S(1)}, u32[]{:S(2)}, u32[]{:S(2)}) async-start(bf16[4,96,768]{2,1,0:T(8,128)(2,1)} %fusion.15), calls=%async_computation.10 | async-start | bytes 1179648 | tf_op jit(solution)/shard_map/all_to_all | solution.py:27
  258.6 8.3 %collective-permute-start.23 = (bf16[128,768]{1,0:T(8,128)(2,1)S(1)}, bf16[128,768]{1,0:T(8,128)(2,1)S(1)}, u32[]{:S(2)}, u32[]{:S(2)}) collective-permute-start(bf16[128,768]{1,0:T(8,128)(2,1)S(1)} %slice.319), channel_id=1, source_target_pairs={{0,2},{1,3},{2,0},{3,1},{4,6},{5,7},{6,4},{7,5},{8,10},{9,11},{10,... | collective-permute-start | bytes 589832 | tf_op jit(solution)/shard_map/ppermute | solution.py:21
  263.3 3.7 %collective-permute-start.28 = (f32[576]{0:T(1024)S(1)}, f32[576]{0:T(1024)S(1)}, u32[]{:S(2)}, u32[]{:S(2)}) collective-permute-start(f32[576]{0:T(1024)S(1)} %reduce_sum.216), channel_id=1, source_target_pairs={{0,1},{1,0},{2,3},{3,2},{4,5},{5,4},{6,7},{7,6},{8,9},{9,8},{10,11... | collective-permute-start | bytes 6920 | tf_op jit(solution)/shard_map/ppermute | solution.py:21
  264.8 11.1 %copy-start.18 = (f32[64,768]{1,0:T(8,128)S(1)}, f32[64,768]{1,0:T(8,128)}, u32[]{:S(2)}) copy-start(f32[64,768]{1,0:T(8,128)} %get-tuple-element.154) | copy-start | bytes 589828
  265.7 24.5 %collective-permute-start.26 = (bf16[4,96,576]{2,1,0:T(8,128)(2,1)}, bf16[4,96,576]{2,1,0:T(8,128)(2,1)}, u32[]{:S(2)}, u32[]{:S(2)}) collective-permute-start(bf16[4,96,576]{2,1,0:T(8,128)(2,1)} %dynamic-slice_bitcast_fusion.2), channel_id=1, source_target_pairs={{0,4},{1,5},{2,6},{3,7},{4,0},{5,1},{6,2},{7,3},{8,12},{9,13},{10,... | collective-permute-start | bytes 1327112 | tf_op jit(solution)/shard_map/ppermute | solution.py:21
  268.0 7.9 %collective-permute-start.24 = (bf16[64,768]{1,0:T(8,128)(2,1)S(1)}, bf16[64,768]{1,0:T(8,128)(2,1)S(1)}, u32[]{:S(2)}, u32[]{:S(2)}) collective-permute-start(bf16[64,768]{1,0:T(8,128)(2,1)S(1)} %slice.323), channel_id=1, source_target_pairs={{0,1},{1,0},{2,3},{3,2},{4,5},{5,4},{6,7},{7,6},{8,9},{9,8},{10,11... | collective-permute-start | bytes 294920 | tf_op jit(solution)/shard_map/ppermute | solution.py:21
  271.3 18.9 %all-to-all-start.11 = ((bf16[4,96,768]{2,1,0:T(8,128)(2,1)}), bf16[4,96,768]{2,1,0:T(8,128)(2,1)S(1)}, u32[]{:S(2)}, u32[]{:S(2)}) async-start(bf16[4,96,768]{2,1,0:T(8,128)(2,1)} %fusion.14), calls=%async_computation.11 | async-start | bytes 1179648 | tf_op jit(solution)/shard_map/all_to_all | solution.py:27
  276.0 20.2 %collective-permute-start.25 = (f32[32,768]{1,0:T(8,128)S(1)}, f32[32,768]{1,0:T(8,128)S(1)}, u32[]{:S(2)}, u32[]{:S(2)}) collective-permute-start(f32[32,768]{1,0:T(8,128)S(1)} %get-tuple-element.181), channel_id=1, source_target_pairs={{0,4},{1,5},{2,6},{3,7},{4,0},{5,1},{6,2},{7,3},{8,12},{9,13},{10,... | collective-permute-start | bytes 294920 | tf_op jit(solution)/shard_map/ppermute | solution.py:21
  276.9 20.1 %collective-permute-start.32 = (f32[48,768]{1,0:T(8,128)S(1)}, f32[48,768]{1,0:T(8,128)S(1)}, u32[]{:S(2)}, u32[]{:S(2)}) collective-permute-start(f32[48,768]{1,0:T(8,128)S(1)} %get-tuple-element.172), channel_id=1, source_target_pairs={{0,2},{1,3},{2,0},{3,1},{4,6},{5,7},{6,4},{7,5},{8,10},{9,11},{10,... | collective-permute-start | bytes 442376 | tf_op jit(solution)/shard_map/ppermute | solution.py:21
  292.1 16.7 %all-to-all-start.7 = ((bf16[4,96,576]{2,1,0:T(8,128)(2,1)}), bf16[4,96,576]{2,1,0:T(8,128)(2,1)S(1)}, u32[]{:S(2)}, u32[]{:S(2)}) async-start(bf16[4,96,576]{2,1,0:T(8,128)(2,1)} %fusion.25), calls=%async_computation.7 | async-start | bytes 983040 | tf_op jit(solution)/shard_map/all_to_all | solution.py:27
  296.1 1.4 collective-permute-start.34
  308.9 2.1 collective-permute-start.27
  (58 other events, 213.4 us)

commit v2 on v1

--- a/solution.py
+++ b/solution.py
@@ -1,6 +1,11 @@
+import functools
+import math
+
 import jax
 import jax.numpy as jnp
 from jax import lax
+from jax.experimental import pallas as pl
+from jax.experimental.pallas import tpu as pltpu
 from jax.sharding import PartitionSpec as P
 
 HD = 64
@@ -380,6 +385,801 @@
         vector_grads[7],
     )
 
+BIT_TP, BIT_CORE, BIT_SIDE, BIT_LOW, BIT_HIGH = 1, 2, 4, 8, 16
+TEAM_BITS = (BIT_TP, BIT_LOW, BIT_TP | BIT_LOW)
+PART_BITS = (BIT_SIDE, BIT_CORE, BIT_SIDE | BIT_CORE)
+
+
+class Place:
+    def __init__(self):
+        fsdp = lax.axis_index("fsdp")
+        self.tp = lax.axis_index("tp")
+        self.core = fsdp & 1
+        self.side = (fsdp >> 1) & 1
+        self.low = (fsdp >> 2) & 1
+        self.high = fsdp >> 3
+        self.quarter = 2 * self.tp + self.low
+
+
+def run_kernel(body, outs, *operands, scratch=(), name=None):
+    specs = [
+        pl.BlockSpec(memory_space=pltpu.SMEM if op.dtype == jnp.int32 else pltpu.VMEM)
+        for op in operands
+    ]
+    return pl.pallas_call(
+        body,
+        out_shape=[jax.ShapeDtypeStruct(shape, kind) for shape, kind in outs],
+        in_specs=specs,
+        out_specs=[pl.BlockSpec(memory_space=pltpu.VMEM)] * len(outs),
+        scratch_shapes=[pltpu.VMEM(shape, kind) for shape, kind in scratch],
+        compiler_params=pltpu.CompilerParams(vmem_limit_bytes=8 << 20),
+        name=name,
+    )(*operands)
+
+
+def mul(left, right, left_dim=1, right_dim=0):
+    return lax.dot_general(
+        left, right, (((left_dim,), (right_dim,)), ((), ())), preferred_element_type=wide
+    )
+
+
+def bit_of(index, stride):
+    return (index // stride) & 1
+
+
+def place_of(index, parts, shard_pos):
+    here = Place()
+    shard = index & (shard_pos - 1)
+    high = here.high ^ bit_of(index, shard_pos)
+    tp = here.tp ^ bit_of(index, 2 * shard_pos)
+    low = here.low ^ bit_of(index, 4 * shard_pos)
+    side, core = here.side, here.core
+    if parts:
+        side = side ^ bit_of(index, 8 * shard_pos)
+        core = core ^ bit_of(index, 16 * shard_pos)
+    block = (high * 2 + low) * 4 + side * 2 + core
+    return (block * 2 + tp) * shard_pos + shard
+
+
+def live_rows_of(lengths_ref, index, parts, shard_pos):
+    return place_of(index, parts, shard_pos) < lengths_ref[Place().high]
+
+
+def row_of(chip, core, rows):
+    return pl.ds(pl.multiple_of((2 * chip + core) * rows, 16), rows)
+
+
+def join_rows(own_ref, core_ref, full_ref, rows, cols):
+    core = Place().core
+    for chip in range(own_ref.shape[0]):
+        full_ref[row_of(chip, core, rows), :] = own_ref[chip, 0:rows, cols]
+        full_ref[row_of(chip, 1 - core, rows), :] = core_ref[chip, 0:rows, cols]
+
+
+def join_pieces(piece_refs, full_ref, rows, cols):
+    here = Place()
+    for part, ref in enumerate(piece_refs):
+        side, core = here.side ^ (part & 1), here.core ^ (part >> 1)
+        for inner in range(4):
+            block = (here.high ^ (inner >> 1)) * 2 + (here.low ^ (inner & 1))
+            full_ref[row_of(block * 2 + side, core, rows), :] = ref[inner, :, cols]
+
+
+def split_rows(full_ref, keep_ref, send_ref, rows, cols):
+    core = Place().core
+    width = cols.stop - cols.start
+    for chip in range(keep_ref.shape[0]):
+        keep_ref[chip, :, cols] = full_ref[row_of(chip, core, rows), 0:width]
+        send_ref[chip, :, cols] = full_ref[row_of(chip, 1 - core, rows), 0:width]
+
+
+def pack_kernel(
+    wq_ref, wk_ref, wv_ref, wo_ref, wu_ref, wd_ref,
+    v0_ref, v1_ref, v2_ref, v3_ref, v4_ref, v5_ref, v6_ref, v7_ref, v8_ref,
+    first_ref, own_ref, send_ref, down_ref, down_send_ref,
+):
+    rows = wq_ref.shape[0]
+    head_cols = wq_ref.shape[1] // 2
+    unit_cols = wu_ref.shape[1] // 2
+    for chip in range(first_ref.shape[0]):
+        half = (chip // 2) % 2
+        heads = slice(half * head_cols, (half + 1) * head_cols)
+        for i, ref in enumerate((wq_ref, wk_ref, wv_ref)):
+            first_ref[chip, 0:rows, i * head_cols : (i + 1) * head_cols] = ref[:, heads]
+    vectors = [
+        r[...].astype(wide).reshape(1, rows)
+        for r in (v0_ref, v1_ref, v2_ref, v3_ref, v4_ref, v5_ref, v6_ref, v7_ref)
+    ]
+    block = jnp.concatenate(
+        [
+            jnp.pad(jnp.concatenate(vectors, 0), ((0, 0), (0, 4 * rows - rows))),
+            v8_ref[...].astype(wide).reshape(1, 4 * rows),
+            jnp.zeros((7, 4 * rows), wide),
+        ],
+        0,
+    ).astype(low_type)
+    for chip in range(first_ref.shape[0]):
+        first_ref[chip, rows : rows + 16, 0 : 4 * rows] = block
+    out_rows = jnp.transpose(wo_ref[...].astype(wide)).astype(low_type)
+    down_rows = jnp.transpose(wd_ref[...].astype(wide)).astype(low_type)
+    low = Place().low
+    for half in range(2):
+        heads = slice(half * head_cols, (half + 1) * head_cols)
+        units = slice(half * unit_cols, (half + 1) * unit_cols)
+
+        def put(up_out_ref, down_half_ref):
+            up_out_ref[:, 0:unit_cols] = wu_ref[:, units]
+            up_out_ref[:, unit_cols : unit_cols + head_cols] = out_rows[:, heads]
+            down_half_ref[...] = down_rows[:, units]
+
+        @pl.when(low == half)
+        def _():
+            put(own_ref, down_ref)
+
+        @pl.when(low != half)
+        def _():
+            put(send_ref, down_send_ref)
+
+
+def project_kernel(
+    keep_ref, got_ref, tp_ref, low_ref, both_ref, own_ref, core_ref,
+    rows_ref, query_ref, pair_ref, weight_ref,
+):
+    rows = own_ref.shape[1] - 16
+    head_cols = query_ref.shape[1]
+    join_rows(own_ref, core_ref, weight_ref, rows, slice(None))
+    shard = keep_ref.shape[0]
+    rows_ref[0:shard, :] = keep_ref[...]
+    rows_ref[shard : 2 * shard, :] = got_ref[...]
+    for i, ref in enumerate((tp_ref, low_ref, both_ref)):
+        rows_ref[2 * shard * (i + 1) : 2 * shard * (i + 2), :] = ref[...]
+    here = Place()
+    even = here.core == 0
+    pieces = []
+    for side in range(2):
+        own = own_ref[2 * here.quarter + side, rows : rows + 16, 0:rows].astype(wide)
+        core = core_ref[2 * here.quarter + side, rows : rows + 16, 0:rows].astype(wide)
+        pieces += [jnp.where(even, own, core), jnp.where(even, core, own)]
+    biases = jnp.concatenate(pieces, 1)
+    query_bias, value_bias = biases[0:1], biases[1:2]
+    made = mul(rows_ref[...], weight_ref[...])
+    query_ref[...] = (made[:, 0:head_cols] + query_bias).astype(low_type)
+    pair_ref[:, 0:head_cols] = made[:, head_cols : 2 * head_cols].astype(low_type)
+    pair_ref[:, head_cols:] = (made[:, 2 * head_cols :] + value_bias).astype(low_type)
+
+
+def head_of(array, head):
+    return array[:, head * HD : (head + 1) * HD]
+
+
+def attend_kernel(shard_pos, lengths_ref, query_ref, p0_ref, p1_ref, p2_ref, p3_ref, low_ref, extra_ref):
+    head_cols = query_ref.shape[1]
+    count = query_ref.shape[0]
+    pair = jnp.concatenate([ref[...] for ref in (p0_ref, p1_ref, p2_ref, p3_ref)], 0)
+    keys, values = pair[:, 0:head_cols], pair[:, head_cols:]
+    queries = query_ref[...] * HD ** (-0.5)
+    lanes = lax.broadcasted_iota(jnp.int32, (1, pair.shape[0]), 1)
+    live = live_rows_of(lengths_ref, lanes, True, shard_pos)
+    column = lax.broadcasted_iota(jnp.int32, (count, 128), 1)
+    stats = jnp.zeros((count, 128), wide)
+    parts = []
+    for head in range(head_cols // HD):
+        scores = mul(head_of(queries, head), head_of(keys, head), 1, 1)
+        scores = jnp.where(live, scores, masked_score)
+        top = jnp.max(scores, axis=1, keepdims=True)
+        grown = jnp.exp(scores - top)
+        total = jnp.sum(grown, axis=1, keepdims=True)
+        weights = (grown * (1.0 / total)).astype(low_type)
+        parts.append(mul(weights, head_of(values, head)))
+        log_total = top + jnp.log(total)
+        for level in range(3):
+            piece = log_total.astype(low_type).astype(wide)
+            log_total = log_total - piece
+            stats = jnp.where(column == 3 * head + level, piece, stats)
+    attended = jnp.concatenate(parts, 1).astype(low_type)
+    low_ref[...] = attended
+    extra_ref[:, 0:head_cols] = query_ref[...]
+    extra_ref[:, head_cols : 2 * head_cols] = attended
+    extra_ref[:, 2 * head_cols :] = stats.astype(low_type)
+
+
+def full_kernel(cols, p0_ref, p1_ref, p2_ref, p3_ref, *outs):
+    pieces = (p0_ref, p1_ref, p2_ref, p3_ref)
+    for out_ref, (begin, end) in zip(outs, cols):
+        join_pieces(pieces, out_ref, p0_ref.shape[1], slice(begin, end))
+
+
+def lines_kernel(own_ref, core_ref, vector_ref, bias_ref):
+    here = Place()
+    rows = own_ref.shape[1] - 16
+    even = here.core == 0
+    vectors = []
+    for chip in range(own_ref.shape[0]):
+        own = own_ref[chip, rows : rows + 16, 0:rows].astype(wide)
+        core = core_ref[chip, rows : rows + 16, 0:rows].astype(wide)
+        vectors += [jnp.where(even, own, core), jnp.where(even, core, own)]
+    vector_ref[...] = jnp.concatenate(vectors, 1)[0:8]
+    biases = []
+    for side in range(2):
+        own = own_ref[2 * here.quarter + side, rows : rows + 16, 0 : 4 * rows].astype(wide)
+        core = core_ref[2 * here.quarter + side, rows : rows + 16, 0 : 4 * rows].astype(wide)
+        biases += [jnp.where(even, own, core), jnp.where(even, core, own)]
+    bias_ref[...] = jnp.concatenate(biases, 1)[8:9]
+
+
+def give_out(partial, keep_ref, sends):
+    count = keep_ref.shape[0]
+    keep_ref[...] = partial[0:count]
+    for i, ref in enumerate(sends):
+        ref[...] = partial[(i + 1) * count : (i + 2) * count].astype(low_type)
+
+
+def collect(keep_ref, *got):
+    total = keep_ref[...]
+    for ref in got:
+        total = total + ref[...].astype(wide)
+    return total
+
+
+def out_kernel(low_ref, weight_ref, keep_ref, *sends):
+    give_out(mul(low_ref[...], weight_ref[...], 1, 1), keep_ref, sends)
+
+
+def vector_row(vector_ref, row):
+    return vector_ref[row : row + 1, :]
+
+
+def first_norm_kernel(
+    keep_ref, got1_ref, got2_ref, got3_ref, own_ref, slot_ref, vector_ref,
+    out_ref, low_ref, normed_ref, scale_ref,
+):
+    branch = collect(keep_ref, got1_ref, got2_ref, got3_ref)
+    rows = jnp.concatenate([own_ref[...], slot_ref[...]], 0).astype(wide)
+    normed, scale = norm_parts(rows + branch + vector_row(vector_ref, 2))
+    out = normed * vector_row(vector_ref, 3) + vector_row(vector_ref, 4)
+    out_ref[...] = out
+    low_ref[...] = out.astype(low_type)
+    normed_ref[...] = normed
+    scale_ref[...] = jnp.broadcast_to(scale, scale_ref.shape)
+
+
+def spread_of(values):
+    scaled = jnp.clip(values * (0.5**0.5), -3.832506856900711, 3.832506856900711)
+    square = scaled * scaled
+    top = jnp.full_like(values, 0.00022905065861350646)
+    for term in (0.0034082910107109506, 0.050955695062380861, 0.18520832239976145, 1.128379143519084):
+        top = top * square + term
+    under = jnp.full_like(values, -1.1791602954361697e-7)
+    for term in (
+        0.000023547966471313185,
+        0.0010179625278914885,
+        0.014070470171167667,
+        0.11098505178285362,
+        0.49746925110067538,
+        1.0,
+    ):
+        under = under * square + term
+    return 0.5 + 0.5 * (scaled * top / under)
+
+
+def hidden_kernel(
+    own_ref, got1_ref, got2_ref, got3_ref, up_ref, down_ref, bias_ref,
+    keep_ref, send1_ref, send2_ref, send3_ref, active_ref, slope_ref, rows_ref,
+):
+    rows = jnp.concatenate([r[...] for r in (own_ref, got1_ref, got2_ref, got3_ref)], 0)
+    rows_ref[...] = rows
+    preact = mul(rows, up_ref[...]) + bias_ref[...]
+    spread = spread_of(preact)
+    active = (preact * spread).astype(low_type)
+    active_ref[...] = active
+    slope_ref[...] = spread + preact * jnp.exp(-0.5 * preact * preact) * (2.0 * math.pi) ** (-0.5)
+    give_out(mul(active, down_ref[...], 1, 1), keep_ref, (send1_ref, send2_ref, send3_ref))
+
+
+def second_norm_kernel(
+    lengths_ref, keep_ref, got1_ref, got2_ref, got3_ref, first_ref, own_ref, slot_ref, vector_ref,
+    output_ref, grad_ref, low_ref, sums_ref,
+):
+    shard_pos = own_ref.shape[0]
+    branch = collect(keep_ref, got1_ref, got2_ref, got3_ref)
+    normed, scale = norm_parts(first_ref[...] + branch + vector_row(vector_ref, 5))
+    gain = vector_row(vector_ref, 6)
+    output_ref[...] = (normed * gain + vector_row(vector_ref, 7)).astype(low_type)
+    index = lax.broadcasted_iota(jnp.int32, (2 * shard_pos, 1), 0)
+    live = live_rows_of(lengths_ref, index, False, shard_pos)
+    grad = jnp.concatenate([own_ref[...], slot_ref[...]], 0).astype(wide)
+    grad = jnp.where(live, grad, 0.0)
+    second = norm_back(grad, normed, scale, gain)
+    grad_ref[...] = second
+    low = second.astype(low_type)
+    low_ref[...] = low
+    sums_ref[0:1, :] = jnp.sum(low.astype(wide), axis=0, keepdims=True)
+    sums_ref[1:2, :] = jnp.sum(grad * normed, axis=0, keepdims=True)
+    sums_ref[2:3, :] = jnp.sum(grad, axis=0, keepdims=True)
+
+
+def hidden_back_kernel(
+    own_ref, got1_ref, got2_ref, got3_ref, slope_ref, up_ref, down_ref,
+    keep_ref, send1_ref, send2_ref, send3_ref, pre_ref, rows_ref, sums_ref,
+):
+    rows = jnp.concatenate([r[...] for r in (own_ref, got1_ref, got2_ref, got3_ref)], 0)
+    rows_ref[...] = rows
+    pre = (mul(rows, down_ref[...]) * slope_ref[...]).astype(low_type)
+    pre_ref[...] = pre
+    sums_ref[...] = jnp.sum(pre.astype(wide), axis=0, keepdims=True)
+    give_out(mul(pre, up_ref[...], 1, 1), keep_ref, (send1_ref, send2_ref, send3_ref))
+
+
+def weight_kernel(pairs, extra, *refs):
+    operands = refs[: 2 * pairs + extra]
+    keep_ref, send_ref, full_ref = refs[2 * pairs + extra :]
+    rows = keep_ref.shape[1]
+    begin = 0
+    for i in range(pairs):
+        left, right = operands[2 * i], operands[2 * i + 1]
+        cols = right.shape[1]
+        full_ref[:, 0:cols] = mul(left[...], right[...], 0, 0).astype(low_type)
+        split_rows(full_ref, keep_ref, send_ref, rows, slice(begin, begin + cols))
+        begin += cols
+    if extra:
+        mine, other = operands[-2:]
+        cols = 128
+        total = mine[...] + other[...]
+        total = jnp.concatenate([total, jnp.zeros((cols - total.shape[0], total.shape[1]), wide)], 0)
+        full_ref[:, 0:cols] = jnp.transpose(total).astype(low_type)
+        split_rows(full_ref, keep_ref, send_ref, rows, slice(begin, begin + cols))
+
+
+def fold_kernel(bits, stride, keep_ref, got_ref, *outs):
+    here = Place()
+    own = [getattr(here, bit) for bit in bits]
+    count = outs[0].shape[0]
+    for choice, out_ref in enumerate(outs):
+        for block in range(count):
+            index = block * stride[0]
+            for i, (bit, step) in enumerate(zip(own, stride[1:])):
+                index = index + (bit ^ ((choice >> i) & 1)) * step
+            total = keep_ref[index].astype(wide) + got_ref[index].astype(wide)
+            out_ref[block] = total.astype(out_ref.dtype)
+
+
+def final_fold_kernel(*refs):
+    inputs, (own_ref, send_ref) = refs[:-2], refs[-2:]
+    low = Place().low
+    for choice, out_ref in ((low, own_ref), (1 - low, send_ref)):
+        total = inputs[0][choice].astype(wide)
+        for ref in inputs[1:]:
+            total = total + ref[choice].astype(wide)
+        out_ref[...] = total.astype(out_ref.dtype)
+
+
+def total_kernel(spans, own_ref, got_ref, *outs):
+    even = Place().low == 0
+    for out_ref, (begin, end, turned) in zip(outs, spans):
+        cols = end - begin
+        own = own_ref[:, begin:end]
+        got = got_ref[:, begin:end].astype(wide)
+        if turned is None:
+            out_ref[...] = jnp.transpose(own + got)
+            continue
+        halves = jnp.where(even, own, got), jnp.where(even, got, own)
+        for i, half in enumerate(halves):
+            if turned:
+                out_ref[i * cols : (i + 1) * cols, :] = jnp.transpose(half)
+            else:
+                out_ref[:, i * cols : (i + 1) * cols] = half
+
+
+def first_back_kernel(
+    keep_ref, got1_ref, got2_ref, got3_ref, second_ref, normed_ref, scale_ref, vector_ref,
+    grad_ref, low_ref, sums_ref,
+):
+    grad = second_ref[...] + collect(keep_ref, got1_ref, got2_ref, got3_ref)
+    normed = normed_ref[...]
+    first = norm_back(grad, normed, scale_ref[:, 0:1], vector_row(vector_ref, 3))
+    grad_ref[...] = first
+    low = first.astype(low_type)
+    low_ref[...] = low
+    sums_ref[0:1, :] = jnp.sum(low.astype(wide), axis=0, keepdims=True)
+    sums_ref[1:2, :] = jnp.sum(grad * normed, axis=0, keepdims=True)
+    sums_ref[2:3, :] = jnp.sum(grad, axis=0, keepdims=True)
+
+
+def attended_back_kernel(
+    own_ref, got1_ref, got2_ref, got3_ref, weight_ref, grad_ref, rows_ref, sums_ref
+):
+    rows = jnp.concatenate([r[...] for r in (own_ref, got1_ref, got2_ref, got3_ref)], 0)
+    rows_ref[...] = rows
+    made = mul(rows, weight_ref[...])
+    grad_ref[...] = made.astype(low_type)
+    sums_ref[...] = jnp.sum(made, axis=0, keepdims=True)
+
+
+def stat_of(extra, head_cols, head):
+    base = 2 * head_cols + 3 * head
+    total = extra[:, base : base + 1].astype(wide)
+    for level in (1, 2):
+        total = total + extra[:, base + level : base + level + 1].astype(wide)
+    return total
+
+
+def query_back_kernel(
+    shard_pos, lengths_ref, extra_ref, grad_ref, p0_ref, p1_ref, p2_ref, p3_ref, out_ref, sums_ref
+):
+    head_cols = out_ref.shape[1]
+    pair = jnp.concatenate([ref[...] for ref in (p0_ref, p1_ref, p2_ref, p3_ref)], 0)
+    keys, values = pair[:, 0:head_cols], pair[:, head_cols:]
+    extra, grad = extra_ref[...], grad_ref[...]
+    queries = extra[:, 0:head_cols] * HD ** (-0.5)
+    both = grad.astype(wide) * extra[:, head_cols : 2 * head_cols].astype(wide)
+    lanes = lax.broadcasted_iota(jnp.int32, (1, pair.shape[0]), 1)
+    live = live_rows_of(lengths_ref, lanes, True, shard_pos)
+    parts = []
+    for head in range(head_cols // HD):
+        scores = mul(head_of(queries, head), head_of(keys, head), 1, 1)
+        scores = jnp.where(live, scores, masked_score)
+        weights = jnp.exp(scores - stat_of(extra, head_cols, head))
+        delta = jnp.sum(head_of(both, head), axis=1, keepdims=True)
+        weight_grad = mul(head_of(grad, head), head_of(values, head), 1, 1)
+        score_grad = (weights * (weight_grad - delta)).astype(low_type)
+        parts.append(mul(score_grad, head_of(keys, head)))
+    made = (jnp.concatenate(parts, 1) * HD ** (-0.5)).astype(low_type)
+    out_ref[...] = made
+    sums_ref[...] = jnp.sum(made.astype(wide), axis=0, keepdims=True)
+
+
+def pair_back_kernel(
+    shard_pos, lengths_ref, pair_ref, query_grad_ref, weight_ref,
+    e0_ref, e1_ref, e2_ref, e3_ref, g0_ref, g1_ref, g2_ref, g3_ref,
+    keep_ref, send1_ref, send2_ref, send3_ref, made_ref,
+):
+    head_cols = query_grad_ref.shape[1]
+    pair = pair_ref[...]
+    keys, values = pair[:, 0:head_cols], pair[:, head_cols:]
+    extra = jnp.concatenate([ref[...] for ref in (e0_ref, e1_ref, e2_ref, e3_ref)], 0)
+    grad = jnp.concatenate([ref[...] for ref in (g0_ref, g1_ref, g2_ref, g3_ref)], 0)
+    queries = extra[:, 0:head_cols] * HD ** (-0.5)
+    both = grad.astype(wide) * extra[:, head_cols : 2 * head_cols].astype(wide)
+    lanes = lax.broadcasted_iota(jnp.int32, (1, pair.shape[0]), 1)
+    live = live_rows_of(lengths_ref, lanes, False, shard_pos)
+    key_parts, value_parts = [], []
+    for head in range(head_cols // HD):
+        scores = mul(head_of(queries, head), head_of(keys, head), 1, 1)
+        scores = jnp.where(live, scores, masked_score)
+        weights = jnp.exp(scores - stat_of(extra, head_cols, head))
+        delta = jnp.sum(head_of(both, head), axis=1, keepdims=True)
+        weight_grad = mul(head_of(grad, head), head_of(values, head), 1, 1)
+        score_grad = (weights * (weight_grad - delta)).astype(low_type)
+        key_parts.append(mul(score_grad, head_of(queries, head), 0, 0))
+        value_parts.append(mul(weights.astype(low_type), head_of(grad, head), 0, 0))
+    made = jnp.concatenate([part.astype(low_type) for part in key_parts + value_parts], 1)
+    made_ref[...] = made
+    made = jnp.concatenate([query_grad_ref[...], made], 1)
+    give_out(mul(made, weight_ref[...], 1, 1), keep_ref, (send1_ref, send2_ref, send3_ref))
+
+
+def last_kernel(keep_ref, got1_ref, got2_ref, got3_ref, first_ref, own_ref, send_ref):
+    total = first_ref[...] + collect(keep_ref, got1_ref, got2_ref, got3_ref)
+    count = own_ref.shape[0]
+    own_ref[...] = total[0:count]
+    send_ref[...] = total[count:]
+
+
+def vectors_kernel(shards, query_ref, value_ref, first_ref, second_ref, unit_ref, out_ref):
+    width = out_ref.shape[1] // shards
+    per = shards // 4
+    quarter = Place().quarter
+    out_ref[...] = jnp.zeros_like(out_ref)
+    out_ref[2:5, :] = first_ref[0:3, :]
+    out_ref[5:8, :] = second_ref[0:3, :]
+    for which in range(4):
+
+        @pl.when(quarter == which)
+        def _():
+            span = slice(which * per * width, (which + 1) * per * width)
+            out_ref[0:1, span] = query_ref[...]
+            out_ref[1:2, span] = value_ref[...]
+            for i in range(4):
+                parts = []
+                for local in range(per):
+                    begin = (4 * local + i) * width
+                    parts.append(unit_ref[:, begin : begin + width])
+                out_ref[8 + i : 9 + i, span] = jnp.concatenate(parts, 1)
+
+
+def send_team(parts):
+    return tuple(swap(part, bit) for part, bit in zip(parts, TEAM_BITS))
+
+
+def gather_team(rows):
+    return tuple(swap(rows, bit) for bit in TEAM_BITS)
+
+
+def gather_parts(rows):
+    side = swap(rows, BIT_SIDE)
+    return rows, side, swap(rows, BIT_CORE), swap(side, BIT_CORE)
+
+
+def over_chips(values):
+    total = device_count()
+    groups = [list(range(first, total, 4)) for first in range(4)]
+    return lax.all_to_all(values, AXES, 0, 0, axis_index_groups=groups)
+
+
+def local_32(
+    hidden_in,
+    cotangent,
+    lengths,
+    w_query,
+    b_query,
+    w_key,
+    w_value,
+    b_value,
+    w_out,
+    b_out,
+    first_gain,
+    first_shift,
+    w_up,
+    b_up,
+    w_down,
+    b_down,
+    second_gain,
+    second_shift,
+):
+    fsdp_index = lax.axis_index("fsdp")
+    tp_bit = lax.axis_index("tp")
+    core_bit = fsdp_index % 2
+    side_bit = (fsdp_index // 2) % 2
+    low_bit = (fsdp_index // 4) % 2
+    high_bit = fsdp_index // 8
+    shard_pos, seq_count, width = hidden_in.shape
+    rows_here = 2 * shard_pos
+    group = 4 * rows_here
+    shard_rows = w_query.shape[0]
+    head_cols = w_query.shape[1] // 2
+    unit_cols = w_up.shape[1] // 2
+    chips = lax.axis_size("fsdp") // 2
+    def slot_parts(values):
+        own = lax.dynamic_index_in_dim(values, high_bit, 1, keepdims=False)
+        other = lax.dynamic_index_in_dim(values, 1 - high_bit, 1, keepdims=False)
+        return own, swap(other, BIT_HIGH)
+
+    def from_slot(own, returned):
+        return in_order(high_bit, own, returned, 1)
+
+    up_out = (shard_rows, unit_cols + head_cols)
+    down = (shard_rows, unit_cols)
+    first_pack, up_own, up_send, down_own, down_send = run_kernel(
+        pack_kernel,
+        [
+            ((chips, shard_rows + 16, 3 * head_cols), low_type),
+            (up_out, low_type),
+            (up_out, low_type),
+            (down, low_type),
+            (down, low_type),
+        ],
+        w_query, w_key, w_value, w_out, w_up, w_down,
+        b_query, b_value, b_out, first_gain, first_shift, b_down, second_gain, second_shift, b_up,
+        name="pack",
+    )
+
+    def all_rows(own, send):
+        pieces = jnp.stack([own, swap(send, BIT_LOW)])
+        pieces = jnp.concatenate([pieces, swap(pieces, BIT_HIGH)], 0)
+        return gather_parts(pieces)
+
+    hidden_own, hidden_slot = slot_parts(hidden_in)
+    first_own = over_chips(first_pack)
+    first_core = swap(first_own, BIT_CORE)
+    team_rows = gather_team(jnp.concatenate([hidden_own, hidden_slot], 0))
+    up_pieces = all_rows(up_own, up_send)
+    down_pieces = all_rows(down_own, down_send)
+    cot_own, cot_slot = slot_parts(cotangent)
+
+    group_rows, queries, pair, qkv_weight = run_kernel(
+        project_kernel,
+        [
+            ((group, width), low_type),
+            ((group, head_cols), low_type),
+            ((group, 2 * head_cols), low_type),
+            ((width, 3 * head_cols), low_type),
+        ],
+        hidden_own, hidden_slot, *team_rows, first_own, first_core,
+        name="project",
+    )
+    pairs = gather_parts(pair)
+    vectors, up_bias = run_kernel(
+        lines_kernel, [((8, width), wide), ((1, unit_cols), wide)], first_own, first_core,
+        name="lines",
+    )
+    attended_low, extra = run_kernel(
+        functools.partial(attend_kernel, shard_pos),
+        [((group, head_cols), low_type), ((group, 2 * head_cols + 128), low_type)],
+        lengths, queries, *pairs,
+        name="attend",
+    )
+    up_weight, out_weight = run_kernel(
+        functools.partial(full_kernel, ((0, unit_cols), (unit_cols, unit_cols + head_cols))),
+        [((width, unit_cols), low_type), ((width, head_cols), low_type)],
+        *up_pieces,
+        name="full_up_out",
+    )
+    (down_weight,) = run_kernel(
+        functools.partial(full_kernel, ((0, unit_cols),)),
+        [((width, unit_cols), low_type)],
+        *down_pieces,
+        name="full_down",
+    )
+    rows_shape = (rows_here, width)
+    given = [(rows_shape, wide)] + [(rows_shape, low_type)] * 3
+
+    keep, *sends = run_kernel(out_kernel, given, attended_low, out_weight, name="out")
+    first_out, first_low, normed, scale = run_kernel(
+        first_norm_kernel,
+        [(rows_shape, wide), (rows_shape, low_type), (rows_shape, wide), ((rows_here, 128), wide)],
+        keep, *send_team(sends), hidden_own, hidden_slot, vectors,
+        name="first_norm",
+    )
+    extras = gather_parts(extra)
+    keep, s1, s2, s3, active, slope, first_rows = run_kernel(
+        hidden_kernel,
+        given
+        + [((group, unit_cols), low_type), ((group, unit_cols), wide), ((group, width), low_type)],
+        first_low, *gather_team(first_low), up_weight, down_weight, up_bias,
+        name="hidden",
+    )
+    output, second_grad, second_low, second_sums = run_kernel(
+        second_norm_kernel,
+        [(rows_shape, low_type), (rows_shape, wide), (rows_shape, low_type), ((8, width), wide)],
+        lengths, keep, *send_team((s1, s2, s3)), first_out, cot_own, cot_slot, vectors,
+        name="second_norm",
+    )
+    keep, s1, s2, s3, pre_grad, second_rows, unit_sums = run_kernel(
+        hidden_back_kernel,
+        given
+        + [((group, unit_cols), low_type), ((group, width), low_type), ((1, unit_cols), wide)],
+        second_low, *gather_team(second_low), slope, up_weight, down_weight,
+        name="hidden_back",
+    )
+    backs = send_team((s1, s2, s3))
+
+    def weight_parts(operands, name, extra=()):
+        cols = sum(right.shape[1] for right in operands[1::2]) + (128 if extra else 0)
+        shape = (chips, shard_rows, cols)
+        most = max(right.shape[1] for right in operands[1::2])
+        kept, sent = run_kernel(
+            functools.partial(weight_kernel, len(operands) // 2, len(extra)),
+            [(shape, low_type), (shape, low_type)],
+            *operands, *extra,
+            scratch=[((width, most), low_type)],
+            name=name,
+        )
+        return kept, swap(sent, BIT_CORE)
+
+    def finish(folded, spans, name):
+        own, send = run_kernel(
+            final_fold_kernel,
+            [(folded[0].shape[1:], wide), (folded[0].shape[1:], low_type)],
+            *folded,
+            name=name + "_low",
+        )
+        outs = []
+        for begin, end, turned in spans:
+            across = 2 * (end - begin)
+            if turned is None:
+                outs.append((end - begin, shard_rows))
+            else:
+                outs.append((across, shard_rows) if turned else (shard_rows, across))
+        return run_kernel(
+            functools.partial(total_kernel, spans), [(s, wide) for s in outs],
+            own, swap(send, BIT_LOW), name=name + "_total",
+        )
+
+    def in_steps(kept, got, spans, name):
+        for bit, stride, mask in (("side", (2, 1), BIT_SIDE), ("high", (1, 2), BIT_HIGH)):
+            shape = (kept.shape[0] // 2,) + kept.shape[1:]
+            kept, sent = run_kernel(
+                functools.partial(fold_kernel, (bit,), stride),
+                [(shape, wide), (shape, low_type)],
+                kept, got,
+                name=name + "_" + bit,
+            )
+            got = swap(sent, mask)
+        return finish((kept, got), spans, name)
+
+    def at_once(kept, got, spans, name):
+        shape = (kept.shape[0] // 4,) + kept.shape[1:]
+        kept, *sent = run_kernel(
+            functools.partial(fold_kernel, ("side", "high"), (2, 1, 4)),
+            [(shape, wide)] + [(shape, low_type)] * 3,
+            kept, got,
+            name=name + "_fold",
+        )
+        masks = (BIT_SIDE, BIT_HIGH, BIT_SIDE | BIT_HIGH)
+        got = [swap(part, mask) for part, mask in zip(sent, masks)]
+        return finish((kept, *got), spans, name)
+
+    down_grad, up_grad = in_steps(
+        *weight_parts((second_rows, active, first_rows, pre_grad), "unit_weights"),
+        ((0, unit_cols, True), (unit_cols, 2 * unit_cols, False)),
+        "units",
+    )
+    first_grad, one_low, first_sums = run_kernel(
+        first_back_kernel,
+        [(rows_shape, wide), (rows_shape, low_type), ((8, width), wide)],
+        keep, *backs, second_grad, normed, scale, vectors,
+        name="first_back",
+    )
+    attended_grad, one_rows, value_sums = run_kernel(
+        attended_back_kernel,
+        [((group, head_cols), low_type), ((group, width), low_type), ((1, head_cols), wide)],
+        one_low, *gather_team(one_low), out_weight,
+        name="attended_back",
+    )
+    grads = gather_parts(attended_grad)
+    query_grad, query_sums = run_kernel(
+        functools.partial(query_back_kernel, shard_pos),
+        [((group, head_cols), low_type), ((1, head_cols), wide)],
+        lengths, extra, attended_grad, *pairs,
+        name="query_back",
+    )
+    (sums,) = run_kernel(
+        functools.partial(vectors_kernel, 2 * chips),
+        [((16, width), wide)],
+        query_sums, value_sums, first_sums, second_sums, unit_sums,
+        name="vectors",
+    )
+    out_grad, query_total, shares = at_once(
+        *weight_parts(
+            (one_rows, attended_low, group_rows, query_grad),
+            "early_weights",
+            (sums, swap(sums, BIT_TP)),
+        ),
+        (
+            (0, head_cols, True),
+            (head_cols, 2 * head_cols, False),
+            (2 * head_cols, 2 * head_cols + 128, None),
+        ),
+        "early",
+    )
+    keep, s1, s2, s3, pair_grad = run_kernel(
+        functools.partial(pair_back_kernel, shard_pos),
+        given + [((group, 2 * head_cols), low_type)],
+        lengths, pair, query_grad, qkv_weight, *extras, *grads,
+        name="pair_back",
+    )
+    lasts = send_team((s1, s2, s3))
+    key_total, value_total = at_once(
+        *weight_parts((group_rows, pair_grad), "late_weights"),
+        ((0, head_cols, False), (head_cols, 2 * head_cols, False)),
+        "late",
+    )
+    grad_own, grad_send = run_kernel(
+        last_kernel,
+        [((shard_pos, width), wide), ((shard_pos, width), wide)],
+        keep, *lasts, first_grad,
+        name="last",
+    )
+    return (
+        from_slot(output[:shard_pos], swap(output[shard_pos:], BIT_HIGH)),
+        from_slot(grad_own, swap(grad_send, BIT_HIGH)),
+        query_total,
+        shares[0],
+        key_total,
+        value_total,
+        shares[1],
+        out_grad,
+        shares[2],
+        shares[3],
+        shares[4],
+        up_grad,
+        shares[8:12].reshape(-1),
+        down_grad,
+        shares[5],
+        shares[6],
+        shares[7],
+    )
+
 
 def solution(mesh):
     in_specs = (
@@ -421,4 +1221,5 @@
         P("fsdp"),
         P("fsdp"),
     )
-    return jax.shard_map(local, mesh=mesh, in_specs=in_specs, out_specs=out_specs, check_vma=False)
+    program = local_32 if mesh.shape["fsdp"] == 16 else local
+    return jax.shard_map(program, mesh=mesh, in_specs=in_specs, out_specs=out_specs, check_vma=False)

time: 316 us -> 204 us (0.65)
  local copies, waits for them, and re-layouts: 64.3 us -> 16.7 us
  other arithmetic: 36.8 us -> 0.15 us
  matrix products: 36.1 us -> 0 us
  Pallas kernels: 0 us -> 23.8 us
  starting transfers between devices: 72.8 us -> 64.6 us
  waiting for transfers between devices: 101 us -> 96.8 us
    all_to_all x12 -> x1, waiting for transfers between devices: 71.6 us -> 4.25 us  [over_chips(): return lax.all_to_all(values, AXES, 0, 0, axis_index_groups=groups)]
    ppermute x35 -> x63, waiting for transfers between devices: 29.8 us -> 92.6 us  [swap(): lax.ppermute(values, AXES, [(i, i ^ bit) for i in range(device_count())])]
    all_to_all x12 -> x1, starting transfers between devices: 47.8 us -> 7.25 us  [over_chips(): return lax.all_to_all(values, AXES, 0, 0, axis_index_groups=groups)]
    dot_general x20 -> x0, matrix products: 36.1 us -> none  [the longest x1 4.06 us: local(): jnp.einsum('hqk,khd->qhd', score_grad, key_all, preferred_element_type=wide)]
    ppermute x35 -> x63, starting transfers between devices: 25.1 us -> 57.4 us  [swap(): lax.ppermute(values, AXES, [(i, i ^ bit) for i in range(device_count())])]
    pallas_call x0 -> x30, Pallas kernels: none -> 23.8 us  [run_kernel(): pl.pallas_call(body, out_shape=[jax.ShapeDtypeStruct(shape, kind) for sha...]
    reshape x29 -> x1, local copies, waits for them, and re-layouts: 19.2 us -> 0.64 us  [local_32(): shares[8:12].reshape(-1)]
    reduce_sum x15 -> x0, other arithmetic: 10 us -> none  [the longest x2 2.02 us: norm_parts(): centre = values - jnp.mean(values, axis=-1, keepdims=True)]
  transfers between devices with their start and end apart: 47 -> 64, of which waited for: 22 -> 33; matrix products, arithmetic and copies ran while one was open for 34% -> 2% of each run, Pallas kernels for 0% -> 8%
where the time goes in v2:
time: 204 us; the launch traced here: 203 us
  waiting for transfers between devices  96.8 us (47%)
  starting transfers between devices  64.6 us (32%)
  Pallas kernels  23.8 us (12%)
  local copies, waits for them, and re-layouts  16.7 us (8%)
    ppermute x63, waiting for transfers between devices, swap(): lax.ppermute(values, AXES, [(i, i ^ bit) for i in range(device_count())])  92.6 us
    ppermute x63, starting transfers between devices, swap(): lax.ppermute(values, AXES, [(i, i ^ bit) for i in range(device_count())])  57.4 us
    pallas_call x30, Pallas kernels, run_kernel(): pl.pallas_call(body, out_shape=[jax.ShapeDtypeStruct(shape, kind) for sha...  23.8 us
    unnamed x42, local copies, waits for them, and re-layouts  14.4 us
    all_to_all x1, starting transfers between devices, over_chips(): return lax.all_to_all(values, AXES, 0, 0, axis_index_groups=groups)  7.25 us
    all_to_all x1, waiting for transfers between devices, over_chips(): return lax.all_to_all(values, AXES, 0, 0, axis_index_groups=groups)  4.25 us
  transfers between devices with their start and end apart: 64, of which 33 were waited for; matrix products, arithmetic and copies ran while one was open for 2% of the time, Pallas kernels for 8%

profile of v2, /device:TPU:0, one launch (start us, length us, event | category | flops | bytes accessed | tf_op | source)
XLA Modules:
  0.0 203.2 jit_solution(6278344835977584966)
XLA Ops:
  1.5 1.1 copy.44.wd_ref
  11.8 1.2 pack.1
  13.0 7.3 %all-to-all-start = ((bf16[8,64,576]{2,1,0:T(8,128)(2,1)}), bf16[8,64,576]{2,1,0:T(8,128)(2,1)S(1)}, u32[]{:S(2)}, u32[]{:S(2)}) async-start(bf16[8,64,576]{2,1,0:T(8,128)(2,1)} %get-tuple-element.104), calls=%async_computation | async-start | bytes 1310720 | tf_op jit(solution)/shard_map/all_to_all | solution.py:906
  20.3 2.0 collective-permute-start.8
  22.3 10.8 %collective-permute-done.8 = bf16[48,960]{1,0:T(8,128)(2,1)S(1)} collective-permute-done((bf16[48,960]{1,0:T(8,128)(2,1)S(1)}, bf16[48,960]{1,0:T(8,128)(2,1)S(1)}, u32[]{:S(2)}, u32[]{:S(2)}) %collective-permute-start.8) | collective-permute-done | bytes 92192 | tf_op jit(solution)/shard_map/ppermute | solution.py:26
  33.1 4.7 %collective-permute-start.9 = (bf16[2,48,960]{2,1,0:T(8,128)(2,1)S(1)}, bf16[2,48,960]{2,1,0:T(8,128)(2,1)S(1)}, u32[]{:S(2)}, u32[]{:S(2)}) collective-permute-start(bf16[2,48,960]{2,1,0:T(8,128)(2,1)S(1)} %pad_maximum_fusion.2), channel_id=1, source_target_pairs={{0,16},{1,17},{2,18},{3,19},{4,20},{5,21},{6,22},{7,23},{8,24},{9,... | collective-permute-start | bytes 552968 | tf_op jit(solution)/shard_map/ppermute | solution.py:26
  37.8 4.3 %all-to-all-done.own_ref = bf16[8,64,576]{2,1,0:T(8,128)(2,1)S(1)} async-done(((bf16[8,64,576]{2,1,0:T(8,128)(2,1)}), bf16[8,64,576]{2,1,0:T(8,128)(2,1)S(1)}, u32[]{:S(2)}, u32[]{:S(2)}) %all-to-all-start) | async-done | bytes 589856 | tf_op jit(solution)/shard_map/all_to_all | solution.py:906
  42.6 5.6 %collective-permute-done.got_ref.slot_ref = bf16[32,768]{1,0:T(8,128)(2,1)S(1)} collective-permute-done((bf16[32,768]{1,0:T(8,128)(2,1)S(1)}, bf16[32,768]{1,0:T(8,128)(2,1)S(1)}, u32[]{:S(2)}, u32[]{:S(2)}) %collective-permute-start) | collective-permute-done | bytes 49184 | tf_op jit(solution)/shard_map/ppermute | solution.py:26
  48.2 1.6 collective-permute-start.1
  49.9 2.3 %collective-permute-start.10 = (bf16[4,48,960]{2,1,0:T(8,128)(2,1)S(1)}, bf16[4,48,960]{2,1,0:T(8,128)(2,1)S(1)}, u32[]{:S(2)}, u32[]{:S(2)}) collective-permute-start(bf16[4,48,960]{2,1,0:T(8,128)(2,1)S(1)} %pad_maximum_fusion.p0_ref), channel_id=1, source_target_pairs={{0,4},{1,5},{2,6},{3,7},{4,0},{5,1},{6,2},{7,3},{8,12},{9,13},{10,... | collective-permute-start | bytes 1105928 | tf_op jit(solution)/shard_map/ppermute | solution.py:26
  52.9 1.7 collective-permute-start.3
  54.6 5.8 %collective-permute-done.2.low_ref = bf16[64,768]{1,0:T(8,128)(2,1)S(1)} collective-permute-done((bf16[64,768]{1,0:T(8,128)(2,1)S(1)}, bf16[64,768]{1,0:T(8,128)(2,1)S(1)}, u32[]{:S(2)}, u32[]{:S(2)}) %collective-permute-start.2) | collective-permute-done | bytes 98336 | tf_op jit(solution)/shard_map/ppermute | solution.py:26
  60.4 1.0 collective-permute-done.3.both_ref
  62.2 2.0 collective-permute-start.5
  64.9 5.2 %collective-permute-done.5.p1_ref = bf16[256,384]{1,0:T(8,128)(2,1)S(1)} collective-permute-done((bf16[256,384]{1,0:T(8,128)(2,1)S(1)}, bf16[256,384]{1,0:T(8,128)(2,1)S(1)}, u32[]{:S(2)}, u32[]{:S(2)}) %collective-permute-start.5) | collective-permute-done | bytes 196640 | tf_op jit(solution)/shard_map/ppermute | solution.py:26
  70.1 4.8 %collective-permute-done.21.p1_ref = bf16[4,48,768]{2,1,0:T(8,128)(2,1)S(1)} collective-permute-done((bf16[4,48,768]{2,1,0:T(8,128)(2,1)S(1)}, bf16[4,48,768]{2,1,0:T(8,128)(2,1)S(1)}, u32[]{:S(2)}, u32[]{:S(2)}) %collective-permute-start.21) | collective-permute-done | bytes 294944 | tf_op jit(solution)/shard_map/ppermute | solution.py:26
  75.5 2.7 %attend.1 = (bf16[256,192]{1,0:T(8,128)(2,1)S(1)}, bf16[256,512]{1,0:T(8,128)(2,1)S(1)}) custom-call(s32[2]{0:T(128)S(1)} %copy-done.4, bf16[256,192]{1,0:T(8,128)(2,1)S(1)} %get-tuple-element.105.query_ref, bf16[256,384]{1,0:T(8,128)(2,1)S(1)} %get-tuple-element.106.p0_ref.pair_ref, bf16[256,384]{1,0:T(8,128)(2,1)S(1)} %collective-permute-done.5.p1_ref, ...), custom_call_target="tpu_custom_call" | custom-call | tf_op jit(solution)/shard_map/attend/pallas_call | solution.py:409
  79.5 2.6 %collective-permute-start.15 = (bf16[64,768]{1,0:T(8,128)(2,1)S(1)}, bf16[64,768]{1,0:T(8,128)(2,1)S(1)}, u32[]{:S(2)}, u32[]{:S(2)}) collective-permute-start(bf16[64,768]{1,0:T(8,128)(2,1)S(1)} %get-tuple-element.114), channel_id=1, source_target_pairs={{0,9},{1,8},{2,11},{3,10},{4,13},{5,12},{6,15},{7,14},{8,1},{9,0},... | collective-permute-start | bytes 294920 | tf_op jit(solution)/shard_map/ppermute | solution.py:26
  82.2 1.1 collective-permute-done.13.got1_ref
  83.3 1.7 collective-permute-done.14.got2_ref
  85.0 1.6 collective-permute-done.15.got3_ref
  86.9 1.0 collective-permute-start.16
  88.5 1.9 collective-permute-start.18
  90.5 1.9 collective-permute-done.16.got1_ref
  92.5 1.6 collective-permute-done.18.got3_ref
  94.1 1.7 hidden.1
  95.8 1.0 collective-permute-start.24
  96.7 1.5 collective-permute-start.25
  98.3 1.1 collective-permute-start.26
  99.8 4.6 %collective-permute-done.27.slot_ref = bf16[32,768]{1,0:T(8,128)(2,1)S(1)} collective-permute-done((bf16[32,768]{1,0:T(8,128)(2,1)S(1)}, bf16[32,768]{1,0:T(8,128)(2,1)S(1)}, u32[]{:S(2)}, u32[]{:S(2)}) %collective-permute-start.27) | collective-permute-done | bytes 49184 | tf_op jit(solution)/shard_map/ppermute | solution.py:26
  106.3 2.0 collective-permute-start.30
  109.0 1.1 collective-permute-done.29.got1_ref
  110.9 2.9 %collective-permute-done.31.got3_ref = bf16[64,768]{1,0:T(8,128)(2,1)S(1)} collective-permute-done((bf16[64,768]{1,0:T(8,128)(2,1)S(1)}, bf16[64,768]{1,0:T(8,128)(2,1)S(1)}, u32[]{:S(2)}, u32[]{:S(2)}) %collective-permute-start.31) | collective-permute-done | bytes 98336 | tf_op jit(solution)/shard_map/ppermute | solution.py:26
  114.8 1.1 unit_weights.1
  116.7 2.1 %collective-permute-done.59.got_ref = bf16[8,48,1536]{2,1,0:T(8,128)(2,1)S(1)} collective-permute-done((bf16[8,48,1536]{2,1,0:T(8,128)(2,1)S(1)}, bf16[8,48,1536]{2,1,0:T(8,128)(2,1)S(1)}, u32[]{:S(2)}, u32[]{:S(2)}) %collective-permute-start.59) | collective-permute-done | bytes 1179680 | tf_op jit(solution)/shard_map/ppermute | solution.py:26
  119.8 1.9 collective-permute-start.32
  121.7 1.5 collective-permute-start.34
  123.3 1.3 collective-permute-done.32.got1_ref
  124.5 2.5 %collective-permute-done.33.got2_ref = bf16[64,768]{1,0:T(8,128)(2,1)S(1)} collective-permute-done((bf16[64,768]{1,0:T(8,128)(2,1)S(1)}, bf16[64,768]{1,0:T(8,128)(2,1)S(1)}, u32[]{:S(2)}, u32[]{:S(2)}) %collective-permute-start.33) | collective-permute-done | bytes 98336 | tf_op jit(solution)/shard_map/ppermute | solution.py:26
  128.2 1.7 collective-permute-start.35
  130.2 1.5 collective-permute-start.37
  131.8 2.2 %collective-permute-done.35.got1_ref = bf16[64,768]{1,0:T(8,128)(2,1)S(1)} collective-permute-done((bf16[64,768]{1,0:T(8,128)(2,1)S(1)}, bf16[64,768]{1,0:T(8,128)(2,1)S(1)}, u32[]{:S(2)}, u32[]{:S(2)}) %collective-permute-start.35) | collective-permute-done | bytes 98336 | tf_op jit(solution)/shard_map/ppermute | solution.py:26
  134.7 1.1 collective-permute-done.37.got3_ref
  136.0 1.1 collective-permute-start.41
  137.1 2.9 %query_back.1 = (bf16[256,192]{1,0:T(8,128)(2,1)S(1)}, f32[1,192]{1,0:T(1,128)S(1)}) custom-call(s32[2]{0:T(128)S(1)} %copy-done.4, bf16[256,512]{1,0:T(8,128)(2,1)S(1)} %get-tuple-element.127.extra_ref.e0_ref, bf16[256,192]{1,0:T(8,128)(2,1)S(1)} %get-tuple-element.138.grad_ref.g0_ref, bf16[256,384]{1,0:T(8,128)(2,1)S(1)} %get-tuple-element.106.p0_ref.pair_ref, ...), custom_call_target="tpu_custom_call" | custom-call | tf_op jit(solution)/shard_map/query_back/pallas_call | solution.py:409
  140.2 1.0 collective-permute-start.48
  141.1 3.2 %collective-permute-done.48.refs_5_ = f32[16,768]{1,0:T(8,128)S(1)} collective-permute-done((f32[16,768]{1,0:T(8,128)S(1)}, f32[16,768]{1,0:T(8,128)S(1)}, u32[]{:S(2)}, u32[]{:S(2)}) %collective-permute-start.48) | collective-permute-done | bytes 49184 | tf_op jit(solution)/shard_map/ppermute | solution.py:26
  145.9 4.2 %pair_back.1 = (f32[64,768]{1,0:T(8,128)S(1)}, bf16[64,768]{1,0:T(8,128)(2,1)S(1)}, bf16[64,768]{1,0:T(8,128)(2,1)S(1)}, bf16[64,768]{1,0:T(8,128)(2,1)S(1)}, bf16[256,384]{1,0:T(8,128)(2,1)S(1)}) custom-call(s32[2]{0:T(128)S(1)} %copy-done.4, bf16[256,384]{1,0:T(8,128)(2,1)S(1)} %get-tuple-element.106.p0_ref.pair_ref, ...), custom_call_target="tpu_custom_call" | custom-call | tf_op jit(solution)/shard_map/pair_back/pallas_call | solution.py:409
  150.1 1.0 collective-permute-start.44
  151.1 1.2 late_weights.1
  152.4 1.2 collective-permute-start.45
  153.6 1.4 collective-permute-start.46
  156.5 1.4 collective-permute-done.45.got2_ref
  158.0 1.4 collective-permute-start.28
  159.4 1.6 collective-permute-done.46.got3_ref
  161.2 1.8 collective-permute-start.50
  162.9 13.9 %collective-permute-done.28 = bf16[32,768]{1,0:T(8,128)(2,1)S(1)} collective-permute-done((bf16[32,768]{1,0:T(8,128)(2,1)}, bf16[32,768]{1,0:T(8,128)(2,1)S(1)}, u32[]{:S(2)}, u32[]{:S(2)}) %collective-permute-start.28) | collective-permute-done | bytes 49184 | tf_op jit(solution)/shard_map/ppermute | solution.py:26
  176.8 3.9 %collective-permute-start.52 = (bf16[2,48,512]{2,1,0:T(8,128)(2,1)S(1)}, bf16[2,48,512]{2,1,0:T(8,128)(2,1)S(1)}, u32[]{:S(2)}, u32[]{:S(2)}) collective-permute-start(bf16[2,48,512]{2,1,0:T(8,128)(2,1)S(1)} %get-tuple-element.160), channel_id=1, source_target_pairs={{0,20},{1,21},{2,22},{3,23},{4,16},{5,17},{6,18},{7,19},{8,28},{9,... | collective-permute-start | bytes 294920 | tf_op jit(solution)/shard_map/ppermute | solution.py:26
  182.1 3.5 %collective-permute-done.51.refs_2_ = bf16[2,48,512]{2,1,0:T(8,128)(2,1)S(1)} collective-permute-done((bf16[2,48,512]{2,1,0:T(8,128)(2,1)S(1)}, bf16[2,48,512]{2,1,0:T(8,128)(2,1)S(1)}, u32[]{:S(2)}, u32[]{:S(2)}) %collective-permute-start.51) | collective-permute-done | bytes 98336 | tf_op jit(solution)/shard_map/ppermute | solution.py:26
  185.6 3.2 %collective-permute-done.52.refs_3_ = bf16[2,48,512]{2,1,0:T(8,128)(2,1)S(1)} collective-permute-done((bf16[2,48,512]{2,1,0:T(8,128)(2,1)S(1)}, bf16[2,48,512]{2,1,0:T(8,128)(2,1)S(1)}, u32[]{:S(2)}, u32[]{:S(2)}) %collective-permute-start.52) | collective-permute-done | bytes 98336 | tf_op jit(solution)/shard_map/ppermute | solution.py:26
  189.6 1.0 collective-permute-start.53
  191.5 3.5 %collective-permute-done.57.refs_3_ = bf16[2,48,384]{2,1,0:T(8,128)(2,1)S(1)} collective-permute-done((bf16[2,48,384]{2,1,0:T(8,128)(2,1)S(1)}, bf16[2,48,384]{2,1,0:T(8,128)(2,1)S(1)}, u32[]{:S(2)}, u32[]{:S(2)}) %collective-permute-start.57) | collective-permute-done | bytes 73760 | tf_op jit(solution)/shard_map/ppermute | solution.py:26
  196.0 2.1 %collective-permute-start.62 = (bf16[48,1536]{1,0:T(8,128)(2,1)S(1)}, bf16[48,1536]{1,0:T(8,128)(2,1)S(1)}, u32[]{:S(2)}, u32[]{:S(2)}) collective-permute-start(bf16[48,1536]{1,0:T(8,128)(2,1)S(1)} %get-tuple-element.188), channel_id=1, source_target_pairs={{0,8},{1,9},{2,10},{3,11},{4,12},{5,13},{6,14},{7,15},{8,0},{9,1},... | collective-permute-start | bytes 442376 | tf_op jit(solution)/shard_map/ppermute | solution.py:26
  202.2 1.0 copy.50
  (148 shorter events, 36.6 us)
Async XLA Ops:
  13.0 29.0 %all-to-all-start = ((bf16[8,64,576]{2,1,0:T(8,128)(2,1)}), bf16[8,64,576]{2,1,0:T(8,128)(2,1)S(1)}, u32[]{:S(2)}, u32[]{:S(2)}) async-start(bf16[8,64,576]{2,1,0:T(8,128)(2,1)} %get-tuple-element.104), calls=%async_computation | async-start | bytes 1310720 | tf_op jit(solution)/shard_map/all_to_all | solution.py:906
  20.3 12.8 %collective-permute-start.8 = (bf16[48,960]{1,0:T(8,128)(2,1)S(1)}, bf16[48,960]{1,0:T(8,128)(2,1)S(1)}, u32[]{:S(2)}, u32[]{:S(2)}) collective-permute-start(bf16[48,960]{1,0:T(8,128)(2,1)S(1)} %get-tuple-element.109), channel_id=1, source_target_pairs={{0,8},{1,9},{2,10},{3,11},{4,12},{5,13},{6,14},{7,15},{8,0},{9,1},... | collective-permute-start | bytes 276488 | tf_op jit(solution)/shard_map/ppermute | solution.py:26
  33.1 16.7 %collective-permute-start.9 = (bf16[2,48,960]{2,1,0:T(8,128)(2,1)S(1)}, bf16[2,48,960]{2,1,0:T(8,128)(2,1)S(1)}, u32[]{:S(2)}, u32[]{:S(2)}) collective-permute-start(bf16[2,48,960]{2,1,0:T(8,128)(2,1)S(1)} %pad_maximum_fusion.2), channel_id=1, source_target_pairs={{0,16},{1,17},{2,18},{3,19},{4,20},{5,21},{6,22},{7,23},{8,24},{9,... | collective-permute-start | bytes 552968 | tf_op jit(solution)/shard_map/ppermute | solution.py:26
  42.0 19.4 %collective-permute-start.4 = (bf16[8,64,576]{2,1,0:T(8,128)(2,1)S(1)}, bf16[8,64,576]{2,1,0:T(8,128)(2,1)S(1)}, u32[]{:S(2)}, u32[]{:S(2)}) collective-permute-start(bf16[8,64,576]{2,1,0:T(8,128)(2,1)S(1)} %all-to-all-done.own_ref), channel_id=1, source_target_pairs={{0,2},{1,3},{2,0},{3,1},{4,6},{5,7},{6,4},{7,5},{8,10},{9,11},{10,... | collective-permute-start | bytes 1769480 | tf_op jit(solution)/shard_map/ppermute | solution.py:26
  42.5 5.7 %collective-permute-start = (bf16[32,768]{1,0:T(8,128)(2,1)S(1)}, bf16[32,768]{1,0:T(8,128)(2,1)S(1)}, u32[]{:S(2)}, u32[]{:S(2)}) collective-permute-start(bf16[32,768]{1,0:T(8,128)(2,1)S(1)} %bitcast.52), channel_id=1, source_target_pairs={{0,16},{1,17},{2,18},{3,19},{4,20},{5,21},{6,22},{7,23},{8,24},{9,... | collective-permute-start | bytes 147464 | tf_op jit(solution)/shard_map/ppermute | solution.py:26
  42.6 9.6 %collective-permute-start.19 = (bf16[48,768]{1,0:T(8,128)(2,1)S(1)}, bf16[48,768]{1,0:T(8,128)(2,1)S(1)}, u32[]{:S(2)}, u32[]{:S(2)}) collective-permute-start(bf16[48,768]{1,0:T(8,128)(2,1)S(1)} %get-tuple-element.119), channel_id=1, source_target_pairs={{0,8},{1,9},{2,10},{3,11},{4,12},{5,13},{6,14},{7,15},{8,0},{9,1},... | collective-permute-start | bytes 221192 | tf_op jit(solution)/shard_map/ppermute | solution.py:26
  48.2 4.7 %collective-permute-start.1 = (bf16[64,768]{1,0:T(8,128)(2,1)S(1)}, bf16[64,768]{1,0:T(8,128)(2,1)S(1)}, u32[]{:S(2)}, u32[]{:S(2)}) collective-permute-start(bf16[64,768]{1,0:T(8,128)(2,1)S(1)} %pad_maximum_fusion.4), channel_id=1, source_target_pairs={{0,1},{1,0},{2,3},{3,2},{4,5},{5,4},{6,7},{7,6},{8,9},{9,8},{10,11... | collective-permute-start | bytes 294920 | tf_op jit(solution)/shard_map/ppermute | solution.py:26
  49.9 14.5 %collective-permute-start.10 = (bf16[4,48,960]{2,1,0:T(8,128)(2,1)S(1)}, bf16[4,48,960]{2,1,0:T(8,128)(2,1)S(1)}, u32[]{:S(2)}, u32[]{:S(2)}) collective-permute-start(bf16[4,48,960]{2,1,0:T(8,128)(2,1)S(1)} %pad_maximum_fusion.p0_ref), channel_id=1, source_target_pairs={{0,4},{1,5},{2,6},{3,7},{4,0},{5,1},{6,2},{7,3},{8,12},{9,13},{10,... | collective-permute-start | bytes 1105928 | tf_op jit(solution)/shard_map/ppermute | solution.py:26
  52.2 11.9 %collective-permute-start.20 = (bf16[2,48,768]{2,1,0:T(8,128)(2,1)S(1)}, bf16[2,48,768]{2,1,0:T(8,128)(2,1)S(1)}, u32[]{:S(2)}, u32[]{:S(2)}) collective-permute-start(bf16[2,48,768]{2,1,0:T(8,128)(2,1)S(1)} %pad_maximum_fusion.3), channel_id=1, source_target_pairs={{0,16},{1,17},{2,18},{3,19},{4,20},{5,21},{6,22},{7,23},{8,24},{9,... | collective-permute-start | bytes 442376 | tf_op jit(solution)/shard_map/ppermute | solution.py:26
  52.6 7.8 %collective-permute-start.2 = (bf16[64,768]{1,0:T(8,128)(2,1)S(1)}, bf16[64,768]{1,0:T(8,128)(2,1)S(1)}, u32[]{:S(2)}, u32[]{:S(2)}) collective-permute-start(bf16[64,768]{1,0:T(8,128)(2,1)S(1)} %pad_maximum_fusion.4), channel_id=1, source_target_pairs={{0,8},{1,9},{2,10},{3,11},{4,12},{5,13},{6,14},{7,15},{8,0},{9,1},... | collective-permute-start | bytes 294920 | tf_op jit(solution)/shard_map/ppermute | solution.py:26
  52.9 8.5 %collective-permute-start.3 = (bf16[64,768]{1,0:T(8,128)(2,1)S(1)}, bf16[64,768]{1,0:T(8,128)(2,1)S(1)}, u32[]{:S(2)}, u32[]{:S(2)}) collective-permute-start(bf16[64,768]{1,0:T(8,128)(2,1)S(1)} %pad_maximum_fusion.4), channel_id=1, source_target_pairs={{0,9},{1,8},{2,11},{3,10},{4,13},{5,12},{6,15},{7,14},{8,1},{9,0},... | collective-permute-start | bytes 294920 | tf_op jit(solution)/shard_map/ppermute | solution.py:26
  60.4 14.5 %collective-permute-start.11 = (bf16[4,48,960]{2,1,0:T(8,128)(2,1)S(1)}, bf16[4,48,960]{2,1,0:T(8,128)(2,1)S(1)}, u32[]{:S(2)}, u32[]{:S(2)}) collective-permute-start(bf16[4,48,960]{2,1,0:T(8,128)(2,1)S(1)} %pad_maximum_fusion.p0_ref), channel_id=1, source_target_pairs={{0,2},{1,3},{2,0},{3,1},{4,6},{5,7},{6,4},{7,5},{8,10},{9,11},{10,... | collective-permute-start | bytes 1105928 | tf_op jit(solution)/shard_map/ppermute | solution.py:26
  62.2 7.9 %collective-permute-start.5 = (bf16[256,384]{1,0:T(8,128)(2,1)S(1)}, bf16[256,384]{1,0:T(8,128)(2,1)S(1)}, u32[]{:S(2)}, u32[]{:S(2)}) collective-permute-start(bf16[256,384]{1,0:T(8,128)(2,1)S(1)} %get-tuple-element.106.p0_ref.pair_ref), channel_id=1, source_target_pairs={{0,4},{1,5},{2,6},{3,7},{4,0},{5,1},{6,2},{7,3},{8,12},{9,13},{10,... | collective-permute-start | bytes 589832 | tf_op jit(solution)/shard_map/ppermute | solution.py:26
  64.2 10.7 %collective-permute-start.21 = (bf16[4,48,768]{2,1,0:T(8,128)(2,1)S(1)}, bf16[4,48,768]{2,1,0:T(8,128)(2,1)S(1)}, u32[]{:S(2)}, u32[]{:S(2)}) collective-permute-start(bf16[4,48,768]{2,1,0:T(8,128)(2,1)S(1)} %pad_maximum_fusion.1.p0_ref), channel_id=1, source_target_pairs={{0,4},{1,5},{2,6},{3,7},{4,0},{5,1},{6,2},{7,3},{8,12},{9,13},{10,... | collective-permute-start | bytes 884744 | tf_op jit(solution)/shard_map/ppermute | solution.py:26
  64.4 11.0 %collective-permute-start.12 = (bf16[4,48,960]{2,1,0:T(8,128)(2,1)S(1)}, bf16[4,48,960]{2,1,0:T(8,128)(2,1)S(1)}, u32[]{:S(2)}, u32[]{:S(2)}) collective-permute-start(bf16[4,48,960]{2,1,0:T(8,128)(2,1)S(1)} %collective-permute-done.10.p1_ref), channel_id=1, source_target_pairs={{0,2},{1,3},{2,0},{3,1},{4,6},{5,7},{6,4},{7,5},{8,10},{9,11},{10,... | collective-permute-start | bytes 1105928 | tf_op jit(solution)/shard_map/ppermute | solution.py:26
  64.4 11.1 %collective-permute-start.6 = (bf16[256,384]{1,0:T(8,128)(2,1)S(1)}, bf16[256,384]{1,0:T(8,128)(2,1)S(1)}, u32[]{:S(2)}, u32[]{:S(2)}) collective-permute-start(bf16[256,384]{1,0:T(8,128)(2,1)S(1)} %get-tuple-element.106.p0_ref.pair_ref), channel_id=1, source_target_pairs={{0,2},{1,3},{2,0},{3,1},{4,6},{5,7},{6,4},{7,5},{8,10},{9,11},{10,... | collective-permute-start | bytes 589832 | tf_op jit(solution)/shard_map/ppermute | solution.py:26
  70.1 5.4 %collective-permute-start.7 = (bf16[256,384]{1,0:T(8,128)(2,1)S(1)}, bf16[256,384]{1,0:T(8,128)(2,1)S(1)}, u32[]{:S(2)}, u32[]{:S(2)}) collective-permute-start(bf16[256,384]{1,0:T(8,128)(2,1)S(1)} %collective-permute-done.5.p1_ref), channel_id=1, source_target_pairs={{0,2},{1,3},{2,0},{3,1},{4,6},{5,7},{6,4},{7,5},{8,10},{9,11},{10,... | collective-permute-start | bytes 589832 | tf_op jit(solution)/shard_map/ppermute | solution.py:26
  74.9 15.6 %collective-permute-start.22 = (bf16[4,48,768]{2,1,0:T(8,128)(2,1)S(1)}, bf16[4,48,768]{2,1,0:T(8,128)(2,1)S(1)}, u32[]{:S(2)}, u32[]{:S(2)}) collective-permute-start(bf16[4,48,768]{2,1,0:T(8,128)(2,1)S(1)} %pad_maximum_fusion.1.p0_ref), channel_id=1, source_target_pairs={{0,2},{1,3},{2,0},{3,1},{4,6},{5,7},{6,4},{7,5},{8,10},{9,11},{10,... | collective-permute-start | bytes 884744 | tf_op jit(solution)/shard_map/ppermute | solution.py:26
  74.9 15.6 %collective-permute-start.23 = (bf16[4,48,768]{2,1,0:T(8,128)(2,1)S(1)}, bf16[4,48,768]{2,1,0:T(8,128)(2,1)S(1)}, u32[]{:S(2)}, u32[]{:S(2)}) collective-permute-start(bf16[4,48,768]{2,1,0:T(8,128)(2,1)S(1)} %collective-permute-done.21.p1_ref), channel_id=1, source_target_pairs={{0,2},{1,3},{2,0},{3,1},{4,6},{5,7},{6,4},{7,5},{8,10},{9,11},{10,... | collective-permute-start | bytes 884744 | tf_op jit(solution)/shard_map/ppermute | solution.py:26
  78.6 4.8 %collective-permute-start.13 = (bf16[64,768]{1,0:T(8,128)(2,1)S(1)}, bf16[64,768]{1,0:T(8,128)(2,1)S(1)}, u32[]{:S(2)}, u32[]{:S(2)}) collective-permute-start(bf16[64,768]{1,0:T(8,128)(2,1)S(1)} %get-tuple-element.112), channel_id=1, source_target_pairs={{0,1},{1,0},{2,3},{3,2},{4,5},{5,4},{6,7},{7,6},{8,9},{9,8},{10,11... | collective-permute-start | bytes 294920 | tf_op jit(solution)/shard_map/ppermute | solution.py:26
  79.5 5.5 %collective-permute-start.14 = (bf16[64,768]{1,0:T(8,128)(2,1)S(1)}, bf16[64,768]{1,0:T(8,128)(2,1)S(1)}, u32[]{:S(2)}, u32[]{:S(2)}) collective-permute-start(bf16[64,768]{1,0:T(8,128)(2,1)S(1)} %get-tuple-element.113), channel_id=1, source_target_pairs={{0,8},{1,9},{2,10},{3,11},{4,12},{5,13},{6,14},{7,15},{8,0},{9,1},... | collective-permute-start | bytes 294920 | tf_op jit(solution)/shard_map/ppermute | solution.py:26
  79.5 7.1 %collective-permute-start.15 = (bf16[64,768]{1,0:T(8,128)(2,1)S(1)}, bf16[64,768]{1,0:T(8,128)(2,1)S(1)}, u32[]{:S(2)}, u32[]{:S(2)}) collective-permute-start(bf16[64,768]{1,0:T(8,128)(2,1)S(1)} %get-tuple-element.114), channel_id=1, source_target_pairs={{0,9},{1,8},{2,11},{3,10},{4,13},{5,12},{6,15},{7,14},{8,1},{9,0},... | collective-permute-start | bytes 294920 | tf_op jit(solution)/shard_map/ppermute | solution.py:26
  86.9 5.5 %collective-permute-start.16 = (bf16[64,768]{1,0:T(8,128)(2,1)S(1)}, bf16[64,768]{1,0:T(8,128)(2,1)S(1)}, u32[]{:S(2)}, u32[]{:S(2)}) collective-permute-start(bf16[64,768]{1,0:T(8,128)(2,1)S(1)} %get-tuple-element.116.own_ref), channel_id=1, source_target_pairs={{0,1},{1,0},{2,3},{3,2},{4,5},{5,4},{6,7},{7,6},{8,9},{9,8},{10,11... | collective-permute-start | bytes 294920 | tf_op jit(solution)/shard_map/ppermute | solution.py:26
  87.9 4.6 %collective-permute-start.17 = (bf16[64,768]{1,0:T(8,128)(2,1)S(1)}, bf16[64,768]{1,0:T(8,128)(2,1)S(1)}, u32[]{:S(2)}, u32[]{:S(2)}) collective-permute-start(bf16[64,768]{1,0:T(8,128)(2,1)S(1)} %get-tuple-element.116.own_ref), channel_id=1, source_target_pairs={{0,8},{1,9},{2,10},{3,11},{4,12},{5,13},{6,14},{7,15},{8,0},{9,1},... | collective-permute-start | bytes 294920 | tf_op jit(solution)/shard_map/ppermute | solution.py:26
  88.5 5.5 %collective-permute-start.18 = (bf16[64,768]{1,0:T(8,128)(2,1)S(1)}, bf16[64,768]{1,0:T(8,128)(2,1)S(1)}, u32[]{:S(2)}, u32[]{:S(2)}) collective-permute-start(bf16[64,768]{1,0:T(8,128)(2,1)S(1)} %get-tuple-element.116.own_ref), channel_id=1, source_target_pairs={{0,9},{1,8},{2,11},{3,10},{4,13},{5,12},{6,15},{7,14},{8,1},{9,0},... | collective-permute-start | bytes 294920 | tf_op jit(solution)/shard_map/ppermute | solution.py:26
  95.8 8.7 %collective-permute-start.24 = (bf16[64,768]{1,0:T(8,128)(2,1)S(1)}, bf16[64,768]{1,0:T(8,128)(2,1)S(1)}, u32[]{:S(2)}, u32[]{:S(2)}) collective-permute-start(bf16[64,768]{1,0:T(8,128)(2,1)S(1)} %get-tuple-element.122), channel_id=1, source_target_pairs={{0,1},{1,0},{2,3},{3,2},{4,5},{5,4},{6,7},{7,6},{8,9},{9,8},{10,11... | collective-permute-start | bytes 294920 | tf_op jit(solution)/shard_map/ppermute | solution.py:26
  96.7 7.8 %collective-permute-start.25 = (bf16[64,768]{1,0:T(8,128)(2,1)S(1)}, bf16[64,768]{1,0:T(8,128)(2,1)S(1)}, u32[]{:S(2)}, u32[]{:S(2)}) collective-permute-start(bf16[64,768]{1,0:T(8,128)(2,1)S(1)} %get-tuple-element.123), channel_id=1, source_target_pairs={{0,8},{1,9},{2,10},{3,11},{4,12},{5,13},{6,14},{7,15},{8,0},{9,1},... | collective-permute-start | bytes 294920 | tf_op jit(solution)/shard_map/ppermute | solution.py:26
  98.3 6.2 %collective-permute-start.26 = (bf16[64,768]{1,0:T(8,128)(2,1)S(1)}, bf16[64,768]{1,0:T(8,128)(2,1)S(1)}, u32[]{:S(2)}, u32[]{:S(2)}) collective-permute-start(bf16[64,768]{1,0:T(8,128)(2,1)S(1)} %get-tuple-element.124), channel_id=1, source_target_pairs={{0,9},{1,8},{2,11},{3,10},{4,13},{5,12},{6,15},{7,14},{8,1},{9,0},... | collective-permute-start | bytes 294920 | tf_op jit(solution)/shard_map/ppermute | solution.py:26
  99.3 5.2 %collective-permute-start.27 = (bf16[32,768]{1,0:T(8,128)(2,1)S(1)}, bf16[32,768]{1,0:T(8,128)(2,1)S(1)}, u32[]{:S(2)}, u32[]{:S(2)}) collective-permute-start(bf16[32,768]{1,0:T(8,128)(2,1)S(1)} %bitcast.53), channel_id=1, source_target_pairs={{0,16},{1,17},{2,18},{3,19},{4,20},{5,21},{6,22},{7,23},{8,24},{9,... | collective-permute-start | bytes 147464 | tf_op jit(solution)/shard_map/ppermute | solution.py:26
  105.4 4.7 %collective-permute-start.29 = (bf16[64,768]{1,0:T(8,128)(2,1)S(1)}, bf16[64,768]{1,0:T(8,128)(2,1)S(1)}, u32[]{:S(2)}, u32[]{:S(2)}) collective-permute-start(bf16[64,768]{1,0:T(8,128)(2,1)S(1)} %get-tuple-element.128.own_ref), channel_id=1, source_target_pairs={{0,1},{1,0},{2,3},{3,2},{4,5},{5,4},{6,7},{7,6},{8,9},{9,8},{10,11... | collective-permute-start | bytes 294920 | tf_op jit(solution)/shard_map/ppermute | solution.py:26
  106.3 4.6 %collective-permute-start.30 = (bf16[64,768]{1,0:T(8,128)(2,1)S(1)}, bf16[64,768]{1,0:T(8,128)(2,1)S(1)}, u32[]{:S(2)}, u32[]{:S(2)}) collective-permute-start(bf16[64,768]{1,0:T(8,128)(2,1)S(1)} %get-tuple-element.128.own_ref), channel_id=1, source_target_pairs={{0,8},{1,9},{2,10},{3,11},{4,12},{5,13},{6,14},{7,15},{8,0},{9,1},... | collective-permute-start | bytes 294920 | tf_op jit(solution)/shard_map/ppermute | solution.py:26
  108.3 5.5 %collective-permute-start.31 = (bf16[64,768]{1,0:T(8,128)(2,1)S(1)}, bf16[64,768]{1,0:T(8,128)(2,1)S(1)}, u32[]{:S(2)}, u32[]{:S(2)}) collective-permute-start(bf16[64,768]{1,0:T(8,128)(2,1)S(1)} %get-tuple-element.128.own_ref), channel_id=1, source_target_pairs={{0,9},{1,8},{2,11},{3,10},{4,13},{5,12},{6,15},{7,14},{8,1},{9,0},... | collective-permute-start | bytes 294920 | tf_op jit(solution)/shard_map/ppermute | solution.py:26
  115.8 2.9 %collective-permute-start.59 = (bf16[8,48,1536]{2,1,0:T(8,128)(2,1)S(1)}, bf16[8,48,1536]{2,1,0:T(8,128)(2,1)S(1)}, u32[]{:S(2)}, u32[]{:S(2)}) collective-permute-start(bf16[8,48,1536]{2,1,0:T(8,128)(2,1)S(1)} %get-tuple-element.182), channel_id=1, source_target_pairs={{0,2},{1,3},{2,0},{3,1},{4,6},{5,7},{6,4},{7,5},{8,10},{9,11},{10,... | collective-permute-start | bytes 3538952 | tf_op jit(solution)/shard_map/ppermute | solution.py:26
  115.9 15.8 %collective-permute-start.38 = (bf16[256,512]{1,0:T(8,128)(2,1)S(1)}, bf16[256,512]{1,0:T(8,128)(2,1)S(1)}, u32[]{:S(2)}, u32[]{:S(2)}) collective-permute-start(bf16[256,512]{1,0:T(8,128)(2,1)S(1)} %get-tuple-element.127.extra_ref.e0_ref), channel_id=1, source_target_pairs={{0,4},{1,5},{2,6},{3,7},{4,0},{5,1},{6,2},{7,3},{8,12},{9,13},{10,... | collective-permute-start | bytes 786440 | tf_op jit(solution)/shard_map/ppermute | solution.py:26
  119.0 34.6 %collective-permute-start.60 = (bf16[4,48,1536]{2,1,0:T(8,128)(2,1)S(1)}, bf16[4,48,1536]{2,1,0:T(8,128)(2,1)S(1)}, u32[]{:S(2)}, u32[]{:S(2)}) collective-permute-start(bf16[4,48,1536]{2,1,0:T(8,128)(2,1)S(1)} %get-tuple-element.184), channel_id=1, source_target_pairs={{0,4},{1,5},{2,6},{3,7},{4,0},{5,1},{6,2},{7,3},{8,12},{9,13},{10,... | collective-permute-start | bytes 1769480 | tf_op jit(solution)/shard_map/ppermute | solution.py:26
  119.8 4.8 %collective-permute-start.32 = (bf16[64,768]{1,0:T(8,128)(2,1)S(1)}, bf16[64,768]{1,0:T(8,128)(2,1)S(1)}, u32[]{:S(2)}, u32[]{:S(2)}) collective-permute-start(bf16[64,768]{1,0:T(8,128)(2,1)S(1)} %get-tuple-element.131), channel_id=1, source_target_pairs={{0,1},{1,0},{2,3},{3,2},{4,5},{5,4},{6,7},{7,6},{8,9},{9,8},{10,11... | collective-permute-start | bytes 294920 | tf_op jit(solution)/shard_map/ppermute | solution.py:26
  121.7 5.3 %collective-permute-start.33 = (bf16[64,768]{1,0:T(8,128)(2,1)S(1)}, bf16[64,768]{1,0:T(8,128)(2,1)S(1)}, u32[]{:S(2)}, u32[]{:S(2)}) collective-permute-start(bf16[64,768]{1,0:T(8,128)(2,1)S(1)} %get-tuple-element.132), channel_id=1, source_target_pairs={{0,8},{1,9},{2,10},{3,11},{4,12},{5,13},{6,14},{7,15},{8,0},{9,1},... | collective-permute-start | bytes 294920 | tf_op jit(solution)/shard_map/ppermute | solution.py:26
  121.7 6.2 %collective-permute-start.34 = (bf16[64,768]{1,0:T(8,128)(2,1)S(1)}, bf16[64,768]{1,0:T(8,128)(2,1)S(1)}, u32[]{:S(2)}, u32[]{:S(2)}) collective-permute-start(bf16[64,768]{1,0:T(8,128)(2,1)S(1)} %get-tuple-element.133), channel_id=1, source_target_pairs={{0,9},{1,8},{2,11},{3,10},{4,13},{5,12},{6,15},{7,14},{8,1},{9,0},... | collective-permute-start | bytes 294920 | tf_op jit(solution)/shard_map/ppermute | solution.py:26
  128.2 5.7 %collective-permute-start.35 = (bf16[64,768]{1,0:T(8,128)(2,1)S(1)}, bf16[64,768]{1,0:T(8,128)(2,1)S(1)}, u32[]{:S(2)}, u32[]{:S(2)}) collective-permute-start(bf16[64,768]{1,0:T(8,128)(2,1)S(1)} %get-tuple-element.137.own_ref), channel_id=1, source_target_pairs={{0,1},{1,0},{2,3},{3,2},{4,5},{5,4},{6,7},{7,6},{8,9},{9,8},{10,11... | collective-permute-start | bytes 294920 | tf_op jit(solution)/shard_map/ppermute | solution.py:26
  129.9 4.8 %collective-permute-start.36 = (bf16[64,768]{1,0:T(8,128)(2,1)S(1)}, bf16[64,768]{1,0:T(8,128)(2,1)S(1)}, u32[]{:S(2)}, u32[]{:S(2)}) collective-permute-start(bf16[64,768]{1,0:T(8,128)(2,1)S(1)} %get-tuple-element.137.own_ref), channel_id=1, source_target_pairs={{0,8},{1,9},{2,10},{3,11},{4,12},{5,13},{6,14},{7,15},{8,0},{9,1},... | collective-permute-start | bytes 294920 | tf_op jit(solution)/shard_map/ppermute | solution.py:26
  130.2 5.5 %collective-permute-start.37 = (bf16[64,768]{1,0:T(8,128)(2,1)S(1)}, bf16[64,768]{1,0:T(8,128)(2,1)S(1)}, u32[]{:S(2)}, u32[]{:S(2)}) collective-permute-start(bf16[64,768]{1,0:T(8,128)(2,1)S(1)} %get-tuple-element.137.own_ref), channel_id=1, source_target_pairs={{0,9},{1,8},{2,11},{3,10},{4,13},{5,12},{6,15},{7,14},{8,1},{9,0},... | collective-permute-start | bytes 294920 | tf_op jit(solution)/shard_map/ppermute | solution.py:26
  131.8 13.9 %collective-permute-start.39 = (bf16[256,512]{1,0:T(8,128)(2,1)S(1)}, bf16[256,512]{1,0:T(8,128)(2,1)S(1)}, u32[]{:S(2)}, u32[]{:S(2)}) collective-permute-start(bf16[256,512]{1,0:T(8,128)(2,1)S(1)} %get-tuple-element.127.extra_ref.e0_ref), channel_id=1, source_target_pairs={{0,2},{1,3},{2,0},{3,1},{4,6},{5,7},{6,4},{7,5},{8,10},{9,11},{10,... | collective-permute-start | bytes 786440 | tf_op jit(solution)/shard_map/ppermute | solution.py:26
  133.9 11.8 %collective-permute-start.40 = (bf16[256,512]{1,0:T(8,128)(2,1)S(1)}, bf16[256,512]{1,0:T(8,128)(2,1)S(1)}, u32[]{:S(2)}, u32[]{:S(2)}) collective-permute-start(bf16[256,512]{1,0:T(8,128)(2,1)S(1)} %collective-permute-done.38.e1_ref), channel_id=1, source_target_pairs={{0,2},{1,3},{2,0},{3,1},{4,6},{5,7},{6,4},{7,5},{8,10},{9,11},{10,... | collective-permute-start | bytes 786440 | tf_op jit(solution)/shard_map/ppermute | solution.py:26
  136.0 8.3 %collective-permute-start.41 = (bf16[256,192]{1,0:T(8,128)(2,1)S(1)}, bf16[256,192]{1,0:T(8,128)(2,1)S(1)}, u32[]{:S(2)}, u32[]{:S(2)}) collective-permute-start(bf16[256,192]{1,0:T(8,128)(2,1)S(1)} %get-tuple-element.138.grad_ref.g0_ref), channel_id=1, source_target_pairs={{0,4},{1,5},{2,6},{3,7},{4,0},{5,1},{6,2},{7,3},{8,12},{9,13},{10,... | collective-permute-start | bytes 294920 | tf_op jit(solution)/shard_map/ppermute | solution.py:26
  140.2 4.2 %collective-permute-start.48 = (f32[16,768]{1,0:T(8,128)S(1)}, f32[16,768]{1,0:T(8,128)S(1)}, u32[]{:S(2)}, u32[]{:S(2)}) collective-permute-start(f32[16,768]{1,0:T(8,128)S(1)} %vectors.1.refs_4_), channel_id=1, source_target_pairs={{0,1},{1,0},{2,3},{3,2},{4,5},{5,4},{6,7},{7,6},{8,9},{9,8},{10,11... | collective-permute-start | bytes 147464 | tf_op jit(solution)/shard_map/ppermute | solution.py:26
  144.3 1.4 collective-permute-start.42
  144.3 1.5 collective-permute-start.43
  145.6 15.4 %collective-permute-start.49 = (bf16[8,48,512]{2,1,0:T(8,128)(2,1)S(1)}, bf16[8,48,512]{2,1,0:T(8,128)(2,1)S(1)}, u32[]{:S(2)}, u32[]{:S(2)}) collective-permute-start(bf16[8,48,512]{2,1,0:T(8,128)(2,1)S(1)} %get-tuple-element.156), channel_id=1, source_target_pairs={{0,2},{1,3},{2,0},{3,1},{4,6},{5,7},{6,4},{7,5},{8,10},{9,11},{10,... | collective-permute-start | bytes 1179656 | tf_op jit(solution)/shard_map/ppermute | solution.py:26
  150.1 5.7 %collective-permute-start.44 = (bf16[64,768]{1,0:T(8,128)(2,1)S(1)}, bf16[64,768]{1,0:T(8,128)(2,1)S(1)}, u32[]{:S(2)}, u32[]{:S(2)}) collective-permute-start(bf16[64,768]{1,0:T(8,128)(2,1)S(1)} %get-tuple-element.142), channel_id=1, source_target_pairs={{0,1},{1,0},{2,3},{3,2},{4,5},{5,4},{6,7},{7,6},{8,9},{9,8},{10,11... | collective-permute-start | bytes 294920 | tf_op jit(solution)/shard_map/ppermute | solution.py:26
  152.3 24.5 %collective-permute-start.54 = (bf16[8,48,384]{2,1,0:T(8,128)(2,1)}, bf16[8,48,384]{2,1,0:T(8,128)(2,1)S(1)}, u32[]{:S(2)}, u32[]{:S(2)}) collective-permute-start(bf16[8,48,384]{2,1,0:T(8,128)(2,1)} %get-tuple-element.167), channel_id=1, source_target_pairs={{0,2},{1,3},{2,0},{3,1},{4,6},{5,7},{6,4},{7,5},{8,10},{9,11},{10,... | collective-permute-start | bytes 884744 | tf_op jit(solution)/shard_map/ppermute | solution.py:26
  152.4 5.6 %collective-permute-start.45 = (bf16[64,768]{1,0:T(8,128)(2,1)S(1)}, bf16[64,768]{1,0:T(8,128)(2,1)S(1)}, u32[]{:S(2)}, u32[]{:S(2)}) collective-permute-start(bf16[64,768]{1,0:T(8,128)(2,1)S(1)} %get-tuple-element.143), channel_id=1, source_target_pairs={{0,8},{1,9},{2,10},{3,11},{4,12},{5,13},{6,14},{7,15},{8,0},{9,1},... | collective-permute-start | bytes 294920 | tf_op jit(solution)/shard_map/ppermute | solution.py:26
  153.6 7.3 %collective-permute-start.46 = (bf16[64,768]{1,0:T(8,128)(2,1)S(1)}, bf16[64,768]{1,0:T(8,128)(2,1)S(1)}, u32[]{:S(2)}, u32[]{:S(2)}) collective-permute-start(bf16[64,768]{1,0:T(8,128)(2,1)S(1)} %get-tuple-element.144), channel_id=1, source_target_pairs={{0,9},{1,8},{2,11},{3,10},{4,13},{5,12},{6,15},{7,14},{8,1},{9,0},... | collective-permute-start | bytes 294920 | tf_op jit(solution)/shard_map/ppermute | solution.py:26
  155.8 40.2 %collective-permute-start.61 = (bf16[2,48,1536]{2,1,0:T(8,128)(2,1)}, bf16[2,48,1536]{2,1,0:T(8,128)(2,1)S(1)}, u32[]{:S(2)}, u32[]{:S(2)}) collective-permute-start(bf16[2,48,1536]{2,1,0:T(8,128)(2,1)} %get-tuple-element.186), channel_id=1, source_target_pairs={{0,16},{1,17},{2,18},{3,19},{4,20},{5,21},{6,22},{7,23},{8,24},{9,... | collective-permute-start | bytes 884744 | tf_op jit(solution)/shard_map/ppermute | solution.py:26
  158.0 18.8 %collective-permute-start.28 = (bf16[32,768]{1,0:T(8,128)(2,1)}, bf16[32,768]{1,0:T(8,128)(2,1)S(1)}, u32[]{:S(2)}, u32[]{:S(2)}) collective-permute-start(bf16[32,768]{1,0:T(8,128)(2,1)} %get-tuple-element.226), channel_id=1, source_target_pairs={{0,16},{1,17},{2,18},{3,19},{4,20},{5,21},{6,22},{7,23},{8,24},{9,... | collective-permute-start | bytes 147464 | tf_op jit(solution)/shard_map/ppermute | solution.py:26
  161.0 28.7 %collective-permute-start.47 = (f32[32,768]{1,0:T(8,128)S(1)}, f32[32,768]{1,0:T(8,128)S(1)}, u32[]{:S(2)}, u32[]{:S(2)}) collective-permute-start(f32[32,768]{1,0:T(8,128)S(1)} %get-tuple-element.147), channel_id=1, source_target_pairs={{0,16},{1,17},{2,18},{3,19},{4,20},{5,21},{6,22},{7,23},{8,24},{9,... | collective-permute-start | bytes 294920 | tf_op jit(solution)/shard_map/ppermute | solution.py:26
  161.2 20.4 %collective-permute-start.50 = (bf16[2,48,512]{2,1,0:T(8,128)(2,1)S(1)}, bf16[2,48,512]{2,1,0:T(8,128)(2,1)S(1)}, u32[]{:S(2)}, u32[]{:S(2)}) collective-permute-start(bf16[2,48,512]{2,1,0:T(8,128)(2,1)S(1)} %get-tuple-element.158), channel_id=1, source_target_pairs={{0,4},{1,5},{2,6},{3,7},{4,0},{5,1},{6,2},{7,3},{8,12},{9,13},{10,... | collective-permute-start | bytes 294920 | tf_op jit(solution)/shard_map/ppermute | solution.py:26
  176.8 8.8 %collective-permute-start.51 = (bf16[2,48,512]{2,1,0:T(8,128)(2,1)S(1)}, bf16[2,48,512]{2,1,0:T(8,128)(2,1)S(1)}, u32[]{:S(2)}, u32[]{:S(2)}) collective-permute-start(bf16[2,48,512]{2,1,0:T(8,128)(2,1)S(1)} %get-tuple-element.159), channel_id=1, source_target_pairs={{0,16},{1,17},{2,18},{3,19},{4,20},{5,21},{6,22},{7,23},{8,24},{9,... | collective-permute-start | bytes 294920 | tf_op jit(solution)/shard_map/ppermute | solution.py:26
  176.8 12.0 %collective-permute-start.52 = (bf16[2,48,512]{2,1,0:T(8,128)(2,1)S(1)}, bf16[2,48,512]{2,1,0:T(8,128)(2,1)S(1)}, u32[]{:S(2)}, u32[]{:S(2)}) collective-permute-start(bf16[2,48,512]{2,1,0:T(8,128)(2,1)S(1)} %get-tuple-element.160), channel_id=1, source_target_pairs={{0,20},{1,21},{2,22},{3,23},{4,16},{5,17},{6,18},{7,19},{8,28},{9,... | collective-permute-start | bytes 294920 | tf_op jit(solution)/shard_map/ppermute | solution.py:26
  181.6 9.9 %collective-permute-start.55 = (bf16[2,48,384]{2,1,0:T(8,128)(2,1)S(1)}, bf16[2,48,384]{2,1,0:T(8,128)(2,1)S(1)}, u32[]{:S(2)}, u32[]{:S(2)}) collective-permute-start(bf16[2,48,384]{2,1,0:T(8,128)(2,1)S(1)} %get-tuple-element.169), channel_id=1, source_target_pairs={{0,4},{1,5},{2,6},{3,7},{4,0},{5,1},{6,2},{7,3},{8,12},{9,13},{10,... | collective-permute-start | bytes 221192 | tf_op jit(solution)/shard_map/ppermute | solution.py:26
  185.6 5.9 %collective-permute-start.56 = (bf16[2,48,384]{2,1,0:T(8,128)(2,1)S(1)}, bf16[2,48,384]{2,1,0:T(8,128)(2,1)S(1)}, u32[]{:S(2)}, u32[]{:S(2)}) collective-permute-start(bf16[2,48,384]{2,1,0:T(8,128)(2,1)S(1)} %get-tuple-element.170), channel_id=1, source_target_pairs={{0,16},{1,17},{2,18},{3,19},{4,20},{5,21},{6,22},{7,23},{8,24},{9,... | collective-permute-start | bytes 221192 | tf_op jit(solution)/shard_map/ppermute | solution.py:26
  188.8 6.2 %collective-permute-start.57 = (bf16[2,48,384]{2,1,0:T(8,128)(2,1)S(1)}, bf16[2,48,384]{2,1,0:T(8,128)(2,1)S(1)}, u32[]{:S(2)}, u32[]{:S(2)}) collective-permute-start(bf16[2,48,384]{2,1,0:T(8,128)(2,1)S(1)} %get-tuple-element.171), channel_id=1, source_target_pairs={{0,20},{1,21},{2,22},{3,23},{4,16},{5,17},{6,18},{7,19},{8,28},{9,... | collective-permute-start | bytes 221192 | tf_op jit(solution)/shard_map/ppermute | solution.py:26
  189.6 5.5 %collective-permute-start.53 = (bf16[48,512]{1,0:T(8,128)(2,1)S(1)}, bf16[48,512]{1,0:T(8,128)(2,1)S(1)}, u32[]{:S(2)}, u32[]{:S(2)}) collective-permute-start(bf16[48,512]{1,0:T(8,128)(2,1)S(1)} %get-tuple-element.162), channel_id=1, source_target_pairs={{0,8},{1,9},{2,10},{3,11},{4,12},{5,13},{6,14},{7,15},{8,0},{9,1},... | collective-permute-start | bytes 147464 | tf_op jit(solution)/shard_map/ppermute | solution.py:26
  195.1 5.0 %collective-permute-start.58 = (bf16[48,384]{1,0:T(8,128)(2,1)S(1)}, bf16[48,384]{1,0:T(8,128)(2,1)S(1)}, u32[]{:S(2)}, u32[]{:S(2)}) collective-permute-start(bf16[48,384]{1,0:T(8,128)(2,1)S(1)} %get-tuple-element.173), channel_id=1, source_target_pairs={{0,8},{1,9},{2,10},{3,11},{4,12},{5,13},{6,14},{7,15},{8,0},{9,1},... | collective-permute-start | bytes 110600 | tf_op jit(solution)/shard_map/ppermute | solution.py:26
  196.0 5.2 %collective-permute-start.62 = (bf16[48,1536]{1,0:T(8,128)(2,1)S(1)}, bf16[48,1536]{1,0:T(8,128)(2,1)S(1)}, u32[]{:S(2)}, u32[]{:S(2)}) collective-permute-start(bf16[48,1536]{1,0:T(8,128)(2,1)S(1)} %get-tuple-element.188), channel_id=1, source_target_pairs={{0,8},{1,9},{2,10},{3,11},{4,12},{5,13},{6,14},{7,15},{8,0},{9,1},... | collective-permute-start | bytes 442376 | tf_op jit(solution)/shard_map/ppermute | solution.py:26
  (16 other events, 82.9 us)

commit v3 on v2

--- a/solution.py
+++ b/solution.py
@@ -401,20 +401,31 @@
         self.quarter = 2 * self.tp + self.low
 
 
-def run_kernel(body, outs, *operands, scratch=(), name=None):
-    specs = [
-        pl.BlockSpec(memory_space=pltpu.SMEM if op.dtype == jnp.int32 else pltpu.VMEM)
-        for op in operands
-    ]
+def run_kernel(body, outs, *operands, scratch=(), sems=0, apart=False, us=1.0, name=None):
+    def space(operand):
+        if operand.dtype == jnp.int32:
+            return pltpu.SMEM
+        return pltpu.HBM if apart else pltpu.VMEM
+
+    scratches = [pltpu.VMEM(shape, kind) for shape, kind in scratch]
+    if sems:
+        scratches.append(pltpu.SemaphoreType.DMA((sems,)))
     return pl.pallas_call(
         body,
         out_shape=[jax.ShapeDtypeStruct(shape, kind) for shape, kind in outs],
-        in_specs=specs,
+        in_specs=[pl.BlockSpec(memory_space=space(operand)) for operand in operands],
         out_specs=[pl.BlockSpec(memory_space=pltpu.VMEM)] * len(outs),
-        scratch_shapes=[pltpu.VMEM(shape, kind) for shape, kind in scratch],
+        scratch_shapes=scratches,
         compiler_params=pltpu.CompilerParams(vmem_limit_bytes=8 << 20),
+        cost_estimate=pl.CostEstimate(
+            flops=int(us * 1.0e7), transcendentals=0, bytes_accessed=int(us * 1.0e4)
+        ),
         name=name,
-    )(*operands)
+    )(*[pltpu.with_memory_space_constraint(op, pltpu.HBM) if apart else op for op in operands])
+
+
+def tie(value, *others):
+    return lax.optimization_barrier((value, others))[0]
 
 
 def mul(left, right, left_dim=1, right_dim=0):
@@ -449,116 +460,149 @@
     return pl.ds(pl.multiple_of((2 * chip + core) * rows, 16), rows)
 
 
-def join_rows(own_ref, core_ref, full_ref, rows, cols):
-    core = Place().core
-    for chip in range(own_ref.shape[0]):
-        full_ref[row_of(chip, core, rows), :] = own_ref[chip, 0:rows, cols]
-        full_ref[row_of(chip, 1 - core, rows), :] = core_ref[chip, 0:rows, cols]
-
-
 def join_pieces(piece_refs, full_ref, rows, cols):
     here = Place()
-    for part, ref in enumerate(piece_refs):
-        side, core = here.side ^ (part & 1), here.core ^ (part >> 1)
-        for inner in range(4):
-            block = (here.high ^ (inner >> 1)) * 2 + (here.low ^ (inner & 1))
-            full_ref[row_of(block * 2 + side, core, rows), :] = ref[inner, :, cols]
-
-
-def split_rows(full_ref, keep_ref, send_ref, rows, cols):
+    for which, ref in enumerate(piece_refs):
+        side, core = here.side ^ ((which >> 1) & 1), here.core ^ (which >> 2)
+        for inner in range(2):
+            block = (here.high ^ (which & 1)) * 2 + (here.low ^ inner)
+            full_ref[row_of(block * 2 + side, core, rows), :] = ref[inner, 0:rows, cols]
+
+
+def split_rows(full_ref, keep_ref, send_ref, begin, cols):
     core = Place().core
-    width = cols.stop - cols.start
+    rows = keep_ref.shape[1]
     for chip in range(keep_ref.shape[0]):
-        keep_ref[chip, :, cols] = full_ref[row_of(chip, core, rows), 0:width]
-        send_ref[chip, :, cols] = full_ref[row_of(chip, 1 - core, rows), 0:width]
-
-
-def pack_kernel(
-    wq_ref, wk_ref, wv_ref, wo_ref, wu_ref, wd_ref,
-    v0_ref, v1_ref, v2_ref, v3_ref, v4_ref, v5_ref, v6_ref, v7_ref, v8_ref,
-    first_ref, own_ref, send_ref, down_ref, down_send_ref,
-):
+        keep_ref[chip, :, begin : begin + cols] = full_ref[row_of(chip, core, rows), 0:cols]
+        send_ref[chip] = full_ref[row_of(chip, 1 - core, rows), 0:cols]
+
+
+def rows_kernel(hidden_hbm, cot_hbm, hidden_ref, cot_ref, other_ref, held0, held1, sems):
+    copies = [
+        pltpu.make_async_copy(source, target, sems.at[i])
+        for i, (source, target) in enumerate(((hidden_hbm, held0), (cot_hbm, held1)))
+    ]
+    for copy in copies:
+        copy.start()
+    near = Place().high == 0
+    shard = hidden_ref.shape[0]
+    for i, (held, out_ref) in enumerate(((held0, hidden_ref), (held1, cot_ref))):
+        copies[i].wait()
+        first, second = held[:, 0, :], held[:, 1, :]
+        out_ref[...] = jnp.where(near, first, second)
+        other_ref[i * shard : (i + 1) * shard, :] = jnp.where(near, second, first)
+
+
+def pack_kernel(count, *refs):
+    sources, refs = refs[:count], refs[count:]
+    outs, held, sems = refs[:4], refs[4:-1], refs[-1]
+    copies = [
+        pltpu.make_async_copy(source, target, sems.at[i])
+        for i, (source, target) in enumerate(zip(sources, held))
+    ]
+    for copy in copies:
+        copy.start()
+    wq_ref, wk_ref, wv_ref, wo_ref, wu_ref, wd_ref = held[:6]
+    own_ref, send_ref, later_own_ref, later_send_ref = outs
     rows = wq_ref.shape[0]
     head_cols = wq_ref.shape[1] // 2
     unit_cols = wu_ref.shape[1] // 2
-    for chip in range(first_ref.shape[0]):
-        half = (chip // 2) % 2
-        heads = slice(half * head_cols, (half + 1) * head_cols)
-        for i, ref in enumerate((wq_ref, wk_ref, wv_ref)):
-            first_ref[chip, 0:rows, i * head_cols : (i + 1) * head_cols] = ref[:, heads]
-    vectors = [
-        r[...].astype(wide).reshape(1, rows)
-        for r in (v0_ref, v1_ref, v2_ref, v3_ref, v4_ref, v5_ref, v6_ref, v7_ref)
-    ]
+    low = Place().low
+    for copy in copies[6:]:
+        copy.wait()
+    vectors = [ref[...].astype(wide).reshape(1, rows) for ref in held[6:14]]
     block = jnp.concatenate(
         [
             jnp.pad(jnp.concatenate(vectors, 0), ((0, 0), (0, 4 * rows - rows))),
-            v8_ref[...].astype(wide).reshape(1, 4 * rows),
+            held[14][...].astype(wide).reshape(1, 4 * rows),
             jnp.zeros((7, 4 * rows), wide),
         ],
         0,
     ).astype(low_type)
-    for chip in range(first_ref.shape[0]):
-        first_ref[chip, rows : rows + 16, 0 : 4 * rows] = block
-    out_rows = jnp.transpose(wo_ref[...].astype(wide)).astype(low_type)
-    down_rows = jnp.transpose(wd_ref[...].astype(wide)).astype(low_type)
-    low = Place().low
+    for out_ref in (own_ref, send_ref):
+        out_ref[rows : rows + 16, 0 : 4 * rows] = block
+        out_ref[rows : rows + 16, 4 * rows :] = jnp.zeros(
+            (16, out_ref.shape[1] - 4 * rows), low_type
+        )
+    for copy in copies[:6]:
+        copy.wait()
     for half in range(2):
         heads = slice(half * head_cols, (half + 1) * head_cols)
         units = slice(half * unit_cols, (half + 1) * unit_cols)
 
-        def put(up_out_ref, down_half_ref):
-            up_out_ref[:, 0:unit_cols] = wu_ref[:, units]
-            up_out_ref[:, unit_cols : unit_cols + head_cols] = out_rows[:, heads]
-            down_half_ref[...] = down_rows[:, units]
+        def put(first_ref, later_ref):
+            for i, ref in enumerate((wq_ref, wk_ref, wv_ref, wo_ref)):
+                first_ref[0:rows, i * head_cols : (i + 1) * head_cols] = ref[:, heads]
+            later_ref[:, 0:unit_cols] = wu_ref[:, units]
+            later_ref[:, unit_cols:] = wd_ref[:, units]
 
         @pl.when(low == half)
         def _():
-            put(own_ref, down_ref)
+            put(own_ref, later_own_ref)
 
         @pl.when(low != half)
         def _():
-            put(send_ref, down_send_ref)
+            put(send_ref, later_send_ref)
+
+
+def by_chip_row(here, refs, high, low, rows, cols):
+    near = high == 0
+    p0, p1, p2, p3 = [
+        jnp.where(
+            near,
+            refs[2 * part][low, rows : rows + 16, 0:cols].astype(wide),
+            refs[2 * part + 1][low, rows : rows + 16, 0:cols].astype(wide),
+        )
+        for part in range(4)
+    ]
+    left = here.side == 0
+    own = jnp.where(left, p0, p1), jnp.where(left, p1, p0)
+    other = jnp.where(left, p2, p3), jnp.where(left, p3, p2)
+    even = here.core == 0
+    result = []
+    for side in range(2):
+        result.append(jnp.where(even, own[side], other[side]))
+        result.append(jnp.where(even, other[side], own[side]))
+    return result
 
 
 def project_kernel(
-    keep_ref, got_ref, tp_ref, low_ref, both_ref, own_ref, core_ref,
-    rows_ref, query_ref, pair_ref, weight_ref,
+    keep_ref, got_ref, tp_ref, low_ref, both_ref, *refs
 ):
-    rows = own_ref.shape[1] - 16
+    parts, outs = refs[:8], refs[8:]
+    rows_ref, query_ref, key_ref, value_ref, weight_ref, out_weight_ref = outs
+    rows = parts[0].shape[1] - 16
     head_cols = query_ref.shape[1]
-    join_rows(own_ref, core_ref, weight_ref, rows, slice(None))
+    join_pieces(parts, weight_ref, rows, slice(0, 3 * head_cols))
+    join_pieces(parts, out_weight_ref, rows, slice(3 * head_cols, 4 * head_cols))
     shard = keep_ref.shape[0]
     rows_ref[0:shard, :] = keep_ref[...]
-    rows_ref[shard : 2 * shard, :] = got_ref[...]
+    rows_ref[shard : 2 * shard, :] = got_ref[0:shard, :]
     for i, ref in enumerate((tp_ref, low_ref, both_ref)):
         rows_ref[2 * shard * (i + 1) : 2 * shard * (i + 2), :] = ref[...]
     here = Place()
-    even = here.core == 0
-    pieces = []
-    for side in range(2):
-        own = own_ref[2 * here.quarter + side, rows : rows + 16, 0:rows].astype(wide)
-        core = core_ref[2 * here.quarter + side, rows : rows + 16, 0:rows].astype(wide)
-        pieces += [jnp.where(even, own, core), jnp.where(even, core, own)]
-    biases = jnp.concatenate(pieces, 1)
+    biases = jnp.concatenate(by_chip_row(here, parts, here.high ^ here.tp, 0, rows, rows), 1)
     query_bias, value_bias = biases[0:1], biases[1:2]
     made = mul(rows_ref[...], weight_ref[...])
     query_ref[...] = (made[:, 0:head_cols] + query_bias).astype(low_type)
-    pair_ref[:, 0:head_cols] = made[:, head_cols : 2 * head_cols].astype(low_type)
-    pair_ref[:, head_cols:] = (made[:, 2 * head_cols :] + value_bias).astype(low_type)
+    key_ref[...] = made[:, head_cols : 2 * head_cols].astype(low_type)
+    value_ref[...] = (made[:, 2 * head_cols :] + value_bias).astype(low_type)
 
 
 def head_of(array, head):
     return array[:, head * HD : (head + 1) * HD]
 
 
-def attend_kernel(shard_pos, lengths_ref, query_ref, p0_ref, p1_ref, p2_ref, p3_ref, low_ref, extra_ref):
+def attend_kernel(
+    shard_pos, lengths_ref, query_ref, *refs
+):
+    pieces, (weight_ref, low_ref, stats_ref, keep_ref, *sends) = refs[:8], refs[8:]
     head_cols = query_ref.shape[1]
     count = query_ref.shape[0]
-    pair = jnp.concatenate([ref[...] for ref in (p0_ref, p1_ref, p2_ref, p3_ref)], 0)
-    keys, values = pair[:, 0:head_cols], pair[:, head_cols:]
+    keys = jnp.concatenate([ref[...] for ref in pieces[:4]], 0)
+    values = jnp.concatenate([ref[...] for ref in pieces[4:]], 0)
     queries = query_ref[...] * HD ** (-0.5)
-    lanes = lax.broadcasted_iota(jnp.int32, (1, pair.shape[0]), 1)
+    lanes = lax.broadcasted_iota(jnp.int32, (1, keys.shape[0]), 1)
     live = live_rows_of(lengths_ref, lanes, True, shard_pos)
     column = lax.broadcasted_iota(jnp.int32, (count, 128), 1)
     stats = jnp.zeros((count, 128), wide)
@@ -571,40 +615,30 @@
         total = jnp.sum(grown, axis=1, keepdims=True)
         weights = (grown * (1.0 / total)).astype(low_type)
         parts.append(mul(weights, head_of(values, head)))
-        log_total = top + jnp.log(total)
-        for level in range(3):
-            piece = log_total.astype(low_type).astype(wide)
-            log_total = log_total - piece
-            stats = jnp.where(column == 3 * head + level, piece, stats)
+        stats = jnp.where(column == head, top + jnp.log(total), stats)
     attended = jnp.concatenate(parts, 1).astype(low_type)
     low_ref[...] = attended
-    extra_ref[:, 0:head_cols] = query_ref[...]
-    extra_ref[:, head_cols : 2 * head_cols] = attended
-    extra_ref[:, 2 * head_cols :] = stats.astype(low_type)
-
-
-def full_kernel(cols, p0_ref, p1_ref, p2_ref, p3_ref, *outs):
-    pieces = (p0_ref, p1_ref, p2_ref, p3_ref)
+    stats_ref[...] = stats
+    give_out(mul(attended, weight_ref[...], 1, 1), keep_ref, sends)
+
+
+def full_kernel(cols, *refs):
+    pieces, outs = refs[:8], refs[8:]
     for out_ref, (begin, end) in zip(outs, cols):
-        join_pieces(pieces, out_ref, p0_ref.shape[1], slice(begin, end))
-
-
-def lines_kernel(own_ref, core_ref, vector_ref, bias_ref):
+        join_pieces(pieces, out_ref, pieces[0].shape[1], slice(begin, end))
+
+
+def lines_kernel(*refs):
+    parts, (vector_ref, bias_ref) = refs[:8], refs[8:]
     here = Place()
-    rows = own_ref.shape[1] - 16
-    even = here.core == 0
+    rows = parts[0].shape[1] - 16
     vectors = []
-    for chip in range(own_ref.shape[0]):
-        own = own_ref[chip, rows : rows + 16, 0:rows].astype(wide)
-        core = core_ref[chip, rows : rows + 16, 0:rows].astype(wide)
-        vectors += [jnp.where(even, own, core), jnp.where(even, core, own)]
+    for block in range(4):
+        high, low = (block >> 1) ^ here.high, (block & 1) ^ here.low
+        vectors += by_chip_row(here, parts, high, low, rows, rows)
     vector_ref[...] = jnp.concatenate(vectors, 1)[0:8]
-    biases = []
-    for side in range(2):
-        own = own_ref[2 * here.quarter + side, rows : rows + 16, 0 : 4 * rows].astype(wide)
-        core = core_ref[2 * here.quarter + side, rows : rows + 16, 0 : 4 * rows].astype(wide)
-        biases += [jnp.where(even, own, core), jnp.where(even, core, own)]
-    bias_ref[...] = jnp.concatenate(biases, 1)[8:9]
+    bias = by_chip_row(here, parts, here.high ^ here.tp, 0, rows, 4 * rows)
+    bias_ref[...] = jnp.concatenate(bias, 1)[8:9]
 
 
 def give_out(partial, keep_ref, sends):
@@ -621,20 +655,16 @@
     return total
 
 
-def out_kernel(low_ref, weight_ref, keep_ref, *sends):
-    give_out(mul(low_ref[...], weight_ref[...], 1, 1), keep_ref, sends)
-
-
 def vector_row(vector_ref, row):
     return vector_ref[row : row + 1, :]
 
 
 def first_norm_kernel(
-    keep_ref, got1_ref, got2_ref, got3_ref, own_ref, slot_ref, vector_ref,
+    keep_ref, got1_ref, got2_ref, got3_ref, own_ref, vector_ref,
     out_ref, low_ref, normed_ref, scale_ref,
 ):
     branch = collect(keep_ref, got1_ref, got2_ref, got3_ref)
-    rows = jnp.concatenate([own_ref[...], slot_ref[...]], 0).astype(wide)
+    rows = own_ref[0 : branch.shape[0], :].astype(wide)
     normed, scale = norm_parts(rows + branch + vector_row(vector_ref, 2))
     out = normed * vector_row(vector_ref, 3) + vector_row(vector_ref, 4)
     out_ref[...] = out
@@ -687,7 +717,7 @@
     output_ref[...] = (normed * gain + vector_row(vector_ref, 7)).astype(low_type)
     index = lax.broadcasted_iota(jnp.int32, (2 * shard_pos, 1), 0)
     live = live_rows_of(lengths_ref, index, False, shard_pos)
-    grad = jnp.concatenate([own_ref[...], slot_ref[...]], 0).astype(wide)
+    grad = jnp.concatenate([own_ref[...], slot_ref[shard_pos:, :]], 0).astype(wide)
     grad = jnp.where(live, grad, 0.0)
     second = norm_back(grad, normed, scale, gain)
     grad_ref[...] = second
@@ -712,35 +742,46 @@
 
 def weight_kernel(pairs, extra, *refs):
     operands = refs[: 2 * pairs + extra]
-    keep_ref, send_ref, full_ref = refs[2 * pairs + extra :]
-    rows = keep_ref.shape[1]
+    keep_ref, *sends, full_ref = refs[2 * pairs + extra :]
     begin = 0
-    for i in range(pairs):
+    for i, send_ref in enumerate(sends):
         left, right = operands[2 * i], operands[2 * i + 1]
         cols = right.shape[1]
         full_ref[:, 0:cols] = mul(left[...], right[...], 0, 0).astype(low_type)
-        split_rows(full_ref, keep_ref, send_ref, rows, slice(begin, begin + cols))
+        if extra and i == pairs - 1:
+            total = operands[-2][...] + operands[-1][...]
+            blank = jnp.zeros((128 - total.shape[0], total.shape[1]), wide)
+            total = jnp.transpose(jnp.concatenate([total, blank], 0))
+            full_ref[:, cols : cols + 128] = total.astype(low_type)
+            cols += 128
+        split_rows(full_ref, keep_ref, send_ref, begin, cols)
         begin += cols
-    if extra:
-        mine, other = operands[-2:]
-        cols = 128
-        total = mine[...] + other[...]
-        total = jnp.concatenate([total, jnp.zeros((cols - total.shape[0], total.shape[1]), wide)], 0)
-        full_ref[:, 0:cols] = jnp.transpose(total).astype(low_type)
-        split_rows(full_ref, keep_ref, send_ref, rows, slice(begin, begin + cols))
-
-
-def fold_kernel(bits, stride, keep_ref, got_ref, *outs):
+
+
+def fold_kernel(count, bit, stride, *refs):
+    keeps, got, outs = refs[:count], refs[count:-2], refs[-2:]
+    own = getattr(Place(), bit)
+    for choice, out_ref in enumerate(outs):
+        for block in range(out_ref.shape[0]):
+            index = block * stride[0] + (own ^ choice) * stride[1]
+            begin = 0
+            for i, got_ref in enumerate(got):
+                end = begin + got_ref.shape[2]
+                if count == 1:
+                    total = keeps[0][index, :, begin:end].astype(wide)
+                else:
+                    total = keeps[i][index].astype(wide)
+                out_ref[block, :, begin:end] = (total + got_ref[index].astype(wide)).astype(
+                    out_ref.dtype
+                )
+                begin = end
+
+
+def block_fold_kernel(keep_ref, got_ref, *outs):
     here = Place()
-    own = [getattr(here, bit) for bit in bits]
-    count = outs[0].shape[0]
     for choice, out_ref in enumerate(outs):
-        for block in range(count):
-            index = block * stride[0]
-            for i, (bit, step) in enumerate(zip(own, stride[1:])):
-                index = index + (bit ^ ((choice >> i) & 1)) * step
-            total = keep_ref[index].astype(wide) + got_ref[index].astype(wide)
-            out_ref[block] = total.astype(out_ref.dtype)
+        index = (here.high ^ (choice >> 1)) * 2 + (here.low ^ (choice & 1))
+        out_ref[...] = (keep_ref[index] + got_ref[index].astype(wide)).astype(out_ref.dtype)
 
 
 def final_fold_kernel(*refs):
@@ -753,21 +794,27 @@
         out_ref[...] = total.astype(out_ref.dtype)
 
 
-def total_kernel(spans, own_ref, got_ref, *outs):
+def total_kernel(spans, count, *refs):
+    sources, outs = refs[:count], refs[count:]
     even = Place().low == 0
-    for out_ref, (begin, end, turned) in zip(outs, spans):
+    own, got = sources[0][...], sources[1][...].astype(wide)
+    if count == 4:
+        own = own + sources[2][...].astype(wide)
+        got = got + sources[3][...].astype(wide)
+    for out_ref, (begin, end) in zip(outs, spans):
         cols = end - begin
-        own = own_ref[:, begin:end]
-        got = got_ref[:, begin:end].astype(wide)
-        if turned is None:
-            out_ref[...] = jnp.transpose(own + got)
-            continue
-        halves = jnp.where(even, own, got), jnp.where(even, got, own)
-        for i, half in enumerate(halves):
-            if turned:
-                out_ref[i * cols : (i + 1) * cols, :] = jnp.transpose(half)
-            else:
-                out_ref[:, i * cols : (i + 1) * cols] = half
+        mine, other = own[:, begin:end], got[:, begin:end]
+        out_ref[:, 0:cols] = jnp.where(even, mine, other)
+        out_ref[:, cols:] = jnp.where(even, other, mine)
+    vectors = outs[len(spans) :]
+    if vectors:
+        end = own.shape[1]
+        rows = jnp.transpose(own[:, end - 128 :] + got[:, end - 128 :])
+        for i, out_ref in enumerate(vectors[:-1]):
+            out_ref[...] = rows[i : i + 1, :].reshape(out_ref.shape)
+        first = len(vectors) - 1
+        parts = [rows[first + i : first + i + 1, :] for i in range(4)]
+        vectors[-1][...] = jnp.concatenate(parts, 1).reshape(vectors[-1].shape)
 
 
 def first_back_kernel(
@@ -786,83 +833,111 @@
 
 
 def attended_back_kernel(
-    own_ref, got1_ref, got2_ref, got3_ref, weight_ref, grad_ref, rows_ref, sums_ref
+    own_ref, got1_ref, got2_ref, got3_ref, weight_ref, low_ref, stats_ref, query_ref,
+    packet_ref, rows_ref, sums_ref,
 ):
     rows = jnp.concatenate([r[...] for r in (own_ref, got1_ref, got2_ref, got3_ref)], 0)
     rows_ref[...] = rows
     made = mul(rows, weight_ref[...])
-    grad_ref[...] = made.astype(low_type)
+    head_cols = made.shape[1]
     sums_ref[...] = jnp.sum(made, axis=0, keepdims=True)
-
-
-def stat_of(extra, head_cols, head):
-    base = 2 * head_cols + 3 * head
-    total = extra[:, base : base + 1].astype(wide)
+    grad = made.astype(low_type)
+    packet_ref[:, 0:head_cols] = grad
+    packet_ref[:, head_cols : 2 * head_cols] = query_ref[...]
+    both = grad.astype(wide) * low_ref[...].astype(wide)
+    column = lax.broadcasted_iota(jnp.int32, (made.shape[0], 128), 1)
+    stats = stats_ref[...]
+    levels = jnp.zeros_like(stats)
+    heads = head_cols // HD
+    for head in range(heads):
+        delta = jnp.sum(head_of(both, head), axis=1, keepdims=True)
+        for place, left in ((head, stats[:, head : head + 1]), (heads + head, delta)):
+            for level in range(3):
+                piece = left.astype(low_type).astype(wide)
+                left = left - piece
+                levels = jnp.where(column == 3 * place + level, piece, levels)
+    packet_ref[:, 2 * head_cols :] = levels.astype(low_type)
+
+
+def stat_of(packet, head_cols, place):
+    base = 2 * head_cols + 3 * place
+    total = packet[:, base : base + 1].astype(wide)
     for level in (1, 2):
-        total = total + extra[:, base + level : base + level + 1].astype(wide)
+        total = total + packet[:, base + level : base + level + 1].astype(wide)
     return total
 
 
-def query_back_kernel(
-    shard_pos, lengths_ref, extra_ref, grad_ref, p0_ref, p1_ref, p2_ref, p3_ref, out_ref, sums_ref
-):
+def query_back_kernel(shard_pos, lengths_ref, packet_ref, *refs):
+    pieces, (out_ref, sums_ref) = refs[:8], refs[8:]
     head_cols = out_ref.shape[1]
-    pair = jnp.concatenate([ref[...] for ref in (p0_ref, p1_ref, p2_ref, p3_ref)], 0)
-    keys, values = pair[:, 0:head_cols], pair[:, head_cols:]
-    extra, grad = extra_ref[...], grad_ref[...]
-    queries = extra[:, 0:head_cols] * HD ** (-0.5)
-    both = grad.astype(wide) * extra[:, head_cols : 2 * head_cols].astype(wide)
-    lanes = lax.broadcasted_iota(jnp.int32, (1, pair.shape[0]), 1)
+    heads = head_cols // HD
+    keys = jnp.concatenate([ref[...] for ref in pieces[:4]], 0)
+    values = jnp.concatenate([ref[...] for ref in pieces[4:]], 0)
+    packet = packet_ref[...]
+    grad = packet[:, 0:head_cols]
+    queries = packet[:, head_cols : 2 * head_cols] * HD ** (-0.5)
+    lanes = lax.broadcasted_iota(jnp.int32, (1, keys.shape[0]), 1)
     live = live_rows_of(lengths_ref, lanes, True, shard_pos)
     parts = []
-    for head in range(head_cols // HD):
+    for head in range(heads):
         scores = mul(head_of(queries, head), head_of(keys, head), 1, 1)
         scores = jnp.where(live, scores, masked_score)
-        weights = jnp.exp(scores - stat_of(extra, head_cols, head))
-        delta = jnp.sum(head_of(both, head), axis=1, keepdims=True)
+        weights = jnp.exp(scores - stat_of(packet, head_cols, head))
         weight_grad = mul(head_of(grad, head), head_of(values, head), 1, 1)
-        score_grad = (weights * (weight_grad - delta)).astype(low_type)
-        parts.append(mul(score_grad, head_of(keys, head)))
+        weight_grad = weight_grad - stat_of(packet, head_cols, heads + head)
+        parts.append(mul((weights * weight_grad).astype(low_type), head_of(keys, head)))
     made = (jnp.concatenate(parts, 1) * HD ** (-0.5)).astype(low_type)
     out_ref[...] = made
     sums_ref[...] = jnp.sum(made.astype(wide), axis=0, keepdims=True)
 
 
 def pair_back_kernel(
-    shard_pos, lengths_ref, pair_ref, query_grad_ref, weight_ref,
-    e0_ref, e1_ref, e2_ref, e3_ref, g0_ref, g1_ref, g2_ref, g3_ref,
+    shard_pos, lengths_ref, key_ref, value_ref, query_grad_ref, weight_ref,
+    g0_ref, g1_ref, g2_ref, g3_ref,
     keep_ref, send1_ref, send2_ref, send3_ref, made_ref,
 ):
     head_cols = query_grad_ref.shape[1]
-    pair = pair_ref[...]
-    keys, values = pair[:, 0:head_cols], pair[:, head_cols:]
-    extra = jnp.concatenate([ref[...] for ref in (e0_ref, e1_ref, e2_ref, e3_ref)], 0)
-    grad = jnp.concatenate([ref[...] for ref in (g0_ref, g1_ref, g2_ref, g3_ref)], 0)
-    queries = extra[:, 0:head_cols] * HD ** (-0.5)
-    both = grad.astype(wide) * extra[:, head_cols : 2 * head_cols].astype(wide)
-    lanes = lax.broadcasted_iota(jnp.int32, (1, pair.shape[0]), 1)
+    heads = head_cols // HD
+    keys, values = key_ref[...], value_ref[...]
+    packet = jnp.concatenate([ref[...] for ref in (g0_ref, g1_ref, g2_ref, g3_ref)], 0)
+    grad = packet[:, 0:head_cols]
+    queries = packet[:, head_cols : 2 * head_cols] * HD ** (-0.5)
+    lanes = lax.broadcasted_iota(jnp.int32, (1, keys.shape[0]), 1)
     live = live_rows_of(lengths_ref, lanes, False, shard_pos)
     key_parts, value_parts = [], []
-    for head in range(head_cols // HD):
+    for head in range(heads):
         scores = mul(head_of(queries, head), head_of(keys, head), 1, 1)
         scores = jnp.where(live, scores, masked_score)
-        weights = jnp.exp(scores - stat_of(extra, head_cols, head))
-        delta = jnp.sum(head_of(both, head), axis=1, keepdims=True)
+        weights = jnp.exp(scores - stat_of(packet, head_cols, head))
         weight_grad = mul(head_of(grad, head), head_of(values, head), 1, 1)
-        score_grad = (weights * (weight_grad - delta)).astype(low_type)
+        weight_grad = weight_grad - stat_of(packet, head_cols, heads + head)
+        score_grad = (weights * weight_grad).astype(low_type)
         key_parts.append(mul(score_grad, head_of(queries, head), 0, 0))
         value_parts.append(mul(weights.astype(low_type), head_of(grad, head), 0, 0))
-    made = jnp.concatenate([part.astype(low_type) for part in key_parts + value_parts], 1)
+    made = jnp.concatenate(
+        [query_grad_ref[...]] + [part.astype(low_type) for part in key_parts + value_parts], 1
+    )
     made_ref[...] = made
-    made = jnp.concatenate([query_grad_ref[...], made], 1)
     give_out(mul(made, weight_ref[...], 1, 1), keep_ref, (send1_ref, send2_ref, send3_ref))
 
 
-def last_kernel(keep_ref, got1_ref, got2_ref, got3_ref, first_ref, own_ref, send_ref):
+def slots_kernel(grad_ref, out_ref, got_ref, output_ref, hidden_grad_ref):
+    near = Place().high == 0
+    count, width = grad_ref.shape
+    for target, own, got in (
+        (hidden_grad_ref, grad_ref[...], got_ref[:, 0:width].astype(wide)),
+        (output_ref, out_ref[0:count, :], got_ref[:, width:]),
+    ):
+        target[:, 0, :] = jnp.where(near, own, got)
+        target[:, 1, :] = jnp.where(near, got, own)
+
+
+def last_kernel(keep_ref, got1_ref, got2_ref, got3_ref, first_ref, output_ref, own_ref, send_ref):
     total = first_ref[...] + collect(keep_ref, got1_ref, got2_ref, got3_ref)
-    count = own_ref.shape[0]
+    count, width = own_ref.shape
     own_ref[...] = total[0:count]
-    send_ref[...] = total[count:]
+    send_ref[:, 0:width] = total[count:].astype(send_ref.dtype)
+    send_ref[:, width:] = output_ref[count:, :]
 
 
 def vectors_kernel(shards, query_ref, value_ref, first_ref, second_ref, unit_ref, out_ref):
@@ -892,18 +967,12 @@
 
 
 def gather_team(rows):
-    return tuple(swap(rows, bit) for bit in TEAM_BITS)
+    return tuple(swap(rows, bit) for bit in TEAM_BITS[::-1])[::-1]
 
 
 def gather_parts(rows):
     side = swap(rows, BIT_SIDE)
     return rows, side, swap(rows, BIT_CORE), swap(side, BIT_CORE)
-
-
-def over_chips(values):
-    total = device_count()
-    groups = [list(range(first, total, 4)) for first in range(4)]
-    return lax.all_to_all(values, AXES, 0, 0, axis_index_groups=groups)
 
 
 def local_32(
@@ -926,12 +995,6 @@
     second_gain,
     second_shift,
 ):
-    fsdp_index = lax.axis_index("fsdp")
-    tp_bit = lax.axis_index("tp")
-    core_bit = fsdp_index % 2
-    side_bit = (fsdp_index // 2) % 2
-    low_bit = (fsdp_index // 4) % 2
-    high_bit = fsdp_index // 8
     shard_pos, seq_count, width = hidden_in.shape
     rows_here = 2 * shard_pos
     group = 4 * rows_here
@@ -939,242 +1002,291 @@
     head_cols = w_query.shape[1] // 2
     unit_cols = w_up.shape[1] // 2
     chips = lax.axis_size("fsdp") // 2
-    def slot_parts(values):
-        own = lax.dynamic_index_in_dim(values, high_bit, 1, keepdims=False)
-        other = lax.dynamic_index_in_dim(values, 1 - high_bit, 1, keepdims=False)
-        return own, swap(other, BIT_HIGH)
-
-    def from_slot(own, returned):
-        return in_order(high_bit, own, returned, 1)
-
-    up_out = (shard_rows, unit_cols + head_cols)
-    down = (shard_rows, unit_cols)
-    first_pack, up_own, up_send, down_own, down_send = run_kernel(
-        pack_kernel,
-        [
-            ((chips, shard_rows + 16, 3 * head_cols), low_type),
-            (up_out, low_type),
-            (up_out, low_type),
-            (down, low_type),
-            (down, low_type),
-        ],
-        w_query, w_key, w_value, w_out, w_up, w_down,
+
+    sources = (
+        w_query, w_key, w_value, jnp.transpose(w_out), w_up, jnp.transpose(w_down),
         b_query, b_value, b_out, first_gain, first_shift, b_down, second_gain, second_shift, b_up,
+    )
+    first = ((shard_rows + 16, 4 * head_cols), low_type)
+    later = ((shard_rows, 2 * unit_cols), low_type)
+    shard = ((shard_pos, width), low_type)
+    hidden_own, cot_own, other = run_kernel(
+        rows_kernel,
+        [shard, shard, ((rows_here, width), low_type)],
+        hidden_in, cotangent,
+        scratch=[(hidden_in.shape, low_type)] * 2,
+        sems=2,
+        apart=True,
+        name="rows",
+    )
+    slot_rows = swap(other, BIT_HIGH)
+    packs = run_kernel(
+        functools.partial(pack_kernel, len(sources)),
+        [first, first, later, later],
+        *tie(sources, other),
+        scratch=[(source.shape, source.dtype) for source in sources],
+        sems=len(sources),
+        apart=True,
+        us=3.0,
         name="pack",
     )
 
-    def all_rows(own, send):
-        pieces = jnp.stack([own, swap(send, BIT_LOW)])
-        pieces = jnp.concatenate([pieces, swap(pieces, BIT_HIGH)], 0)
-        return gather_parts(pieces)
-
-    hidden_own, hidden_slot = slot_parts(hidden_in)
-    first_own = over_chips(first_pack)
-    first_core = swap(first_own, BIT_CORE)
-    team_rows = gather_team(jnp.concatenate([hidden_own, hidden_slot], 0))
-    up_pieces = all_rows(up_own, up_send)
-    down_pieces = all_rows(down_own, down_send)
-    cot_own, cot_slot = slot_parts(cotangent)
-
-    group_rows, queries, pair, qkv_weight = run_kernel(
+    def over_blocks_of(own, send):
+        return own, swap(send, BIT_LOW), swap(own, BIT_HIGH), swap(send, BIT_HIGH | BIT_LOW)
+
+    first_own, first_send, later_own, later_send = tuple(packs)
+    f0, f1, f2, f3 = over_blocks_of(first_own, first_send)
+    first_near = jnp.stack([f0, f1])
+    first_near_side = swap(first_near, BIT_SIDE)
+    team_rows = gather_team(
+        tie(jnp.concatenate([hidden_own, slot_rows[:shard_pos]], 0), packs)
+    )
+    first_far = tie(jnp.stack([f2, f3]), first_near_side)
+    first_far_side = swap(first_far, BIT_SIDE)
+    later_near = jnp.stack([later_own, swap(tie(later_send, first_near), BIT_LOW)])
+    later_far = swap(tie(later_near, first_far), BIT_HIGH)
+    first_pieces = (
+        first_near,
+        first_far,
+        first_near_side,
+        first_far_side,
+        swap(first_near, BIT_CORE),
+        swap(first_far, BIT_CORE),
+        swap(first_near_side, BIT_CORE),
+        swap(tie(first_far_side, team_rows, later_near), BIT_CORE),
+    )
+
+    group_rows, queries, keys, values, qkv_weight, out_weight = run_kernel(
         project_kernel,
         [
             ((group, width), low_type),
             ((group, head_cols), low_type),
-            ((group, 2 * head_cols), low_type),
+            ((group, head_cols), low_type),
+            ((group, head_cols), low_type),
             ((width, 3 * head_cols), low_type),
+            ((width, head_cols), low_type),
         ],
-        hidden_own, hidden_slot, *team_rows, first_own, first_core,
+        hidden_own, slot_rows, *team_rows, *first_pieces,
         name="project",
     )
-    pairs = gather_parts(pair)
+    key_parts, value_parts = gather_parts(keys), gather_parts(values)
+    later_near_side = swap(tie(later_near, key_parts[1]), BIT_SIDE)
     vectors, up_bias = run_kernel(
-        lines_kernel, [((8, width), wide), ((1, unit_cols), wide)], first_own, first_core,
+        lines_kernel,
+        [((8, width), wide), ((1, unit_cols), wide)],
+        *tie(first_pieces, keys),
+        us=0.5,
         name="lines",
-    )
-    attended_low, extra = run_kernel(
-        functools.partial(attend_kernel, shard_pos),
-        [((group, head_cols), low_type), ((group, 2 * head_cols + 128), low_type)],
-        lengths, queries, *pairs,
-        name="attend",
-    )
-    up_weight, out_weight = run_kernel(
-        functools.partial(full_kernel, ((0, unit_cols), (unit_cols, unit_cols + head_cols))),
-        [((width, unit_cols), low_type), ((width, head_cols), low_type)],
-        *up_pieces,
-        name="full_up_out",
-    )
-    (down_weight,) = run_kernel(
-        functools.partial(full_kernel, ((0, unit_cols),)),
-        [((width, unit_cols), low_type)],
-        *down_pieces,
-        name="full_down",
     )
     rows_shape = (rows_here, width)
     given = [(rows_shape, wide)] + [(rows_shape, low_type)] * 3
-
-    keep, *sends = run_kernel(out_kernel, given, attended_low, out_weight, name="out")
+    attended_low, stats, keep, *sends = run_kernel(
+        functools.partial(attend_kernel, shard_pos),
+        [((group, head_cols), low_type), ((group, 128), wide)] + given,
+        lengths, tie(queries, vectors), *key_parts, *value_parts, out_weight,
+        us=3.0,
+        name="attend",
+    )
+    sends = send_team(sends)
+    later_far_side = swap(tie(later_far, attended_low), BIT_SIDE)
     first_out, first_low, normed, scale = run_kernel(
         first_norm_kernel,
         [(rows_shape, wide), (rows_shape, low_type), (rows_shape, wide), ((rows_here, 128), wide)],
-        keep, *send_team(sends), hidden_own, hidden_slot, vectors,
+        keep, *sends, group_rows, vectors,
+        us=0.5,
         name="first_norm",
     )
-    extras = gather_parts(extra)
+    first_team = gather_team(first_low)
+    later_sides = tie((later_near, later_far, later_near_side, later_far_side), first_low)
+    later_pieces = later_sides + tuple(swap(part, BIT_CORE) for part in later_sides)
+    up_weight, down_weight = run_kernel(
+        functools.partial(full_kernel, ((0, unit_cols), (unit_cols, 2 * unit_cols))),
+        [((width, unit_cols), low_type)] * 2,
+        *later_pieces,
+        us=1.0,
+        name="full_units",
+    )
     keep, s1, s2, s3, active, slope, first_rows = run_kernel(
         hidden_kernel,
         given
         + [((group, unit_cols), low_type), ((group, unit_cols), wide), ((group, width), low_type)],
-        first_low, *gather_team(first_low), up_weight, down_weight, up_bias,
+        first_low, *first_team, up_weight, down_weight, up_bias,
+        us=2.0,
         name="hidden",
     )
+    sends = send_team((s1, s2, s3))
     output, second_grad, second_low, second_sums = run_kernel(
         second_norm_kernel,
         [(rows_shape, low_type), (rows_shape, wide), (rows_shape, low_type), ((8, width), wide)],
-        lengths, keep, *send_team((s1, s2, s3)), first_out, cot_own, cot_slot, vectors,
+        lengths, keep, *sends, first_out, cot_own, slot_rows, vectors,
         name="second_norm",
     )
+    second_team = gather_team(second_low)
+    def weight_parts(operands, name, extra=()):
+        parts = [right.shape[1] for right in operands[1::2]]
+        parts[-1] += 128 if extra else 0
+        shapes = [(chips, shard_rows, cols) for cols in [sum(parts)] + parts]
+        kept, *sent = run_kernel(
+            functools.partial(weight_kernel, len(parts), len(extra)),
+            [(shape, low_type) for shape in shapes],
+            *operands, *extra,
+            scratch=[((width, max(parts)), low_type)],
+            name=name,
+        )
+        return kept, sent
+
+    def finish(sources, spans, name, vectors=()):
+        outs = [(shard_rows, 2 * (end - begin)) for begin, end in spans] + list(vectors)
+        return run_kernel(
+            functools.partial(total_kernel, spans, len(sources)),
+            [(shape, wide) for shape in outs],
+            *sources,
+            us=0.7,
+            name=name,
+        )
+
+    def fold(bit, stride, kept, got, name):
+        cols = sum(part.shape[2] for part in kept)
+        shape = (kept[0].shape[0] // 2, shard_rows, cols)
+        return run_kernel(
+            functools.partial(fold_kernel, len(kept), bit, stride),
+            [(shape, wide), (shape, low_type)],
+            *kept, *got,
+            us=0.7,
+            name=name + "_fold_" + bit,
+        )
+
     keep, s1, s2, s3, pre_grad, second_rows, unit_sums = run_kernel(
         hidden_back_kernel,
         given
         + [((group, unit_cols), low_type), ((group, width), low_type), ((1, unit_cols), wide)],
-        second_low, *gather_team(second_low), slope, up_weight, down_weight,
+        second_low, *second_team, slope, up_weight, down_weight,
+        us=1.5,
         name="hidden_back",
     )
-    backs = send_team((s1, s2, s3))
-
-    def weight_parts(operands, name, extra=()):
-        cols = sum(right.shape[1] for right in operands[1::2]) + (128 if extra else 0)
-        shape = (chips, shard_rows, cols)
-        most = max(right.shape[1] for right in operands[1::2])
-        kept, sent = run_kernel(
-            functools.partial(weight_kernel, len(operands) // 2, len(extra)),
-            [(shape, low_type), (shape, low_type)],
-            *operands, *extra,
-            scratch=[((width, most), low_type)],
-            name=name,
-        )
-        return kept, swap(sent, BIT_CORE)
-
-    def finish(folded, spans, name):
-        own, send = run_kernel(
-            final_fold_kernel,
-            [(folded[0].shape[1:], wide), (folded[0].shape[1:], low_type)],
-            *folded,
-            name=name + "_low",
-        )
-        outs = []
-        for begin, end, turned in spans:
-            across = 2 * (end - begin)
-            if turned is None:
-                outs.append((end - begin, shard_rows))
-            else:
-                outs.append((across, shard_rows) if turned else (shard_rows, across))
-        return run_kernel(
-            functools.partial(total_kernel, spans), [(s, wide) for s in outs],
-            own, swap(send, BIT_LOW), name=name + "_total",
-        )
-
-    def in_steps(kept, got, spans, name):
-        for bit, stride, mask in (("side", (2, 1), BIT_SIDE), ("high", (1, 2), BIT_HIGH)):
-            shape = (kept.shape[0] // 2,) + kept.shape[1:]
-            kept, sent = run_kernel(
-                functools.partial(fold_kernel, (bit,), stride),
-                [(shape, wide), (shape, low_type)],
-                kept, got,
-                name=name + "_" + bit,
-            )
-            got = swap(sent, mask)
-        return finish((kept, got), spans, name)
-
-    def at_once(kept, got, spans, name):
-        shape = (kept.shape[0] // 4,) + kept.shape[1:]
-        kept, *sent = run_kernel(
-            functools.partial(fold_kernel, ("side", "high"), (2, 1, 4)),
-            [(shape, wide)] + [(shape, low_type)] * 3,
-            kept, got,
-            name=name + "_fold",
-        )
-        masks = (BIT_SIDE, BIT_HIGH, BIT_SIDE | BIT_HIGH)
-        got = [swap(part, mask) for part, mask in zip(sent, masks)]
-        return finish((kept, *got), spans, name)
-
-    down_grad, up_grad = in_steps(
-        *weight_parts((second_rows, active, first_rows, pre_grad), "unit_weights"),
-        ((0, unit_cols, True), (unit_cols, 2 * unit_cols, False)),
-        "units",
-    )
+    unit_kept, unit_sent = weight_parts(
+        (second_rows, active, first_rows, pre_grad), "unit_weights"
+    )
+    unit_got = [swap(part, BIT_CORE) for part in unit_sent]
+    unit_kept, unit_sent = fold("side", (2, 1), [unit_kept], unit_got, "unit")
+    unit_got = swap(unit_sent, BIT_SIDE)
+    sends = send_team(tie((s1, s2, s3), unit_sent))
     first_grad, one_low, first_sums = run_kernel(
         first_back_kernel,
         [(rows_shape, wide), (rows_shape, low_type), ((8, width), wide)],
-        keep, *backs, second_grad, normed, scale, vectors,
+        keep, *sends, second_grad, normed, scale, vectors,
+        us=0.7,
         name="first_back",
     )
-    attended_grad, one_rows, value_sums = run_kernel(
+    one_team = gather_team(one_low)
+    packet, one_rows, value_sums = run_kernel(
         attended_back_kernel,
-        [((group, head_cols), low_type), ((group, width), low_type), ((1, head_cols), wide)],
-        one_low, *gather_team(one_low), out_weight,
+        [
+            ((group, 2 * head_cols + 128), low_type),
+            ((group, width), low_type),
+            ((1, head_cols), wide),
+        ],
+        one_low, *one_team, out_weight, attended_low, stats, queries,
+        us=0.7,
         name="attended_back",
     )
-    grads = gather_parts(attended_grad)
+    packet_side = swap(packet, BIT_SIDE)
     query_grad, query_sums = run_kernel(
         functools.partial(query_back_kernel, shard_pos),
         [((group, head_cols), low_type), ((1, head_cols), wide)],
-        lengths, extra, attended_grad, *pairs,
+        lengths, packet, *key_parts, *value_parts,
+        us=3.0,
         name="query_back",
+    )
+    packets = (
+        packet,
+        packet_side,
+        swap(packet, BIT_CORE),
+        swap(tie(packet_side, query_grad), BIT_CORE),
     )
     (sums,) = run_kernel(
         functools.partial(vectors_kernel, 2 * chips),
         [((16, width), wide)],
         query_sums, value_sums, first_sums, second_sums, unit_sums,
+        us=0.5,
         name="vectors",
     )
-    out_grad, query_total, shares = at_once(
-        *weight_parts(
-            (one_rows, attended_low, group_rows, query_grad),
-            "early_weights",
-            (sums, swap(sums, BIT_TP)),
-        ),
-        (
-            (0, head_cols, True),
-            (head_cols, 2 * head_cols, False),
-            (2 * head_cols, 2 * head_cols + 128, None),
-        ),
-        "early",
-    )
-    keep, s1, s2, s3, pair_grad = run_kernel(
+    sums_got = swap(sums, BIT_TP)
+    unit_kept, unit_sent = fold("high", (1, 2), [tie(unit_kept, packet)], [unit_got], "unit")
+    unit_got = swap(unit_sent, BIT_HIGH)
+    keep, s1, s2, s3, qkv_grad = run_kernel(
         functools.partial(pair_back_kernel, shard_pos),
-        given + [((group, 2 * head_cols), low_type)],
-        lengths, pair, query_grad, qkv_weight, *extras, *grads,
+        given + [((group, 3 * head_cols), low_type)],
+        lengths, tie(keys, unit_kept), values, query_grad, qkv_weight, *packets,
+        us=4.0,
         name="pair_back",
     )
-    lasts = send_team((s1, s2, s3))
-    key_total, value_total = at_once(
-        *weight_parts((group_rows, pair_grad), "late_weights"),
-        ((0, head_cols, False), (head_cols, 2 * head_cols, False)),
-        "late",
+    late_kept, late_sent = weight_parts(
+        (one_rows, attended_low, group_rows, tie(qkv_grad, unit_got)),
+        "head_weights",
+        (sums, sums_got),
+    )
+    late_got = [swap(part, BIT_CORE) for part in late_sent]
+    lasts = send_team(tie((s1, s2, s3), *late_sent))
+    late_kept, late_sent = fold("side", (2, 1), [late_kept], late_got, "late")
+    late_got = swap(late_sent, BIT_SIDE)
+    late_shape = late_kept.shape[1:]
+    late_own, s1, s2, s3 = run_kernel(
+        block_fold_kernel,
+        [(late_shape, wide)] + [(late_shape, low_type)] * 3,
+        late_kept, late_got,
+        us=0.5,
+        name="late_block",
+    )
+    late_sums = (
+        late_own, swap(s1, BIT_LOW), swap(s2, BIT_HIGH), swap(s3, BIT_HIGH | BIT_LOW)
     )
     grad_own, grad_send = run_kernel(
         last_kernel,
-        [((shard_pos, width), wide), ((shard_pos, width), wide)],
-        keep, *lasts, first_grad,
+        [((shard_pos, width), wide), ((shard_pos, 2 * width), low_type)],
+        tie(keep, late_kept), *lasts, first_grad, output,
+        us=0.5,
         name="last",
     )
+    grad_got = swap(grad_send, BIT_HIGH)
+    unit_own, unit_sent = run_kernel(
+        final_fold_kernel,
+        [(unit_kept.shape[1:], wide), (unit_kept.shape[1:], low_type)],
+        unit_kept, unit_got,
+        us=0.5,
+        name="unit_low",
+    )
+    down_grad, up_grad = finish(
+        (unit_own, swap(unit_sent, BIT_LOW)), ((0, unit_cols), (unit_cols, 2 * unit_cols)), "unit_total"
+    )
+    out_grad, query_total, key_total, value_total, *shares = finish(
+        tie(late_sums, down_grad, up_grad),
+        [(i * head_cols, (i + 1) * head_cols) for i in range(4)],
+        "late_total",
+        [(shard_rows,)] * 8 + [b_up.shape],
+    )
+    whole_output, hidden_grad = run_kernel(
+        slots_kernel,
+        [(hidden_in.shape, low_type), (hidden_in.shape, wide)],
+        grad_own, output, grad_got,
+        us=0.5,
+        name="slots",
+    )
     return (
-        from_slot(output[:shard_pos], swap(output[shard_pos:], BIT_HIGH)),
-        from_slot(grad_own, swap(grad_send, BIT_HIGH)),
+        whole_output,
+        hidden_grad,
         query_total,
         shares[0],
         key_total,
         value_total,
         shares[1],
-        out_grad,
+        jnp.transpose(out_grad),
         shares[2],
         shares[3],
         shares[4],
         up_grad,
-        shares[8:12].reshape(-1),
-        down_grad,
+        shares[8],
+        jnp.transpose(down_grad),
         shares[5],
         shares[6],
         shares[7],

time: 204 us -> 149 us (0.73)
  waiting for transfers between devices: 96.8 us -> 62.4 us
  local copies, waits for them, and re-layouts: 16.7 us -> 0.01 us
  starting transfers between devices: 64.6 us -> 62.1 us
    ppermute x63 -> x64, waiting for transfers between devices: 92.6 us -> 62.4 us  [swap(): lax.ppermute(values, AXES, [(i, i ^ bit) for i in range(device_count())])]
    unnamed x42 -> x2, local copies, waits for them, and re-layouts: 14.4 us -> 0.01 us
    all_to_all x1 -> x0, starting transfers between devices: 7.25 us -> none  [over_chips(): return lax.all_to_all(values, AXES, 0, 0, axis_index_groups=groups)]
    ppermute x63 -> x64, starting transfers between devices: 57.4 us -> 62.1 us  [swap(): lax.ppermute(values, AXES, [(i, i ^ bit) for i in range(device_count())])]
    all_to_all x1 -> x0, waiting for transfers between devices: 4.25 us -> none  [over_chips(): return lax.all_to_all(values, AXES, 0, 0, axis_index_groups=groups)]
    pallas_call x30 -> x26, Pallas kernels: 23.8 us -> 23.3 us  [run_kernel(): pl.pallas_call(body, out_shape=[jax.ShapeDtypeStruct(shape, kind) for sha...]
  transfers between devices with their start and end apart: 64 -> 64, of which waited for: 33 -> 37; matrix products, arithmetic and copies ran while one was open for 2% -> 0% of each run, Pallas kernels for 8% -> 9%
where the time goes in v3:
time: 149 us
  waiting for transfers between devices  62.4 us (42%)
  starting transfers between devices  62.1 us (42%)
  Pallas kernels  23.3 us (16%)
    ppermute x64, waiting for transfers between devices, swap(): lax.ppermute(values, AXES, [(i, i ^ bit) for i in range(device_count())])  62.4 us
    ppermute x64, starting transfers between devices, swap(): lax.ppermute(values, AXES, [(i, i ^ bit) for i in range(device_count())])  62.1 us
    pallas_call x26, Pallas kernels, run_kernel(): pl.pallas_call(body, out_shape=[jax.ShapeDtypeStruct(shape, kind) for sha...  23.3 us
  transfers between devices with their start and end apart: 64, of which 37 were waited for; matrix products, arithmetic and copies ran while one was open for 0% of the time, Pallas kernels for 9%

profile of v3, /device:TPU:0, one launch (start us, length us, event | category | flops | bytes accessed | tf_op | source)
XLA Modules:
  0.0 149.0 jit_solution(13817998943625819909)
XLA Ops:
  0.7 1.4 rows.1
  2.1 1.4 pack.1
  3.5 3.1 %collective-permute-start.4 = (bf16[64,768]{1,0:T(8,128)(2,1)S(1)}, bf16[64,768]{1,0:T(8,128)(2,1)S(1)}, u32[]{:S(2)}, u32[]{:S(2)}) collective-permute-start(bf16[64,768]{1,0:T(8,128)(2,1)S(1)} %get-tuple-element.180), channel_id=1, source_target_pairs={{0,8},{1,9},{2,10},{3,11},{4,12},{5,13},{6,14},{7,15},{8,0},{9,1},... | collective-permute-start | bytes 294920 | tf_op jit(solution)/shard_map/ppermute | solution.py:26
  6.5 2.6 %collective-permute-start = (bf16[64,768]{1,0:T(8,128)(2,1)S(1)}, bf16[64,768]{1,0:T(8,128)(2,1)S(1)}, u32[]{:S(2)}, u32[]{:S(2)}) collective-permute-start(bf16[64,768]{1,0:T(8,128)(2,1)S(1)} %get-tuple-element.163), channel_id=1, source_target_pairs={{0,16},{1,17},{2,18},{3,19},{4,20},{5,21},{6,22},{7,23},{8,24},{9,... | collective-permute-start | bytes 294920 | tf_op jit(solution)/shard_map/ppermute | solution.py:26
  9.1 1.9 %collective-permute-start.5 = (bf16[64,768]{1,0:T(8,128)(2,1)S(1)}, bf16[64,768]{1,0:T(8,128)(2,1)S(1)}, u32[]{:S(2)}, u32[]{:S(2)}) collective-permute-start(bf16[64,768]{1,0:T(8,128)(2,1)S(1)} %get-tuple-element.179), channel_id=1, source_target_pairs={{0,16},{1,17},{2,18},{3,19},{4,20},{5,21},{6,22},{7,23},{8,24},{9,... | collective-permute-start | bytes 294920 | tf_op jit(solution)/shard_map/ppermute | solution.py:26
  11.1 1.6 %collective-permute-start.7 = (bf16[2,64,768]{2,1,0:T(8,128)(2,1)S(1)}, bf16[2,64,768]{2,1,0:T(8,128)(2,1)S(1)}, u32[]{:S(2)}, u32[]{:S(2)}) collective-permute-start(bf16[2,64,768]{2,1,0:T(8,128)(2,1)S(1)} %pad_maximum_fusion.1.refs_0_), channel_id=1, source_target_pairs={{0,4},{1,5},{2,6},{3,7},{4,0},{5,1},{6,2},{7,3},{8,12},{9,13},{10,... | collective-permute-start | bytes 589832 | tf_op jit(solution)/shard_map/ppermute | solution.py:26
  12.6 2.5 %collective-permute-start.12 = (bf16[48,1536]{1,0:T(8,128)(2,1)S(1)}, bf16[48,1536]{1,0:T(8,128)(2,1)S(1)}, u32[]{:S(2)}, u32[]{:S(2)}) collective-permute-start(bf16[48,1536]{1,0:T(8,128)(2,1)S(1)} %get-tuple-element.185), channel_id=1, source_target_pairs={{0,8},{1,9},{2,10},{3,11},{4,12},{5,13},{6,14},{7,15},{8,0},{9,1},... | collective-permute-start | bytes 442376 | tf_op jit(solution)/shard_map/ppermute | solution.py:26
  15.1 4.1 %collective-permute-done.got_ref.slot_ref = bf16[64,768]{1,0:T(8,128)(2,1)S(1)} collective-permute-done((bf16[64,768]{1,0:T(8,128)(2,1)S(1)}, bf16[64,768]{1,0:T(8,128)(2,1)S(1)}, u32[]{:S(2)}, u32[]{:S(2)}) %collective-permute-start) | collective-permute-done | bytes 98336 | tf_op jit(solution)/shard_map/ppermute | solution.py:26
  19.9 2.4 %collective-permute-done.5 = bf16[64,768]{1,0:T(8,128)(2,1)S(1)} collective-permute-done((bf16[64,768]{1,0:T(8,128)(2,1)S(1)}, bf16[64,768]{1,0:T(8,128)(2,1)S(1)}, u32[]{:S(2)}, u32[]{:S(2)}) %collective-permute-start.5) | collective-permute-done | bytes 98336 | tf_op jit(solution)/shard_map/ppermute | solution.py:26
  22.2 1.5 %collective-permute-start.1 = (bf16[64,768]{1,0:T(8,128)(2,1)S(1)}, bf16[64,768]{1,0:T(8,128)(2,1)S(1)}, u32[]{:S(2)}, u32[]{:S(2)}) collective-permute-start(bf16[64,768]{1,0:T(8,128)(2,1)S(1)} %pad_maximum_fusion.3), channel_id=1, source_target_pairs={{0,1},{1,0},{2,3},{3,2},{4,5},{5,4},{6,7},{7,6},{8,9},{9,8},{10,11... | collective-permute-start | bytes 294920 | tf_op jit(solution)/shard_map/ppermute | solution.py:26
  23.9 1.6 %collective-permute-start.8 = (bf16[2,64,768]{2,1,0:T(8,128)(2,1)S(1)}, bf16[2,64,768]{2,1,0:T(8,128)(2,1)S(1)}, u32[]{:S(2)}, u32[]{:S(2)}) collective-permute-start(bf16[2,64,768]{2,1,0:T(8,128)(2,1)S(1)} %pad_maximum_fusion.2.refs_1_), channel_id=1, source_target_pairs={{0,4},{1,5},{2,6},{3,7},{4,0},{5,1},{6,2},{7,3},{8,12},{9,13},{10,... | collective-permute-start | bytes 589832 | tf_op jit(solution)/shard_map/ppermute | solution.py:26
  25.7 1.1 collective-permute-done.2.low_ref
  26.9 4.3 %collective-permute-done.8.refs_3_ = bf16[2,64,768]{2,1,0:T(8,128)(2,1)S(1)} collective-permute-done((bf16[2,64,768]{2,1,0:T(8,128)(2,1)S(1)}, bf16[2,64,768]{2,1,0:T(8,128)(2,1)S(1)}, u32[]{:S(2)}, u32[]{:S(2)}) %collective-permute-start.8) | collective-permute-done | bytes 196640 | tf_op jit(solution)/shard_map/ppermute | solution.py:26
  31.2 3.0 %collective-permute-start.26 = (bf16[2,48,1536]{2,1,0:T(8,128)(2,1)S(1)}, bf16[2,48,1536]{2,1,0:T(8,128)(2,1)S(1)}, u32[]{:S(2)}, u32[]{:S(2)}) collective-permute-start(bf16[2,48,1536]{2,1,0:T(8,128)(2,1)S(1)} %pad_maximum_fusion.refs_0_), channel_id=1, source_target_pairs={{0,16},{1,17},{2,18},{3,19},{4,20},{5,21},{6,22},{7,23},{8,24},{9,... | collective-permute-start | bytes 884744 | tf_op jit(solution)/shard_map/ppermute | solution.py:26
  34.9 1.6 %collective-permute-start.17 = (bf16[256,192]{1,0:T(8,128)(2,1)S(1)}, bf16[256,192]{1,0:T(8,128)(2,1)S(1)}, u32[]{:S(2)}, u32[]{:S(2)}) collective-permute-start(bf16[256,192]{1,0:T(8,128)(2,1)S(1)} %get-tuple-element.199.refs_4_.value_ref), channel_id=1, source_target_pairs={{0,4},{1,5},{2,6},{3,7},{4,0},{5,1},{6,2},{7,3},{8,12},{9,13},{10,... | collective-permute-start | bytes 294920 | tf_op jit(solution)/shard_map/ppermute | solution.py:26
  37.5 3.8 %collective-permute-done.17.refs_5_ = bf16[256,192]{1,0:T(8,128)(2,1)S(1)} collective-permute-done((bf16[256,192]{1,0:T(8,128)(2,1)S(1)}, bf16[256,192]{1,0:T(8,128)(2,1)S(1)}, u32[]{:S(2)}, u32[]{:S(2)}) %collective-permute-start.17) | collective-permute-done | bytes 98336 | tf_op jit(solution)/shard_map/ppermute | solution.py:26
  41.3 2.1 %collective-permute-done.14.refs_1_ = bf16[256,192]{1,0:T(8,128)(2,1)S(1)} collective-permute-done((bf16[256,192]{1,0:T(8,128)(2,1)S(1)}, bf16[256,192]{1,0:T(8,128)(2,1)S(1)}, u32[]{:S(2)}, u32[]{:S(2)}) %collective-permute-start.14) | collective-permute-done | bytes 98336 | tf_op jit(solution)/shard_map/ppermute | solution.py:26
  43.5 1.6 %collective-permute-start.27 = (bf16[2,48,1536]{2,1,0:T(8,128)(2,1)S(1)}, bf16[2,48,1536]{2,1,0:T(8,128)(2,1)S(1)}, u32[]{:S(2)}, u32[]{:S(2)}) collective-permute-start(bf16[2,48,1536]{2,1,0:T(8,128)(2,1)S(1)} %pad_maximum_fusion.refs_0_), channel_id=1, source_target_pairs={{0,4},{1,5},{2,6},{3,7},{4,0},{5,1},{6,2},{7,3},{8,12},{9,13},{10,... | collective-permute-start | bytes 884744 | tf_op jit(solution)/shard_map/ppermute | solution.py:26
  45.1 2.8 %attend.1 = (bf16[256,192]{1,0:T(8,128)(2,1)S(1)}, f32[256,128]{1,0:T(8,128)S(1)}, f32[64,768]{1,0:T(8,128)S(1)}, bf16[64,768]{1,0:T(8,128)(2,1)S(1)}, bf16[64,7...) custom-call(s32[2]{0:T(128)S(1)} %copy-done, bf16[256,192]{1,0:T(8,128)(2,1)S(1)} %get-tuple-element.198.query_ref, ...), custom_call_target="tpu_custom_call" | custom-call | flops 30000000 | bytes 30000 | tf_op jit(solution)/shard_map/attend/pallas_call | solution.py:413
  48.2 1.5 %collective-permute-start.28 = (bf16[2,48,1536]{2,1,0:T(8,128)(2,1)S(1)}, bf16[2,48,1536]{2,1,0:T(8,128)(2,1)S(1)}, u32[]{:S(2)}, u32[]{:S(2)}) collective-permute-start(bf16[2,48,1536]{2,1,0:T(8,128)(2,1)S(1)} %collective-permute-done.26.refs_1_), channel_id=1, source_target_pairs={{0,4},{1,5},{2,6},{3,7},{4,0},{5,1},{6,2},{7,3},{8,12},{9,13},{10,... | collective-permute-start | bytes 884744 | tf_op jit(solution)/shard_map/ppermute | solution.py:26
  50.2 3.0 %collective-permute-start.22 = (bf16[64,768]{1,0:T(8,128)(2,1)S(1)}, bf16[64,768]{1,0:T(8,128)(2,1)S(1)}, u32[]{:S(2)}, u32[]{:S(2)}) collective-permute-start(bf16[64,768]{1,0:T(8,128)(2,1)S(1)} %get-tuple-element.204), channel_id=1, source_target_pairs={{0,9},{1,8},{2,11},{3,10},{4,13},{5,12},{6,15},{7,14},{8,1},{9,0},... | collective-permute-start | bytes 294920 | tf_op jit(solution)/shard_map/ppermute | solution.py:26
  53.2 1.9 %collective-permute-done.20.got1_ref = bf16[64,768]{1,0:T(8,128)(2,1)S(1)} collective-permute-done((bf16[64,768]{1,0:T(8,128)(2,1)S(1)}, bf16[64,768]{1,0:T(8,128)(2,1)S(1)}, u32[]{:S(2)}, u32[]{:S(2)}) %collective-permute-start.20) | collective-permute-done | bytes 98336 | tf_op jit(solution)/shard_map/ppermute | solution.py:26
  55.4 2.0 %collective-permute-done.22.got3_ref = bf16[64,768]{1,0:T(8,128)(2,1)S(1)} collective-permute-done((bf16[64,768]{1,0:T(8,128)(2,1)S(1)}, bf16[64,768]{1,0:T(8,128)(2,1)S(1)}, u32[]{:S(2)}, u32[]{:S(2)}) %collective-permute-start.22) | collective-permute-done | bytes 98336 | tf_op jit(solution)/shard_map/ppermute | solution.py:26
  57.6 1.7 %collective-permute-done.28.refs_3_ = bf16[2,48,1536]{2,1,0:T(8,128)(2,1)S(1)} collective-permute-done((bf16[2,48,1536]{2,1,0:T(8,128)(2,1)S(1)}, bf16[2,48,1536]{2,1,0:T(8,128)(2,1)S(1)}, u32[]{:S(2)}, u32[]{:S(2)}) %collective-permute-start.28) | collective-permute-done | bytes 294944 | tf_op jit(solution)/shard_map/ppermute | solution.py:26
  60.9 1.4 collective-permute-start.24
  62.3 1.5 %collective-permute-start.23 = (bf16[64,768]{1,0:T(8,128)(2,1)S(1)}, bf16[64,768]{1,0:T(8,128)(2,1)S(1)}, u32[]{:S(2)}, u32[]{:S(2)}) collective-permute-start(bf16[64,768]{1,0:T(8,128)(2,1)S(1)} %get-tuple-element.206.own_ref), channel_id=1, source_target_pairs={{0,1},{1,0},{2,3},{3,2},{4,5},{5,4},{6,7},{7,6},{8,9},{9,8},{10,11... | collective-permute-start | bytes 294920 | tf_op jit(solution)/shard_map/ppermute | solution.py:26
  64.0 2.9 %collective-permute-done.25.got3_ref = bf16[64,768]{1,0:T(8,128)(2,1)S(1)} collective-permute-done((bf16[64,768]{1,0:T(8,128)(2,1)S(1)}, bf16[64,768]{1,0:T(8,128)(2,1)S(1)}, u32[]{:S(2)}, u32[]{:S(2)}) %collective-permute-start.25) | collective-permute-done | bytes 98336 | tf_op jit(solution)/shard_map/ppermute | solution.py:26
  67.1 0.9 collective-permute-done.23.got1_ref
  68.0 1.6 %hidden.1 = (f32[64,768]{1,0:T(8,128)S(1)}, bf16[64,768]{1,0:T(8,128)(2,1)S(1)}, bf16[64,768]{1,0:T(8,128)(2,1)S(1)}, bf16[64,768]{1,0:T(8,128)(2,1)S(1)}, bf16[...) custom-call(bf16[64,768]{1,0:T(8,128)(2,1)S(1)} %get-tuple-element.206.own_ref, ...), custom_call_target="tpu_custom_call" | custom-call | flops 20000000 | bytes 20000 | tf_op jit(solution)/shard_map/hidden/pallas_call | solution.py:413
  70.7 2.5 %collective-permute-start.35 = (bf16[64,768]{1,0:T(8,128)(2,1)S(1)}, bf16[64,768]{1,0:T(8,128)(2,1)S(1)}, u32[]{:S(2)}, u32[]{:S(2)}) collective-permute-start(bf16[64,768]{1,0:T(8,128)(2,1)S(1)} %get-tuple-element.221), channel_id=1, source_target_pairs={{0,9},{1,8},{2,11},{3,10},{4,13},{5,12},{6,15},{7,14},{8,1},{9,0},... | collective-permute-start | bytes 294920 | tf_op jit(solution)/shard_map/ppermute | solution.py:26
  73.2 2.0 %collective-permute-done.33.got1_ref = bf16[64,768]{1,0:T(8,128)(2,1)S(1)} collective-permute-done((bf16[64,768]{1,0:T(8,128)(2,1)S(1)}, bf16[64,768]{1,0:T(8,128)(2,1)S(1)}, u32[]{:S(2)}, u32[]{:S(2)}) %collective-permute-start.33) | collective-permute-done | bytes 98336 | tf_op jit(solution)/shard_map/ppermute | solution.py:26
  75.3 2.1 %collective-permute-done.35.got3_ref = bf16[64,768]{1,0:T(8,128)(2,1)S(1)} collective-permute-done((bf16[64,768]{1,0:T(8,128)(2,1)S(1)}, bf16[64,768]{1,0:T(8,128)(2,1)S(1)}, u32[]{:S(2)}, u32[]{:S(2)}) %collective-permute-start.35) | collective-permute-done | bytes 98336 | tf_op jit(solution)/shard_map/ppermute | solution.py:26
  78.3 1.5 collective-permute-start.38
  80.2 1.6 %collective-permute-start.36 = (bf16[64,768]{1,0:T(8,128)(2,1)S(1)}, bf16[64,768]{1,0:T(8,128)(2,1)S(1)}, u32[]{:S(2)}, u32[]{:S(2)}) collective-permute-start(bf16[64,768]{1,0:T(8,128)(2,1)S(1)} %get-tuple-element.224.own_ref), channel_id=1, source_target_pairs={{0,1},{1,0},{2,3},{3,2},{4,5},{5,4},{6,7},{7,6},{8,9},{9,8},{10,11... | collective-permute-start | bytes 294920 | tf_op jit(solution)/shard_map/ppermute | solution.py:26
  81.8 2.0 %collective-permute-done.38.got3_ref = bf16[64,768]{1,0:T(8,128)(2,1)S(1)} collective-permute-done((bf16[64,768]{1,0:T(8,128)(2,1)S(1)}, bf16[64,768]{1,0:T(8,128)(2,1)S(1)}, u32[]{:S(2)}, u32[]{:S(2)}) %collective-permute-start.38) | collective-permute-done | bytes 98336 | tf_op jit(solution)/shard_map/ppermute | solution.py:26
  85.8 1.1 unit_weights.1
  87.5 1.5 %collective-permute-done.39.refs_1_ = bf16[8,48,768]{2,1,0:T(8,128)(2,1)S(1)} collective-permute-done((bf16[8,48,768]{2,1,0:T(8,128)(2,1)S(1)}, bf16[8,48,768]{2,1,0:T(8,128)(2,1)S(1)}, u32[]{:S(2)}, u32[]{:S(2)}) %collective-permute-start.39) | collective-permute-done | bytes 589856 | tf_op jit(solution)/shard_map/ppermute | solution.py:26
  90.1 1.6 %collective-permute-start.47 = (bf16[4,48,1536]{2,1,0:T(8,128)(2,1)S(1)}, bf16[4,48,1536]{2,1,0:T(8,128)(2,1)S(1)}, u32[]{:S(2)}, u32[]{:S(2)}) collective-permute-start(bf16[4,48,1536]{2,1,0:T(8,128)(2,1)S(1)} %get-tuple-element.238), channel_id=1, source_target_pairs={{0,4},{1,5},{2,6},{3,7},{4,0},{5,1},{6,2},{7,3},{8,12},{9,13},{10,... | collective-permute-start | bytes 1769480 | tf_op jit(solution)/shard_map/ppermute | solution.py:26
  91.6 1.5 %collective-permute-start.41 = (bf16[64,768]{1,0:T(8,128)(2,1)S(1)}, bf16[64,768]{1,0:T(8,128)(2,1)S(1)}, u32[]{:S(2)}, u32[]{:S(2)}) collective-permute-start(bf16[64,768]{1,0:T(8,128)(2,1)S(1)} %get-tuple-element.239), channel_id=1, source_target_pairs={{0,1},{1,0},{2,3},{3,2},{4,5},{5,4},{6,7},{7,6},{8,9},{9,8},{10,11... | collective-permute-start | bytes 294920 | tf_op jit(solution)/shard_map/ppermute | solution.py:26
  93.8 1.3 collective-permute-start.43
  95.1 1.1 collective-permute-done.41.got1_ref
  96.2 2.3 %collective-permute-done.42.got2_ref = bf16[64,768]{1,0:T(8,128)(2,1)S(1)} collective-permute-done((bf16[64,768]{1,0:T(8,128)(2,1)S(1)}, bf16[64,768]{1,0:T(8,128)(2,1)S(1)}, u32[]{:S(2)}, u32[]{:S(2)}) %collective-permute-start.42) | collective-permute-done | bytes 98336 | tf_op jit(solution)/shard_map/ppermute | solution.py:26
  98.6 1.2 collective-permute-done.43.got3_ref
  100.0 1.4 collective-permute-start.46
  101.4 1.5 collective-permute-start.45
  103.6 2.0 %collective-permute-done.46.got3_ref = bf16[64,768]{1,0:T(8,128)(2,1)S(1)} collective-permute-done((bf16[64,768]{1,0:T(8,128)(2,1)S(1)}, bf16[64,768]{1,0:T(8,128)(2,1)S(1)}, u32[]{:S(2)}, u32[]{:S(2)}) %collective-permute-start.46) | collective-permute-done | bytes 98336 | tf_op jit(solution)/shard_map/ppermute | solution.py:26
  106.5 1.0 collective-permute-done.44.got1_ref
  107.5 1.0 attended_back.1
  109.2 1.4 collective-permute-start.51
  110.6 2.5 %query_back.1 = (bf16[256,192]{1,0:T(8,128)(2,1)S(1)}, f32[1,192]{1,0:T(1,128)S(1)}) custom-call(s32[2]{0:T(128)S(1)} %copy-done, bf16[256,512]{1,0:T(8,128)(2,1)S(1)} %get-tuple-element.247.packet_ref.g0_ref, bf16[256,192]{1,0:T(8,128)(2,1)S(1)} %get-tuple-element.250.refs_0_.key_ref, bf16[256,192]{1,0:T(8,128)(2,1)S(1)} %collective-permute-done.14.refs_1_, ...), custom_call_target="tpu_custom_call" | custom-call | flops 30000000 | bytes 30000 | tf_op jit(solution)/shard_map/query_back/pallas_call | solution.py:413
  113.1 1.8 %collective-permute-done.48.g1_ref = bf16[256,512]{1,0:T(8,128)(2,1)S(1)} collective-permute-done((bf16[256,512]{1,0:T(8,128)(2,1)S(1)}, bf16[256,512]{1,0:T(8,128)(2,1)S(1)}, u32[]{:S(2)}, u32[]{:S(2)}) %collective-permute-start.48) | collective-permute-done | bytes 262176 | tf_op jit(solution)/shard_map/ppermute | solution.py:26
  116.5 3.7 %pair_back.1 = (f32[64,768]{1,0:T(8,128)S(1)}, bf16[64,768]{1,0:T(8,128)(2,1)S(1)}, bf16[64,768]{1,0:T(8,128)(2,1)S(1)}, bf16[64,768]{1,0:T(8,128)(2,1)S(1)}, bf16[256,576]{1,0:T(8,128)(2,1)S(1)}) custom-call(s32[2]{0:T(128)S(1)} %copy-done, bf16[256,192]{1,0:T(8,128)(2,1)S(1)} %get-tuple-element.250.refs_0_.key_ref, ...), custom_call_target="tpu_custom_call" | custom-call | flops 40000000 | bytes 40000 | tf_op jit(solution)/shard_map/pair_back/pallas_call | solution.py:413
  120.2 2.0 %collective-permute-done.51.refs_1_ = bf16[2,48,1536]{2,1,0:T(8,128)(2,1)S(1)} collective-permute-done((bf16[2,48,1536]{2,1,0:T(8,128)(2,1)S(1)}, bf16[2,48,1536]{2,1,0:T(8,128)(2,1)S(1)}, u32[]{:S(2)}, u32[]{:S(2)}) %collective-permute-start.51) | collective-permute-done | bytes 294944 | tf_op jit(solution)/shard_map/ppermute | solution.py:26
  122.2 1.1 head_weights.1
  123.9 1.8 %collective-permute-done.53.refs_1_ = bf16[8,48,192]{2,1,0:T(8,128)(2,1)S(1)} collective-permute-done((bf16[8,48,192]{2,1,0:T(8,128)(2,1)S(1)}, bf16[8,48,192]{2,1,0:T(8,128)(2,1)S(1)}, u32[]{:S(2)}, u32[]{:S(2)}) %collective-permute-start.53) | collective-permute-done | bytes 147488 | tf_op jit(solution)/shard_map/ppermute | solution.py:26
  126.0 1.6 %collective-permute-start.59 = (bf16[4,48,896]{2,1,0:T(8,128)(2,1)S(1)}, bf16[4,48,896]{2,1,0:T(8,128)(2,1)S(1)}, u32[]{:S(2)}, u32[]{:S(2)}) collective-permute-start(bf16[4,48,896]{2,1,0:T(8,128)(2,1)S(1)} %get-tuple-element.281), channel_id=1, source_target_pairs={{0,4},{1,5},{2,6},{3,7},{4,0},{5,1},{6,2},{7,3},{8,12},{9,13},{10,... | collective-permute-start | bytes 1032200 | tf_op jit(solution)/shard_map/ppermute | solution.py:26
  127.5 1.0 collective-permute-start.55
  128.6 2.4 %collective-permute-start.57 = (bf16[64,768]{1,0:T(8,128)(2,1)S(1)}, bf16[64,768]{1,0:T(8,128)(2,1)S(1)}, u32[]{:S(2)}, u32[]{:S(2)}) collective-permute-start(bf16[64,768]{1,0:T(8,128)(2,1)S(1)} %get-tuple-element.274), channel_id=1, source_target_pairs={{0,9},{1,8},{2,11},{3,10},{4,13},{5,12},{6,15},{7,14},{8,1},{9,0},... | collective-permute-start | bytes 294920 | tf_op jit(solution)/shard_map/ppermute | solution.py:26
  131.2 1.0 collective-permute-done.55.got1_ref
  132.2 2.2 %collective-permute-done.56.got2_ref = bf16[64,768]{1,0:T(8,128)(2,1)S(1)} collective-permute-done((bf16[64,768]{1,0:T(8,128)(2,1)S(1)}, bf16[64,768]{1,0:T(8,128)(2,1)S(1)}, u32[]{:S(2)}, u32[]{:S(2)}) %collective-permute-start.56) | collective-permute-done | bytes 98336 | tf_op jit(solution)/shard_map/ppermute | solution.py:26
  134.3 2.5 %collective-permute-done.57.got3_ref = bf16[64,768]{1,0:T(8,128)(2,1)S(1)} collective-permute-done((bf16[64,768]{1,0:T(8,128)(2,1)S(1)}, bf16[64,768]{1,0:T(8,128)(2,1)S(1)}, u32[]{:S(2)}, u32[]{:S(2)}) %collective-permute-start.57) | collective-permute-done | bytes 98336 | tf_op jit(solution)/shard_map/ppermute | solution.py:26
  137.9 1.7 %collective-permute-start.60 = (bf16[48,896]{1,0:T(8,128)(2,1)S(1)}, bf16[48,896]{1,0:T(8,128)(2,1)S(1)}, u32[]{:S(2)}, u32[]{:S(2)}) collective-permute-start(bf16[48,896]{1,0:T(8,128)(2,1)S(1)} %get-tuple-element.283), channel_id=1, source_target_pairs={{0,8},{1,9},{2,10},{3,11},{4,12},{5,13},{6,14},{7,15},{8,0},{9,1},... | collective-permute-start | bytes 258056 | tf_op jit(solution)/shard_map/ppermute | solution.py:26
  140.5 1.9 %collective-permute-start.62 = (bf16[48,896]{1,0:T(8,128)(2,1)S(1)}, bf16[48,896]{1,0:T(8,128)(2,1)S(1)}, u32[]{:S(2)}, u32[]{:S(2)}) collective-permute-start(bf16[48,896]{1,0:T(8,128)(2,1)S(1)} %get-tuple-element.285), channel_id=1, source_target_pairs={{0,24},{1,25},{2,26},{3,27},{4,28},{5,29},{6,30},{7,31},{8,16},{9,... | collective-permute-start | bytes 258056 | tf_op jit(solution)/shard_map/ppermute | solution.py:26
  143.2 3.9 %collective-permute-done.58.got_ref = bf16[32,1536]{1,0:T(8,128)(2,1)S(1)} collective-permute-done((bf16[32,1536]{1,0:T(8,128)(2,1)S(1)}, bf16[32,1536]{1,0:T(8,128)(2,1)S(1)}, u32[]{:S(2)}, u32[]{:S(2)}) %collective-permute-start.58) | collective-permute-done | bytes 98336 | tf_op jit(solution)/shard_map/ppermute | solution.py:26
  (97 shorter events, 22.5 us)
Async XLA Ops:
  3.5 7.6 %collective-permute-start.4 = (bf16[64,768]{1,0:T(8,128)(2,1)S(1)}, bf16[64,768]{1,0:T(8,128)(2,1)S(1)}, u32[]{:S(2)}, u32[]{:S(2)}) collective-permute-start(bf16[64,768]{1,0:T(8,128)(2,1)S(1)} %get-tuple-element.180), channel_id=1, source_target_pairs={{0,8},{1,9},{2,10},{3,11},{4,12},{5,13},{6,14},{7,15},{8,0},{9,1},... | collective-permute-start | bytes 294920 | tf_op jit(solution)/shard_map/ppermute | solution.py:26
  6.5 12.6 %collective-permute-start = (bf16[64,768]{1,0:T(8,128)(2,1)S(1)}, bf16[64,768]{1,0:T(8,128)(2,1)S(1)}, u32[]{:S(2)}, u32[]{:S(2)}) collective-permute-start(bf16[64,768]{1,0:T(8,128)(2,1)S(1)} %get-tuple-element.163), channel_id=1, source_target_pairs={{0,16},{1,17},{2,18},{3,19},{4,20},{5,21},{6,22},{7,23},{8,24},{9,... | collective-permute-start | bytes 294920 | tf_op jit(solution)/shard_map/ppermute | solution.py:26
  9.1 13.1 %collective-permute-start.6 = (bf16[64,768]{1,0:T(8,128)(2,1)S(1)}, bf16[64,768]{1,0:T(8,128)(2,1)S(1)}, u32[]{:S(2)}, u32[]{:S(2)}) collective-permute-start(bf16[64,768]{1,0:T(8,128)(2,1)S(1)} %get-tuple-element.180), channel_id=1, source_target_pairs={{0,24},{1,25},{2,26},{3,27},{4,28},{5,29},{6,30},{7,31},{8,16},{9,... | collective-permute-start | bytes 294920 | tf_op jit(solution)/shard_map/ppermute | solution.py:26
  9.1 13.1 %collective-permute-start.5 = (bf16[64,768]{1,0:T(8,128)(2,1)S(1)}, bf16[64,768]{1,0:T(8,128)(2,1)S(1)}, u32[]{:S(2)}, u32[]{:S(2)}) collective-permute-start(bf16[64,768]{1,0:T(8,128)(2,1)S(1)} %get-tuple-element.179), channel_id=1, source_target_pairs={{0,16},{1,17},{2,18},{3,19},{4,20},{5,21},{6,22},{7,23},{8,24},{9,... | collective-permute-start | bytes 294920 | tf_op jit(solution)/shard_map/ppermute | solution.py:26
  11.1 12.7 %collective-permute-start.7 = (bf16[2,64,768]{2,1,0:T(8,128)(2,1)S(1)}, bf16[2,64,768]{2,1,0:T(8,128)(2,1)S(1)}, u32[]{:S(2)}, u32[]{:S(2)}) collective-permute-start(bf16[2,64,768]{2,1,0:T(8,128)(2,1)S(1)} %pad_maximum_fusion.1.refs_0_), channel_id=1, source_target_pairs={{0,4},{1,5},{2,6},{3,7},{4,0},{5,1},{6,2},{7,3},{8,12},{9,13},{10,... | collective-permute-start | bytes 589832 | tf_op jit(solution)/shard_map/ppermute | solution.py:26
  12.6 11.2 %collective-permute-start.12 = (bf16[48,1536]{1,0:T(8,128)(2,1)S(1)}, bf16[48,1536]{1,0:T(8,128)(2,1)S(1)}, u32[]{:S(2)}, u32[]{:S(2)}) collective-permute-start(bf16[48,1536]{1,0:T(8,128)(2,1)S(1)} %get-tuple-element.185), channel_id=1, source_target_pairs={{0,8},{1,9},{2,10},{3,11},{4,12},{5,13},{6,14},{7,15},{8,0},{9,1},... | collective-permute-start | bytes 442376 | tf_op jit(solution)/shard_map/ppermute | solution.py:26
  19.2 6.3 %collective-permute-start.3 = (bf16[64,768]{1,0:T(8,128)(2,1)S(1)}, bf16[64,768]{1,0:T(8,128)(2,1)S(1)}, u32[]{:S(2)}, u32[]{:S(2)}) collective-permute-start(bf16[64,768]{1,0:T(8,128)(2,1)S(1)} %pad_maximum_fusion.3), channel_id=1, source_target_pairs={{0,9},{1,8},{2,11},{3,10},{4,13},{5,12},{6,15},{7,14},{8,1},{9,0},... | collective-permute-start | bytes 294920 | tf_op jit(solution)/shard_map/ppermute | solution.py:26
  22.2 4.6 %collective-permute-start.2 = (bf16[64,768]{1,0:T(8,128)(2,1)S(1)}, bf16[64,768]{1,0:T(8,128)(2,1)S(1)}, u32[]{:S(2)}, u32[]{:S(2)}) collective-permute-start(bf16[64,768]{1,0:T(8,128)(2,1)S(1)} %pad_maximum_fusion.3), channel_id=1, source_target_pairs={{0,8},{1,9},{2,10},{3,11},{4,12},{5,13},{6,14},{7,15},{8,0},{9,1},... | collective-permute-start | bytes 294920 | tf_op jit(solution)/shard_map/ppermute | solution.py:26
  22.2 4.6 %collective-permute-start.1 = (bf16[64,768]{1,0:T(8,128)(2,1)S(1)}, bf16[64,768]{1,0:T(8,128)(2,1)S(1)}, u32[]{:S(2)}, u32[]{:S(2)}) collective-permute-start(bf16[64,768]{1,0:T(8,128)(2,1)S(1)} %pad_maximum_fusion.3), channel_id=1, source_target_pairs={{0,1},{1,0},{2,3},{3,2},{4,5},{5,4},{6,7},{7,6},{8,9},{9,8},{10,11... | collective-permute-start | bytes 294920 | tf_op jit(solution)/shard_map/ppermute | solution.py:26
  23.8 10.4 %collective-permute-start.9 = (bf16[2,64,768]{2,1,0:T(8,128)(2,1)S(1)}, bf16[2,64,768]{2,1,0:T(8,128)(2,1)S(1)}, u32[]{:S(2)}, u32[]{:S(2)}) collective-permute-start(bf16[2,64,768]{2,1,0:T(8,128)(2,1)S(1)} %pad_maximum_fusion.1.refs_0_), channel_id=1, source_target_pairs={{0,2},{1,3},{2,0},{3,1},{4,6},{5,7},{6,4},{7,5},{8,10},{9,11},{10,... | collective-permute-start | bytes 589832 | tf_op jit(solution)/shard_map/ppermute | solution.py:26
  23.9 7.3 %collective-permute-start.8 = (bf16[2,64,768]{2,1,0:T(8,128)(2,1)S(1)}, bf16[2,64,768]{2,1,0:T(8,128)(2,1)S(1)}, u32[]{:S(2)}, u32[]{:S(2)}) collective-permute-start(bf16[2,64,768]{2,1,0:T(8,128)(2,1)S(1)} %pad_maximum_fusion.2.refs_1_), channel_id=1, source_target_pairs={{0,4},{1,5},{2,6},{3,7},{4,0},{5,1},{6,2},{7,3},{8,12},{9,13},{10,... | collective-permute-start | bytes 589832 | tf_op jit(solution)/shard_map/ppermute | solution.py:26
  25.5 8.8 %collective-permute-start.10 = (bf16[2,64,768]{2,1,0:T(8,128)(2,1)S(1)}, bf16[2,64,768]{2,1,0:T(8,128)(2,1)S(1)}, u32[]{:S(2)}, u32[]{:S(2)}) collective-permute-start(bf16[2,64,768]{2,1,0:T(8,128)(2,1)S(1)} %pad_maximum_fusion.2.refs_1_), channel_id=1, source_target_pairs={{0,2},{1,3},{2,0},{3,1},{4,6},{5,7},{6,4},{7,5},{8,10},{9,11},{10,... | collective-permute-start | bytes 589832 | tf_op jit(solution)/shard_map/ppermute | solution.py:26
  26.9 7.4 %collective-permute-start.11 = (bf16[2,64,768]{2,1,0:T(8,128)(2,1)S(1)}, bf16[2,64,768]{2,1,0:T(8,128)(2,1)S(1)}, u32[]{:S(2)}, u32[]{:S(2)}) collective-permute-start(bf16[2,64,768]{2,1,0:T(8,128)(2,1)S(1)} %collective-permute-done.7.refs_2_), channel_id=1, source_target_pairs={{0,2},{1,3},{2,0},{3,1},{4,6},{5,7},{6,4},{7,5},{8,10},{9,11},{10,... | collective-permute-start | bytes 589832 | tf_op jit(solution)/shard_map/ppermute | solution.py:26
  31.2 3.0 %collective-permute-start.13 = (bf16[2,64,768]{2,1,0:T(8,128)(2,1)S(1)}, bf16[2,64,768]{2,1,0:T(8,128)(2,1)S(1)}, u32[]{:S(2)}, u32[]{:S(2)}) collective-permute-start(bf16[2,64,768]{2,1,0:T(8,128)(2,1)S(1)} %collective-permute-done.8.refs_3_), channel_id=1, source_target_pairs={{0,2},{1,3},{2,0},{3,1},{4,6},{5,7},{6,4},{7,5},{8,10},{9,11},{10,... | collective-permute-start | bytes 589832 | tf_op jit(solution)/shard_map/ppermute | solution.py:26
  31.2 17.0 %collective-permute-start.26 = (bf16[2,48,1536]{2,1,0:T(8,128)(2,1)S(1)}, bf16[2,48,1536]{2,1,0:T(8,128)(2,1)S(1)}, u32[]{:S(2)}, u32[]{:S(2)}) collective-permute-start(bf16[2,48,1536]{2,1,0:T(8,128)(2,1)S(1)} %pad_maximum_fusion.refs_0_), channel_id=1, source_target_pairs={{0,16},{1,17},{2,18},{3,19},{4,20},{5,21},{6,22},{7,23},{8,24},{9,... | collective-permute-start | bytes 884744 | tf_op jit(solution)/shard_map/ppermute | solution.py:26
  34.9 6.4 %collective-permute-start.17 = (bf16[256,192]{1,0:T(8,128)(2,1)S(1)}, bf16[256,192]{1,0:T(8,128)(2,1)S(1)}, u32[]{:S(2)}, u32[]{:S(2)}) collective-permute-start(bf16[256,192]{1,0:T(8,128)(2,1)S(1)} %get-tuple-element.199.refs_4_.value_ref), channel_id=1, source_target_pairs={{0,4},{1,5},{2,6},{3,7},{4,0},{5,1},{6,2},{7,3},{8,12},{9,13},{10,... | collective-permute-start | bytes 294920 | tf_op jit(solution)/shard_map/ppermute | solution.py:26
  36.4 6.9 %collective-permute-start.14 = (bf16[256,192]{1,0:T(8,128)(2,1)S(1)}, bf16[256,192]{1,0:T(8,128)(2,1)S(1)}, u32[]{:S(2)}, u32[]{:S(2)}) collective-permute-start(bf16[256,192]{1,0:T(8,128)(2,1)S(1)} %get-tuple-element.250.refs_0_.key_ref), channel_id=1, source_target_pairs={{0,4},{1,5},{2,6},{3,7},{4,0},{5,1},{6,2},{7,3},{8,12},{9,13},{10,... | collective-permute-start | bytes 294920 | tf_op jit(solution)/shard_map/ppermute | solution.py:26
  37.0 6.5 %collective-permute-start.18 = (bf16[256,192]{1,0:T(8,128)(2,1)S(1)}, bf16[256,192]{1,0:T(8,128)(2,1)S(1)}, u32[]{:S(2)}, u32[]{:S(2)}) collective-permute-start(bf16[256,192]{1,0:T(8,128)(2,1)S(1)} %get-tuple-element.199.refs_4_.value_ref), channel_id=1, source_target_pairs={{0,2},{1,3},{2,0},{3,1},{4,6},{5,7},{6,4},{7,5},{8,10},{9,11},{10,... | collective-permute-start | bytes 294920 | tf_op jit(solution)/shard_map/ppermute | solution.py:26
  37.0 8.1 %collective-permute-start.15 = (bf16[256,192]{1,0:T(8,128)(2,1)S(1)}, bf16[256,192]{1,0:T(8,128)(2,1)S(1)}, u32[]{:S(2)}, u32[]{:S(2)}) collective-permute-start(bf16[256,192]{1,0:T(8,128)(2,1)S(1)} %get-tuple-element.250.refs_0_.key_ref), channel_id=1, source_target_pairs={{0,2},{1,3},{2,0},{3,1},{4,6},{5,7},{6,4},{7,5},{8,10},{9,11},{10,... | collective-permute-start | bytes 294920 | tf_op jit(solution)/shard_map/ppermute | solution.py:26
  41.3 3.8 %collective-permute-start.19 = (bf16[256,192]{1,0:T(8,128)(2,1)S(1)}, bf16[256,192]{1,0:T(8,128)(2,1)S(1)}, u32[]{:S(2)}, u32[]{:S(2)}) collective-permute-start(bf16[256,192]{1,0:T(8,128)(2,1)S(1)} %collective-permute-done.17.refs_5_), channel_id=1, source_target_pairs={{0,2},{1,3},{2,0},{3,1},{4,6},{5,7},{6,4},{7,5},{8,10},{9,11},{10,... | collective-permute-start | bytes 294920 | tf_op jit(solution)/shard_map/ppermute | solution.py:26
  43.4 1.7 %collective-permute-start.16 = (bf16[256,192]{1,0:T(8,128)(2,1)S(1)}, bf16[256,192]{1,0:T(8,128)(2,1)S(1)}, u32[]{:S(2)}, u32[]{:S(2)}) collective-permute-start(bf16[256,192]{1,0:T(8,128)(2,1)S(1)} %collective-permute-done.14.refs_1_), channel_id=1, source_target_pairs={{0,2},{1,3},{2,0},{3,1},{4,6},{5,7},{6,4},{7,5},{8,10},{9,11},{10,... | collective-permute-start | bytes 294920 | tf_op jit(solution)/shard_map/ppermute | solution.py:26
  43.5 14.1 %collective-permute-start.27 = (bf16[2,48,1536]{2,1,0:T(8,128)(2,1)S(1)}, bf16[2,48,1536]{2,1,0:T(8,128)(2,1)S(1)}, u32[]{:S(2)}, u32[]{:S(2)}) collective-permute-start(bf16[2,48,1536]{2,1,0:T(8,128)(2,1)S(1)} %pad_maximum_fusion.refs_0_), channel_id=1, source_target_pairs={{0,4},{1,5},{2,6},{3,7},{4,0},{5,1},{6,2},{7,3},{8,12},{9,13},{10,... | collective-permute-start | bytes 884744 | tf_op jit(solution)/shard_map/ppermute | solution.py:26
  48.2 11.1 %collective-permute-start.28 = (bf16[2,48,1536]{2,1,0:T(8,128)(2,1)S(1)}, bf16[2,48,1536]{2,1,0:T(8,128)(2,1)S(1)}, u32[]{:S(2)}, u32[]{:S(2)}) collective-permute-start(bf16[2,48,1536]{2,1,0:T(8,128)(2,1)S(1)} %collective-permute-done.26.refs_1_), channel_id=1, source_target_pairs={{0,4},{1,5},{2,6},{3,7},{4,0},{5,1},{6,2},{7,3},{8,12},{9,13},{10,... | collective-permute-start | bytes 884744 | tf_op jit(solution)/shard_map/ppermute | solution.py:26
  49.7 5.4 %collective-permute-start.20 = (bf16[64,768]{1,0:T(8,128)(2,1)S(1)}, bf16[64,768]{1,0:T(8,128)(2,1)S(1)}, u32[]{:S(2)}, u32[]{:S(2)}) collective-permute-start(bf16[64,768]{1,0:T(8,128)(2,1)S(1)} %get-tuple-element.202), channel_id=1, source_target_pairs={{0,1},{1,0},{2,3},{3,2},{4,5},{5,4},{6,7},{7,6},{8,9},{9,8},{10,11... | collective-permute-start | bytes 294920 | tf_op jit(solution)/shard_map/ppermute | solution.py:26
  50.2 5.1 %collective-permute-start.21 = (bf16[64,768]{1,0:T(8,128)(2,1)S(1)}, bf16[64,768]{1,0:T(8,128)(2,1)S(1)}, u32[]{:S(2)}, u32[]{:S(2)}) collective-permute-start(bf16[64,768]{1,0:T(8,128)(2,1)S(1)} %get-tuple-element.203), channel_id=1, source_target_pairs={{0,8},{1,9},{2,10},{3,11},{4,12},{5,13},{6,14},{7,15},{8,0},{9,1},... | collective-permute-start | bytes 294920 | tf_op jit(solution)/shard_map/ppermute | solution.py:26
  50.2 7.1 %collective-permute-start.22 = (bf16[64,768]{1,0:T(8,128)(2,1)S(1)}, bf16[64,768]{1,0:T(8,128)(2,1)S(1)}, u32[]{:S(2)}, u32[]{:S(2)}) collective-permute-start(bf16[64,768]{1,0:T(8,128)(2,1)S(1)} %get-tuple-element.204), channel_id=1, source_target_pairs={{0,9},{1,8},{2,11},{3,10},{4,13},{5,12},{6,15},{7,14},{8,1},{9,0},... | collective-permute-start | bytes 294920 | tf_op jit(solution)/shard_map/ppermute | solution.py:26
  59.3 1.6 %collective-permute-start.29 = (bf16[2,48,1536]{2,1,0:T(8,128)(2,1)S(1)}, bf16[2,48,1536]{2,1,0:T(8,128)(2,1)S(1)}, u32[]{:S(2)}, u32[]{:S(2)}) collective-permute-start(bf16[2,48,1536]{2,1,0:T(8,128)(2,1)S(1)} %pad_maximum_fusion.refs_0_), channel_id=1, source_target_pairs={{0,2},{1,3},{2,0},{3,1},{4,6},{5,7},{6,4},{7,5},{8,10},{9,11},{10,... | collective-permute-start | bytes 884744 | tf_op jit(solution)/shard_map/ppermute | solution.py:26
  59.3 3.0 %collective-permute-start.30 = (bf16[2,48,1536]{2,1,0:T(8,128)(2,1)S(1)}, bf16[2,48,1536]{2,1,0:T(8,128)(2,1)S(1)}, u32[]{:S(2)}, u32[]{:S(2)}) collective-permute-start(bf16[2,48,1536]{2,1,0:T(8,128)(2,1)S(1)} %collective-permute-done.26.refs_1_), channel_id=1, source_target_pairs={{0,2},{1,3},{2,0},{3,1},{4,6},{5,7},{6,4},{7,5},{8,10},{9,11},{10,... | collective-permute-start | bytes 884744 | tf_op jit(solution)/shard_map/ppermute | solution.py:26
  59.8 4.0 %collective-permute-start.31 = (bf16[2,48,1536]{2,1,0:T(8,128)(2,1)S(1)}, bf16[2,48,1536]{2,1,0:T(8,128)(2,1)S(1)}, u32[]{:S(2)}, u32[]{:S(2)}) collective-permute-start(bf16[2,48,1536]{2,1,0:T(8,128)(2,1)S(1)} %collective-permute-done.27.refs_2_), channel_id=1, source_target_pairs={{0,2},{1,3},{2,0},{3,1},{4,6},{5,7},{6,4},{7,5},{8,10},{9,11},{10,... | collective-permute-start | bytes 884744 | tf_op jit(solution)/shard_map/ppermute | solution.py:26
  59.8 4.0 %collective-permute-start.32 = (bf16[2,48,1536]{2,1,0:T(8,128)(2,1)S(1)}, bf16[2,48,1536]{2,1,0:T(8,128)(2,1)S(1)}, u32[]{:S(2)}, u32[]{:S(2)}) collective-permute-start(bf16[2,48,1536]{2,1,0:T(8,128)(2,1)S(1)} %collective-permute-done.28.refs_3_), channel_id=1, source_target_pairs={{0,2},{1,3},{2,0},{3,1},{4,6},{5,7},{6,4},{7,5},{8,10},{9,11},{10,... | collective-permute-start | bytes 884744 | tf_op jit(solution)/shard_map/ppermute | solution.py:26
  60.3 6.6 %collective-permute-start.25 = (bf16[64,768]{1,0:T(8,128)(2,1)S(1)}, bf16[64,768]{1,0:T(8,128)(2,1)S(1)}, u32[]{:S(2)}, u32[]{:S(2)}) collective-permute-start(bf16[64,768]{1,0:T(8,128)(2,1)S(1)} %get-tuple-element.206.own_ref), channel_id=1, source_target_pairs={{0,9},{1,8},{2,11},{3,10},{4,13},{5,12},{6,15},{7,14},{8,1},{9,0},... | collective-permute-start | bytes 294920 | tf_op jit(solution)/shard_map/ppermute | solution.py:26
  60.9 6.2 %collective-permute-start.24 = (bf16[64,768]{1,0:T(8,128)(2,1)S(1)}, bf16[64,768]{1,0:T(8,128)(2,1)S(1)}, u32[]{:S(2)}, u32[]{:S(2)}) collective-permute-start(bf16[64,768]{1,0:T(8,128)(2,1)S(1)} %get-tuple-element.206.own_ref), channel_id=1, source_target_pairs={{0,8},{1,9},{2,10},{3,11},{4,12},{5,13},{6,14},{7,15},{8,0},{9,1},... | collective-permute-start | bytes 294920 | tf_op jit(solution)/shard_map/ppermute | solution.py:26
  62.3 5.7 %collective-permute-start.23 = (bf16[64,768]{1,0:T(8,128)(2,1)S(1)}, bf16[64,768]{1,0:T(8,128)(2,1)S(1)}, u32[]{:S(2)}, u32[]{:S(2)}) collective-permute-start(bf16[64,768]{1,0:T(8,128)(2,1)S(1)} %get-tuple-element.206.own_ref), channel_id=1, source_target_pairs={{0,1},{1,0},{2,3},{3,2},{4,5},{5,4},{6,7},{7,6},{8,9},{9,8},{10,11... | collective-permute-start | bytes 294920 | tf_op jit(solution)/shard_map/ppermute | solution.py:26
  69.7 5.5 %collective-permute-start.33 = (bf16[64,768]{1,0:T(8,128)(2,1)S(1)}, bf16[64,768]{1,0:T(8,128)(2,1)S(1)}, u32[]{:S(2)}, u32[]{:S(2)}) collective-permute-start(bf16[64,768]{1,0:T(8,128)(2,1)S(1)} %get-tuple-element.219), channel_id=1, source_target_pairs={{0,1},{1,0},{2,3},{3,2},{4,5},{5,4},{6,7},{7,6},{8,9},{9,8},{10,11... | collective-permute-start | bytes 294920 | tf_op jit(solution)/shard_map/ppermute | solution.py:26
  70.5 4.8 %collective-permute-start.34 = (bf16[64,768]{1,0:T(8,128)(2,1)S(1)}, bf16[64,768]{1,0:T(8,128)(2,1)S(1)}, u32[]{:S(2)}, u32[]{:S(2)}) collective-permute-start(bf16[64,768]{1,0:T(8,128)(2,1)S(1)} %get-tuple-element.220), channel_id=1, source_target_pairs={{0,8},{1,9},{2,10},{3,11},{4,12},{5,13},{6,14},{7,15},{8,0},{9,1},... | collective-permute-start | bytes 294920 | tf_op jit(solution)/shard_map/ppermute | solution.py:26
  70.7 6.6 %collective-permute-start.35 = (bf16[64,768]{1,0:T(8,128)(2,1)S(1)}, bf16[64,768]{1,0:T(8,128)(2,1)S(1)}, u32[]{:S(2)}, u32[]{:S(2)}) collective-permute-start(bf16[64,768]{1,0:T(8,128)(2,1)S(1)} %get-tuple-element.221), channel_id=1, source_target_pairs={{0,9},{1,8},{2,11},{3,10},{4,13},{5,12},{6,15},{7,14},{8,1},{9,0},... | collective-permute-start | bytes 294920 | tf_op jit(solution)/shard_map/ppermute | solution.py:26
  78.3 5.6 %collective-permute-start.38 = (bf16[64,768]{1,0:T(8,128)(2,1)S(1)}, bf16[64,768]{1,0:T(8,128)(2,1)S(1)}, u32[]{:S(2)}, u32[]{:S(2)}) collective-permute-start(bf16[64,768]{1,0:T(8,128)(2,1)S(1)} %get-tuple-element.224.own_ref), channel_id=1, source_target_pairs={{0,9},{1,8},{2,11},{3,10},{4,13},{5,12},{6,15},{7,14},{8,1},{9,0},... | collective-permute-start | bytes 294920 | tf_op jit(solution)/shard_map/ppermute | solution.py:26
  79.8 4.6 %collective-permute-start.37 = (bf16[64,768]{1,0:T(8,128)(2,1)S(1)}, bf16[64,768]{1,0:T(8,128)(2,1)S(1)}, u32[]{:S(2)}, u32[]{:S(2)}) collective-permute-start(bf16[64,768]{1,0:T(8,128)(2,1)S(1)} %get-tuple-element.224.own_ref), channel_id=1, source_target_pairs={{0,8},{1,9},{2,10},{3,11},{4,12},{5,13},{6,14},{7,15},{8,0},{9,1},... | collective-permute-start | bytes 294920 | tf_op jit(solution)/shard_map/ppermute | solution.py:26
  80.2 4.7 %collective-permute-start.36 = (bf16[64,768]{1,0:T(8,128)(2,1)S(1)}, bf16[64,768]{1,0:T(8,128)(2,1)S(1)}, u32[]{:S(2)}, u32[]{:S(2)}) collective-permute-start(bf16[64,768]{1,0:T(8,128)(2,1)S(1)} %get-tuple-element.224.own_ref), channel_id=1, source_target_pairs={{0,1},{1,0},{2,3},{3,2},{4,5},{5,4},{6,7},{7,6},{8,9},{9,8},{10,11... | collective-permute-start | bytes 294920 | tf_op jit(solution)/shard_map/ppermute | solution.py:26
  86.9 2.1 %collective-permute-start.39 = (bf16[8,48,768]{2,1,0:T(8,128)(2,1)S(1)}, bf16[8,48,768]{2,1,0:T(8,128)(2,1)S(1)}, u32[]{:S(2)}, u32[]{:S(2)}) collective-permute-start(bf16[8,48,768]{2,1,0:T(8,128)(2,1)S(1)} %get-tuple-element.231), channel_id=1, source_target_pairs={{0,2},{1,3},{2,0},{3,1},{4,6},{5,7},{6,4},{7,5},{8,10},{9,11},{10,... | collective-permute-start | bytes 1769480 | tf_op jit(solution)/shard_map/ppermute | solution.py:26
  87.0 2.8 %collective-permute-start.40 = (bf16[8,48,768]{2,1,0:T(8,128)(2,1)S(1)}, bf16[8,48,768]{2,1,0:T(8,128)(2,1)S(1)}, u32[]{:S(2)}, u32[]{:S(2)}) collective-permute-start(bf16[8,48,768]{2,1,0:T(8,128)(2,1)S(1)} %get-tuple-element.232), channel_id=1, source_target_pairs={{0,2},{1,3},{2,0},{3,1},{4,6},{5,7},{6,4},{7,5},{8,10},{9,11},{10,... | collective-permute-start | bytes 1769480 | tf_op jit(solution)/shard_map/ppermute | solution.py:26
  90.1 19.0 %collective-permute-start.47 = (bf16[4,48,1536]{2,1,0:T(8,128)(2,1)S(1)}, bf16[4,48,1536]{2,1,0:T(8,128)(2,1)S(1)}, u32[]{:S(2)}, u32[]{:S(2)}) collective-permute-start(bf16[4,48,1536]{2,1,0:T(8,128)(2,1)S(1)} %get-tuple-element.238), channel_id=1, source_target_pairs={{0,4},{1,5},{2,6},{3,7},{4,0},{5,1},{6,2},{7,3},{8,12},{9,13},{10,... | collective-permute-start | bytes 1769480 | tf_op jit(solution)/shard_map/ppermute | solution.py:26
  91.6 4.6 %collective-permute-start.41 = (bf16[64,768]{1,0:T(8,128)(2,1)S(1)}, bf16[64,768]{1,0:T(8,128)(2,1)S(1)}, u32[]{:S(2)}, u32[]{:S(2)}) collective-permute-start(bf16[64,768]{1,0:T(8,128)(2,1)S(1)} %get-tuple-element.239), channel_id=1, source_target_pairs={{0,1},{1,0},{2,3},{3,2},{4,5},{5,4},{6,7},{7,6},{8,9},{9,8},{10,11... | collective-permute-start | bytes 294920 | tf_op jit(solution)/shard_map/ppermute | solution.py:26
  93.2 5.4 %collective-permute-start.42 = (bf16[64,768]{1,0:T(8,128)(2,1)S(1)}, bf16[64,768]{1,0:T(8,128)(2,1)S(1)}, u32[]{:S(2)}, u32[]{:S(2)}) collective-permute-start(bf16[64,768]{1,0:T(8,128)(2,1)S(1)} %get-tuple-element.240), channel_id=1, source_target_pairs={{0,8},{1,9},{2,10},{3,11},{4,12},{5,13},{6,14},{7,15},{8,0},{9,1},... | collective-permute-start | bytes 294920 | tf_op jit(solution)/shard_map/ppermute | solution.py:26
  93.8 5.9 %collective-permute-start.43 = (bf16[64,768]{1,0:T(8,128)(2,1)S(1)}, bf16[64,768]{1,0:T(8,128)(2,1)S(1)}, u32[]{:S(2)}, u32[]{:S(2)}) collective-permute-start(bf16[64,768]{1,0:T(8,128)(2,1)S(1)} %get-tuple-element.241), channel_id=1, source_target_pairs={{0,9},{1,8},{2,11},{3,10},{4,13},{5,12},{6,15},{7,14},{8,1},{9,0},... | collective-permute-start | bytes 294920 | tf_op jit(solution)/shard_map/ppermute | solution.py:26
  100.0 5.6 %collective-permute-start.46 = (bf16[64,768]{1,0:T(8,128)(2,1)S(1)}, bf16[64,768]{1,0:T(8,128)(2,1)S(1)}, u32[]{:S(2)}, u32[]{:S(2)}) collective-permute-start(bf16[64,768]{1,0:T(8,128)(2,1)S(1)} %get-tuple-element.245.own_ref), channel_id=1, source_target_pairs={{0,9},{1,8},{2,11},{3,10},{4,13},{5,12},{6,15},{7,14},{8,1},{9,0},... | collective-permute-start | bytes 294920 | tf_op jit(solution)/shard_map/ppermute | solution.py:26
  101.4 5.1 %collective-permute-start.45 = (bf16[64,768]{1,0:T(8,128)(2,1)S(1)}, bf16[64,768]{1,0:T(8,128)(2,1)S(1)}, u32[]{:S(2)}, u32[]{:S(2)}) collective-permute-start(bf16[64,768]{1,0:T(8,128)(2,1)S(1)} %get-tuple-element.245.own_ref), channel_id=1, source_target_pairs={{0,8},{1,9},{2,10},{3,11},{4,12},{5,13},{6,14},{7,15},{8,0},{9,1},... | collective-permute-start | bytes 294920 | tf_op jit(solution)/shard_map/ppermute | solution.py:26
  102.9 4.6 %collective-permute-start.44 = (bf16[64,768]{1,0:T(8,128)(2,1)S(1)}, bf16[64,768]{1,0:T(8,128)(2,1)S(1)}, u32[]{:S(2)}, u32[]{:S(2)}) collective-permute-start(bf16[64,768]{1,0:T(8,128)(2,1)S(1)} %get-tuple-element.245.own_ref), channel_id=1, source_target_pairs={{0,1},{1,0},{2,3},{3,2},{4,5},{5,4},{6,7},{7,6},{8,9},{9,8},{10,11... | collective-permute-start | bytes 294920 | tf_op jit(solution)/shard_map/ppermute | solution.py:26
  108.5 6.4 %collective-permute-start.48 = (bf16[256,512]{1,0:T(8,128)(2,1)S(1)}, bf16[256,512]{1,0:T(8,128)(2,1)S(1)}, u32[]{:S(2)}, u32[]{:S(2)}) collective-permute-start(bf16[256,512]{1,0:T(8,128)(2,1)S(1)} %get-tuple-element.247.packet_ref.g0_ref), channel_id=1, source_target_pairs={{0,4},{1,5},{2,6},{3,7},{4,0},{5,1},{6,2},{7,3},{8,12},{9,13},{10,... | collective-permute-start | bytes 786440 | tf_op jit(solution)/shard_map/ppermute | solution.py:26
  109.2 13.0 %collective-permute-start.51 = (bf16[2,48,1536]{2,1,0:T(8,128)(2,1)S(1)}, bf16[2,48,1536]{2,1,0:T(8,128)(2,1)S(1)}, u32[]{:S(2)}, u32[]{:S(2)}) collective-permute-start(bf16[2,48,1536]{2,1,0:T(8,128)(2,1)S(1)} %get-tuple-element.257), channel_id=1, source_target_pairs={{0,16},{1,17},{2,18},{3,19},{4,20},{5,21},{6,22},{7,23},{8,24},{9,... | collective-permute-start | bytes 884744 | tf_op jit(solution)/shard_map/ppermute | solution.py:26
  110.6 5.2 %collective-permute-start.49 = (bf16[256,512]{1,0:T(8,128)(2,1)S(1)}, bf16[256,512]{1,0:T(8,128)(2,1)S(1)}, u32[]{:S(2)}, u32[]{:S(2)}) collective-permute-start(bf16[256,512]{1,0:T(8,128)(2,1)S(1)} %get-tuple-element.247.packet_ref.g0_ref), channel_id=1, source_target_pairs={{0,2},{1,3},{2,0},{3,1},{4,6},{5,7},{6,4},{7,5},{8,10},{9,11},{10,... | collective-permute-start | bytes 786440 | tf_op jit(solution)/shard_map/ppermute | solution.py:26
  114.9 1.5 %collective-permute-start.50 = (bf16[256,512]{1,0:T(8,128)(2,1)S(1)}, bf16[256,512]{1,0:T(8,128)(2,1)S(1)}, u32[]{:S(2)}, u32[]{:S(2)}) collective-permute-start(bf16[256,512]{1,0:T(8,128)(2,1)S(1)} %collective-permute-done.48.g1_ref), channel_id=1, source_target_pairs={{0,2},{1,3},{2,0},{3,1},{4,6},{5,7},{6,4},{7,5},{8,10},{9,11},{10,... | collective-permute-start | bytes 786440 | tf_op jit(solution)/shard_map/ppermute | solution.py:26
  115.0 7.2 %collective-permute-start.52 = (f32[16,768]{1,0:T(8,128)S(1)}, f32[16,768]{1,0:T(8,128)S(1)}, u32[]{:S(2)}, u32[]{:S(2)}) collective-permute-start(f32[16,768]{1,0:T(8,128)S(1)} %vectors.1.refs_4_), channel_id=1, source_target_pairs={{0,1},{1,0},{2,3},{3,2},{4,5},{5,4},{6,7},{7,6},{8,9},{9,8},{10,11... | collective-permute-start | bytes 147464 | tf_op jit(solution)/shard_map/ppermute | solution.py:26
  123.4 2.4 %collective-permute-start.54 = (bf16[8,48,704]{2,1,0:T(8,128)(2,1)S(1)}, bf16[8,48,704]{2,1,0:T(8,128)(2,1)S(1)}, u32[]{:S(2)}, u32[]{:S(2)}) collective-permute-start(bf16[8,48,704]{2,1,0:T(8,128)(2,1)S(1)} %get-tuple-element.266), channel_id=1, source_target_pairs={{0,2},{1,3},{2,0},{3,1},{4,6},{5,7},{6,4},{7,5},{8,10},{9,11},{10,... | collective-permute-start | bytes 1622024 | tf_op jit(solution)/shard_map/ppermute | solution.py:26
  123.4 2.3 %collective-permute-start.53 = (bf16[8,48,192]{2,1,0:T(8,128)(2,1)S(1)}, bf16[8,48,192]{2,1,0:T(8,128)(2,1)S(1)}, u32[]{:S(2)}, u32[]{:S(2)}) collective-permute-start(bf16[8,48,192]{2,1,0:T(8,128)(2,1)S(1)} %get-tuple-element.265), channel_id=1, source_target_pairs={{0,2},{1,3},{2,0},{3,1},{4,6},{5,7},{6,4},{7,5},{8,10},{9,11},{10,... | collective-permute-start | bytes 442376 | tf_op jit(solution)/shard_map/ppermute | solution.py:26
  126.0 11.8 %collective-permute-start.59 = (bf16[4,48,896]{2,1,0:T(8,128)(2,1)S(1)}, bf16[4,48,896]{2,1,0:T(8,128)(2,1)S(1)}, u32[]{:S(2)}, u32[]{:S(2)}) collective-permute-start(bf16[4,48,896]{2,1,0:T(8,128)(2,1)S(1)} %get-tuple-element.281), channel_id=1, source_target_pairs={{0,4},{1,5},{2,6},{3,7},{4,0},{5,1},{6,2},{7,3},{8,12},{9,13},{10,... | collective-permute-start | bytes 1032200 | tf_op jit(solution)/shard_map/ppermute | solution.py:26
  127.5 4.6 %collective-permute-start.55 = (bf16[64,768]{1,0:T(8,128)(2,1)S(1)}, bf16[64,768]{1,0:T(8,128)(2,1)S(1)}, u32[]{:S(2)}, u32[]{:S(2)}) collective-permute-start(bf16[64,768]{1,0:T(8,128)(2,1)S(1)} %get-tuple-element.272), channel_id=1, source_target_pairs={{0,1},{1,0},{2,3},{3,2},{4,5},{5,4},{6,7},{7,6},{8,9},{9,8},{10,11... | collective-permute-start | bytes 294920 | tf_op jit(solution)/shard_map/ppermute | solution.py:26
  128.6 5.7 %collective-permute-start.56 = (bf16[64,768]{1,0:T(8,128)(2,1)S(1)}, bf16[64,768]{1,0:T(8,128)(2,1)S(1)}, u32[]{:S(2)}, u32[]{:S(2)}) collective-permute-start(bf16[64,768]{1,0:T(8,128)(2,1)S(1)} %get-tuple-element.273), channel_id=1, source_target_pairs={{0,8},{1,9},{2,10},{3,11},{4,12},{5,13},{6,14},{7,15},{8,0},{9,1},... | collective-permute-start | bytes 294920 | tf_op jit(solution)/shard_map/ppermute | solution.py:26
  128.6 8.2 %collective-permute-start.57 = (bf16[64,768]{1,0:T(8,128)(2,1)S(1)}, bf16[64,768]{1,0:T(8,128)(2,1)S(1)}, u32[]{:S(2)}, u32[]{:S(2)}) collective-permute-start(bf16[64,768]{1,0:T(8,128)(2,1)S(1)} %get-tuple-element.274), channel_id=1, source_target_pairs={{0,9},{1,8},{2,11},{3,10},{4,13},{5,12},{6,15},{7,14},{8,1},{9,0},... | collective-permute-start | bytes 294920 | tf_op jit(solution)/shard_map/ppermute | solution.py:26
  131.1 11.3 %collective-permute-start.63 = (bf16[48,1536]{1,0:T(8,128)(2,1)S(1)}, bf16[48,1536]{1,0:T(8,128)(2,1)S(1)}, u32[]{:S(2)}, u32[]{:S(2)}) collective-permute-start(bf16[48,1536]{1,0:T(8,128)(2,1)S(1)} %get-tuple-element.287), channel_id=1, source_target_pairs={{0,8},{1,9},{2,10},{3,11},{4,12},{5,13},{6,14},{7,15},{8,0},{9,1},... | collective-permute-start | bytes 442376 | tf_op jit(solution)/shard_map/ppermute | solution.py:26
  136.9 10.2 %collective-permute-start.58 = (bf16[32,1536]{1,0:T(8,128)(2,1)S(1)}, bf16[32,1536]{1,0:T(8,128)(2,1)S(1)}, u32[]{:S(2)}, u32[]{:S(2)}) collective-permute-start(bf16[32,1536]{1,0:T(8,128)(2,1)S(1)} %get-tuple-element.278), channel_id=1, source_target_pairs={{0,16},{1,17},{2,18},{3,19},{4,20},{5,21},{6,22},{7,23},{8,24},{9,... | collective-permute-start | bytes 294920 | tf_op jit(solution)/shard_map/ppermute | solution.py:26
  137.9 10.0 %collective-permute-start.60 = (bf16[48,896]{1,0:T(8,128)(2,1)S(1)}, bf16[48,896]{1,0:T(8,128)(2,1)S(1)}, u32[]{:S(2)}, u32[]{:S(2)}) collective-permute-start(bf16[48,896]{1,0:T(8,128)(2,1)S(1)} %get-tuple-element.283), channel_id=1, source_target_pairs={{0,8},{1,9},{2,10},{3,11},{4,12},{5,13},{6,14},{7,15},{8,0},{9,1},... | collective-permute-start | bytes 258056 | tf_op jit(solution)/shard_map/ppermute | solution.py:26
  139.6 8.4 %collective-permute-start.61 = (bf16[48,896]{1,0:T(8,128)(2,1)S(1)}, bf16[48,896]{1,0:T(8,128)(2,1)S(1)}, u32[]{:S(2)}, u32[]{:S(2)}) collective-permute-start(bf16[48,896]{1,0:T(8,128)(2,1)S(1)} %get-tuple-element.284), channel_id=1, source_target_pairs={{0,16},{1,17},{2,18},{3,19},{4,20},{5,21},{6,22},{7,23},{8,24},{9,... | collective-permute-start | bytes 258056 | tf_op jit(solution)/shard_map/ppermute | solution.py:26
  140.5 7.6 %collective-permute-start.62 = (bf16[48,896]{1,0:T(8,128)(2,1)S(1)}, bf16[48,896]{1,0:T(8,128)(2,1)S(1)}, u32[]{:S(2)}, u32[]{:S(2)}) collective-permute-start(bf16[48,896]{1,0:T(8,128)(2,1)S(1)} %get-tuple-element.285), channel_id=1, source_target_pairs={{0,24},{1,25},{2,26},{3,27},{4,28},{5,29},{6,30},{7,31},{8,16},{9,... | collective-permute-start | bytes 258056 | tf_op jit(solution)/shard_map/ppermute | solution.py:26
  (1 other events, 10.2 us)

commit v4 on v3

--- a/solution.py
+++ b/solution.py
@@ -570,7 +570,7 @@
     keep_ref, got_ref, tp_ref, low_ref, both_ref, *refs
 ):
     parts, outs = refs[:8], refs[8:]
-    rows_ref, query_ref, key_ref, value_ref, weight_ref, out_weight_ref = outs
+    rows_ref, query_ref, pair_ref, rest_ref, weight_ref, out_weight_ref = outs
     rows = parts[0].shape[1] - 16
     head_cols = query_ref.shape[1]
     join_pieces(parts, weight_ref, rows, slice(0, 3 * head_cols))
@@ -585,8 +585,17 @@
     query_bias, value_bias = biases[0:1], biases[1:2]
     made = mul(rows_ref[...], weight_ref[...])
     query_ref[...] = (made[:, 0:head_cols] + query_bias).astype(low_type)
-    key_ref[...] = made[:, head_cols : 2 * head_cols].astype(low_type)
-    value_ref[...] = (made[:, 2 * head_cols :] + value_bias).astype(low_type)
+    values = made[:, 2 * head_cols :] + value_bias
+    split = pair_ref.shape[1] - head_cols
+    pair_ref[:, 0:head_cols] = made[:, head_cols : 2 * head_cols].astype(low_type)
+    pair_ref[:, head_cols:] = values[:, 0:split].astype(low_type)
+    rest_ref[...] = values[:, split:].astype(low_type)
+
+
+def joined_pair(pairs, rests, head_cols):
+    pair = jnp.concatenate([ref[...] for ref in pairs], 0)
+    rest = jnp.concatenate([ref[...] for ref in rests], 0)
+    return pair[:, 0:head_cols], jnp.concatenate([pair[:, head_cols:], rest], 1)
 
 
 def head_of(array, head):
@@ -599,8 +608,7 @@
     pieces, (weight_ref, low_ref, stats_ref, keep_ref, *sends) = refs[:8], refs[8:]
     head_cols = query_ref.shape[1]
     count = query_ref.shape[0]
-    keys = jnp.concatenate([ref[...] for ref in pieces[:4]], 0)
-    values = jnp.concatenate([ref[...] for ref in pieces[4:]], 0)
+    keys, values = joined_pair(pieces[:4], pieces[4:], head_cols)
     queries = query_ref[...] * HD ** (-0.5)
     lanes = lax.broadcasted_iota(jnp.int32, (1, keys.shape[0]), 1)
     live = live_rows_of(lengths_ref, lanes, True, shard_pos)
@@ -852,27 +860,24 @@
     for head in range(heads):
         delta = jnp.sum(head_of(both, head), axis=1, keepdims=True)
         for place, left in ((head, stats[:, head : head + 1]), (heads + head, delta)):
-            for level in range(3):
+            for level in range(2):
                 piece = left.astype(low_type).astype(wide)
                 left = left - piece
-                levels = jnp.where(column == 3 * place + level, piece, levels)
+                levels = jnp.where(column == 2 * place + level, piece, levels)
     packet_ref[:, 2 * head_cols :] = levels.astype(low_type)
 
 
 def stat_of(packet, head_cols, place):
-    base = 2 * head_cols + 3 * place
-    total = packet[:, base : base + 1].astype(wide)
-    for level in (1, 2):
-        total = total + packet[:, base + level : base + level + 1].astype(wide)
-    return total
+    base = 2 * head_cols + 2 * place
+    first, second = packet[:, base : base + 1], packet[:, base + 1 : base + 2]
+    return first.astype(wide) + second.astype(wide)
 
 
 def query_back_kernel(shard_pos, lengths_ref, packet_ref, *refs):
     pieces, (out_ref, sums_ref) = refs[:8], refs[8:]
     head_cols = out_ref.shape[1]
     heads = head_cols // HD
-    keys = jnp.concatenate([ref[...] for ref in pieces[:4]], 0)
-    values = jnp.concatenate([ref[...] for ref in pieces[4:]], 0)
+    keys, values = joined_pair(pieces[:4], pieces[4:], head_cols)
     packet = packet_ref[...]
     grad = packet[:, 0:head_cols]
     queries = packet[:, head_cols : 2 * head_cols] * HD ** (-0.5)
@@ -892,28 +897,31 @@
 
 
 def pair_back_kernel(
-    shard_pos, lengths_ref, key_ref, value_ref, query_grad_ref, weight_ref,
+    shard_pos, lengths_ref, pair_ref, rest_ref, query_grad_ref, weight_ref,
     g0_ref, g1_ref, g2_ref, g3_ref,
     keep_ref, send1_ref, send2_ref, send3_ref, made_ref,
 ):
     head_cols = query_grad_ref.shape[1]
     heads = head_cols // HD
-    keys, values = key_ref[...], value_ref[...]
+    keys, values = joined_pair((pair_ref,), (rest_ref,), head_cols)
     packet = jnp.concatenate([ref[...] for ref in (g0_ref, g1_ref, g2_ref, g3_ref)], 0)
     grad = packet[:, 0:head_cols]
     queries = packet[:, head_cols : 2 * head_cols] * HD ** (-0.5)
-    lanes = lax.broadcasted_iota(jnp.int32, (1, keys.shape[0]), 1)
-    live = live_rows_of(lengths_ref, lanes, False, shard_pos)
+    index = lax.broadcasted_iota(jnp.int32, (keys.shape[0], 1), 0)
+    live = live_rows_of(lengths_ref, index, False, shard_pos)
+    stats = jnp.transpose(packet[:, 2 * head_cols :].astype(wide))
     key_parts, value_parts = [], []
     for head in range(heads):
-        scores = mul(head_of(queries, head), head_of(keys, head), 1, 1)
+        log_total = stats[2 * head : 2 * head + 1] + stats[2 * head + 1 : 2 * head + 2]
+        at = 2 * (heads + head)
+        delta = stats[at : at + 1] + stats[at + 1 : at + 2]
+        scores = mul(head_of(keys, head), head_of(queries, head), 1, 1)
         scores = jnp.where(live, scores, masked_score)
-        weights = jnp.exp(scores - stat_of(packet, head_cols, head))
-        weight_grad = mul(head_of(grad, head), head_of(values, head), 1, 1)
-        weight_grad = weight_grad - stat_of(packet, head_cols, heads + head)
-        score_grad = (weights * weight_grad).astype(low_type)
-        key_parts.append(mul(score_grad, head_of(queries, head), 0, 0))
-        value_parts.append(mul(weights.astype(low_type), head_of(grad, head), 0, 0))
+        weights = jnp.exp(scores - log_total)
+        weight_grad = mul(head_of(values, head), head_of(grad, head), 1, 1)
+        score_grad = (weights * (weight_grad - delta)).astype(low_type)
+        key_parts.append(mul(score_grad, head_of(queries, head)))
+        value_parts.append(mul(weights.astype(low_type), head_of(grad, head)))
     made = jnp.concatenate(
         [query_grad_ref[...]] + [part.astype(low_type) for part in key_parts + value_parts], 1
     )
@@ -963,7 +971,7 @@
 
 
 def send_team(parts):
-    return tuple(swap(part, bit) for part, bit in zip(parts, TEAM_BITS))
+    return tuple(swap(parts[i], TEAM_BITS[i]) for i in (1, 0, 2))
 
 
 def gather_team(rows):
@@ -1002,6 +1010,7 @@
     head_cols = w_query.shape[1] // 2
     unit_cols = w_up.shape[1] // 2
     chips = lax.axis_size("fsdp") // 2
+    pair_cols = -(-head_cols // 128) * 128
 
     sources = (
         w_query, w_key, w_value, jnp.transpose(w_out), w_up, jnp.transpose(w_down),
@@ -1056,25 +1065,25 @@
         swap(tie(first_far_side, team_rows, later_near), BIT_CORE),
     )
 
-    group_rows, queries, keys, values, qkv_weight, out_weight = run_kernel(
+    group_rows, queries, pair, rest, qkv_weight, out_weight = run_kernel(
         project_kernel,
         [
             ((group, width), low_type),
             ((group, head_cols), low_type),
-            ((group, head_cols), low_type),
-            ((group, head_cols), low_type),
+            ((group, pair_cols), low_type),
+            ((group, 2 * head_cols - pair_cols), low_type),
             ((width, 3 * head_cols), low_type),
             ((width, head_cols), low_type),
         ],
         hidden_own, slot_rows, *team_rows, *first_pieces,
         name="project",
     )
-    key_parts, value_parts = gather_parts(keys), gather_parts(values)
-    later_near_side = swap(tie(later_near, key_parts[1]), BIT_SIDE)
+    pair_parts, rest_parts = gather_parts(pair), gather_parts(rest)
+    later_near_side = swap(tie(later_near, pair_parts[1]), BIT_SIDE)
     vectors, up_bias = run_kernel(
         lines_kernel,
         [((8, width), wide), ((1, unit_cols), wide)],
-        *tie(first_pieces, keys),
+        *tie(first_pieces, pair),
         us=0.5,
         name="lines",
     )
@@ -1083,7 +1092,7 @@
     attended_low, stats, keep, *sends = run_kernel(
         functools.partial(attend_kernel, shard_pos),
         [((group, head_cols), low_type), ((group, 128), wide)] + given,
-        lengths, tie(queries, vectors), *key_parts, *value_parts, out_weight,
+        lengths, tie(queries, vectors), *pair_parts, *rest_parts, out_weight,
         us=3.0,
         name="attend",
     )
@@ -1194,7 +1203,7 @@
     query_grad, query_sums = run_kernel(
         functools.partial(query_back_kernel, shard_pos),
         [((group, head_cols), low_type), ((1, head_cols), wide)],
-        lengths, packet, *key_parts, *value_parts,
+        lengths, packet, *pair_parts, *rest_parts,
         us=3.0,
         name="query_back",
     )
@@ -1217,7 +1226,7 @@
     keep, s1, s2, s3, qkv_grad = run_kernel(
         functools.partial(pair_back_kernel, shard_pos),
         given + [((group, 3 * head_cols), low_type)],
-        lengths, tie(keys, unit_kept), values, query_grad, qkv_weight, *packets,
+        lengths, tie(pair, unit_kept), rest, query_grad, qkv_weight, *packets,
         us=4.0,
         name="pair_back",
     )
@@ -1227,7 +1236,7 @@
         (sums, sums_got),
     )
     late_got = [swap(part, BIT_CORE) for part in late_sent]
-    lasts = send_team(tie((s1, s2, s3), *late_sent))
+    lasts = send_team((s1, s2, s3))
     late_kept, late_sent = fold("side", (2, 1), [late_kept], late_got, "late")
     late_got = swap(late_sent, BIT_SIDE)
     late_shape = late_kept.shape[1:]

time: 149 us -> 148 us (level)
  waiting for transfers between devices: 62.4 us -> 59.7 us
  starting transfers between devices: 62.1 us -> 64 us
    ppermute x64, waiting for transfers between devices: 62.4 us -> 59.7 us  [swap(): lax.ppermute(values, AXES, [(i, i ^ bit) for i in range(device_count())])]
    ppermute x64, starting transfers between devices: 62.1 us -> 64 us  [swap(): lax.ppermute(values, AXES, [(i, i ^ bit) for i in range(device_count())])]
  transfers between devices with their start and end apart: 64 -> 64, of which waited for: 37 -> 35; matrix products, arithmetic and copies ran while one was open for 0% -> 0% of each run, Pallas kernels for 9% -> 9%
where the time goes in v4:
time: 148 us
  starting transfers between devices  64 us (43%)
  waiting for transfers between devices  59.7 us (40%)
  Pallas kernels  22.6 us (15%)
    ppermute x64, starting transfers between devices, swap(): lax.ppermute(values, AXES, [(i, i ^ bit) for i in range(device_count())])  64 us
    ppermute x64, waiting for transfers between devices, swap(): lax.ppermute(values, AXES, [(i, i ^ bit) for i in range(device_count())])  59.7 us
    pallas_call x26, Pallas kernels, run_kernel(): pl.pallas_call(body, out_shape=[jax.ShapeDtypeStruct(shape, kind) for sha...  22.6 us
  transfers between devices with their start and end apart: 64, of which 35 were waited for; matrix products, arithmetic and copies ran while one was open for 0% of the time, Pallas kernels for 9%

profile of v4, /device:TPU:0, one launch (start us, length us, event | category | flops | bytes accessed | tf_op | source)
XLA Modules:
  0.0 147.5 jit_solution(1383095689553740146)
XLA Ops:
  0.7 1.4 rows.1
  2.1 1.4 pack.1
  3.5 3.1 %collective-permute-start.4 = (bf16[64,768]{1,0:T(8,128)(2,1)S(1)}, bf16[64,768]{1,0:T(8,128)(2,1)S(1)}, u32[]{:S(2)}, u32[]{:S(2)}) collective-permute-start(bf16[64,768]{1,0:T(8,128)(2,1)S(1)} %get-tuple-element.177), channel_id=1, source_target_pairs={{0,8},{1,9},{2,10},{3,11},{4,12},{5,13},{6,14},{7,15},{8,0},{9,1},... | collective-permute-start | bytes 294920 | tf_op jit(solution)/shard_map/ppermute | solution.py:26
  6.5 2.6 %collective-permute-start = (bf16[64,768]{1,0:T(8,128)(2,1)S(1)}, bf16[64,768]{1,0:T(8,128)(2,1)S(1)}, u32[]{:S(2)}, u32[]{:S(2)}) collective-permute-start(bf16[64,768]{1,0:T(8,128)(2,1)S(1)} %get-tuple-element.160), channel_id=1, source_target_pairs={{0,16},{1,17},{2,18},{3,19},{4,20},{5,21},{6,22},{7,23},{8,24},{9,... | collective-permute-start | bytes 294920 | tf_op jit(solution)/shard_map/ppermute | solution.py:26
  9.1 1.9 %collective-permute-start.5 = (bf16[64,768]{1,0:T(8,128)(2,1)S(1)}, bf16[64,768]{1,0:T(8,128)(2,1)S(1)}, u32[]{:S(2)}, u32[]{:S(2)}) collective-permute-start(bf16[64,768]{1,0:T(8,128)(2,1)S(1)} %get-tuple-element.176), channel_id=1, source_target_pairs={{0,16},{1,17},{2,18},{3,19},{4,20},{5,21},{6,22},{7,23},{8,24},{9,... | collective-permute-start | bytes 294920 | tf_op jit(solution)/shard_map/ppermute | solution.py:26
  11.1 1.6 %collective-permute-start.7 = (bf16[2,64,768]{2,1,0:T(8,128)(2,1)S(1)}, bf16[2,64,768]{2,1,0:T(8,128)(2,1)S(1)}, u32[]{:S(2)}, u32[]{:S(2)}) collective-permute-start(bf16[2,64,768]{2,1,0:T(8,128)(2,1)S(1)} %pad_maximum_fusion.1.refs_0_), channel_id=1, source_target_pairs={{0,4},{1,5},{2,6},{3,7},{4,0},{5,1},{6,2},{7,3},{8,12},{9,13},{10,... | collective-permute-start | bytes 589832 | tf_op jit(solution)/shard_map/ppermute | solution.py:26
  12.6 2.5 %collective-permute-start.12 = (bf16[48,1536]{1,0:T(8,128)(2,1)S(1)}, bf16[48,1536]{1,0:T(8,128)(2,1)S(1)}, u32[]{:S(2)}, u32[]{:S(2)}) collective-permute-start(bf16[48,1536]{1,0:T(8,128)(2,1)S(1)} %get-tuple-element.182), channel_id=1, source_target_pairs={{0,8},{1,9},{2,10},{3,11},{4,12},{5,13},{6,14},{7,15},{8,0},{9,1},... | collective-permute-start | bytes 442376 | tf_op jit(solution)/shard_map/ppermute | solution.py:26
  15.1 4.1 %collective-permute-done.got_ref.slot_ref = bf16[64,768]{1,0:T(8,128)(2,1)S(1)} collective-permute-done((bf16[64,768]{1,0:T(8,128)(2,1)S(1)}, bf16[64,768]{1,0:T(8,128)(2,1)S(1)}, u32[]{:S(2)}, u32[]{:S(2)}) %collective-permute-start) | collective-permute-done | bytes 98336 | tf_op jit(solution)/shard_map/ppermute | solution.py:26
  19.9 2.4 %collective-permute-done.5 = bf16[64,768]{1,0:T(8,128)(2,1)S(1)} collective-permute-done((bf16[64,768]{1,0:T(8,128)(2,1)S(1)}, bf16[64,768]{1,0:T(8,128)(2,1)S(1)}, u32[]{:S(2)}, u32[]{:S(2)}) %collective-permute-start.5) | collective-permute-done | bytes 98336 | tf_op jit(solution)/shard_map/ppermute | solution.py:26
  22.2 1.5 %collective-permute-start.1 = (bf16[64,768]{1,0:T(8,128)(2,1)S(1)}, bf16[64,768]{1,0:T(8,128)(2,1)S(1)}, u32[]{:S(2)}, u32[]{:S(2)}) collective-permute-start(bf16[64,768]{1,0:T(8,128)(2,1)S(1)} %pad_maximum_fusion.3), channel_id=1, source_target_pairs={{0,1},{1,0},{2,3},{3,2},{4,5},{5,4},{6,7},{7,6},{8,9},{9,8},{10,11... | collective-permute-start | bytes 294920 | tf_op jit(solution)/shard_map/ppermute | solution.py:26
  23.9 1.6 %collective-permute-start.8 = (bf16[2,64,768]{2,1,0:T(8,128)(2,1)S(1)}, bf16[2,64,768]{2,1,0:T(8,128)(2,1)S(1)}, u32[]{:S(2)}, u32[]{:S(2)}) collective-permute-start(bf16[2,64,768]{2,1,0:T(8,128)(2,1)S(1)} %pad_maximum_fusion.2.refs_1_), channel_id=1, source_target_pairs={{0,4},{1,5},{2,6},{3,7},{4,0},{5,1},{6,2},{7,3},{8,12},{9,13},{10,... | collective-permute-start | bytes 589832 | tf_op jit(solution)/shard_map/ppermute | solution.py:26
  25.7 1.1 collective-permute-done.2.low_ref
  26.9 4.3 %collective-permute-done.8.refs_3_ = bf16[2,64,768]{2,1,0:T(8,128)(2,1)S(1)} collective-permute-done((bf16[2,64,768]{2,1,0:T(8,128)(2,1)S(1)}, bf16[2,64,768]{2,1,0:T(8,128)(2,1)S(1)}, u32[]{:S(2)}, u32[]{:S(2)}) %collective-permute-start.8) | collective-permute-done | bytes 196640 | tf_op jit(solution)/shard_map/ppermute | solution.py:26
  31.2 3.0 %collective-permute-start.26 = (bf16[2,48,1536]{2,1,0:T(8,128)(2,1)S(1)}, bf16[2,48,1536]{2,1,0:T(8,128)(2,1)S(1)}, u32[]{:S(2)}, u32[]{:S(2)}) collective-permute-start(bf16[2,48,1536]{2,1,0:T(8,128)(2,1)S(1)} %pad_maximum_fusion.refs_0_), channel_id=1, source_target_pairs={{0,16},{1,17},{2,18},{3,19},{4,20},{5,21},{6,22},{7,23},{8,24},{9,... | collective-permute-start | bytes 884744 | tf_op jit(solution)/shard_map/ppermute | solution.py:26
  35.0 1.6 %collective-permute-start.14 = (bf16[256,256]{1,0:T(8,128)(2,1)S(1)}, bf16[256,256]{1,0:T(8,128)(2,1)S(1)}, u32[]{:S(2)}, u32[]{:S(2)}) collective-permute-start(bf16[256,256]{1,0:T(8,128)(2,1)S(1)} %get-tuple-element.247.refs_0_.pair_ref), channel_id=1, source_target_pairs={{0,4},{1,5},{2,6},{3,7},{4,0},{5,1},{6,2},{7,3},{8,12},{9,13},{10,... | collective-permute-start | bytes 393224 | tf_op jit(solution)/shard_map/ppermute | solution.py:26
  37.1 4.3 %collective-permute-done.14.refs_1_ = bf16[256,256]{1,0:T(8,128)(2,1)S(1)} collective-permute-done((bf16[256,256]{1,0:T(8,128)(2,1)S(1)}, bf16[256,256]{1,0:T(8,128)(2,1)S(1)}, u32[]{:S(2)}, u32[]{:S(2)}) %collective-permute-start.14) | collective-permute-done | bytes 131104 | tf_op jit(solution)/shard_map/ppermute | solution.py:26
  42.8 1.5 %collective-permute-start.27 = (bf16[2,48,1536]{2,1,0:T(8,128)(2,1)S(1)}, bf16[2,48,1536]{2,1,0:T(8,128)(2,1)S(1)}, u32[]{:S(2)}, u32[]{:S(2)}) collective-permute-start(bf16[2,48,1536]{2,1,0:T(8,128)(2,1)S(1)} %pad_maximum_fusion.refs_0_), channel_id=1, source_target_pairs={{0,4},{1,5},{2,6},{3,7},{4,0},{5,1},{6,2},{7,3},{8,12},{9,13},{10,... | collective-permute-start | bytes 884744 | tf_op jit(solution)/shard_map/ppermute | solution.py:26
  44.3 2.8 %attend.1 = (bf16[256,192]{1,0:T(8,128)(2,1)S(1)}, f32[256,128]{1,0:T(8,128)S(1)}, f32[64,768]{1,0:T(8,128)S(1)}, bf16[64,768]{1,0:T(8,128)(2,1)S(1)}, bf16[64,7...) custom-call(s32[2]{0:T(128)S(1)} %copy-done, bf16[256,192]{1,0:T(8,128)(2,1)S(1)} %get-tuple-element.195.query_ref, ...), custom_call_target="tpu_custom_call" | custom-call | flops 30000000 | bytes 30000 | tf_op jit(solution)/shard_map/attend/pallas_call | solution.py:413
  47.2 1.1 collective-permute-done.26.refs_1_
  48.2 1.5 %collective-permute-start.28 = (bf16[2,48,1536]{2,1,0:T(8,128)(2,1)S(1)}, bf16[2,48,1536]{2,1,0:T(8,128)(2,1)S(1)}, u32[]{:S(2)}, u32[]{:S(2)}) collective-permute-start(bf16[2,48,1536]{2,1,0:T(8,128)(2,1)S(1)} %collective-permute-done.26.refs_1_), channel_id=1, source_target_pairs={{0,4},{1,5},{2,6},{3,7},{4,0},{5,1},{6,2},{7,3},{8,12},{9,13},{10,... | collective-permute-start | bytes 884744 | tf_op jit(solution)/shard_map/ppermute | solution.py:26
  50.2 3.0 %collective-permute-start.22 = (bf16[64,768]{1,0:T(8,128)(2,1)S(1)}, bf16[64,768]{1,0:T(8,128)(2,1)S(1)}, u32[]{:S(2)}, u32[]{:S(2)}) collective-permute-start(bf16[64,768]{1,0:T(8,128)(2,1)S(1)} %get-tuple-element.201), channel_id=1, source_target_pairs={{0,9},{1,8},{2,11},{3,10},{4,13},{5,12},{6,15},{7,14},{8,1},{9,0},... | collective-permute-start | bytes 294920 | tf_op jit(solution)/shard_map/ppermute | solution.py:26
  53.2 2.0 %collective-permute-done.20.got1_ref = bf16[64,768]{1,0:T(8,128)(2,1)S(1)} collective-permute-done((bf16[64,768]{1,0:T(8,128)(2,1)S(1)}, bf16[64,768]{1,0:T(8,128)(2,1)S(1)}, u32[]{:S(2)}, u32[]{:S(2)}) %collective-permute-start.20) | collective-permute-done | bytes 98336 | tf_op jit(solution)/shard_map/ppermute | solution.py:26
  55.3 1.0 collective-permute-done.22.got3_ref
  56.6 1.8 %collective-permute-done.28.refs_3_ = bf16[2,48,1536]{2,1,0:T(8,128)(2,1)S(1)} collective-permute-done((bf16[2,48,1536]{2,1,0:T(8,128)(2,1)S(1)}, bf16[2,48,1536]{2,1,0:T(8,128)(2,1)S(1)}, u32[]{:S(2)}, u32[]{:S(2)}) %collective-permute-start.28) | collective-permute-done | bytes 294944 | tf_op jit(solution)/shard_map/ppermute | solution.py:26
  60.1 1.3 collective-permute-start.24
  61.4 1.5 %collective-permute-start.23 = (bf16[64,768]{1,0:T(8,128)(2,1)S(1)}, bf16[64,768]{1,0:T(8,128)(2,1)S(1)}, u32[]{:S(2)}, u32[]{:S(2)}) collective-permute-start(bf16[64,768]{1,0:T(8,128)(2,1)S(1)} %get-tuple-element.203.own_ref), channel_id=1, source_target_pairs={{0,1},{1,0},{2,3},{3,2},{4,5},{5,4},{6,7},{7,6},{8,9},{9,8},{10,11... | collective-permute-start | bytes 294920 | tf_op jit(solution)/shard_map/ppermute | solution.py:26
  63.1 2.9 %collective-permute-done.25.got3_ref = bf16[64,768]{1,0:T(8,128)(2,1)S(1)} collective-permute-done((bf16[64,768]{1,0:T(8,128)(2,1)S(1)}, bf16[64,768]{1,0:T(8,128)(2,1)S(1)}, u32[]{:S(2)}, u32[]{:S(2)}) %collective-permute-start.25) | collective-permute-done | bytes 98336 | tf_op jit(solution)/shard_map/ppermute | solution.py:26
  67.1 1.6 %hidden.1 = (f32[64,768]{1,0:T(8,128)S(1)}, bf16[64,768]{1,0:T(8,128)(2,1)S(1)}, bf16[64,768]{1,0:T(8,128)(2,1)S(1)}, bf16[64,768]{1,0:T(8,128)(2,1)S(1)}, bf16[...) custom-call(bf16[64,768]{1,0:T(8,128)(2,1)S(1)} %get-tuple-element.203.own_ref, ...), custom_call_target="tpu_custom_call" | custom-call | flops 20000000 | bytes 20000 | tf_op jit(solution)/shard_map/hidden/pallas_call | solution.py:413
  69.1 1.1 collective-permute-start.34
  70.2 2.1 %collective-permute-start.35 = (bf16[64,768]{1,0:T(8,128)(2,1)S(1)}, bf16[64,768]{1,0:T(8,128)(2,1)S(1)}, u32[]{:S(2)}, u32[]{:S(2)}) collective-permute-start(bf16[64,768]{1,0:T(8,128)(2,1)S(1)} %get-tuple-element.218), channel_id=1, source_target_pairs={{0,9},{1,8},{2,11},{3,10},{4,13},{5,12},{6,15},{7,14},{8,1},{9,0},... | collective-permute-start | bytes 294920 | tf_op jit(solution)/shard_map/ppermute | solution.py:26
  72.3 2.1 %collective-permute-done.33.got1_ref = bf16[64,768]{1,0:T(8,128)(2,1)S(1)} collective-permute-done((bf16[64,768]{1,0:T(8,128)(2,1)S(1)}, bf16[64,768]{1,0:T(8,128)(2,1)S(1)}, u32[]{:S(2)}, u32[]{:S(2)}) %collective-permute-start.33) | collective-permute-done | bytes 98336 | tf_op jit(solution)/shard_map/ppermute | solution.py:26
  74.7 1.0 collective-permute-done.35.got3_ref
  76.7 2.1 %collective-permute-start.38 = (bf16[64,768]{1,0:T(8,128)(2,1)S(1)}, bf16[64,768]{1,0:T(8,128)(2,1)S(1)}, u32[]{:S(2)}, u32[]{:S(2)}) collective-permute-start(bf16[64,768]{1,0:T(8,128)(2,1)S(1)} %get-tuple-element.221.own_ref), channel_id=1, source_target_pairs={{0,9},{1,8},{2,11},{3,10},{4,13},{5,12},{6,15},{7,14},{8,1},{9,0},... | collective-permute-start | bytes 294920 | tf_op jit(solution)/shard_map/ppermute | solution.py:26
  80.2 2.0 %collective-permute-done.38.got3_ref = bf16[64,768]{1,0:T(8,128)(2,1)S(1)} collective-permute-done((bf16[64,768]{1,0:T(8,128)(2,1)S(1)}, bf16[64,768]{1,0:T(8,128)(2,1)S(1)}, u32[]{:S(2)}, u32[]{:S(2)}) %collective-permute-start.38) | collective-permute-done | bytes 98336 | tf_op jit(solution)/shard_map/ppermute | solution.py:26
  82.2 1.2 collective-permute-done.37.got2_ref
  84.9 1.1 unit_weights.1
  86.5 1.5 %collective-permute-done.39.refs_1_ = bf16[8,48,768]{2,1,0:T(8,128)(2,1)S(1)} collective-permute-done((bf16[8,48,768]{2,1,0:T(8,128)(2,1)S(1)}, bf16[8,48,768]{2,1,0:T(8,128)(2,1)S(1)}, u32[]{:S(2)}, u32[]{:S(2)}) %collective-permute-start.39) | collective-permute-done | bytes 589856 | tf_op jit(solution)/shard_map/ppermute | solution.py:26
  89.1 1.6 %collective-permute-start.47 = (bf16[4,48,1536]{2,1,0:T(8,128)(2,1)S(1)}, bf16[4,48,1536]{2,1,0:T(8,128)(2,1)S(1)}, u32[]{:S(2)}, u32[]{:S(2)}) collective-permute-start(bf16[4,48,1536]{2,1,0:T(8,128)(2,1)S(1)} %get-tuple-element.235), channel_id=1, source_target_pairs={{0,4},{1,5},{2,6},{3,7},{4,0},{5,1},{6,2},{7,3},{8,12},{9,13},{10,... | collective-permute-start | bytes 1769480 | tf_op jit(solution)/shard_map/ppermute | solution.py:26
  90.7 1.5 %collective-permute-start.41 = (bf16[64,768]{1,0:T(8,128)(2,1)S(1)}, bf16[64,768]{1,0:T(8,128)(2,1)S(1)}, u32[]{:S(2)}, u32[]{:S(2)}) collective-permute-start(bf16[64,768]{1,0:T(8,128)(2,1)S(1)} %get-tuple-element.236), channel_id=1, source_target_pairs={{0,8},{1,9},{2,10},{3,11},{4,12},{5,13},{6,14},{7,15},{8,0},{9,1},... | collective-permute-start | bytes 294920 | tf_op jit(solution)/shard_map/ppermute | solution.py:26
  92.9 1.3 collective-permute-start.43
  94.2 1.1 collective-permute-done.41.got1_ref
  95.3 3.5 %collective-permute-done.42.got2_ref = bf16[64,768]{1,0:T(8,128)(2,1)S(1)} collective-permute-done((bf16[64,768]{1,0:T(8,128)(2,1)S(1)}, bf16[64,768]{1,0:T(8,128)(2,1)S(1)}, u32[]{:S(2)}, u32[]{:S(2)}) %collective-permute-start.42) | collective-permute-done | bytes 98336 | tf_op jit(solution)/shard_map/ppermute | solution.py:26
  99.1 1.0 collective-permute-start.46
  100.1 1.4 collective-permute-start.45
  101.5 1.1 collective-permute-start.44
  102.6 2.0 %collective-permute-done.46.got3_ref = bf16[64,768]{1,0:T(8,128)(2,1)S(1)} collective-permute-done((bf16[64,768]{1,0:T(8,128)(2,1)S(1)}, bf16[64,768]{1,0:T(8,128)(2,1)S(1)}, u32[]{:S(2)}, u32[]{:S(2)}) %collective-permute-start.46) | collective-permute-done | bytes 98336 | tf_op jit(solution)/shard_map/ppermute | solution.py:26
  105.1 1.0 collective-permute-done.44.got1_ref
  107.7 1.4 collective-permute-start.51
  109.2 2.6 %query_back.1 = (bf16[256,192]{1,0:T(8,128)(2,1)S(1)}, f32[1,192]{1,0:T(1,128)S(1)}) custom-call(s32[2]{0:T(128)S(1)} %copy-done, bf16[256,512]{1,0:T(8,128)(2,1)S(1)} %get-tuple-element.244.packet_ref.g0_ref, bf16[256,256]{1,0:T(8,128)(2,1)S(1)} %get-tuple-element.247.refs_0_.pair_ref, bf16[256,256]{1,0:T(8,128)(2,1)S(1)} %collective-permute-done.14.refs_1_, ...), custom_call_target="tpu_custom_call" | custom-call | flops 30000000 | bytes 30000 | tf_op jit(solution)/shard_map/query_back/pallas_call | solution.py:413
  111.7 1.7 %collective-permute-done.48.g1_ref = bf16[256,512]{1,0:T(8,128)(2,1)S(1)} collective-permute-done((bf16[256,512]{1,0:T(8,128)(2,1)S(1)}, bf16[256,512]{1,0:T(8,128)(2,1)S(1)}, u32[]{:S(2)}, u32[]{:S(2)}) %collective-permute-start.48) | collective-permute-done | bytes 262176 | tf_op jit(solution)/shard_map/ppermute | solution.py:26
  113.6 1.2 collective-permute-start.52
  115.0 3.0 %pair_back.1 = (f32[64,768]{1,0:T(8,128)S(1)}, bf16[64,768]{1,0:T(8,128)(2,1)S(1)}, bf16[64,768]{1,0:T(8,128)(2,1)S(1)}, bf16[64,768]{1,0:T(8,128)(2,1)S(1)}, bf16[256,576]{1,0:T(8,128)(2,1)S(1)}) custom-call(s32[2]{0:T(128)S(1)} %copy-done, bf16[256,256]{1,0:T(8,128)(2,1)S(1)} %get-tuple-element.247.refs_0_.pair_ref, ...), custom_call_target="tpu_custom_call" | custom-call | flops 40000000 | bytes 40000 | tf_op jit(solution)/shard_map/pair_back/pallas_call | solution.py:413
  118.0 2.5 %collective-permute-done.51.refs_1_ = bf16[2,48,1536]{2,1,0:T(8,128)(2,1)S(1)} collective-permute-done((bf16[2,48,1536]{2,1,0:T(8,128)(2,1)S(1)}, bf16[2,48,1536]{2,1,0:T(8,128)(2,1)S(1)}, u32[]{:S(2)}, u32[]{:S(2)}) %collective-permute-start.51) | collective-permute-done | bytes 294944 | tf_op jit(solution)/shard_map/ppermute | solution.py:26
  120.5 1.1 head_weights.1
  122.2 1.8 %collective-permute-done.53.refs_1_ = bf16[8,48,192]{2,1,0:T(8,128)(2,1)S(1)} collective-permute-done((bf16[8,48,192]{2,1,0:T(8,128)(2,1)S(1)}, bf16[8,48,192]{2,1,0:T(8,128)(2,1)S(1)}, u32[]{:S(2)}, u32[]{:S(2)}) %collective-permute-start.53) | collective-permute-done | bytes 147488 | tf_op jit(solution)/shard_map/ppermute | solution.py:26
  124.2 1.6 %collective-permute-start.59 = (bf16[4,48,896]{2,1,0:T(8,128)(2,1)S(1)}, bf16[4,48,896]{2,1,0:T(8,128)(2,1)S(1)}, u32[]{:S(2)}, u32[]{:S(2)}) collective-permute-start(bf16[4,48,896]{2,1,0:T(8,128)(2,1)S(1)} %get-tuple-element.275), channel_id=1, source_target_pairs={{0,4},{1,5},{2,6},{3,7},{4,0},{5,1},{6,2},{7,3},{8,12},{9,13},{10,... | collective-permute-start | bytes 1032200 | tf_op jit(solution)/shard_map/ppermute | solution.py:26
  125.8 1.0 collective-permute-start.56
  126.9 2.4 %collective-permute-start.57 = (bf16[64,768]{1,0:T(8,128)(2,1)S(1)}, bf16[64,768]{1,0:T(8,128)(2,1)S(1)}, u32[]{:S(2)}, u32[]{:S(2)}) collective-permute-start(bf16[64,768]{1,0:T(8,128)(2,1)S(1)} %get-tuple-element.268), channel_id=1, source_target_pairs={{0,9},{1,8},{2,11},{3,10},{4,13},{5,12},{6,15},{7,14},{8,1},{9,0},... | collective-permute-start | bytes 294920 | tf_op jit(solution)/shard_map/ppermute | solution.py:26
  129.4 2.0 %collective-permute-done.55.got1_ref = bf16[64,768]{1,0:T(8,128)(2,1)S(1)} collective-permute-done((bf16[64,768]{1,0:T(8,128)(2,1)S(1)}, bf16[64,768]{1,0:T(8,128)(2,1)S(1)}, u32[]{:S(2)}, u32[]{:S(2)}) %collective-permute-start.55) | collective-permute-done | bytes 98336 | tf_op jit(solution)/shard_map/ppermute | solution.py:26
  131.4 2.6 %collective-permute-done.57.got3_ref = bf16[64,768]{1,0:T(8,128)(2,1)S(1)} collective-permute-done((bf16[64,768]{1,0:T(8,128)(2,1)S(1)}, bf16[64,768]{1,0:T(8,128)(2,1)S(1)}, u32[]{:S(2)}, u32[]{:S(2)}) %collective-permute-start.57) | collective-permute-done | bytes 98336 | tf_op jit(solution)/shard_map/ppermute | solution.py:26
  134.1 2.0 %collective-permute-start.58 = (bf16[32,1536]{1,0:T(8,128)(2,1)S(1)}, bf16[32,1536]{1,0:T(8,128)(2,1)S(1)}, u32[]{:S(2)}, u32[]{:S(2)}) collective-permute-start(bf16[32,1536]{1,0:T(8,128)(2,1)S(1)} %get-tuple-element.272), channel_id=1, source_target_pairs={{0,16},{1,17},{2,18},{3,19},{4,20},{5,21},{6,22},{7,23},{8,24},{9,... | collective-permute-start | bytes 294920 | tf_op jit(solution)/shard_map/ppermute | solution.py:26
  136.9 1.7 %collective-permute-start.61 = (bf16[48,896]{1,0:T(8,128)(2,1)S(1)}, bf16[48,896]{1,0:T(8,128)(2,1)S(1)}, u32[]{:S(2)}, u32[]{:S(2)}) collective-permute-start(bf16[48,896]{1,0:T(8,128)(2,1)S(1)} %get-tuple-element.278), channel_id=1, source_target_pairs={{0,16},{1,17},{2,18},{3,19},{4,20},{5,21},{6,22},{7,23},{8,24},{9,... | collective-permute-start | bytes 258056 | tf_op jit(solution)/shard_map/ppermute | solution.py:26
  138.6 2.0 %collective-permute-start.62 = (bf16[48,896]{1,0:T(8,128)(2,1)S(1)}, bf16[48,896]{1,0:T(8,128)(2,1)S(1)}, u32[]{:S(2)}, u32[]{:S(2)}) collective-permute-start(bf16[48,896]{1,0:T(8,128)(2,1)S(1)} %get-tuple-element.279), channel_id=1, source_target_pairs={{0,24},{1,25},{2,26},{3,27},{4,28},{5,29},{6,30},{7,31},{8,16},{9,... | collective-permute-start | bytes 258056 | tf_op jit(solution)/shard_map/ppermute | solution.py:26
  141.5 3.9 %collective-permute-done.58.got_ref = bf16[32,1536]{1,0:T(8,128)(2,1)S(1)} collective-permute-done((bf16[32,1536]{1,0:T(8,128)(2,1)S(1)}, bf16[32,1536]{1,0:T(8,128)(2,1)S(1)}, u32[]{:S(2)}, u32[]{:S(2)}) %collective-permute-start.58) | collective-permute-done | bytes 98336 | tf_op jit(solution)/shard_map/ppermute | solution.py:26
  (97 shorter events, 21.8 us)
Async XLA Ops:
  3.5 7.6 %collective-permute-start.4 = (bf16[64,768]{1,0:T(8,128)(2,1)S(1)}, bf16[64,768]{1,0:T(8,128)(2,1)S(1)}, u32[]{:S(2)}, u32[]{:S(2)}) collective-permute-start(bf16[64,768]{1,0:T(8,128)(2,1)S(1)} %get-tuple-element.177), channel_id=1, source_target_pairs={{0,8},{1,9},{2,10},{3,11},{4,12},{5,13},{6,14},{7,15},{8,0},{9,1},... | collective-permute-start | bytes 294920 | tf_op jit(solution)/shard_map/ppermute | solution.py:26
  6.5 12.6 %collective-permute-start = (bf16[64,768]{1,0:T(8,128)(2,1)S(1)}, bf16[64,768]{1,0:T(8,128)(2,1)S(1)}, u32[]{:S(2)}, u32[]{:S(2)}) collective-permute-start(bf16[64,768]{1,0:T(8,128)(2,1)S(1)} %get-tuple-element.160), channel_id=1, source_target_pairs={{0,16},{1,17},{2,18},{3,19},{4,20},{5,21},{6,22},{7,23},{8,24},{9,... | collective-permute-start | bytes 294920 | tf_op jit(solution)/shard_map/ppermute | solution.py:26
  9.1 13.1 %collective-permute-start.6 = (bf16[64,768]{1,0:T(8,128)(2,1)S(1)}, bf16[64,768]{1,0:T(8,128)(2,1)S(1)}, u32[]{:S(2)}, u32[]{:S(2)}) collective-permute-start(bf16[64,768]{1,0:T(8,128)(2,1)S(1)} %get-tuple-element.177), channel_id=1, source_target_pairs={{0,24},{1,25},{2,26},{3,27},{4,28},{5,29},{6,30},{7,31},{8,16},{9,... | collective-permute-start | bytes 294920 | tf_op jit(solution)/shard_map/ppermute | solution.py:26
  9.1 13.1 %collective-permute-start.5 = (bf16[64,768]{1,0:T(8,128)(2,1)S(1)}, bf16[64,768]{1,0:T(8,128)(2,1)S(1)}, u32[]{:S(2)}, u32[]{:S(2)}) collective-permute-start(bf16[64,768]{1,0:T(8,128)(2,1)S(1)} %get-tuple-element.176), channel_id=1, source_target_pairs={{0,16},{1,17},{2,18},{3,19},{4,20},{5,21},{6,22},{7,23},{8,24},{9,... | collective-permute-start | bytes 294920 | tf_op jit(solution)/shard_map/ppermute | solution.py:26
  11.1 12.7 %collective-permute-start.7 = (bf16[2,64,768]{2,1,0:T(8,128)(2,1)S(1)}, bf16[2,64,768]{2,1,0:T(8,128)(2,1)S(1)}, u32[]{:S(2)}, u32[]{:S(2)}) collective-permute-start(bf16[2,64,768]{2,1,0:T(8,128)(2,1)S(1)} %pad_maximum_fusion.1.refs_0_), channel_id=1, source_target_pairs={{0,4},{1,5},{2,6},{3,7},{4,0},{5,1},{6,2},{7,3},{8,12},{9,13},{10,... | collective-permute-start | bytes 589832 | tf_op jit(solution)/shard_map/ppermute | solution.py:26
  12.6 11.2 %collective-permute-start.12 = (bf16[48,1536]{1,0:T(8,128)(2,1)S(1)}, bf16[48,1536]{1,0:T(8,128)(2,1)S(1)}, u32[]{:S(2)}, u32[]{:S(2)}) collective-permute-start(bf16[48,1536]{1,0:T(8,128)(2,1)S(1)} %get-tuple-element.182), channel_id=1, source_target_pairs={{0,8},{1,9},{2,10},{3,11},{4,12},{5,13},{6,14},{7,15},{8,0},{9,1},... | collective-permute-start | bytes 442376 | tf_op jit(solution)/shard_map/ppermute | solution.py:26
  19.2 6.3 %collective-permute-start.3 = (bf16[64,768]{1,0:T(8,128)(2,1)S(1)}, bf16[64,768]{1,0:T(8,128)(2,1)S(1)}, u32[]{:S(2)}, u32[]{:S(2)}) collective-permute-start(bf16[64,768]{1,0:T(8,128)(2,1)S(1)} %pad_maximum_fusion.3), channel_id=1, source_target_pairs={{0,9},{1,8},{2,11},{3,10},{4,13},{5,12},{6,15},{7,14},{8,1},{9,0},... | collective-permute-start | bytes 294920 | tf_op jit(solution)/shard_map/ppermute | solution.py:26
  22.2 4.6 %collective-permute-start.2 = (bf16[64,768]{1,0:T(8,128)(2,1)S(1)}, bf16[64,768]{1,0:T(8,128)(2,1)S(1)}, u32[]{:S(2)}, u32[]{:S(2)}) collective-permute-start(bf16[64,768]{1,0:T(8,128)(2,1)S(1)} %pad_maximum_fusion.3), channel_id=1, source_target_pairs={{0,8},{1,9},{2,10},{3,11},{4,12},{5,13},{6,14},{7,15},{8,0},{9,1},... | collective-permute-start | bytes 294920 | tf_op jit(solution)/shard_map/ppermute | solution.py:26
  22.2 4.6 %collective-permute-start.1 = (bf16[64,768]{1,0:T(8,128)(2,1)S(1)}, bf16[64,768]{1,0:T(8,128)(2,1)S(1)}, u32[]{:S(2)}, u32[]{:S(2)}) collective-permute-start(bf16[64,768]{1,0:T(8,128)(2,1)S(1)} %pad_maximum_fusion.3), channel_id=1, source_target_pairs={{0,1},{1,0},{2,3},{3,2},{4,5},{5,4},{6,7},{7,6},{8,9},{9,8},{10,11... | collective-permute-start | bytes 294920 | tf_op jit(solution)/shard_map/ppermute | solution.py:26
  23.8 10.4 %collective-permute-start.9 = (bf16[2,64,768]{2,1,0:T(8,128)(2,1)S(1)}, bf16[2,64,768]{2,1,0:T(8,128)(2,1)S(1)}, u32[]{:S(2)}, u32[]{:S(2)}) collective-permute-start(bf16[2,64,768]{2,1,0:T(8,128)(2,1)S(1)} %pad_maximum_fusion.1.refs_0_), channel_id=1, source_target_pairs={{0,2},{1,3},{2,0},{3,1},{4,6},{5,7},{6,4},{7,5},{8,10},{9,11},{10,... | collective-permute-start | bytes 589832 | tf_op jit(solution)/shard_map/ppermute | solution.py:26
  23.9 7.3 %collective-permute-start.8 = (bf16[2,64,768]{2,1,0:T(8,128)(2,1)S(1)}, bf16[2,64,768]{2,1,0:T(8,128)(2,1)S(1)}, u32[]{:S(2)}, u32[]{:S(2)}) collective-permute-start(bf16[2,64,768]{2,1,0:T(8,128)(2,1)S(1)} %pad_maximum_fusion.2.refs_1_), channel_id=1, source_target_pairs={{0,4},{1,5},{2,6},{3,7},{4,0},{5,1},{6,2},{7,3},{8,12},{9,13},{10,... | collective-permute-start | bytes 589832 | tf_op jit(solution)/shard_map/ppermute | solution.py:26
  25.5 8.8 %collective-permute-start.10 = (bf16[2,64,768]{2,1,0:T(8,128)(2,1)S(1)}, bf16[2,64,768]{2,1,0:T(8,128)(2,1)S(1)}, u32[]{:S(2)}, u32[]{:S(2)}) collective-permute-start(bf16[2,64,768]{2,1,0:T(8,128)(2,1)S(1)} %pad_maximum_fusion.2.refs_1_), channel_id=1, source_target_pairs={{0,2},{1,3},{2,0},{3,1},{4,6},{5,7},{6,4},{7,5},{8,10},{9,11},{10,... | collective-permute-start | bytes 589832 | tf_op jit(solution)/shard_map/ppermute | solution.py:26
  26.9 7.4 %collective-permute-start.11 = (bf16[2,64,768]{2,1,0:T(8,128)(2,1)S(1)}, bf16[2,64,768]{2,1,0:T(8,128)(2,1)S(1)}, u32[]{:S(2)}, u32[]{:S(2)}) collective-permute-start(bf16[2,64,768]{2,1,0:T(8,128)(2,1)S(1)} %collective-permute-done.7.refs_2_), channel_id=1, source_target_pairs={{0,2},{1,3},{2,0},{3,1},{4,6},{5,7},{6,4},{7,5},{8,10},{9,11},{10,... | collective-permute-start | bytes 589832 | tf_op jit(solution)/shard_map/ppermute | solution.py:26
  31.2 3.0 %collective-permute-start.13 = (bf16[2,64,768]{2,1,0:T(8,128)(2,1)S(1)}, bf16[2,64,768]{2,1,0:T(8,128)(2,1)S(1)}, u32[]{:S(2)}, u32[]{:S(2)}) collective-permute-start(bf16[2,64,768]{2,1,0:T(8,128)(2,1)S(1)} %collective-permute-done.8.refs_3_), channel_id=1, source_target_pairs={{0,2},{1,3},{2,0},{3,1},{4,6},{5,7},{6,4},{7,5},{8,10},{9,11},{10,... | collective-permute-start | bytes 589832 | tf_op jit(solution)/shard_map/ppermute | solution.py:26
  31.2 17.0 %collective-permute-start.26 = (bf16[2,48,1536]{2,1,0:T(8,128)(2,1)S(1)}, bf16[2,48,1536]{2,1,0:T(8,128)(2,1)S(1)}, u32[]{:S(2)}, u32[]{:S(2)}) collective-permute-start(bf16[2,48,1536]{2,1,0:T(8,128)(2,1)S(1)} %pad_maximum_fusion.refs_0_), channel_id=1, source_target_pairs={{0,16},{1,17},{2,18},{3,19},{4,20},{5,21},{6,22},{7,23},{8,24},{9,... | collective-permute-start | bytes 884744 | tf_op jit(solution)/shard_map/ppermute | solution.py:26
  35.0 6.4 %collective-permute-start.14 = (bf16[256,256]{1,0:T(8,128)(2,1)S(1)}, bf16[256,256]{1,0:T(8,128)(2,1)S(1)}, u32[]{:S(2)}, u32[]{:S(2)}) collective-permute-start(bf16[256,256]{1,0:T(8,128)(2,1)S(1)} %get-tuple-element.247.refs_0_.pair_ref), channel_id=1, source_target_pairs={{0,4},{1,5},{2,6},{3,7},{4,0},{5,1},{6,2},{7,3},{8,12},{9,13},{10,... | collective-permute-start | bytes 393224 | tf_op jit(solution)/shard_map/ppermute | solution.py:26
  36.5 5.5 %collective-permute-start.17 = (bf16[256,128]{1,0:T(8,128)(2,1)S(1)}, bf16[256,128]{1,0:T(8,128)(2,1)S(1)}, u32[]{:S(2)}, u32[]{:S(2)}) collective-permute-start(bf16[256,128]{1,0:T(8,128)(2,1)S(1)} %get-tuple-element.196.refs_4_.rest_ref), channel_id=1, source_target_pairs={{0,4},{1,5},{2,6},{3,7},{4,0},{5,1},{6,2},{7,3},{8,12},{9,13},{10,... | collective-permute-start | bytes 196616 | tf_op jit(solution)/shard_map/ppermute | solution.py:26
  37.1 7.2 %collective-permute-start.15 = (bf16[256,256]{1,0:T(8,128)(2,1)S(1)}, bf16[256,256]{1,0:T(8,128)(2,1)S(1)}, u32[]{:S(2)}, u32[]{:S(2)}) collective-permute-start(bf16[256,256]{1,0:T(8,128)(2,1)S(1)} %get-tuple-element.247.refs_0_.pair_ref), channel_id=1, source_target_pairs={{0,2},{1,3},{2,0},{3,1},{4,6},{5,7},{6,4},{7,5},{8,10},{9,11},{10,... | collective-permute-start | bytes 393224 | tf_op jit(solution)/shard_map/ppermute | solution.py:26
  41.4 2.9 %collective-permute-start.16 = (bf16[256,256]{1,0:T(8,128)(2,1)S(1)}, bf16[256,256]{1,0:T(8,128)(2,1)S(1)}, u32[]{:S(2)}, u32[]{:S(2)}) collective-permute-start(bf16[256,256]{1,0:T(8,128)(2,1)S(1)} %collective-permute-done.14.refs_1_), channel_id=1, source_target_pairs={{0,2},{1,3},{2,0},{3,1},{4,6},{5,7},{6,4},{7,5},{8,10},{9,11},{10,... | collective-permute-start | bytes 393224 | tf_op jit(solution)/shard_map/ppermute | solution.py:26
  41.4 1.4 collective-permute-start.18
  42.1 2.2 %collective-permute-start.19 = (bf16[256,128]{1,0:T(8,128)(2,1)S(1)}, bf16[256,128]{1,0:T(8,128)(2,1)S(1)}, u32[]{:S(2)}, u32[]{:S(2)}) collective-permute-start(bf16[256,128]{1,0:T(8,128)(2,1)S(1)} %collective-permute-done.17.refs_5_), channel_id=1, source_target_pairs={{0,2},{1,3},{2,0},{3,1},{4,6},{5,7},{6,4},{7,5},{8,10},{9,11},{10,... | collective-permute-start | bytes 196616 | tf_op jit(solution)/shard_map/ppermute | solution.py:26
  42.8 13.8 %collective-permute-start.27 = (bf16[2,48,1536]{2,1,0:T(8,128)(2,1)S(1)}, bf16[2,48,1536]{2,1,0:T(8,128)(2,1)S(1)}, u32[]{:S(2)}, u32[]{:S(2)}) collective-permute-start(bf16[2,48,1536]{2,1,0:T(8,128)(2,1)S(1)} %pad_maximum_fusion.refs_0_), channel_id=1, source_target_pairs={{0,4},{1,5},{2,6},{3,7},{4,0},{5,1},{6,2},{7,3},{8,12},{9,13},{10,... | collective-permute-start | bytes 884744 | tf_op jit(solution)/shard_map/ppermute | solution.py:26
  48.2 10.1 %collective-permute-start.28 = (bf16[2,48,1536]{2,1,0:T(8,128)(2,1)S(1)}, bf16[2,48,1536]{2,1,0:T(8,128)(2,1)S(1)}, u32[]{:S(2)}, u32[]{:S(2)}) collective-permute-start(bf16[2,48,1536]{2,1,0:T(8,128)(2,1)S(1)} %collective-permute-done.26.refs_1_), channel_id=1, source_target_pairs={{0,4},{1,5},{2,6},{3,7},{4,0},{5,1},{6,2},{7,3},{8,12},{9,13},{10,... | collective-permute-start | bytes 884744 | tf_op jit(solution)/shard_map/ppermute | solution.py:26
  49.7 5.5 %collective-permute-start.20 = (bf16[64,768]{1,0:T(8,128)(2,1)S(1)}, bf16[64,768]{1,0:T(8,128)(2,1)S(1)}, u32[]{:S(2)}, u32[]{:S(2)}) collective-permute-start(bf16[64,768]{1,0:T(8,128)(2,1)S(1)} %get-tuple-element.199), channel_id=1, source_target_pairs={{0,8},{1,9},{2,10},{3,11},{4,12},{5,13},{6,14},{7,15},{8,0},{9,1},... | collective-permute-start | bytes 294920 | tf_op jit(solution)/shard_map/ppermute | solution.py:26
  49.7 5.6 %collective-permute-start.21 = (bf16[64,768]{1,0:T(8,128)(2,1)S(1)}, bf16[64,768]{1,0:T(8,128)(2,1)S(1)}, u32[]{:S(2)}, u32[]{:S(2)}) collective-permute-start(bf16[64,768]{1,0:T(8,128)(2,1)S(1)} %get-tuple-element.200), channel_id=1, source_target_pairs={{0,1},{1,0},{2,3},{3,2},{4,5},{5,4},{6,7},{7,6},{8,9},{9,8},{10,11... | collective-permute-start | bytes 294920 | tf_op jit(solution)/shard_map/ppermute | solution.py:26
  50.2 6.1 %collective-permute-start.22 = (bf16[64,768]{1,0:T(8,128)(2,1)S(1)}, bf16[64,768]{1,0:T(8,128)(2,1)S(1)}, u32[]{:S(2)}, u32[]{:S(2)}) collective-permute-start(bf16[64,768]{1,0:T(8,128)(2,1)S(1)} %get-tuple-element.201), channel_id=1, source_target_pairs={{0,9},{1,8},{2,11},{3,10},{4,13},{5,12},{6,15},{7,14},{8,1},{9,0},... | collective-permute-start | bytes 294920 | tf_op jit(solution)/shard_map/ppermute | solution.py:26
  58.4 1.7 %collective-permute-start.29 = (bf16[2,48,1536]{2,1,0:T(8,128)(2,1)S(1)}, bf16[2,48,1536]{2,1,0:T(8,128)(2,1)S(1)}, u32[]{:S(2)}, u32[]{:S(2)}) collective-permute-start(bf16[2,48,1536]{2,1,0:T(8,128)(2,1)S(1)} %pad_maximum_fusion.refs_0_), channel_id=1, source_target_pairs={{0,2},{1,3},{2,0},{3,1},{4,6},{5,7},{6,4},{7,5},{8,10},{9,11},{10,... | collective-permute-start | bytes 884744 | tf_op jit(solution)/shard_map/ppermute | solution.py:26
  58.4 3.0 %collective-permute-start.30 = (bf16[2,48,1536]{2,1,0:T(8,128)(2,1)S(1)}, bf16[2,48,1536]{2,1,0:T(8,128)(2,1)S(1)}, u32[]{:S(2)}, u32[]{:S(2)}) collective-permute-start(bf16[2,48,1536]{2,1,0:T(8,128)(2,1)S(1)} %collective-permute-done.26.refs_1_), channel_id=1, source_target_pairs={{0,2},{1,3},{2,0},{3,1},{4,6},{5,7},{6,4},{7,5},{8,10},{9,11},{10,... | collective-permute-start | bytes 884744 | tf_op jit(solution)/shard_map/ppermute | solution.py:26
  58.9 4.0 %collective-permute-start.31 = (bf16[2,48,1536]{2,1,0:T(8,128)(2,1)S(1)}, bf16[2,48,1536]{2,1,0:T(8,128)(2,1)S(1)}, u32[]{:S(2)}, u32[]{:S(2)}) collective-permute-start(bf16[2,48,1536]{2,1,0:T(8,128)(2,1)S(1)} %collective-permute-done.27.refs_2_), channel_id=1, source_target_pairs={{0,2},{1,3},{2,0},{3,1},{4,6},{5,7},{6,4},{7,5},{8,10},{9,11},{10,... | collective-permute-start | bytes 884744 | tf_op jit(solution)/shard_map/ppermute | solution.py:26
  58.9 4.0 %collective-permute-start.32 = (bf16[2,48,1536]{2,1,0:T(8,128)(2,1)S(1)}, bf16[2,48,1536]{2,1,0:T(8,128)(2,1)S(1)}, u32[]{:S(2)}, u32[]{:S(2)}) collective-permute-start(bf16[2,48,1536]{2,1,0:T(8,128)(2,1)S(1)} %collective-permute-done.28.refs_3_), channel_id=1, source_target_pairs={{0,2},{1,3},{2,0},{3,1},{4,6},{5,7},{6,4},{7,5},{8,10},{9,11},{10,... | collective-permute-start | bytes 884744 | tf_op jit(solution)/shard_map/ppermute | solution.py:26
  59.4 6.6 %collective-permute-start.25 = (bf16[64,768]{1,0:T(8,128)(2,1)S(1)}, bf16[64,768]{1,0:T(8,128)(2,1)S(1)}, u32[]{:S(2)}, u32[]{:S(2)}) collective-permute-start(bf16[64,768]{1,0:T(8,128)(2,1)S(1)} %get-tuple-element.203.own_ref), channel_id=1, source_target_pairs={{0,9},{1,8},{2,11},{3,10},{4,13},{5,12},{6,15},{7,14},{8,1},{9,0},... | collective-permute-start | bytes 294920 | tf_op jit(solution)/shard_map/ppermute | solution.py:26
  60.1 6.0 %collective-permute-start.24 = (bf16[64,768]{1,0:T(8,128)(2,1)S(1)}, bf16[64,768]{1,0:T(8,128)(2,1)S(1)}, u32[]{:S(2)}, u32[]{:S(2)}) collective-permute-start(bf16[64,768]{1,0:T(8,128)(2,1)S(1)} %get-tuple-element.203.own_ref), channel_id=1, source_target_pairs={{0,8},{1,9},{2,10},{3,11},{4,12},{5,13},{6,14},{7,15},{8,0},{9,1},... | collective-permute-start | bytes 294920 | tf_op jit(solution)/shard_map/ppermute | solution.py:26
  61.4 5.7 %collective-permute-start.23 = (bf16[64,768]{1,0:T(8,128)(2,1)S(1)}, bf16[64,768]{1,0:T(8,128)(2,1)S(1)}, u32[]{:S(2)}, u32[]{:S(2)}) collective-permute-start(bf16[64,768]{1,0:T(8,128)(2,1)S(1)} %get-tuple-element.203.own_ref), channel_id=1, source_target_pairs={{0,1},{1,0},{2,3},{3,2},{4,5},{5,4},{6,7},{7,6},{8,9},{9,8},{10,11... | collective-permute-start | bytes 294920 | tf_op jit(solution)/shard_map/ppermute | solution.py:26
  68.7 5.6 %collective-permute-start.33 = (bf16[64,768]{1,0:T(8,128)(2,1)S(1)}, bf16[64,768]{1,0:T(8,128)(2,1)S(1)}, u32[]{:S(2)}, u32[]{:S(2)}) collective-permute-start(bf16[64,768]{1,0:T(8,128)(2,1)S(1)} %get-tuple-element.216), channel_id=1, source_target_pairs={{0,8},{1,9},{2,10},{3,11},{4,12},{5,13},{6,14},{7,15},{8,0},{9,1},... | collective-permute-start | bytes 294920 | tf_op jit(solution)/shard_map/ppermute | solution.py:26
  69.1 5.6 %collective-permute-start.34 = (bf16[64,768]{1,0:T(8,128)(2,1)S(1)}, bf16[64,768]{1,0:T(8,128)(2,1)S(1)}, u32[]{:S(2)}, u32[]{:S(2)}) collective-permute-start(bf16[64,768]{1,0:T(8,128)(2,1)S(1)} %get-tuple-element.217), channel_id=1, source_target_pairs={{0,1},{1,0},{2,3},{3,2},{4,5},{5,4},{6,7},{7,6},{8,9},{9,8},{10,11... | collective-permute-start | bytes 294920 | tf_op jit(solution)/shard_map/ppermute | solution.py:26
  70.2 5.6 %collective-permute-start.35 = (bf16[64,768]{1,0:T(8,128)(2,1)S(1)}, bf16[64,768]{1,0:T(8,128)(2,1)S(1)}, u32[]{:S(2)}, u32[]{:S(2)}) collective-permute-start(bf16[64,768]{1,0:T(8,128)(2,1)S(1)} %get-tuple-element.218), channel_id=1, source_target_pairs={{0,9},{1,8},{2,11},{3,10},{4,13},{5,12},{6,15},{7,14},{8,1},{9,0},... | collective-permute-start | bytes 294920 | tf_op jit(solution)/shard_map/ppermute | solution.py:26
  76.7 5.6 %collective-permute-start.38 = (bf16[64,768]{1,0:T(8,128)(2,1)S(1)}, bf16[64,768]{1,0:T(8,128)(2,1)S(1)}, u32[]{:S(2)}, u32[]{:S(2)}) collective-permute-start(bf16[64,768]{1,0:T(8,128)(2,1)S(1)} %get-tuple-element.221.own_ref), channel_id=1, source_target_pairs={{0,9},{1,8},{2,11},{3,10},{4,13},{5,12},{6,15},{7,14},{8,1},{9,0},... | collective-permute-start | bytes 294920 | tf_op jit(solution)/shard_map/ppermute | solution.py:26
  78.8 4.6 %collective-permute-start.37 = (bf16[64,768]{1,0:T(8,128)(2,1)S(1)}, bf16[64,768]{1,0:T(8,128)(2,1)S(1)}, u32[]{:S(2)}, u32[]{:S(2)}) collective-permute-start(bf16[64,768]{1,0:T(8,128)(2,1)S(1)} %get-tuple-element.221.own_ref), channel_id=1, source_target_pairs={{0,8},{1,9},{2,10},{3,11},{4,12},{5,13},{6,14},{7,15},{8,0},{9,1},... | collective-permute-start | bytes 294920 | tf_op jit(solution)/shard_map/ppermute | solution.py:26
  79.3 4.6 %collective-permute-start.36 = (bf16[64,768]{1,0:T(8,128)(2,1)S(1)}, bf16[64,768]{1,0:T(8,128)(2,1)S(1)}, u32[]{:S(2)}, u32[]{:S(2)}) collective-permute-start(bf16[64,768]{1,0:T(8,128)(2,1)S(1)} %get-tuple-element.221.own_ref), channel_id=1, source_target_pairs={{0,1},{1,0},{2,3},{3,2},{4,5},{5,4},{6,7},{7,6},{8,9},{9,8},{10,11... | collective-permute-start | bytes 294920 | tf_op jit(solution)/shard_map/ppermute | solution.py:26
  85.9 2.1 %collective-permute-start.39 = (bf16[8,48,768]{2,1,0:T(8,128)(2,1)S(1)}, bf16[8,48,768]{2,1,0:T(8,128)(2,1)S(1)}, u32[]{:S(2)}, u32[]{:S(2)}) collective-permute-start(bf16[8,48,768]{2,1,0:T(8,128)(2,1)S(1)} %get-tuple-element.228), channel_id=1, source_target_pairs={{0,2},{1,3},{2,0},{3,1},{4,6},{5,7},{6,4},{7,5},{8,10},{9,11},{10,... | collective-permute-start | bytes 1769480 | tf_op jit(solution)/shard_map/ppermute | solution.py:26
  86.0 2.8 %collective-permute-start.40 = (bf16[8,48,768]{2,1,0:T(8,128)(2,1)S(1)}, bf16[8,48,768]{2,1,0:T(8,128)(2,1)S(1)}, u32[]{:S(2)}, u32[]{:S(2)}) collective-permute-start(bf16[8,48,768]{2,1,0:T(8,128)(2,1)S(1)} %get-tuple-element.229), channel_id=1, source_target_pairs={{0,2},{1,3},{2,0},{3,1},{4,6},{5,7},{6,4},{7,5},{8,10},{9,11},{10,... | collective-permute-start | bytes 1769480 | tf_op jit(solution)/shard_map/ppermute | solution.py:26
  89.1 18.5 %collective-permute-start.47 = (bf16[4,48,1536]{2,1,0:T(8,128)(2,1)S(1)}, bf16[4,48,1536]{2,1,0:T(8,128)(2,1)S(1)}, u32[]{:S(2)}, u32[]{:S(2)}) collective-permute-start(bf16[4,48,1536]{2,1,0:T(8,128)(2,1)S(1)} %get-tuple-element.235), channel_id=1, source_target_pairs={{0,4},{1,5},{2,6},{3,7},{4,0},{5,1},{6,2},{7,3},{8,12},{9,13},{10,... | collective-permute-start | bytes 1769480 | tf_op jit(solution)/shard_map/ppermute | solution.py:26
  90.7 4.6 %collective-permute-start.41 = (bf16[64,768]{1,0:T(8,128)(2,1)S(1)}, bf16[64,768]{1,0:T(8,128)(2,1)S(1)}, u32[]{:S(2)}, u32[]{:S(2)}) collective-permute-start(bf16[64,768]{1,0:T(8,128)(2,1)S(1)} %get-tuple-element.236), channel_id=1, source_target_pairs={{0,8},{1,9},{2,10},{3,11},{4,12},{5,13},{6,14},{7,15},{8,0},{9,1},... | collective-permute-start | bytes 294920 | tf_op jit(solution)/shard_map/ppermute | solution.py:26
  92.2 6.6 %collective-permute-start.42 = (bf16[64,768]{1,0:T(8,128)(2,1)S(1)}, bf16[64,768]{1,0:T(8,128)(2,1)S(1)}, u32[]{:S(2)}, u32[]{:S(2)}) collective-permute-start(bf16[64,768]{1,0:T(8,128)(2,1)S(1)} %get-tuple-element.237), channel_id=1, source_target_pairs={{0,1},{1,0},{2,3},{3,2},{4,5},{5,4},{6,7},{7,6},{8,9},{9,8},{10,11... | collective-permute-start | bytes 294920 | tf_op jit(solution)/shard_map/ppermute | solution.py:26
  92.9 6.0 %collective-permute-start.43 = (bf16[64,768]{1,0:T(8,128)(2,1)S(1)}, bf16[64,768]{1,0:T(8,128)(2,1)S(1)}, u32[]{:S(2)}, u32[]{:S(2)}) collective-permute-start(bf16[64,768]{1,0:T(8,128)(2,1)S(1)} %get-tuple-element.238), channel_id=1, source_target_pairs={{0,9},{1,8},{2,11},{3,10},{4,13},{5,12},{6,15},{7,14},{8,1},{9,0},... | collective-permute-start | bytes 294920 | tf_op jit(solution)/shard_map/ppermute | solution.py:26
  99.1 5.6 %collective-permute-start.46 = (bf16[64,768]{1,0:T(8,128)(2,1)S(1)}, bf16[64,768]{1,0:T(8,128)(2,1)S(1)}, u32[]{:S(2)}, u32[]{:S(2)}) collective-permute-start(bf16[64,768]{1,0:T(8,128)(2,1)S(1)} %get-tuple-element.242.own_ref), channel_id=1, source_target_pairs={{0,9},{1,8},{2,11},{3,10},{4,13},{5,12},{6,15},{7,14},{8,1},{9,0},... | collective-permute-start | bytes 294920 | tf_op jit(solution)/shard_map/ppermute | solution.py:26
  100.1 5.0 %collective-permute-start.45 = (bf16[64,768]{1,0:T(8,128)(2,1)S(1)}, bf16[64,768]{1,0:T(8,128)(2,1)S(1)}, u32[]{:S(2)}, u32[]{:S(2)}) collective-permute-start(bf16[64,768]{1,0:T(8,128)(2,1)S(1)} %get-tuple-element.242.own_ref), channel_id=1, source_target_pairs={{0,8},{1,9},{2,10},{3,11},{4,12},{5,13},{6,14},{7,15},{8,0},{9,1},... | collective-permute-start | bytes 294920 | tf_op jit(solution)/shard_map/ppermute | solution.py:26
  101.5 4.6 %collective-permute-start.44 = (bf16[64,768]{1,0:T(8,128)(2,1)S(1)}, bf16[64,768]{1,0:T(8,128)(2,1)S(1)}, u32[]{:S(2)}, u32[]{:S(2)}) collective-permute-start(bf16[64,768]{1,0:T(8,128)(2,1)S(1)} %get-tuple-element.242.own_ref), channel_id=1, source_target_pairs={{0,1},{1,0},{2,3},{3,2},{4,5},{5,4},{6,7},{7,6},{8,9},{9,8},{10,11... | collective-permute-start | bytes 294920 | tf_op jit(solution)/shard_map/ppermute | solution.py:26
  107.0 6.4 %collective-permute-start.48 = (bf16[256,512]{1,0:T(8,128)(2,1)S(1)}, bf16[256,512]{1,0:T(8,128)(2,1)S(1)}, u32[]{:S(2)}, u32[]{:S(2)}) collective-permute-start(bf16[256,512]{1,0:T(8,128)(2,1)S(1)} %get-tuple-element.244.packet_ref.g0_ref), channel_id=1, source_target_pairs={{0,4},{1,5},{2,6},{3,7},{4,0},{5,1},{6,2},{7,3},{8,12},{9,13},{10,... | collective-permute-start | bytes 786440 | tf_op jit(solution)/shard_map/ppermute | solution.py:26
  107.7 12.7 %collective-permute-start.51 = (bf16[2,48,1536]{2,1,0:T(8,128)(2,1)S(1)}, bf16[2,48,1536]{2,1,0:T(8,128)(2,1)S(1)}, u32[]{:S(2)}, u32[]{:S(2)}) collective-permute-start(bf16[2,48,1536]{2,1,0:T(8,128)(2,1)S(1)} %get-tuple-element.254), channel_id=1, source_target_pairs={{0,16},{1,17},{2,18},{3,19},{4,20},{5,21},{6,22},{7,23},{8,24},{9,... | collective-permute-start | bytes 884744 | tf_op jit(solution)/shard_map/ppermute | solution.py:26
  109.2 5.6 %collective-permute-start.49 = (bf16[256,512]{1,0:T(8,128)(2,1)S(1)}, bf16[256,512]{1,0:T(8,128)(2,1)S(1)}, u32[]{:S(2)}, u32[]{:S(2)}) collective-permute-start(bf16[256,512]{1,0:T(8,128)(2,1)S(1)} %get-tuple-element.244.packet_ref.g0_ref), channel_id=1, source_target_pairs={{0,2},{1,3},{2,0},{3,1},{4,6},{5,7},{6,4},{7,5},{8,10},{9,11},{10,... | collective-permute-start | bytes 786440 | tf_op jit(solution)/shard_map/ppermute | solution.py:26
  113.4 1.5 %collective-permute-start.50 = (bf16[256,512]{1,0:T(8,128)(2,1)S(1)}, bf16[256,512]{1,0:T(8,128)(2,1)S(1)}, u32[]{:S(2)}, u32[]{:S(2)}) collective-permute-start(bf16[256,512]{1,0:T(8,128)(2,1)S(1)} %collective-permute-done.48.g1_ref), channel_id=1, source_target_pairs={{0,2},{1,3},{2,0},{3,1},{4,6},{5,7},{6,4},{7,5},{8,10},{9,11},{10,... | collective-permute-start | bytes 786440 | tf_op jit(solution)/shard_map/ppermute | solution.py:26
  113.6 6.9 %collective-permute-start.52 = (f32[16,768]{1,0:T(8,128)S(1)}, f32[16,768]{1,0:T(8,128)S(1)}, u32[]{:S(2)}, u32[]{:S(2)}) collective-permute-start(f32[16,768]{1,0:T(8,128)S(1)} %vectors.1.refs_4_), channel_id=1, source_target_pairs={{0,1},{1,0},{2,3},{3,2},{4,5},{5,4},{6,7},{7,6},{8,9},{9,8},{10,11... | collective-permute-start | bytes 147464 | tf_op jit(solution)/shard_map/ppermute | solution.py:26
  121.6 2.4 %collective-permute-start.54 = (bf16[8,48,704]{2,1,0:T(8,128)(2,1)S(1)}, bf16[8,48,704]{2,1,0:T(8,128)(2,1)S(1)}, u32[]{:S(2)}, u32[]{:S(2)}) collective-permute-start(bf16[8,48,704]{2,1,0:T(8,128)(2,1)S(1)} %get-tuple-element.263), channel_id=1, source_target_pairs={{0,2},{1,3},{2,0},{3,1},{4,6},{5,7},{6,4},{7,5},{8,10},{9,11},{10,... | collective-permute-start | bytes 1622024 | tf_op jit(solution)/shard_map/ppermute | solution.py:26
  121.7 2.3 %collective-permute-start.53 = (bf16[8,48,192]{2,1,0:T(8,128)(2,1)S(1)}, bf16[8,48,192]{2,1,0:T(8,128)(2,1)S(1)}, u32[]{:S(2)}, u32[]{:S(2)}) collective-permute-start(bf16[8,48,192]{2,1,0:T(8,128)(2,1)S(1)} %get-tuple-element.262), channel_id=1, source_target_pairs={{0,2},{1,3},{2,0},{3,1},{4,6},{5,7},{6,4},{7,5},{8,10},{9,11},{10,... | collective-permute-start | bytes 442376 | tf_op jit(solution)/shard_map/ppermute | solution.py:26
  124.2 11.9 %collective-permute-start.59 = (bf16[4,48,896]{2,1,0:T(8,128)(2,1)S(1)}, bf16[4,48,896]{2,1,0:T(8,128)(2,1)S(1)}, u32[]{:S(2)}, u32[]{:S(2)}) collective-permute-start(bf16[4,48,896]{2,1,0:T(8,128)(2,1)S(1)} %get-tuple-element.275), channel_id=1, source_target_pairs={{0,4},{1,5},{2,6},{3,7},{4,0},{5,1},{6,2},{7,3},{8,12},{9,13},{10,... | collective-permute-start | bytes 1032200 | tf_op jit(solution)/shard_map/ppermute | solution.py:26
  125.8 5.6 %collective-permute-start.55 = (bf16[64,768]{1,0:T(8,128)(2,1)S(1)}, bf16[64,768]{1,0:T(8,128)(2,1)S(1)}, u32[]{:S(2)}, u32[]{:S(2)}) collective-permute-start(bf16[64,768]{1,0:T(8,128)(2,1)S(1)} %get-tuple-element.266), channel_id=1, source_target_pairs={{0,8},{1,9},{2,10},{3,11},{4,12},{5,13},{6,14},{7,15},{8,0},{9,1},... | collective-permute-start | bytes 294920 | tf_op jit(solution)/shard_map/ppermute | solution.py:26
  125.8 5.6 %collective-permute-start.56 = (bf16[64,768]{1,0:T(8,128)(2,1)S(1)}, bf16[64,768]{1,0:T(8,128)(2,1)S(1)}, u32[]{:S(2)}, u32[]{:S(2)}) collective-permute-start(bf16[64,768]{1,0:T(8,128)(2,1)S(1)} %get-tuple-element.267), channel_id=1, source_target_pairs={{0,1},{1,0},{2,3},{3,2},{4,5},{5,4},{6,7},{7,6},{8,9},{9,8},{10,11... | collective-permute-start | bytes 294920 | tf_op jit(solution)/shard_map/ppermute | solution.py:26
  126.9 7.1 %collective-permute-start.57 = (bf16[64,768]{1,0:T(8,128)(2,1)S(1)}, bf16[64,768]{1,0:T(8,128)(2,1)S(1)}, u32[]{:S(2)}, u32[]{:S(2)}) collective-permute-start(bf16[64,768]{1,0:T(8,128)(2,1)S(1)} %get-tuple-element.268), channel_id=1, source_target_pairs={{0,9},{1,8},{2,11},{3,10},{4,13},{5,12},{6,15},{7,14},{8,1},{9,0},... | collective-permute-start | bytes 294920 | tf_op jit(solution)/shard_map/ppermute | solution.py:26
  129.3 11.3 %collective-permute-start.63 = (bf16[48,1536]{1,0:T(8,128)(2,1)S(1)}, bf16[48,1536]{1,0:T(8,128)(2,1)S(1)}, u32[]{:S(2)}, u32[]{:S(2)}) collective-permute-start(bf16[48,1536]{1,0:T(8,128)(2,1)S(1)} %get-tuple-element.281), channel_id=1, source_target_pairs={{0,8},{1,9},{2,10},{3,11},{4,12},{5,13},{6,14},{7,15},{8,0},{9,1},... | collective-permute-start | bytes 442376 | tf_op jit(solution)/shard_map/ppermute | solution.py:26
  134.1 11.3 %collective-permute-start.58 = (bf16[32,1536]{1,0:T(8,128)(2,1)S(1)}, bf16[32,1536]{1,0:T(8,128)(2,1)S(1)}, u32[]{:S(2)}, u32[]{:S(2)}) collective-permute-start(bf16[32,1536]{1,0:T(8,128)(2,1)S(1)} %get-tuple-element.272), channel_id=1, source_target_pairs={{0,16},{1,17},{2,18},{3,19},{4,20},{5,21},{6,22},{7,23},{8,24},{9,... | collective-permute-start | bytes 294920 | tf_op jit(solution)/shard_map/ppermute | solution.py:26
  136.2 10.0 %collective-permute-start.60 = (bf16[48,896]{1,0:T(8,128)(2,1)S(1)}, bf16[48,896]{1,0:T(8,128)(2,1)S(1)}, u32[]{:S(2)}, u32[]{:S(2)}) collective-permute-start(bf16[48,896]{1,0:T(8,128)(2,1)S(1)} %get-tuple-element.277), channel_id=1, source_target_pairs={{0,8},{1,9},{2,10},{3,11},{4,12},{5,13},{6,14},{7,15},{8,0},{9,1},... | collective-permute-start | bytes 258056 | tf_op jit(solution)/shard_map/ppermute | solution.py:26
  136.9 9.6 %collective-permute-start.61 = (bf16[48,896]{1,0:T(8,128)(2,1)S(1)}, bf16[48,896]{1,0:T(8,128)(2,1)S(1)}, u32[]{:S(2)}, u32[]{:S(2)}) collective-permute-start(bf16[48,896]{1,0:T(8,128)(2,1)S(1)} %get-tuple-element.278), channel_id=1, source_target_pairs={{0,16},{1,17},{2,18},{3,19},{4,20},{5,21},{6,22},{7,23},{8,24},{9,... | collective-permute-start | bytes 258056 | tf_op jit(solution)/shard_map/ppermute | solution.py:26
  138.6 7.9 %collective-permute-start.62 = (bf16[48,896]{1,0:T(8,128)(2,1)S(1)}, bf16[48,896]{1,0:T(8,128)(2,1)S(1)}, u32[]{:S(2)}, u32[]{:S(2)}) collective-permute-start(bf16[48,896]{1,0:T(8,128)(2,1)S(1)} %get-tuple-element.279), channel_id=1, source_target_pairs={{0,24},{1,25},{2,26},{3,27},{4,28},{5,29},{6,30},{7,31},{8,16},{9,... | collective-permute-start | bytes 258056 | tf_op jit(solution)/shard_map/ppermute | solution.py:26
  (1 other events, 9.4 us)

commit v5 on v4

--- a/solution.py
+++ b/solution.py
@@ -460,13 +460,14 @@
     return pl.ds(pl.multiple_of((2 * chip + core) * rows, 16), rows)
 
 
-def join_pieces(piece_refs, full_ref, rows, cols):
+def join_pieces(piece_refs, full_ref, rows, begin, cols=slice(None)):
     here = Place()
     for which, ref in enumerate(piece_refs):
         side, core = here.side ^ ((which >> 1) & 1), here.core ^ (which >> 2)
         for inner in range(2):
             block = (here.high ^ (which & 1)) * 2 + (here.low ^ inner)
-            full_ref[row_of(block * 2 + side, core, rows), :] = ref[inner, 0:rows, cols]
+            piece = ref[inner, begin : begin + rows, cols]
+            full_ref[row_of(block * 2 + side, core, rows), :] = piece
 
 
 def split_rows(full_ref, keep_ref, send_ref, begin, cols):
@@ -503,7 +504,8 @@
     for copy in copies:
         copy.start()
     wq_ref, wk_ref, wv_ref, wo_ref, wu_ref, wd_ref = held[:6]
-    own_ref, send_ref, later_own_ref, later_send_ref = outs
+    own_ref, send_ref, later_own_ref, near_ref = outs
+    size = send_ref.shape[0]
     rows = wq_ref.shape[0]
     head_cols = wq_ref.shape[1] // 2
     unit_cols = wu_ref.shape[1] // 2
@@ -519,7 +521,7 @@
         ],
         0,
     ).astype(low_type)
-    for out_ref in (own_ref, send_ref):
+    for out_ref in (own_ref, send_ref, near_ref):
         out_ref[rows : rows + 16, 0 : 4 * rows] = block
         out_ref[rows : rows + 16, 4 * rows :] = jnp.zeros(
             (16, out_ref.shape[1] - 4 * rows), low_type
@@ -530,19 +532,24 @@
         heads = slice(half * head_cols, (half + 1) * head_cols)
         units = slice(half * unit_cols, (half + 1) * unit_cols)
 
-        def put(first_ref, later_ref):
+        def put_first(first_ref):
             for i, ref in enumerate((wq_ref, wk_ref, wv_ref, wo_ref)):
                 first_ref[0:rows, i * head_cols : (i + 1) * head_cols] = ref[:, heads]
-            later_ref[:, 0:unit_cols] = wu_ref[:, units]
-            later_ref[:, unit_cols:] = wd_ref[:, units]
+
+        def put_later(later_ref, begin):
+            later_ref[begin : begin + rows, :] = wu_ref[:, units]
+            later_ref[begin + rows : begin + 2 * rows, :] = wd_ref[:, units]
 
         @pl.when(low == half)
         def _():
-            put(own_ref, later_own_ref)
+            put_first(own_ref)
+            put_later(later_own_ref, 0)
 
         @pl.when(low != half)
         def _():
-            put(send_ref, later_send_ref)
+            put_first(send_ref)
+            put_first(near_ref)
+            put_later(near_ref, size)
 
 
 def by_chip_row(here, refs, high, low, rows, cols):
@@ -573,8 +580,8 @@
     rows_ref, query_ref, pair_ref, rest_ref, weight_ref, out_weight_ref = outs
     rows = parts[0].shape[1] - 16
     head_cols = query_ref.shape[1]
-    join_pieces(parts, weight_ref, rows, slice(0, 3 * head_cols))
-    join_pieces(parts, out_weight_ref, rows, slice(3 * head_cols, 4 * head_cols))
+    join_pieces(parts, weight_ref, rows, 0, slice(0, 3 * head_cols))
+    join_pieces(parts, out_weight_ref, rows, 0, slice(3 * head_cols, 4 * head_cols))
     shard = keep_ref.shape[0]
     rows_ref[0:shard, :] = keep_ref[...]
     rows_ref[shard : 2 * shard, :] = got_ref[0:shard, :]
@@ -630,10 +637,11 @@
     give_out(mul(attended, weight_ref[...], 1, 1), keep_ref, sends)
 
 
-def full_kernel(cols, *refs):
+def full_kernel(*refs):
     pieces, outs = refs[:8], refs[8:]
-    for out_ref, (begin, end) in zip(outs, cols):
-        join_pieces(pieces, out_ref, pieces[0].shape[1], slice(begin, end))
+    rows = pieces[0].shape[1] // 2
+    for i, out_ref in enumerate(outs):
+        join_pieces(pieces, out_ref, rows, i * rows)
 
 
 def lines_kernel(*refs):
@@ -1017,7 +1025,8 @@
         b_query, b_value, b_out, first_gain, first_shift, b_down, second_gain, second_shift, b_up,
     )
     first = ((shard_rows + 16, 4 * head_cols), low_type)
-    later = ((shard_rows, 2 * unit_cols), low_type)
+    later = ((2 * shard_rows, unit_cols), low_type)
+    near = ((3 * shard_rows + 16, unit_cols), low_type)
     shard = ((shard_pos, width), low_type)
     hidden_own, cot_own, other = run_kernel(
         rows_kernel,
@@ -1031,7 +1040,7 @@
     slot_rows = swap(other, BIT_HIGH)
     packs = run_kernel(
         functools.partial(pack_kernel, len(sources)),
-        [first, first, later, later],
+        [first, first, later, near],
         *tie(sources, other),
         scratch=[(source.shape, source.dtype) for source in sources],
         sems=len(sources),
@@ -1040,19 +1049,18 @@
         name="pack",
     )
 
-    def over_blocks_of(own, send):
-        return own, swap(send, BIT_LOW), swap(own, BIT_HIGH), swap(send, BIT_HIGH | BIT_LOW)
-
-    first_own, first_send, later_own, later_send = tuple(packs)
-    f0, f1, f2, f3 = over_blocks_of(first_own, first_send)
-    first_near = jnp.stack([f0, f1])
+    first_own, first_send, later_own, near_send = tuple(packs)
+    near_got = swap(near_send, BIT_LOW)
+    size = first_own.shape[0]
+    f2, f3 = swap(first_own, BIT_HIGH), swap(first_send, BIT_HIGH | BIT_LOW)
+    first_near = jnp.stack([first_own, near_got[:size]])
     first_near_side = swap(first_near, BIT_SIDE)
     team_rows = gather_team(
         tie(jnp.concatenate([hidden_own, slot_rows[:shard_pos]], 0), packs)
     )
     first_far = tie(jnp.stack([f2, f3]), first_near_side)
     first_far_side = swap(first_far, BIT_SIDE)
-    later_near = jnp.stack([later_own, swap(tie(later_send, first_near), BIT_LOW)])
+    later_near = jnp.stack([later_own, near_got[size:]])
     later_far = swap(tie(later_near, first_far), BIT_HIGH)
     first_pieces = (
         first_near,
@@ -1109,7 +1117,7 @@
     later_sides = tie((later_near, later_far, later_near_side, later_far_side), first_low)
     later_pieces = later_sides + tuple(swap(part, BIT_CORE) for part in later_sides)
     up_weight, down_weight = run_kernel(
-        functools.partial(full_kernel, ((0, unit_cols), (unit_cols, 2 * unit_cols))),
+        full_kernel,
         [((width, unit_cols), low_type)] * 2,
         *later_pieces,
         us=1.0,

time: 148 us -> 146 us (0.986)
  starting transfers between devices: 64 us -> 62 us
    ppermute x64 -> x63, starting transfers between devices: 64 us -> 62 us  [swap(): lax.ppermute(values, AXES, [(i, i ^ bit) for i in range(device_count())])]
    ppermute x64 -> x63, waiting for transfers between devices: 59.7 us -> 60.5 us  [swap(): lax.ppermute(values, AXES, [(i, i ^ bit) for i in range(device_count())])]
  transfers between devices with their start and end apart: 64 -> 63, of which waited for: 35 -> 37; matrix products, arithmetic and copies ran while one was open for 0% -> 0% of each run, Pallas kernels for 9% -> 9%
where the time goes in v5:
time: 146 us
  starting transfers between devices  62 us (42%)
  waiting for transfers between devices  60.5 us (41%)
  Pallas kernels  22.6 us (15%)
    ppermute x63, starting transfers between devices, swap(): lax.ppermute(values, AXES, [(i, i ^ bit) for i in range(device_count())])  62 us
    ppermute x63, waiting for transfers between devices, swap(): lax.ppermute(values, AXES, [(i, i ^ bit) for i in range(device_count())])  60.5 us
    pallas_call x26, Pallas kernels, run_kernel(): pl.pallas_call(body, out_shape=[jax.ShapeDtypeStruct(shape, kind) for sha...  22.6 us
  transfers between devices with their start and end apart: 63, of which 37 were waited for; matrix products, arithmetic and copies ran while one was open for 0% of the time, Pallas kernels for 9%

profile of v5, /device:TPU:0, one launch (start us, length us, event | category | flops | bytes accessed | tf_op | source)
XLA Modules:
  0.0 146.3 jit_solution(3891403174505821816)
XLA Ops:
  0.7 1.4 rows.1
  2.1 1.4 pack.1
  3.5 3.1 %collective-permute-start.4 = (bf16[160,768]{1,0:T(8,128)(2,1)S(1)}, bf16[160,768]{1,0:T(8,128)(2,1)S(1)}, u32[]{:S(2)}, u32[]{:S(2)}) collective-permute-start(bf16[160,768]{1,0:T(8,128)(2,1)S(1)} %get-tuple-element.178), channel_id=1, source_target_pairs={{0,8},{1,9},{2,10},{3,11},{4,12},{5,13},{6,14},{7,15},{8,0},{9,1},... | collective-permute-start | bytes 737288 | tf_op jit(solution)/shard_map/ppermute | solution.py:26
  6.6 2.6 %collective-permute-start = (bf16[64,768]{1,0:T(8,128)(2,1)S(1)}, bf16[64,768]{1,0:T(8,128)(2,1)S(1)}, u32[]{:S(2)}, u32[]{:S(2)}) collective-permute-start(bf16[64,768]{1,0:T(8,128)(2,1)S(1)} %get-tuple-element.159), channel_id=1, source_target_pairs={{0,16},{1,17},{2,18},{3,19},{4,20},{5,21},{6,22},{7,23},{8,24},{9,... | collective-permute-start | bytes 294920 | tf_op jit(solution)/shard_map/ppermute | solution.py:26
  9.2 1.9 %collective-permute-start.5 = (bf16[64,768]{1,0:T(8,128)(2,1)S(1)}, bf16[64,768]{1,0:T(8,128)(2,1)S(1)}, u32[]{:S(2)}, u32[]{:S(2)}) collective-permute-start(bf16[64,768]{1,0:T(8,128)(2,1)S(1)} %get-tuple-element.175), channel_id=1, source_target_pairs={{0,16},{1,17},{2,18},{3,19},{4,20},{5,21},{6,22},{7,23},{8,24},{9,... | collective-permute-start | bytes 294920 | tf_op jit(solution)/shard_map/ppermute | solution.py:26
  11.1 4.0 %collective-permute-done.got_ref.slot_ref = bf16[64,768]{1,0:T(8,128)(2,1)S(1)} collective-permute-done((bf16[64,768]{1,0:T(8,128)(2,1)S(1)}, bf16[64,768]{1,0:T(8,128)(2,1)S(1)}, u32[]{:S(2)}, u32[]{:S(2)}) %collective-permute-start) | collective-permute-done | bytes 98336 | tf_op jit(solution)/shard_map/ppermute | solution.py:26
  15.5 1.8 %collective-permute-start.7 = (bf16[2,64,768]{2,1,0:T(8,128)(2,1)S(1)}, bf16[2,64,768]{2,1,0:T(8,128)(2,1)S(1)}, u32[]{:S(2)}, u32[]{:S(2)}) collective-permute-start(bf16[2,64,768]{2,1,0:T(8,128)(2,1)S(1)} %pad_maximum_fusion.1.refs_0_), channel_id=1, source_target_pairs={{0,4},{1,5},{2,6},{3,7},{4,0},{5,1},{6,2},{7,3},{8,12},{9,13},{10,... | collective-permute-start | bytes 589832 | tf_op jit(solution)/shard_map/ppermute | solution.py:26
  17.2 4.0 %collective-permute-start.3 = (bf16[64,768]{1,0:T(8,128)(2,1)S(1)}, bf16[64,768]{1,0:T(8,128)(2,1)S(1)}, u32[]{:S(2)}, u32[]{:S(2)}) collective-permute-start(bf16[64,768]{1,0:T(8,128)(2,1)S(1)} %pad_maximum_fusion.3), channel_id=1, source_target_pairs={{0,9},{1,8},{2,11},{3,10},{4,13},{5,12},{6,15},{7,14},{8,1},{9,0},... | collective-permute-start | bytes 294920 | tf_op jit(solution)/shard_map/ppermute | solution.py:26
  22.7 1.5 collective-permute-start.8
  24.5 1.4 collective-permute-done.2.low_ref
  25.9 4.1 %collective-permute-done.8.refs_3_ = bf16[2,64,768]{2,1,0:T(8,128)(2,1)S(1)} collective-permute-done((bf16[2,64,768]{2,1,0:T(8,128)(2,1)S(1)}, bf16[2,64,768]{2,1,0:T(8,128)(2,1)S(1)}, u32[]{:S(2)}, u32[]{:S(2)}) %collective-permute-start.8) | collective-permute-done | bytes 196640 | tf_op jit(solution)/shard_map/ppermute | solution.py:26
  30.0 1.7 %collective-permute-start.25 = (bf16[2,96,768]{2,1,0:T(8,128)(2,1)S(1)}, bf16[2,96,768]{2,1,0:T(8,128)(2,1)S(1)}, u32[]{:S(2)}, u32[]{:S(2)}) collective-permute-start(bf16[2,96,768]{2,1,0:T(8,128)(2,1)S(1)} %pad_maximum_fusion.refs_0_), channel_id=1, source_target_pairs={{0,16},{1,17},{2,18},{3,19},{4,20},{5,21},{6,22},{7,23},{8,24},{9,... | collective-permute-start | bytes 884744 | tf_op jit(solution)/shard_map/ppermute | solution.py:26
  32.5 1.6 %collective-permute-start.13 = (bf16[256,256]{1,0:T(8,128)(2,1)S(1)}, bf16[256,256]{1,0:T(8,128)(2,1)S(1)}, u32[]{:S(2)}, u32[]{:S(2)}) collective-permute-start(bf16[256,256]{1,0:T(8,128)(2,1)S(1)} %get-tuple-element.245.refs_0_.pair_ref), channel_id=1, source_target_pairs={{0,4},{1,5},{2,6},{3,7},{4,0},{5,1},{6,2},{7,3},{8,12},{9,13},{10,... | collective-permute-start | bytes 393224 | tf_op jit(solution)/shard_map/ppermute | solution.py:26
  34.6 4.3 %collective-permute-done.13.refs_1_ = bf16[256,256]{1,0:T(8,128)(2,1)S(1)} collective-permute-done((bf16[256,256]{1,0:T(8,128)(2,1)S(1)}, bf16[256,256]{1,0:T(8,128)(2,1)S(1)}, u32[]{:S(2)}, u32[]{:S(2)}) %collective-permute-start.13) | collective-permute-done | bytes 131104 | tf_op jit(solution)/shard_map/ppermute | solution.py:26
  40.3 1.5 %collective-permute-start.26 = (bf16[2,96,768]{2,1,0:T(8,128)(2,1)S(1)}, bf16[2,96,768]{2,1,0:T(8,128)(2,1)S(1)}, u32[]{:S(2)}, u32[]{:S(2)}) collective-permute-start(bf16[2,96,768]{2,1,0:T(8,128)(2,1)S(1)} %pad_maximum_fusion.refs_0_), channel_id=1, source_target_pairs={{0,4},{1,5},{2,6},{3,7},{4,0},{5,1},{6,2},{7,3},{8,12},{9,13},{10,... | collective-permute-start | bytes 884744 | tf_op jit(solution)/shard_map/ppermute | solution.py:26
  41.8 2.8 %attend.1 = (bf16[256,192]{1,0:T(8,128)(2,1)S(1)}, f32[256,128]{1,0:T(8,128)S(1)}, f32[64,768]{1,0:T(8,128)S(1)}, bf16[64,768]{1,0:T(8,128)(2,1)S(1)}, bf16[64,7...) custom-call(s32[2]{0:T(128)S(1)} %copy-done, bf16[256,192]{1,0:T(8,128)(2,1)S(1)} %get-tuple-element.193.query_ref, ...), custom_call_target="tpu_custom_call" | custom-call | flops 30000000 | bytes 30000 | tf_op jit(solution)/shard_map/attend/pallas_call | solution.py:413
  44.7 2.0 %collective-permute-done.25.refs_1_ = bf16[2,96,768]{2,1,0:T(8,128)(2,1)S(1)} collective-permute-done((bf16[2,96,768]{2,1,0:T(8,128)(2,1)S(1)}, bf16[2,96,768]{2,1,0:T(8,128)(2,1)S(1)}, u32[]{:S(2)}, u32[]{:S(2)}) %collective-permute-start.25) | collective-permute-done | bytes 294944 | tf_op jit(solution)/shard_map/ppermute | solution.py:26
  46.7 1.2 collective-permute-start.27
  47.8 1.5 %collective-permute-start.20 = (bf16[64,768]{1,0:T(8,128)(2,1)S(1)}, bf16[64,768]{1,0:T(8,128)(2,1)S(1)}, u32[]{:S(2)}, u32[]{:S(2)}) collective-permute-start(bf16[64,768]{1,0:T(8,128)(2,1)S(1)} %get-tuple-element.198), channel_id=1, source_target_pairs={{0,1},{1,0},{2,3},{3,2},{4,5},{5,4},{6,7},{7,6},{8,9},{9,8},{10,11... | collective-permute-start | bytes 294920 | tf_op jit(solution)/shard_map/ppermute | solution.py:26
  49.3 2.0 %collective-permute-start.21 = (bf16[64,768]{1,0:T(8,128)(2,1)S(1)}, bf16[64,768]{1,0:T(8,128)(2,1)S(1)}, u32[]{:S(2)}, u32[]{:S(2)}) collective-permute-start(bf16[64,768]{1,0:T(8,128)(2,1)S(1)} %get-tuple-element.199), channel_id=1, source_target_pairs={{0,9},{1,8},{2,11},{3,10},{4,13},{5,12},{6,15},{7,14},{8,1},{9,0},... | collective-permute-start | bytes 294920 | tf_op jit(solution)/shard_map/ppermute | solution.py:26
  51.3 2.1 %collective-permute-done.19.got1_ref = bf16[64,768]{1,0:T(8,128)(2,1)S(1)} collective-permute-done((bf16[64,768]{1,0:T(8,128)(2,1)S(1)}, bf16[64,768]{1,0:T(8,128)(2,1)S(1)}, u32[]{:S(2)}, u32[]{:S(2)}) %collective-permute-start.19) | collective-permute-done | bytes 98336 | tf_op jit(solution)/shard_map/ppermute | solution.py:26
  53.4 2.1 %collective-permute-done.21.got3_ref = bf16[64,768]{1,0:T(8,128)(2,1)S(1)} collective-permute-done((bf16[64,768]{1,0:T(8,128)(2,1)S(1)}, bf16[64,768]{1,0:T(8,128)(2,1)S(1)}, u32[]{:S(2)}, u32[]{:S(2)}) %collective-permute-start.21) | collective-permute-done | bytes 98336 | tf_op jit(solution)/shard_map/ppermute | solution.py:26
  56.9 2.7 %collective-permute-start.24 = (bf16[64,768]{1,0:T(8,128)(2,1)S(1)}, bf16[64,768]{1,0:T(8,128)(2,1)S(1)}, u32[]{:S(2)}, u32[]{:S(2)}) collective-permute-start(bf16[64,768]{1,0:T(8,128)(2,1)S(1)} %get-tuple-element.201.own_ref), channel_id=1, source_target_pairs={{0,9},{1,8},{2,11},{3,10},{4,13},{5,12},{6,15},{7,14},{8,1},{9,0},... | collective-permute-start | bytes 294920 | tf_op jit(solution)/shard_map/ppermute | solution.py:26
  59.6 1.1 collective-permute-start.22
  60.9 2.4 %collective-permute-done.24.got3_ref = bf16[64,768]{1,0:T(8,128)(2,1)S(1)} collective-permute-done((bf16[64,768]{1,0:T(8,128)(2,1)S(1)}, bf16[64,768]{1,0:T(8,128)(2,1)S(1)}, u32[]{:S(2)}, u32[]{:S(2)}) %collective-permute-start.24) | collective-permute-done | bytes 98336 | tf_op jit(solution)/shard_map/ppermute | solution.py:26
  63.3 1.1 collective-permute-done.23.got2_ref
  64.8 1.6 %hidden.1 = (f32[64,768]{1,0:T(8,128)S(1)}, bf16[64,768]{1,0:T(8,128)(2,1)S(1)}, bf16[64,768]{1,0:T(8,128)(2,1)S(1)}, bf16[64,768]{1,0:T(8,128)(2,1)S(1)}, bf16[...) custom-call(bf16[64,768]{1,0:T(8,128)(2,1)S(1)} %get-tuple-element.201.own_ref, ...), custom_call_target="tpu_custom_call" | custom-call | flops 20000000 | bytes 20000 | tf_op jit(solution)/shard_map/hidden/pallas_call | solution.py:413
  66.4 1.8 %collective-permute-start.32 = (bf16[64,768]{1,0:T(8,128)(2,1)S(1)}, bf16[64,768]{1,0:T(8,128)(2,1)S(1)}, u32[]{:S(2)}, u32[]{:S(2)}) collective-permute-start(bf16[64,768]{1,0:T(8,128)(2,1)S(1)} %get-tuple-element.214), channel_id=1, source_target_pairs={{0,8},{1,9},{2,10},{3,11},{4,12},{5,13},{6,14},{7,15},{8,0},{9,1},... | collective-permute-start | bytes 294920 | tf_op jit(solution)/shard_map/ppermute | solution.py:26
  68.3 1.3 collective-permute-start.33
  70.0 1.2 collective-permute-done.32.got1_ref
  71.2 2.8 %collective-permute-done.33.got2_ref = bf16[64,768]{1,0:T(8,128)(2,1)S(1)} collective-permute-done((bf16[64,768]{1,0:T(8,128)(2,1)S(1)}, bf16[64,768]{1,0:T(8,128)(2,1)S(1)}, u32[]{:S(2)}, u32[]{:S(2)}) %collective-permute-start.33) | collective-permute-done | bytes 98336 | tf_op jit(solution)/shard_map/ppermute | solution.py:26
  74.0 1.2 collective-permute-done.34.got3_ref
  76.6 1.7 %collective-permute-start.36 = (bf16[64,768]{1,0:T(8,128)(2,1)S(1)}, bf16[64,768]{1,0:T(8,128)(2,1)S(1)}, u32[]{:S(2)}, u32[]{:S(2)}) collective-permute-start(bf16[64,768]{1,0:T(8,128)(2,1)S(1)} %get-tuple-element.219.own_ref), channel_id=1, source_target_pairs={{0,8},{1,9},{2,10},{3,11},{4,12},{5,13},{6,14},{7,15},{8,0},{9,1},... | collective-permute-start | bytes 294920 | tf_op jit(solution)/shard_map/ppermute | solution.py:26
  78.3 1.3 collective-permute-start.35
  79.6 2.0 %collective-permute-done.37.got3_ref = bf16[64,768]{1,0:T(8,128)(2,1)S(1)} collective-permute-done((bf16[64,768]{1,0:T(8,128)(2,1)S(1)}, bf16[64,768]{1,0:T(8,128)(2,1)S(1)}, u32[]{:S(2)}, u32[]{:S(2)}) %collective-permute-start.37) | collective-permute-done | bytes 98336 | tf_op jit(solution)/shard_map/ppermute | solution.py:26
  81.9 1.0 collective-permute-done.35.got1_ref
  82.9 0.9 hidden_back.1
  83.8 1.1 unit_weights.1
  85.5 1.5 %collective-permute-done.38.refs_1_ = bf16[8,48,768]{2,1,0:T(8,128)(2,1)S(1)} collective-permute-done((bf16[8,48,768]{2,1,0:T(8,128)(2,1)S(1)}, bf16[8,48,768]{2,1,0:T(8,128)(2,1)S(1)}, u32[]{:S(2)}, u32[]{:S(2)}) %collective-permute-start.38) | collective-permute-done | bytes 589856 | tf_op jit(solution)/shard_map/ppermute | solution.py:26
  88.1 1.0 collective-permute-start.46
  89.8 1.0 collective-permute-start.41
  90.8 1.8 %collective-permute-start.42 = (bf16[64,768]{1,0:T(8,128)(2,1)S(1)}, bf16[64,768]{1,0:T(8,128)(2,1)S(1)}, u32[]{:S(2)}, u32[]{:S(2)}) collective-permute-start(bf16[64,768]{1,0:T(8,128)(2,1)S(1)} %get-tuple-element.236), channel_id=1, source_target_pairs={{0,9},{1,8},{2,11},{3,10},{4,13},{5,12},{6,15},{7,14},{8,1},{9,0},... | collective-permute-start | bytes 294920 | tf_op jit(solution)/shard_map/ppermute | solution.py:26
  92.6 1.8 %collective-permute-done.40.got1_ref = bf16[64,768]{1,0:T(8,128)(2,1)S(1)} collective-permute-done((bf16[64,768]{1,0:T(8,128)(2,1)S(1)}, bf16[64,768]{1,0:T(8,128)(2,1)S(1)}, u32[]{:S(2)}, u32[]{:S(2)}) %collective-permute-start.40) | collective-permute-done | bytes 98336 | tf_op jit(solution)/shard_map/ppermute | solution.py:26
  95.1 1.4 collective-permute-done.42.got3_ref
  96.7 2.0 %collective-permute-start.45 = (bf16[64,768]{1,0:T(8,128)(2,1)S(1)}, bf16[64,768]{1,0:T(8,128)(2,1)S(1)}, u32[]{:S(2)}, u32[]{:S(2)}) collective-permute-start(bf16[64,768]{1,0:T(8,128)(2,1)S(1)} %get-tuple-element.240.own_ref), channel_id=1, source_target_pairs={{0,9},{1,8},{2,11},{3,10},{4,13},{5,12},{6,15},{7,14},{8,1},{9,0},... | collective-permute-start | bytes 294920 | tf_op jit(solution)/shard_map/ppermute | solution.py:26
  99.3 1.0 collective-permute-start.43
  100.3 2.2 %collective-permute-done.45.got3_ref = bf16[64,768]{1,0:T(8,128)(2,1)S(1)} collective-permute-done((bf16[64,768]{1,0:T(8,128)(2,1)S(1)}, bf16[64,768]{1,0:T(8,128)(2,1)S(1)}, u32[]{:S(2)}, u32[]{:S(2)}) %collective-permute-start.45) | collective-permute-done | bytes 98336 | tf_op jit(solution)/shard_map/ppermute | solution.py:26
  104.8 1.2 collective-permute-start.47
  106.1 1.6 %collective-permute-start.50 = (bf16[2,48,1536]{2,1,0:T(8,128)(2,1)S(1)}, bf16[2,48,1536]{2,1,0:T(8,128)(2,1)S(1)}, u32[]{:S(2)}, u32[]{:S(2)}) collective-permute-start(bf16[2,48,1536]{2,1,0:T(8,128)(2,1)S(1)} %get-tuple-element.252), channel_id=1, source_target_pairs={{0,16},{1,17},{2,18},{3,19},{4,20},{5,21},{6,22},{7,23},{8,24},{9,... | collective-permute-start | bytes 884744 | tf_op jit(solution)/shard_map/ppermute | solution.py:26
  107.7 2.6 %query_back.1 = (bf16[256,192]{1,0:T(8,128)(2,1)S(1)}, f32[1,192]{1,0:T(1,128)S(1)}) custom-call(s32[2]{0:T(128)S(1)} %copy-done, bf16[256,512]{1,0:T(8,128)(2,1)S(1)} %get-tuple-element.242.packet_ref.g0_ref, bf16[256,256]{1,0:T(8,128)(2,1)S(1)} %get-tuple-element.245.refs_0_.pair_ref, bf16[256,256]{1,0:T(8,128)(2,1)S(1)} %collective-permute-done.13.refs_1_, ...), custom_call_target="tpu_custom_call" | custom-call | flops 30000000 | bytes 30000 | tf_op jit(solution)/shard_map/query_back/pallas_call | solution.py:413
  110.2 1.0 collective-permute-done.47.g1_ref
  111.3 1.6 %collective-permute-start.51 = (f32[16,768]{1,0:T(8,128)S(1)}, f32[16,768]{1,0:T(8,128)S(1)}, u32[]{:S(2)}, u32[]{:S(2)}) collective-permute-start(f32[16,768]{1,0:T(8,128)S(1)} %vectors.1.refs_4_), channel_id=1, source_target_pairs={{0,1},{1,0},{2,3},{3,2},{4,5},{5,4},{6,7},{7,6},{8,9},{9,8},{10,11... | collective-permute-start | bytes 147464 | tf_op jit(solution)/shard_map/ppermute | solution.py:26
  112.9 3.0 %pair_back.1 = (f32[64,768]{1,0:T(8,128)S(1)}, bf16[64,768]{1,0:T(8,128)(2,1)S(1)}, bf16[64,768]{1,0:T(8,128)(2,1)S(1)}, bf16[64,768]{1,0:T(8,128)(2,1)S(1)}, bf16[256,576]{1,0:T(8,128)(2,1)S(1)}) custom-call(s32[2]{0:T(128)S(1)} %copy-done, bf16[256,256]{1,0:T(8,128)(2,1)S(1)} %get-tuple-element.245.refs_0_.pair_ref, ...), custom_call_target="tpu_custom_call" | custom-call | flops 40000000 | bytes 40000 | tf_op jit(solution)/shard_map/pair_back/pallas_call | solution.py:413
  115.9 3.8 %collective-permute-done.50.refs_1_ = bf16[2,48,1536]{2,1,0:T(8,128)(2,1)S(1)} collective-permute-done((bf16[2,48,1536]{2,1,0:T(8,128)(2,1)S(1)}, bf16[2,48,1536]{2,1,0:T(8,128)(2,1)S(1)}, u32[]{:S(2)}, u32[]{:S(2)}) %collective-permute-start.50) | collective-permute-done | bytes 294944 | tf_op jit(solution)/shard_map/ppermute | solution.py:26
  119.7 1.1 head_weights.1
  121.4 1.8 %collective-permute-done.52.refs_1_ = bf16[8,48,192]{2,1,0:T(8,128)(2,1)S(1)} collective-permute-done((bf16[8,48,192]{2,1,0:T(8,128)(2,1)S(1)}, bf16[8,48,192]{2,1,0:T(8,128)(2,1)S(1)}, u32[]{:S(2)}, u32[]{:S(2)}) %collective-permute-start.52) | collective-permute-done | bytes 147488 | tf_op jit(solution)/shard_map/ppermute | solution.py:26
  124.3 1.0 collective-permute-start.55
  125.3 2.5 %collective-permute-start.56 = (bf16[64,768]{1,0:T(8,128)(2,1)S(1)}, bf16[64,768]{1,0:T(8,128)(2,1)S(1)}, u32[]{:S(2)}, u32[]{:S(2)}) collective-permute-start(bf16[64,768]{1,0:T(8,128)(2,1)S(1)} %get-tuple-element.266), channel_id=1, source_target_pairs={{0,9},{1,8},{2,11},{3,10},{4,13},{5,12},{6,15},{7,14},{8,1},{9,0},... | collective-permute-start | bytes 294920 | tf_op jit(solution)/shard_map/ppermute | solution.py:26
  128.0 2.0 %collective-permute-done.54.got1_ref = bf16[64,768]{1,0:T(8,128)(2,1)S(1)} collective-permute-done((bf16[64,768]{1,0:T(8,128)(2,1)S(1)}, bf16[64,768]{1,0:T(8,128)(2,1)S(1)}, u32[]{:S(2)}, u32[]{:S(2)}) %collective-permute-start.54) | collective-permute-done | bytes 98336 | tf_op jit(solution)/shard_map/ppermute | solution.py:26
  129.9 2.5 %collective-permute-done.56.got3_ref = bf16[64,768]{1,0:T(8,128)(2,1)S(1)} collective-permute-done((bf16[64,768]{1,0:T(8,128)(2,1)S(1)}, bf16[64,768]{1,0:T(8,128)(2,1)S(1)}, u32[]{:S(2)}, u32[]{:S(2)}) %collective-permute-start.56) | collective-permute-done | bytes 98336 | tf_op jit(solution)/shard_map/ppermute | solution.py:26
  132.5 1.6 %collective-permute-start.57 = (bf16[32,1536]{1,0:T(8,128)(2,1)S(1)}, bf16[32,1536]{1,0:T(8,128)(2,1)S(1)}, u32[]{:S(2)}, u32[]{:S(2)}) collective-permute-start(bf16[32,1536]{1,0:T(8,128)(2,1)S(1)} %get-tuple-element.270), channel_id=1, source_target_pairs={{0,16},{1,17},{2,18},{3,19},{4,20},{5,21},{6,22},{7,23},{8,24},{9,... | collective-permute-start | bytes 294920 | tf_op jit(solution)/shard_map/ppermute | solution.py:26
  134.9 2.2 %collective-permute-start.60 = (bf16[48,896]{1,0:T(8,128)(2,1)S(1)}, bf16[48,896]{1,0:T(8,128)(2,1)S(1)}, u32[]{:S(2)}, u32[]{:S(2)}) collective-permute-start(bf16[48,896]{1,0:T(8,128)(2,1)S(1)} %get-tuple-element.276), channel_id=1, source_target_pairs={{0,16},{1,17},{2,18},{3,19},{4,20},{5,21},{6,22},{7,23},{8,24},{9,... | collective-permute-start | bytes 258056 | tf_op jit(solution)/shard_map/ppermute | solution.py:26
  137.1 1.6 %collective-permute-start.61 = (bf16[48,896]{1,0:T(8,128)(2,1)S(1)}, bf16[48,896]{1,0:T(8,128)(2,1)S(1)}, u32[]{:S(2)}, u32[]{:S(2)}) collective-permute-start(bf16[48,896]{1,0:T(8,128)(2,1)S(1)} %get-tuple-element.277), channel_id=1, source_target_pairs={{0,24},{1,25},{2,26},{3,27},{4,28},{5,29},{6,30},{7,31},{8,16},{9,... | collective-permute-start | bytes 258056 | tf_op jit(solution)/shard_map/ppermute | solution.py:26
  139.5 4.4 %collective-permute-done.57.got_ref = bf16[32,1536]{1,0:T(8,128)(2,1)S(1)} collective-permute-done((bf16[32,1536]{1,0:T(8,128)(2,1)S(1)}, bf16[32,1536]{1,0:T(8,128)(2,1)S(1)}, u32[]{:S(2)}, u32[]{:S(2)}) %collective-permute-start.57) | collective-permute-done | bytes 98336 | tf_op jit(solution)/shard_map/ppermute | solution.py:26
  (97 shorter events, 21.0 us)
Async XLA Ops:
  3.5 11.9 %collective-permute-start.4 = (bf16[160,768]{1,0:T(8,128)(2,1)S(1)}, bf16[160,768]{1,0:T(8,128)(2,1)S(1)}, u32[]{:S(2)}, u32[]{:S(2)}) collective-permute-start(bf16[160,768]{1,0:T(8,128)(2,1)S(1)} %get-tuple-element.178), channel_id=1, source_target_pairs={{0,8},{1,9},{2,10},{3,11},{4,12},{5,13},{6,14},{7,15},{8,0},{9,1},... | collective-permute-start | bytes 737288 | tf_op jit(solution)/shard_map/ppermute | solution.py:26
  6.6 8.5 %collective-permute-start = (bf16[64,768]{1,0:T(8,128)(2,1)S(1)}, bf16[64,768]{1,0:T(8,128)(2,1)S(1)}, u32[]{:S(2)}, u32[]{:S(2)}) collective-permute-start(bf16[64,768]{1,0:T(8,128)(2,1)S(1)} %get-tuple-element.159), channel_id=1, source_target_pairs={{0,16},{1,17},{2,18},{3,19},{4,20},{5,21},{6,22},{7,23},{8,24},{9,... | collective-permute-start | bytes 294920 | tf_op jit(solution)/shard_map/ppermute | solution.py:26
  9.1 12.1 %collective-permute-start.6 = (bf16[64,768]{1,0:T(8,128)(2,1)S(1)}, bf16[64,768]{1,0:T(8,128)(2,1)S(1)}, u32[]{:S(2)}, u32[]{:S(2)}) collective-permute-start(bf16[64,768]{1,0:T(8,128)(2,1)S(1)} %get-tuple-element.176), channel_id=1, source_target_pairs={{0,24},{1,25},{2,26},{3,27},{4,28},{5,29},{6,30},{7,31},{8,16},{9,... | collective-permute-start | bytes 294920 | tf_op jit(solution)/shard_map/ppermute | solution.py:26
  9.2 13.4 %collective-permute-start.5 = (bf16[64,768]{1,0:T(8,128)(2,1)S(1)}, bf16[64,768]{1,0:T(8,128)(2,1)S(1)}, u32[]{:S(2)}, u32[]{:S(2)}) collective-permute-start(bf16[64,768]{1,0:T(8,128)(2,1)S(1)} %get-tuple-element.175), channel_id=1, source_target_pairs={{0,16},{1,17},{2,18},{3,19},{4,20},{5,21},{6,22},{7,23},{8,24},{9,... | collective-permute-start | bytes 294920 | tf_op jit(solution)/shard_map/ppermute | solution.py:26
  15.5 7.2 %collective-permute-start.7 = (bf16[2,64,768]{2,1,0:T(8,128)(2,1)S(1)}, bf16[2,64,768]{2,1,0:T(8,128)(2,1)S(1)}, u32[]{:S(2)}, u32[]{:S(2)}) collective-permute-start(bf16[2,64,768]{2,1,0:T(8,128)(2,1)S(1)} %pad_maximum_fusion.1.refs_0_), channel_id=1, source_target_pairs={{0,4},{1,5},{2,6},{3,7},{4,0},{5,1},{6,2},{7,3},{8,12},{9,13},{10,... | collective-permute-start | bytes 589832 | tf_op jit(solution)/shard_map/ppermute | solution.py:26
  17.2 7.3 %collective-permute-start.3 = (bf16[64,768]{1,0:T(8,128)(2,1)S(1)}, bf16[64,768]{1,0:T(8,128)(2,1)S(1)}, u32[]{:S(2)}, u32[]{:S(2)}) collective-permute-start(bf16[64,768]{1,0:T(8,128)(2,1)S(1)} %pad_maximum_fusion.3), channel_id=1, source_target_pairs={{0,9},{1,8},{2,11},{3,10},{4,13},{5,12},{6,15},{7,14},{8,1},{9,0},... | collective-permute-start | bytes 294920 | tf_op jit(solution)/shard_map/ppermute | solution.py:26
  21.3 4.6 %collective-permute-start.2 = (bf16[64,768]{1,0:T(8,128)(2,1)S(1)}, bf16[64,768]{1,0:T(8,128)(2,1)S(1)}, u32[]{:S(2)}, u32[]{:S(2)}) collective-permute-start(bf16[64,768]{1,0:T(8,128)(2,1)S(1)} %pad_maximum_fusion.3), channel_id=1, source_target_pairs={{0,8},{1,9},{2,10},{3,11},{4,12},{5,13},{6,14},{7,15},{8,0},{9,1},... | collective-permute-start | bytes 294920 | tf_op jit(solution)/shard_map/ppermute | solution.py:26
  21.3 4.6 %collective-permute-start.1 = (bf16[64,768]{1,0:T(8,128)(2,1)S(1)}, bf16[64,768]{1,0:T(8,128)(2,1)S(1)}, u32[]{:S(2)}, u32[]{:S(2)}) collective-permute-start(bf16[64,768]{1,0:T(8,128)(2,1)S(1)} %pad_maximum_fusion.3), channel_id=1, source_target_pairs={{0,1},{1,0},{2,3},{3,2},{4,5},{5,4},{6,7},{7,6},{8,9},{9,8},{10,11... | collective-permute-start | bytes 294920 | tf_op jit(solution)/shard_map/ppermute | solution.py:26
  22.6 9.2 %collective-permute-start.9 = (bf16[2,64,768]{2,1,0:T(8,128)(2,1)S(1)}, bf16[2,64,768]{2,1,0:T(8,128)(2,1)S(1)}, u32[]{:S(2)}, u32[]{:S(2)}) collective-permute-start(bf16[2,64,768]{2,1,0:T(8,128)(2,1)S(1)} %pad_maximum_fusion.1.refs_0_), channel_id=1, source_target_pairs={{0,2},{1,3},{2,0},{3,1},{4,6},{5,7},{6,4},{7,5},{8,10},{9,11},{10,... | collective-permute-start | bytes 589832 | tf_op jit(solution)/shard_map/ppermute | solution.py:26
  22.7 7.3 %collective-permute-start.8 = (bf16[2,64,768]{2,1,0:T(8,128)(2,1)S(1)}, bf16[2,64,768]{2,1,0:T(8,128)(2,1)S(1)}, u32[]{:S(2)}, u32[]{:S(2)}) collective-permute-start(bf16[2,64,768]{2,1,0:T(8,128)(2,1)S(1)} %pad_maximum_fusion.2.refs_1_), channel_id=1, source_target_pairs={{0,4},{1,5},{2,6},{3,7},{4,0},{5,1},{6,2},{7,3},{8,12},{9,13},{10,... | collective-permute-start | bytes 589832 | tf_op jit(solution)/shard_map/ppermute | solution.py:26
  24.5 7.3 %collective-permute-start.10 = (bf16[2,64,768]{2,1,0:T(8,128)(2,1)S(1)}, bf16[2,64,768]{2,1,0:T(8,128)(2,1)S(1)}, u32[]{:S(2)}, u32[]{:S(2)}) collective-permute-start(bf16[2,64,768]{2,1,0:T(8,128)(2,1)S(1)} %pad_maximum_fusion.2.refs_1_), channel_id=1, source_target_pairs={{0,2},{1,3},{2,0},{3,1},{4,6},{5,7},{6,4},{7,5},{8,10},{9,11},{10,... | collective-permute-start | bytes 589832 | tf_op jit(solution)/shard_map/ppermute | solution.py:26
  25.9 5.9 %collective-permute-start.11 = (bf16[2,64,768]{2,1,0:T(8,128)(2,1)S(1)}, bf16[2,64,768]{2,1,0:T(8,128)(2,1)S(1)}, u32[]{:S(2)}, u32[]{:S(2)}) collective-permute-start(bf16[2,64,768]{2,1,0:T(8,128)(2,1)S(1)} %collective-permute-done.7.refs_2_), channel_id=1, source_target_pairs={{0,2},{1,3},{2,0},{3,1},{4,6},{5,7},{6,4},{7,5},{8,10},{9,11},{10,... | collective-permute-start | bytes 589832 | tf_op jit(solution)/shard_map/ppermute | solution.py:26
  30.0 1.8 %collective-permute-start.12 = (bf16[2,64,768]{2,1,0:T(8,128)(2,1)S(1)}, bf16[2,64,768]{2,1,0:T(8,128)(2,1)S(1)}, u32[]{:S(2)}, u32[]{:S(2)}) collective-permute-start(bf16[2,64,768]{2,1,0:T(8,128)(2,1)S(1)} %collective-permute-done.8.refs_3_), channel_id=1, source_target_pairs={{0,2},{1,3},{2,0},{3,1},{4,6},{5,7},{6,4},{7,5},{8,10},{9,11},{10,... | collective-permute-start | bytes 589832 | tf_op jit(solution)/shard_map/ppermute | solution.py:26
  30.0 16.6 %collective-permute-start.25 = (bf16[2,96,768]{2,1,0:T(8,128)(2,1)S(1)}, bf16[2,96,768]{2,1,0:T(8,128)(2,1)S(1)}, u32[]{:S(2)}, u32[]{:S(2)}) collective-permute-start(bf16[2,96,768]{2,1,0:T(8,128)(2,1)S(1)} %pad_maximum_fusion.refs_0_), channel_id=1, source_target_pairs={{0,16},{1,17},{2,18},{3,19},{4,20},{5,21},{6,22},{7,23},{8,24},{9,... | collective-permute-start | bytes 884744 | tf_op jit(solution)/shard_map/ppermute | solution.py:26
  32.5 9.4 %copy-start = (s32[2]{0:T(128)S(1)}, s32[2]{0:T(128)}, u32[]{:S(2)}) copy-start(s32[2]{0:T(128)} %lengths_ref.7) | copy-start | bytes 28
  32.5 6.4 %collective-permute-start.13 = (bf16[256,256]{1,0:T(8,128)(2,1)S(1)}, bf16[256,256]{1,0:T(8,128)(2,1)S(1)}, u32[]{:S(2)}, u32[]{:S(2)}) collective-permute-start(bf16[256,256]{1,0:T(8,128)(2,1)S(1)} %get-tuple-element.245.refs_0_.pair_ref), channel_id=1, source_target_pairs={{0,4},{1,5},{2,6},{3,7},{4,0},{5,1},{6,2},{7,3},{8,12},{9,13},{10,... | collective-permute-start | bytes 393224 | tf_op jit(solution)/shard_map/ppermute | solution.py:26
  34.0 7.8 %collective-permute-start.14 = (bf16[256,256]{1,0:T(8,128)(2,1)S(1)}, bf16[256,256]{1,0:T(8,128)(2,1)S(1)}, u32[]{:S(2)}, u32[]{:S(2)}) collective-permute-start(bf16[256,256]{1,0:T(8,128)(2,1)S(1)} %get-tuple-element.245.refs_0_.pair_ref), channel_id=1, source_target_pairs={{0,2},{1,3},{2,0},{3,1},{4,6},{5,7},{6,4},{7,5},{8,10},{9,11},{10,... | collective-permute-start | bytes 393224 | tf_op jit(solution)/shard_map/ppermute | solution.py:26
  34.1 5.5 %collective-permute-start.16 = (bf16[256,128]{1,0:T(8,128)(2,1)S(1)}, bf16[256,128]{1,0:T(8,128)(2,1)S(1)}, u32[]{:S(2)}, u32[]{:S(2)}) collective-permute-start(bf16[256,128]{1,0:T(8,128)(2,1)S(1)} %get-tuple-element.194.refs_4_.rest_ref), channel_id=1, source_target_pairs={{0,4},{1,5},{2,6},{3,7},{4,0},{5,1},{6,2},{7,3},{8,12},{9,13},{10,... | collective-permute-start | bytes 196616 | tf_op jit(solution)/shard_map/ppermute | solution.py:26
  38.9 2.9 %collective-permute-start.15 = (bf16[256,256]{1,0:T(8,128)(2,1)S(1)}, bf16[256,256]{1,0:T(8,128)(2,1)S(1)}, u32[]{:S(2)}, u32[]{:S(2)}) collective-permute-start(bf16[256,256]{1,0:T(8,128)(2,1)S(1)} %collective-permute-done.13.refs_1_), channel_id=1, source_target_pairs={{0,2},{1,3},{2,0},{3,1},{4,6},{5,7},{6,4},{7,5},{8,10},{9,11},{10,... | collective-permute-start | bytes 393224 | tf_op jit(solution)/shard_map/ppermute | solution.py:26
  38.9 1.4 collective-permute-start.17
  39.6 2.2 %collective-permute-start.18 = (bf16[256,128]{1,0:T(8,128)(2,1)S(1)}, bf16[256,128]{1,0:T(8,128)(2,1)S(1)}, u32[]{:S(2)}, u32[]{:S(2)}) collective-permute-start(bf16[256,128]{1,0:T(8,128)(2,1)S(1)} %collective-permute-done.16.refs_5_), channel_id=1, source_target_pairs={{0,2},{1,3},{2,0},{3,1},{4,6},{5,7},{6,4},{7,5},{8,10},{9,11},{10,... | collective-permute-start | bytes 196616 | tf_op jit(solution)/shard_map/ppermute | solution.py:26
  40.3 15.4 %collective-permute-start.26 = (bf16[2,96,768]{2,1,0:T(8,128)(2,1)S(1)}, bf16[2,96,768]{2,1,0:T(8,128)(2,1)S(1)}, u32[]{:S(2)}, u32[]{:S(2)}) collective-permute-start(bf16[2,96,768]{2,1,0:T(8,128)(2,1)S(1)} %pad_maximum_fusion.refs_0_), channel_id=1, source_target_pairs={{0,4},{1,5},{2,6},{3,7},{4,0},{5,1},{6,2},{7,3},{8,12},{9,13},{10,... | collective-permute-start | bytes 884744 | tf_op jit(solution)/shard_map/ppermute | solution.py:26
  46.7 9.2 %collective-permute-start.27 = (bf16[2,96,768]{2,1,0:T(8,128)(2,1)S(1)}, bf16[2,96,768]{2,1,0:T(8,128)(2,1)S(1)}, u32[]{:S(2)}, u32[]{:S(2)}) collective-permute-start(bf16[2,96,768]{2,1,0:T(8,128)(2,1)S(1)} %collective-permute-done.25.refs_1_), channel_id=1, source_target_pairs={{0,4},{1,5},{2,6},{3,7},{4,0},{5,1},{6,2},{7,3},{8,12},{9,13},{10,... | collective-permute-start | bytes 884744 | tf_op jit(solution)/shard_map/ppermute | solution.py:26
  47.8 5.6 %collective-permute-start.19 = (bf16[64,768]{1,0:T(8,128)(2,1)S(1)}, bf16[64,768]{1,0:T(8,128)(2,1)S(1)}, u32[]{:S(2)}, u32[]{:S(2)}) collective-permute-start(bf16[64,768]{1,0:T(8,128)(2,1)S(1)} %get-tuple-element.197), channel_id=1, source_target_pairs={{0,8},{1,9},{2,10},{3,11},{4,12},{5,13},{6,14},{7,15},{8,0},{9,1},... | collective-permute-start | bytes 294920 | tf_op jit(solution)/shard_map/ppermute | solution.py:26
  47.8 5.6 %collective-permute-start.20 = (bf16[64,768]{1,0:T(8,128)(2,1)S(1)}, bf16[64,768]{1,0:T(8,128)(2,1)S(1)}, u32[]{:S(2)}, u32[]{:S(2)}) collective-permute-start(bf16[64,768]{1,0:T(8,128)(2,1)S(1)} %get-tuple-element.198), channel_id=1, source_target_pairs={{0,1},{1,0},{2,3},{3,2},{4,5},{5,4},{6,7},{7,6},{8,9},{9,8},{10,11... | collective-permute-start | bytes 294920 | tf_op jit(solution)/shard_map/ppermute | solution.py:26
  49.3 6.2 %collective-permute-start.21 = (bf16[64,768]{1,0:T(8,128)(2,1)S(1)}, bf16[64,768]{1,0:T(8,128)(2,1)S(1)}, u32[]{:S(2)}, u32[]{:S(2)}) collective-permute-start(bf16[64,768]{1,0:T(8,128)(2,1)S(1)} %get-tuple-element.199), channel_id=1, source_target_pairs={{0,9},{1,8},{2,11},{3,10},{4,13},{5,12},{6,15},{7,14},{8,1},{9,0},... | collective-permute-start | bytes 294920 | tf_op jit(solution)/shard_map/ppermute | solution.py:26
  55.9 3.7 %collective-permute-start.28 = (bf16[2,96,768]{2,1,0:T(8,128)(2,1)S(1)}, bf16[2,96,768]{2,1,0:T(8,128)(2,1)S(1)}, u32[]{:S(2)}, u32[]{:S(2)}) collective-permute-start(bf16[2,96,768]{2,1,0:T(8,128)(2,1)S(1)} %pad_maximum_fusion.refs_0_), channel_id=1, source_target_pairs={{0,2},{1,3},{2,0},{3,1},{4,6},{5,7},{6,4},{7,5},{8,10},{9,11},{10,... | collective-permute-start | bytes 884744 | tf_op jit(solution)/shard_map/ppermute | solution.py:26
  55.9 3.7 %collective-permute-start.29 = (bf16[2,96,768]{2,1,0:T(8,128)(2,1)S(1)}, bf16[2,96,768]{2,1,0:T(8,128)(2,1)S(1)}, u32[]{:S(2)}, u32[]{:S(2)}) collective-permute-start(bf16[2,96,768]{2,1,0:T(8,128)(2,1)S(1)} %collective-permute-done.25.refs_1_), channel_id=1, source_target_pairs={{0,2},{1,3},{2,0},{3,1},{4,6},{5,7},{6,4},{7,5},{8,10},{9,11},{10,... | collective-permute-start | bytes 884744 | tf_op jit(solution)/shard_map/ppermute | solution.py:26
  56.4 4.3 %collective-permute-start.30 = (bf16[2,96,768]{2,1,0:T(8,128)(2,1)S(1)}, bf16[2,96,768]{2,1,0:T(8,128)(2,1)S(1)}, u32[]{:S(2)}, u32[]{:S(2)}) collective-permute-start(bf16[2,96,768]{2,1,0:T(8,128)(2,1)S(1)} %collective-permute-done.26.refs_2_), channel_id=1, source_target_pairs={{0,2},{1,3},{2,0},{3,1},{4,6},{5,7},{6,4},{7,5},{8,10},{9,11},{10,... | collective-permute-start | bytes 884744 | tf_op jit(solution)/shard_map/ppermute | solution.py:26
  56.4 4.3 %collective-permute-start.31 = (bf16[2,96,768]{2,1,0:T(8,128)(2,1)S(1)}, bf16[2,96,768]{2,1,0:T(8,128)(2,1)S(1)}, u32[]{:S(2)}, u32[]{:S(2)}) collective-permute-start(bf16[2,96,768]{2,1,0:T(8,128)(2,1)S(1)} %collective-permute-done.27.refs_3_), channel_id=1, source_target_pairs={{0,2},{1,3},{2,0},{3,1},{4,6},{5,7},{6,4},{7,5},{8,10},{9,11},{10,... | collective-permute-start | bytes 884744 | tf_op jit(solution)/shard_map/ppermute | solution.py:26
  56.9 6.4 %collective-permute-start.24 = (bf16[64,768]{1,0:T(8,128)(2,1)S(1)}, bf16[64,768]{1,0:T(8,128)(2,1)S(1)}, u32[]{:S(2)}, u32[]{:S(2)}) collective-permute-start(bf16[64,768]{1,0:T(8,128)(2,1)S(1)} %get-tuple-element.201.own_ref), channel_id=1, source_target_pairs={{0,9},{1,8},{2,11},{3,10},{4,13},{5,12},{6,15},{7,14},{8,1},{9,0},... | collective-permute-start | bytes 294920 | tf_op jit(solution)/shard_map/ppermute | solution.py:26
  59.6 4.8 %collective-permute-start.23 = (bf16[64,768]{1,0:T(8,128)(2,1)S(1)}, bf16[64,768]{1,0:T(8,128)(2,1)S(1)}, u32[]{:S(2)}, u32[]{:S(2)}) collective-permute-start(bf16[64,768]{1,0:T(8,128)(2,1)S(1)} %get-tuple-element.201.own_ref), channel_id=1, source_target_pairs={{0,8},{1,9},{2,10},{3,11},{4,12},{5,13},{6,14},{7,15},{8,0},{9,1},... | collective-permute-start | bytes 294920 | tf_op jit(solution)/shard_map/ppermute | solution.py:26
  59.6 5.2 %collective-permute-start.22 = (bf16[64,768]{1,0:T(8,128)(2,1)S(1)}, bf16[64,768]{1,0:T(8,128)(2,1)S(1)}, u32[]{:S(2)}, u32[]{:S(2)}) collective-permute-start(bf16[64,768]{1,0:T(8,128)(2,1)S(1)} %get-tuple-element.201.own_ref), channel_id=1, source_target_pairs={{0,1},{1,0},{2,3},{3,2},{4,5},{5,4},{6,7},{7,6},{8,9},{9,8},{10,11... | collective-permute-start | bytes 294920 | tf_op jit(solution)/shard_map/ppermute | solution.py:26
  66.4 4.7 %collective-permute-start.32 = (bf16[64,768]{1,0:T(8,128)(2,1)S(1)}, bf16[64,768]{1,0:T(8,128)(2,1)S(1)}, u32[]{:S(2)}, u32[]{:S(2)}) collective-permute-start(bf16[64,768]{1,0:T(8,128)(2,1)S(1)} %get-tuple-element.214), channel_id=1, source_target_pairs={{0,8},{1,9},{2,10},{3,11},{4,12},{5,13},{6,14},{7,15},{8,0},{9,1},... | collective-permute-start | bytes 294920 | tf_op jit(solution)/shard_map/ppermute | solution.py:26
  68.3 5.7 %collective-permute-start.33 = (bf16[64,768]{1,0:T(8,128)(2,1)S(1)}, bf16[64,768]{1,0:T(8,128)(2,1)S(1)}, u32[]{:S(2)}, u32[]{:S(2)}) collective-permute-start(bf16[64,768]{1,0:T(8,128)(2,1)S(1)} %get-tuple-element.215), channel_id=1, source_target_pairs={{0,1},{1,0},{2,3},{3,2},{4,5},{5,4},{6,7},{7,6},{8,9},{9,8},{10,11... | collective-permute-start | bytes 294920 | tf_op jit(solution)/shard_map/ppermute | solution.py:26
  69.6 5.5 %collective-permute-start.34 = (bf16[64,768]{1,0:T(8,128)(2,1)S(1)}, bf16[64,768]{1,0:T(8,128)(2,1)S(1)}, u32[]{:S(2)}, u32[]{:S(2)}) collective-permute-start(bf16[64,768]{1,0:T(8,128)(2,1)S(1)} %get-tuple-element.216), channel_id=1, source_target_pairs={{0,9},{1,8},{2,11},{3,10},{4,13},{5,12},{6,15},{7,14},{8,1},{9,0},... | collective-permute-start | bytes 294920 | tf_op jit(solution)/shard_map/ppermute | solution.py:26
  76.0 5.6 %collective-permute-start.37 = (bf16[64,768]{1,0:T(8,128)(2,1)S(1)}, bf16[64,768]{1,0:T(8,128)(2,1)S(1)}, u32[]{:S(2)}, u32[]{:S(2)}) collective-permute-start(bf16[64,768]{1,0:T(8,128)(2,1)S(1)} %get-tuple-element.219.own_ref), channel_id=1, source_target_pairs={{0,9},{1,8},{2,11},{3,10},{4,13},{5,12},{6,15},{7,14},{8,1},{9,0},... | collective-permute-start | bytes 294920 | tf_op jit(solution)/shard_map/ppermute | solution.py:26
  76.6 5.4 %collective-permute-start.36 = (bf16[64,768]{1,0:T(8,128)(2,1)S(1)}, bf16[64,768]{1,0:T(8,128)(2,1)S(1)}, u32[]{:S(2)}, u32[]{:S(2)}) collective-permute-start(bf16[64,768]{1,0:T(8,128)(2,1)S(1)} %get-tuple-element.219.own_ref), channel_id=1, source_target_pairs={{0,8},{1,9},{2,10},{3,11},{4,12},{5,13},{6,14},{7,15},{8,0},{9,1},... | collective-permute-start | bytes 294920 | tf_op jit(solution)/shard_map/ppermute | solution.py:26
  78.3 4.6 %collective-permute-start.35 = (bf16[64,768]{1,0:T(8,128)(2,1)S(1)}, bf16[64,768]{1,0:T(8,128)(2,1)S(1)}, u32[]{:S(2)}, u32[]{:S(2)}) collective-permute-start(bf16[64,768]{1,0:T(8,128)(2,1)S(1)} %get-tuple-element.219.own_ref), channel_id=1, source_target_pairs={{0,1},{1,0},{2,3},{3,2},{4,5},{5,4},{6,7},{7,6},{8,9},{9,8},{10,11... | collective-permute-start | bytes 294920 | tf_op jit(solution)/shard_map/ppermute | solution.py:26
  84.9 2.1 %collective-permute-start.38 = (bf16[8,48,768]{2,1,0:T(8,128)(2,1)S(1)}, bf16[8,48,768]{2,1,0:T(8,128)(2,1)S(1)}, u32[]{:S(2)}, u32[]{:S(2)}) collective-permute-start(bf16[8,48,768]{2,1,0:T(8,128)(2,1)S(1)} %get-tuple-element.226), channel_id=1, source_target_pairs={{0,2},{1,3},{2,0},{3,1},{4,6},{5,7},{6,4},{7,5},{8,10},{9,11},{10,... | collective-permute-start | bytes 1769480 | tf_op jit(solution)/shard_map/ppermute | solution.py:26
  85.0 2.8 %collective-permute-start.39 = (bf16[8,48,768]{2,1,0:T(8,128)(2,1)S(1)}, bf16[8,48,768]{2,1,0:T(8,128)(2,1)S(1)}, u32[]{:S(2)}, u32[]{:S(2)}) collective-permute-start(bf16[8,48,768]{2,1,0:T(8,128)(2,1)S(1)} %get-tuple-element.227), channel_id=1, source_target_pairs={{0,2},{1,3},{2,0},{3,1},{4,6},{5,7},{6,4},{7,5},{8,10},{9,11},{10,... | collective-permute-start | bytes 1769480 | tf_op jit(solution)/shard_map/ppermute | solution.py:26
  88.1 17.9 %collective-permute-start.46 = (bf16[4,48,1536]{2,1,0:T(8,128)(2,1)S(1)}, bf16[4,48,1536]{2,1,0:T(8,128)(2,1)S(1)}, u32[]{:S(2)}, u32[]{:S(2)}) collective-permute-start(bf16[4,48,1536]{2,1,0:T(8,128)(2,1)S(1)} %get-tuple-element.233), channel_id=1, source_target_pairs={{0,4},{1,5},{2,6},{3,7},{4,0},{5,1},{6,2},{7,3},{8,12},{9,13},{10,... | collective-permute-start | bytes 1769480 | tf_op jit(solution)/shard_map/ppermute | solution.py:26
  89.1 5.3 %collective-permute-start.40 = (bf16[64,768]{1,0:T(8,128)(2,1)S(1)}, bf16[64,768]{1,0:T(8,128)(2,1)S(1)}, u32[]{:S(2)}, u32[]{:S(2)}) collective-permute-start(bf16[64,768]{1,0:T(8,128)(2,1)S(1)} %get-tuple-element.234), channel_id=1, source_target_pairs={{0,8},{1,9},{2,10},{3,11},{4,12},{5,13},{6,14},{7,15},{8,0},{9,1},... | collective-permute-start | bytes 294920 | tf_op jit(solution)/shard_map/ppermute | solution.py:26
  89.8 5.4 %collective-permute-start.41 = (bf16[64,768]{1,0:T(8,128)(2,1)S(1)}, bf16[64,768]{1,0:T(8,128)(2,1)S(1)}, u32[]{:S(2)}, u32[]{:S(2)}) collective-permute-start(bf16[64,768]{1,0:T(8,128)(2,1)S(1)} %get-tuple-element.235), channel_id=1, source_target_pairs={{0,1},{1,0},{2,3},{3,2},{4,5},{5,4},{6,7},{7,6},{8,9},{9,8},{10,11... | collective-permute-start | bytes 294920 | tf_op jit(solution)/shard_map/ppermute | solution.py:26
  90.8 5.7 %collective-permute-start.42 = (bf16[64,768]{1,0:T(8,128)(2,1)S(1)}, bf16[64,768]{1,0:T(8,128)(2,1)S(1)}, u32[]{:S(2)}, u32[]{:S(2)}) collective-permute-start(bf16[64,768]{1,0:T(8,128)(2,1)S(1)} %get-tuple-element.236), channel_id=1, source_target_pairs={{0,9},{1,8},{2,11},{3,10},{4,13},{5,12},{6,15},{7,14},{8,1},{9,0},... | collective-permute-start | bytes 294920 | tf_op jit(solution)/shard_map/ppermute | solution.py:26
  96.7 5.7 %collective-permute-start.45 = (bf16[64,768]{1,0:T(8,128)(2,1)S(1)}, bf16[64,768]{1,0:T(8,128)(2,1)S(1)}, u32[]{:S(2)}, u32[]{:S(2)}) collective-permute-start(bf16[64,768]{1,0:T(8,128)(2,1)S(1)} %get-tuple-element.240.own_ref), channel_id=1, source_target_pairs={{0,9},{1,8},{2,11},{3,10},{4,13},{5,12},{6,15},{7,14},{8,1},{9,0},... | collective-permute-start | bytes 294920 | tf_op jit(solution)/shard_map/ppermute | solution.py:26
  98.7 4.6 %collective-permute-start.44 = (bf16[64,768]{1,0:T(8,128)(2,1)S(1)}, bf16[64,768]{1,0:T(8,128)(2,1)S(1)}, u32[]{:S(2)}, u32[]{:S(2)}) collective-permute-start(bf16[64,768]{1,0:T(8,128)(2,1)S(1)} %get-tuple-element.240.own_ref), channel_id=1, source_target_pairs={{0,8},{1,9},{2,10},{3,11},{4,12},{5,13},{6,14},{7,15},{8,0},{9,1},... | collective-permute-start | bytes 294920 | tf_op jit(solution)/shard_map/ppermute | solution.py:26
  99.3 4.6 %collective-permute-start.43 = (bf16[64,768]{1,0:T(8,128)(2,1)S(1)}, bf16[64,768]{1,0:T(8,128)(2,1)S(1)}, u32[]{:S(2)}, u32[]{:S(2)}) collective-permute-start(bf16[64,768]{1,0:T(8,128)(2,1)S(1)} %get-tuple-element.240.own_ref), channel_id=1, source_target_pairs={{0,1},{1,0},{2,3},{3,2},{4,5},{5,4},{6,7},{7,6},{8,9},{9,8},{10,11... | collective-permute-start | bytes 294920 | tf_op jit(solution)/shard_map/ppermute | solution.py:26
  104.8 6.4 %collective-permute-start.47 = (bf16[256,512]{1,0:T(8,128)(2,1)S(1)}, bf16[256,512]{1,0:T(8,128)(2,1)S(1)}, u32[]{:S(2)}, u32[]{:S(2)}) collective-permute-start(bf16[256,512]{1,0:T(8,128)(2,1)S(1)} %get-tuple-element.242.packet_ref.g0_ref), channel_id=1, source_target_pairs={{0,4},{1,5},{2,6},{3,7},{4,0},{5,1},{6,2},{7,3},{8,12},{9,13},{10,... | collective-permute-start | bytes 786440 | tf_op jit(solution)/shard_map/ppermute | solution.py:26
  106.1 13.7 %collective-permute-start.50 = (bf16[2,48,1536]{2,1,0:T(8,128)(2,1)S(1)}, bf16[2,48,1536]{2,1,0:T(8,128)(2,1)S(1)}, u32[]{:S(2)}, u32[]{:S(2)}) collective-permute-start(bf16[2,48,1536]{2,1,0:T(8,128)(2,1)S(1)} %get-tuple-element.252), channel_id=1, source_target_pairs={{0,16},{1,17},{2,18},{3,19},{4,20},{5,21},{6,22},{7,23},{8,24},{9,... | collective-permute-start | bytes 884744 | tf_op jit(solution)/shard_map/ppermute | solution.py:26
  107.7 5.2 %collective-permute-start.48 = (bf16[256,512]{1,0:T(8,128)(2,1)S(1)}, bf16[256,512]{1,0:T(8,128)(2,1)S(1)}, u32[]{:S(2)}, u32[]{:S(2)}) collective-permute-start(bf16[256,512]{1,0:T(8,128)(2,1)S(1)} %get-tuple-element.242.packet_ref.g0_ref), channel_id=1, source_target_pairs={{0,2},{1,3},{2,0},{3,1},{4,6},{5,7},{6,4},{7,5},{8,10},{9,11},{10,... | collective-permute-start | bytes 786440 | tf_op jit(solution)/shard_map/ppermute | solution.py:26
  111.2 1.7 %collective-permute-start.49 = (bf16[256,512]{1,0:T(8,128)(2,1)S(1)}, bf16[256,512]{1,0:T(8,128)(2,1)S(1)}, u32[]{:S(2)}, u32[]{:S(2)}) collective-permute-start(bf16[256,512]{1,0:T(8,128)(2,1)S(1)} %collective-permute-done.47.g1_ref), channel_id=1, source_target_pairs={{0,2},{1,3},{2,0},{3,1},{4,6},{5,7},{6,4},{7,5},{8,10},{9,11},{10,... | collective-permute-start | bytes 786440 | tf_op jit(solution)/shard_map/ppermute | solution.py:26
  111.3 8.4 %collective-permute-start.51 = (f32[16,768]{1,0:T(8,128)S(1)}, f32[16,768]{1,0:T(8,128)S(1)}, u32[]{:S(2)}, u32[]{:S(2)}) collective-permute-start(f32[16,768]{1,0:T(8,128)S(1)} %vectors.1.refs_4_), channel_id=1, source_target_pairs={{0,1},{1,0},{2,3},{3,2},{4,5},{5,4},{6,7},{7,6},{8,9},{9,8},{10,11... | collective-permute-start | bytes 147464 | tf_op jit(solution)/shard_map/ppermute | solution.py:26
  120.9 2.4 %collective-permute-start.53 = (bf16[8,48,704]{2,1,0:T(8,128)(2,1)S(1)}, bf16[8,48,704]{2,1,0:T(8,128)(2,1)S(1)}, u32[]{:S(2)}, u32[]{:S(2)}) collective-permute-start(bf16[8,48,704]{2,1,0:T(8,128)(2,1)S(1)} %get-tuple-element.261), channel_id=1, source_target_pairs={{0,2},{1,3},{2,0},{3,1},{4,6},{5,7},{6,4},{7,5},{8,10},{9,11},{10,... | collective-permute-start | bytes 1622024 | tf_op jit(solution)/shard_map/ppermute | solution.py:26
  121.0 2.3 %collective-permute-start.52 = (bf16[8,48,192]{2,1,0:T(8,128)(2,1)S(1)}, bf16[8,48,192]{2,1,0:T(8,128)(2,1)S(1)}, u32[]{:S(2)}, u32[]{:S(2)}) collective-permute-start(bf16[8,48,192]{2,1,0:T(8,128)(2,1)S(1)} %get-tuple-element.260), channel_id=1, source_target_pairs={{0,2},{1,3},{2,0},{3,1},{4,6},{5,7},{6,4},{7,5},{8,10},{9,11},{10,... | collective-permute-start | bytes 442376 | tf_op jit(solution)/shard_map/ppermute | solution.py:26
  123.5 10.6 %collective-permute-start.58 = (bf16[4,48,896]{2,1,0:T(8,128)(2,1)S(1)}, bf16[4,48,896]{2,1,0:T(8,128)(2,1)S(1)}, u32[]{:S(2)}, u32[]{:S(2)}) collective-permute-start(bf16[4,48,896]{2,1,0:T(8,128)(2,1)S(1)} %get-tuple-element.273), channel_id=1, source_target_pairs={{0,4},{1,5},{2,6},{3,7},{4,0},{5,1},{6,2},{7,3},{8,12},{9,13},{10,... | collective-permute-start | bytes 1032200 | tf_op jit(solution)/shard_map/ppermute | solution.py:26
  124.3 5.6 %collective-permute-start.54 = (bf16[64,768]{1,0:T(8,128)(2,1)S(1)}, bf16[64,768]{1,0:T(8,128)(2,1)S(1)}, u32[]{:S(2)}, u32[]{:S(2)}) collective-permute-start(bf16[64,768]{1,0:T(8,128)(2,1)S(1)} %get-tuple-element.264), channel_id=1, source_target_pairs={{0,8},{1,9},{2,10},{3,11},{4,12},{5,13},{6,14},{7,15},{8,0},{9,1},... | collective-permute-start | bytes 294920 | tf_op jit(solution)/shard_map/ppermute | solution.py:26
  124.3 5.6 %collective-permute-start.55 = (bf16[64,768]{1,0:T(8,128)(2,1)S(1)}, bf16[64,768]{1,0:T(8,128)(2,1)S(1)}, u32[]{:S(2)}, u32[]{:S(2)}) collective-permute-start(bf16[64,768]{1,0:T(8,128)(2,1)S(1)} %get-tuple-element.265), channel_id=1, source_target_pairs={{0,1},{1,0},{2,3},{3,2},{4,5},{5,4},{6,7},{7,6},{8,9},{9,8},{10,11... | collective-permute-start | bytes 294920 | tf_op jit(solution)/shard_map/ppermute | solution.py:26
  125.3 7.1 %collective-permute-start.56 = (bf16[64,768]{1,0:T(8,128)(2,1)S(1)}, bf16[64,768]{1,0:T(8,128)(2,1)S(1)}, u32[]{:S(2)}, u32[]{:S(2)}) collective-permute-start(bf16[64,768]{1,0:T(8,128)(2,1)S(1)} %get-tuple-element.266), channel_id=1, source_target_pairs={{0,9},{1,8},{2,11},{3,10},{4,13},{5,12},{6,15},{7,14},{8,1},{9,0},... | collective-permute-start | bytes 294920 | tf_op jit(solution)/shard_map/ppermute | solution.py:26
  127.9 10.8 %collective-permute-start.62 = (bf16[48,1536]{1,0:T(8,128)(2,1)S(1)}, bf16[48,1536]{1,0:T(8,128)(2,1)S(1)}, u32[]{:S(2)}, u32[]{:S(2)}) collective-permute-start(bf16[48,1536]{1,0:T(8,128)(2,1)S(1)} %get-tuple-element.279), channel_id=1, source_target_pairs={{0,8},{1,9},{2,10},{3,11},{4,12},{5,13},{6,14},{7,15},{8,0},{9,1},... | collective-permute-start | bytes 442376 | tf_op jit(solution)/shard_map/ppermute | solution.py:26
  132.5 11.4 %collective-permute-start.57 = (bf16[32,1536]{1,0:T(8,128)(2,1)S(1)}, bf16[32,1536]{1,0:T(8,128)(2,1)S(1)}, u32[]{:S(2)}, u32[]{:S(2)}) collective-permute-start(bf16[32,1536]{1,0:T(8,128)(2,1)S(1)} %get-tuple-element.270), channel_id=1, source_target_pairs={{0,16},{1,17},{2,18},{3,19},{4,20},{5,21},{6,22},{7,23},{8,24},{9,... | collective-permute-start | bytes 294920 | tf_op jit(solution)/shard_map/ppermute | solution.py:26
  134.2 10.5 %collective-permute-start.59 = (bf16[48,896]{1,0:T(8,128)(2,1)S(1)}, bf16[48,896]{1,0:T(8,128)(2,1)S(1)}, u32[]{:S(2)}, u32[]{:S(2)}) collective-permute-start(bf16[48,896]{1,0:T(8,128)(2,1)S(1)} %get-tuple-element.275), channel_id=1, source_target_pairs={{0,8},{1,9},{2,10},{3,11},{4,12},{5,13},{6,14},{7,15},{8,0},{9,1},... | collective-permute-start | bytes 258056 | tf_op jit(solution)/shard_map/ppermute | solution.py:26
  134.9 10.4 %collective-permute-start.60 = (bf16[48,896]{1,0:T(8,128)(2,1)S(1)}, bf16[48,896]{1,0:T(8,128)(2,1)S(1)}, u32[]{:S(2)}, u32[]{:S(2)}) collective-permute-start(bf16[48,896]{1,0:T(8,128)(2,1)S(1)} %get-tuple-element.276), channel_id=1, source_target_pairs={{0,16},{1,17},{2,18},{3,19},{4,20},{5,21},{6,22},{7,23},{8,24},{9,... | collective-permute-start | bytes 258056 | tf_op jit(solution)/shard_map/ppermute | solution.py:26
  137.1 8.2 %collective-permute-start.61 = (bf16[48,896]{1,0:T(8,128)(2,1)S(1)}, bf16[48,896]{1,0:T(8,128)(2,1)S(1)}, u32[]{:S(2)}, u32[]{:S(2)}) collective-permute-start(bf16[48,896]{1,0:T(8,128)(2,1)S(1)} %get-tuple-element.277), channel_id=1, source_target_pairs={{0,24},{1,25},{2,26},{3,27},{4,28},{5,29},{6,30},{7,31},{8,16},{9,... | collective-permute-start | bytes 258056 | tf_op jit(solution)/shard_map/ppermute | solution.py:26

commit v6 on v5

--- a/solution.py
+++ b/solution.py
@@ -478,25 +478,9 @@
         send_ref[chip] = full_ref[row_of(chip, 1 - core, rows), 0:cols]
 
 
-def rows_kernel(hidden_hbm, cot_hbm, hidden_ref, cot_ref, other_ref, held0, held1, sems):
-    copies = [
-        pltpu.make_async_copy(source, target, sems.at[i])
-        for i, (source, target) in enumerate(((hidden_hbm, held0), (cot_hbm, held1)))
-    ]
-    for copy in copies:
-        copy.start()
-    near = Place().high == 0
-    shard = hidden_ref.shape[0]
-    for i, (held, out_ref) in enumerate(((held0, hidden_ref), (held1, cot_ref))):
-        copies[i].wait()
-        first, second = held[:, 0, :], held[:, 1, :]
-        out_ref[...] = jnp.where(near, first, second)
-        other_ref[i * shard : (i + 1) * shard, :] = jnp.where(near, second, first)
-
-
 def pack_kernel(count, *refs):
     sources, refs = refs[:count], refs[count:]
-    outs, held, sems = refs[:4], refs[4:-1], refs[-1]
+    outs, held, sems = refs[:7], refs[7:-1], refs[-1]
     copies = [
         pltpu.make_async_copy(source, target, sems.at[i])
         for i, (source, target) in enumerate(zip(sources, held))
@@ -504,13 +488,19 @@
     for copy in copies:
         copy.start()
     wq_ref, wk_ref, wv_ref, wo_ref, wu_ref, wd_ref = held[:6]
-    own_ref, send_ref, later_own_ref, near_ref = outs
-    size = send_ref.shape[0]
+    own_ref, send_ref, later_own_ref, near_ref, hidden_ref, cot_ref, other_ref = outs
+    size, shard = send_ref.shape[0], hidden_ref.shape[0]
     rows = wq_ref.shape[0]
     head_cols = wq_ref.shape[1] // 2
     unit_cols = wu_ref.shape[1] // 2
     low = Place().low
-    for copy in copies[6:]:
+    near = Place().high == 0
+    for i, out_ref in ((15, hidden_ref), (16, cot_ref)):
+        copies[i].wait()
+        first, second = held[i][:, 0, :], held[i][:, 1, :]
+        out_ref[...] = jnp.where(near, first, second)
+        other_ref[(i - 15) * shard : (i - 14) * shard, :] = jnp.where(near, second, first)
+    for copy in copies[6:15]:
         copy.wait()
     vectors = [ref[...].astype(wide).reshape(1, rows) for ref in held[6:14]]
     block = jnp.concatenate(
@@ -1023,25 +1013,16 @@
     sources = (
         w_query, w_key, w_value, jnp.transpose(w_out), w_up, jnp.transpose(w_down),
         b_query, b_value, b_out, first_gain, first_shift, b_down, second_gain, second_shift, b_up,
+        hidden_in, cotangent,
     )
     first = ((shard_rows + 16, 4 * head_cols), low_type)
     later = ((2 * shard_rows, unit_cols), low_type)
     near = ((3 * shard_rows + 16, unit_cols), low_type)
     shard = ((shard_pos, width), low_type)
-    hidden_own, cot_own, other = run_kernel(
-        rows_kernel,
-        [shard, shard, ((rows_here, width), low_type)],
-        hidden_in, cotangent,
-        scratch=[(hidden_in.shape, low_type)] * 2,
-        sems=2,
-        apart=True,
-        name="rows",
-    )
-    slot_rows = swap(other, BIT_HIGH)
-    packs = run_kernel(
+    *packs, hidden_own, cot_own, other = run_kernel(
         functools.partial(pack_kernel, len(sources)),
-        [first, first, later, near],
-        *tie(sources, other),
+        [first, first, later, near, shard, shard, ((rows_here, width), low_type)],
+        *sources,
         scratch=[(source.shape, source.dtype) for source in sources],
         sems=len(sources),
         apart=True,
@@ -1049,6 +1030,7 @@
         name="pack",
     )
 
+    slot_rows = swap(other, BIT_HIGH)
     first_own, first_send, later_own, near_send = tuple(packs)
     near_got = swap(near_send, BIT_LOW)
     size = first_own.shape[0]

time: 146 us -> 146 us (level)
    pallas_call x26 -> x25, Pallas kernels: 22.6 us -> 21.8 us  [run_kernel(): pl.pallas_call(body, out_shape=[jax.ShapeDtypeStruct(shape, kind) for sha...]
  transfers between devices with their start and end apart: 63 -> 63, of which waited for: 37 -> 38; matrix products, arithmetic and copies ran while one was open for 0% -> 0% of each run, Pallas kernels for 9% -> 9%
where the time goes in v6:
time: 146 us
  starting transfers between devices  61.5 us (42%)
  waiting for transfers between devices  60.9 us (42%)
  Pallas kernels  21.8 us (15%)
    ppermute x63, starting transfers between devices, swap(): lax.ppermute(values, AXES, [(i, i ^ bit) for i in range(device_count())])  61.5 us
    ppermute x63, waiting for transfers between devices, swap(): lax.ppermute(values, AXES, [(i, i ^ bit) for i in range(device_count())])  60.9 us
    pallas_call x25, Pallas kernels, run_kernel(): pl.pallas_call(body, out_shape=[jax.ShapeDtypeStruct(shape, kind) for sha...  21.8 us
  transfers between devices with their start and end apart: 63, of which 38 were waited for; matrix products, arithmetic and copies ran while one was open for 0% of the time, Pallas kernels for 9%

profile of v6, /device:TPU:0, one launch (start us, length us, event | category | flops | bytes accessed | tf_op | source)
XLA Modules:
  0.0 145.5 jit_solution(17150428237190628156)
XLA Ops:
  0.7 2.0 %pack.1 = (bf16[64,768]{1,0:T(8,128)(2,1)S(1)}, bf16[64,768]{1,0:T(8,128)(2,1)S(1)}, bf16[96,768]{1,0:T(8,128)(2,1)S(1)}, bf16[160,768]{1,0:T(8,128)(2,1)S(1)}, ...) custom-call(bf16[48,384]{1,0:T(8,128)(2,1)} %refs_0_.1, ...), custom_call_target="tpu_custom_call" | custom-call | flops 30000000 | bytes 30000 | tf_op jit(solution)/shard_map/pack/pallas_call | solution.py:413
  2.7 3.1 %collective-permute-start.4 = (bf16[160,768]{1,0:T(8,128)(2,1)S(1)}, bf16[160,768]{1,0:T(8,128)(2,1)S(1)}, u32[]{:S(2)}, u32[]{:S(2)}) collective-permute-start(bf16[160,768]{1,0:T(8,128)(2,1)S(1)} %get-tuple-element.148), channel_id=1, source_target_pairs={{0,8},{1,9},{2,10},{3,11},{4,12},{5,13},{6,14},{7,15},{8,0},{9,1},... | collective-permute-start | bytes 737288 | tf_op jit(solution)/shard_map/ppermute | solution.py:26
  5.8 2.6 %collective-permute-start = (bf16[64,768]{1,0:T(8,128)(2,1)S(1)}, bf16[64,768]{1,0:T(8,128)(2,1)S(1)}, u32[]{:S(2)}, u32[]{:S(2)}) collective-permute-start(bf16[64,768]{1,0:T(8,128)(2,1)S(1)} %get-tuple-element.144), channel_id=1, source_target_pairs={{0,16},{1,17},{2,18},{3,19},{4,20},{5,21},{6,22},{7,23},{8,24},{9,... | collective-permute-start | bytes 294920 | tf_op jit(solution)/shard_map/ppermute | solution.py:26
  8.4 1.9 %collective-permute-start.5 = (bf16[64,768]{1,0:T(8,128)(2,1)S(1)}, bf16[64,768]{1,0:T(8,128)(2,1)S(1)}, u32[]{:S(2)}, u32[]{:S(2)}) collective-permute-start(bf16[64,768]{1,0:T(8,128)(2,1)S(1)} %get-tuple-element.145), channel_id=1, source_target_pairs={{0,16},{1,17},{2,18},{3,19},{4,20},{5,21},{6,22},{7,23},{8,24},{9,... | collective-permute-start | bytes 294920 | tf_op jit(solution)/shard_map/ppermute | solution.py:26
  10.3 4.0 %collective-permute-done.got_ref.slot_ref = bf16[64,768]{1,0:T(8,128)(2,1)S(1)} collective-permute-done((bf16[64,768]{1,0:T(8,128)(2,1)S(1)}, bf16[64,768]{1,0:T(8,128)(2,1)S(1)}, u32[]{:S(2)}, u32[]{:S(2)}) %collective-permute-start) | collective-permute-done | bytes 98336 | tf_op jit(solution)/shard_map/ppermute | solution.py:26
  14.7 1.8 %collective-permute-start.7 = (bf16[2,64,768]{2,1,0:T(8,128)(2,1)S(1)}, bf16[2,64,768]{2,1,0:T(8,128)(2,1)S(1)}, u32[]{:S(2)}, u32[]{:S(2)}) collective-permute-start(bf16[2,64,768]{2,1,0:T(8,128)(2,1)S(1)} %pad_maximum_fusion.1.refs_0_), channel_id=1, source_target_pairs={{0,4},{1,5},{2,6},{3,7},{4,0},{5,1},{6,2},{7,3},{8,12},{9,13},{10,... | collective-permute-start | bytes 589832 | tf_op jit(solution)/shard_map/ppermute | solution.py:26
  16.5 4.0 %collective-permute-start.3 = (bf16[64,768]{1,0:T(8,128)(2,1)S(1)}, bf16[64,768]{1,0:T(8,128)(2,1)S(1)}, u32[]{:S(2)}, u32[]{:S(2)}) collective-permute-start(bf16[64,768]{1,0:T(8,128)(2,1)S(1)} %pad_maximum_fusion.3), channel_id=1, source_target_pairs={{0,9},{1,8},{2,11},{3,10},{4,13},{5,12},{6,15},{7,14},{8,1},{9,0},... | collective-permute-start | bytes 294920 | tf_op jit(solution)/shard_map/ppermute | solution.py:26
  22.0 1.5 %collective-permute-start.8 = (bf16[2,64,768]{2,1,0:T(8,128)(2,1)S(1)}, bf16[2,64,768]{2,1,0:T(8,128)(2,1)S(1)}, u32[]{:S(2)}, u32[]{:S(2)}) collective-permute-start(bf16[2,64,768]{2,1,0:T(8,128)(2,1)S(1)} %pad_maximum_fusion.2.refs_1_), channel_id=1, source_target_pairs={{0,4},{1,5},{2,6},{3,7},{4,0},{5,1},{6,2},{7,3},{8,12},{9,13},{10,... | collective-permute-start | bytes 589832 | tf_op jit(solution)/shard_map/ppermute | solution.py:26
  23.7 1.4 collective-permute-done.2.low_ref
  25.1 4.1 %collective-permute-done.8.refs_3_ = bf16[2,64,768]{2,1,0:T(8,128)(2,1)S(1)} collective-permute-done((bf16[2,64,768]{2,1,0:T(8,128)(2,1)S(1)}, bf16[2,64,768]{2,1,0:T(8,128)(2,1)S(1)}, u32[]{:S(2)}, u32[]{:S(2)}) %collective-permute-start.8) | collective-permute-done | bytes 196640 | tf_op jit(solution)/shard_map/ppermute | solution.py:26
  29.3 1.7 %collective-permute-start.25 = (bf16[2,96,768]{2,1,0:T(8,128)(2,1)S(1)}, bf16[2,96,768]{2,1,0:T(8,128)(2,1)S(1)}, u32[]{:S(2)}, u32[]{:S(2)}) collective-permute-start(bf16[2,96,768]{2,1,0:T(8,128)(2,1)S(1)} %pad_maximum_fusion.refs_0_), channel_id=1, source_target_pairs={{0,16},{1,17},{2,18},{3,19},{4,20},{5,21},{6,22},{7,23},{8,24},{9,... | collective-permute-start | bytes 884744 | tf_op jit(solution)/shard_map/ppermute | solution.py:26
  31.7 1.6 %collective-permute-start.13 = (bf16[256,256]{1,0:T(8,128)(2,1)S(1)}, bf16[256,256]{1,0:T(8,128)(2,1)S(1)}, u32[]{:S(2)}, u32[]{:S(2)}) collective-permute-start(bf16[256,256]{1,0:T(8,128)(2,1)S(1)} %get-tuple-element.215.refs_0_.pair_ref), channel_id=1, source_target_pairs={{0,4},{1,5},{2,6},{3,7},{4,0},{5,1},{6,2},{7,3},{8,12},{9,13},{10,... | collective-permute-start | bytes 393224 | tf_op jit(solution)/shard_map/ppermute | solution.py:26
  33.8 4.3 %collective-permute-done.13.refs_1_ = bf16[256,256]{1,0:T(8,128)(2,1)S(1)} collective-permute-done((bf16[256,256]{1,0:T(8,128)(2,1)S(1)}, bf16[256,256]{1,0:T(8,128)(2,1)S(1)}, u32[]{:S(2)}, u32[]{:S(2)}) %collective-permute-start.13) | collective-permute-done | bytes 131104 | tf_op jit(solution)/shard_map/ppermute | solution.py:26
  39.6 1.5 %collective-permute-start.26 = (bf16[2,96,768]{2,1,0:T(8,128)(2,1)S(1)}, bf16[2,96,768]{2,1,0:T(8,128)(2,1)S(1)}, u32[]{:S(2)}, u32[]{:S(2)}) collective-permute-start(bf16[2,96,768]{2,1,0:T(8,128)(2,1)S(1)} %pad_maximum_fusion.refs_0_), channel_id=1, source_target_pairs={{0,4},{1,5},{2,6},{3,7},{4,0},{5,1},{6,2},{7,3},{8,12},{9,13},{10,... | collective-permute-start | bytes 884744 | tf_op jit(solution)/shard_map/ppermute | solution.py:26
  41.1 2.8 %attend.1 = (bf16[256,192]{1,0:T(8,128)(2,1)S(1)}, f32[256,128]{1,0:T(8,128)S(1)}, f32[64,768]{1,0:T(8,128)S(1)}, bf16[64,768]{1,0:T(8,128)(2,1)S(1)}, bf16[64,7...) custom-call(s32[2]{0:T(128)S(1)} %copy-done, bf16[256,192]{1,0:T(8,128)(2,1)S(1)} %get-tuple-element.163.query_ref, ...), custom_call_target="tpu_custom_call" | custom-call | flops 30000000 | bytes 30000 | tf_op jit(solution)/shard_map/attend/pallas_call | solution.py:413
  43.9 2.0 %collective-permute-done.25.refs_1_ = bf16[2,96,768]{2,1,0:T(8,128)(2,1)S(1)} collective-permute-done((bf16[2,96,768]{2,1,0:T(8,128)(2,1)S(1)}, bf16[2,96,768]{2,1,0:T(8,128)(2,1)S(1)}, u32[]{:S(2)}, u32[]{:S(2)}) %collective-permute-start.25) | collective-permute-done | bytes 294944 | tf_op jit(solution)/shard_map/ppermute | solution.py:26
  45.9 1.2 collective-permute-start.27
  47.1 1.5 %collective-permute-start.20 = (bf16[64,768]{1,0:T(8,128)(2,1)S(1)}, bf16[64,768]{1,0:T(8,128)(2,1)S(1)}, u32[]{:S(2)}, u32[]{:S(2)}) collective-permute-start(bf16[64,768]{1,0:T(8,128)(2,1)S(1)} %get-tuple-element.168), channel_id=1, source_target_pairs={{0,1},{1,0},{2,3},{3,2},{4,5},{5,4},{6,7},{7,6},{8,9},{9,8},{10,11... | collective-permute-start | bytes 294920 | tf_op jit(solution)/shard_map/ppermute | solution.py:26
  48.6 2.0 %collective-permute-start.21 = (bf16[64,768]{1,0:T(8,128)(2,1)S(1)}, bf16[64,768]{1,0:T(8,128)(2,1)S(1)}, u32[]{:S(2)}, u32[]{:S(2)}) collective-permute-start(bf16[64,768]{1,0:T(8,128)(2,1)S(1)} %get-tuple-element.169), channel_id=1, source_target_pairs={{0,9},{1,8},{2,11},{3,10},{4,13},{5,12},{6,15},{7,14},{8,1},{9,0},... | collective-permute-start | bytes 294920 | tf_op jit(solution)/shard_map/ppermute | solution.py:26
  50.6 2.1 %collective-permute-done.19.got1_ref = bf16[64,768]{1,0:T(8,128)(2,1)S(1)} collective-permute-done((bf16[64,768]{1,0:T(8,128)(2,1)S(1)}, bf16[64,768]{1,0:T(8,128)(2,1)S(1)}, u32[]{:S(2)}, u32[]{:S(2)}) %collective-permute-start.19) | collective-permute-done | bytes 98336 | tf_op jit(solution)/shard_map/ppermute | solution.py:26
  52.7 2.1 %collective-permute-done.21.got3_ref = bf16[64,768]{1,0:T(8,128)(2,1)S(1)} collective-permute-done((bf16[64,768]{1,0:T(8,128)(2,1)S(1)}, bf16[64,768]{1,0:T(8,128)(2,1)S(1)}, u32[]{:S(2)}, u32[]{:S(2)}) %collective-permute-start.21) | collective-permute-done | bytes 98336 | tf_op jit(solution)/shard_map/ppermute | solution.py:26
  56.1 2.7 %collective-permute-start.24 = (bf16[64,768]{1,0:T(8,128)(2,1)S(1)}, bf16[64,768]{1,0:T(8,128)(2,1)S(1)}, u32[]{:S(2)}, u32[]{:S(2)}) collective-permute-start(bf16[64,768]{1,0:T(8,128)(2,1)S(1)} %get-tuple-element.171.own_ref), channel_id=1, source_target_pairs={{0,9},{1,8},{2,11},{3,10},{4,13},{5,12},{6,15},{7,14},{8,1},{9,0},... | collective-permute-start | bytes 294920 | tf_op jit(solution)/shard_map/ppermute | solution.py:26
  58.9 1.1 collective-permute-start.22
  60.2 2.4 %collective-permute-done.24.got3_ref = bf16[64,768]{1,0:T(8,128)(2,1)S(1)} collective-permute-done((bf16[64,768]{1,0:T(8,128)(2,1)S(1)}, bf16[64,768]{1,0:T(8,128)(2,1)S(1)}, u32[]{:S(2)}, u32[]{:S(2)}) %collective-permute-start.24) | collective-permute-done | bytes 98336 | tf_op jit(solution)/shard_map/ppermute | solution.py:26
  62.6 1.1 collective-permute-done.23.got2_ref
  64.0 1.6 %hidden.1 = (f32[64,768]{1,0:T(8,128)S(1)}, bf16[64,768]{1,0:T(8,128)(2,1)S(1)}, bf16[64,768]{1,0:T(8,128)(2,1)S(1)}, bf16[64,768]{1,0:T(8,128)(2,1)S(1)}, bf16[...) custom-call(bf16[64,768]{1,0:T(8,128)(2,1)S(1)} %get-tuple-element.171.own_ref, ...), custom_call_target="tpu_custom_call" | custom-call | flops 20000000 | bytes 20000 | tf_op jit(solution)/shard_map/hidden/pallas_call | solution.py:413
  65.7 1.9 %collective-permute-start.32 = (bf16[64,768]{1,0:T(8,128)(2,1)S(1)}, bf16[64,768]{1,0:T(8,128)(2,1)S(1)}, u32[]{:S(2)}, u32[]{:S(2)}) collective-permute-start(bf16[64,768]{1,0:T(8,128)(2,1)S(1)} %get-tuple-element.184), channel_id=1, source_target_pairs={{0,8},{1,9},{2,10},{3,11},{4,12},{5,13},{6,14},{7,15},{8,0},{9,1},... | collective-permute-start | bytes 294920 | tf_op jit(solution)/shard_map/ppermute | solution.py:26
  67.5 1.3 collective-permute-start.33
  69.2 1.2 collective-permute-done.32.got1_ref
  70.4 2.8 %collective-permute-done.33.got2_ref = bf16[64,768]{1,0:T(8,128)(2,1)S(1)} collective-permute-done((bf16[64,768]{1,0:T(8,128)(2,1)S(1)}, bf16[64,768]{1,0:T(8,128)(2,1)S(1)}, u32[]{:S(2)}, u32[]{:S(2)}) %collective-permute-start.33) | collective-permute-done | bytes 98336 | tf_op jit(solution)/shard_map/ppermute | solution.py:26
  73.2 1.2 collective-permute-done.34.got3_ref
  74.4 0.9 second_norm.1
  75.8 1.7 %collective-permute-start.36 = (bf16[64,768]{1,0:T(8,128)(2,1)S(1)}, bf16[64,768]{1,0:T(8,128)(2,1)S(1)}, u32[]{:S(2)}, u32[]{:S(2)}) collective-permute-start(bf16[64,768]{1,0:T(8,128)(2,1)S(1)} %get-tuple-element.189.own_ref), channel_id=1, source_target_pairs={{0,8},{1,9},{2,10},{3,11},{4,12},{5,13},{6,14},{7,15},{8,0},{9,1},... | collective-permute-start | bytes 294920 | tf_op jit(solution)/shard_map/ppermute | solution.py:26
  77.5 1.3 collective-permute-start.35
  78.9 2.0 %collective-permute-done.37.got3_ref = bf16[64,768]{1,0:T(8,128)(2,1)S(1)} collective-permute-done((bf16[64,768]{1,0:T(8,128)(2,1)S(1)}, bf16[64,768]{1,0:T(8,128)(2,1)S(1)}, u32[]{:S(2)}, u32[]{:S(2)}) %collective-permute-start.37) | collective-permute-done | bytes 98336 | tf_op jit(solution)/shard_map/ppermute | solution.py:26
  81.2 1.0 collective-permute-done.35.got1_ref
  82.1 0.9 hidden_back.1
  83.1 1.1 unit_weights.1
  84.7 1.5 %collective-permute-done.38.refs_1_ = bf16[8,48,768]{2,1,0:T(8,128)(2,1)S(1)} collective-permute-done((bf16[8,48,768]{2,1,0:T(8,128)(2,1)S(1)}, bf16[8,48,768]{2,1,0:T(8,128)(2,1)S(1)}, u32[]{:S(2)}, u32[]{:S(2)}) %collective-permute-start.38) | collective-permute-done | bytes 589856 | tf_op jit(solution)/shard_map/ppermute | solution.py:26
  87.3 1.0 collective-permute-start.46
  89.0 1.0 collective-permute-start.41
  90.0 1.8 %collective-permute-start.42 = (bf16[64,768]{1,0:T(8,128)(2,1)S(1)}, bf16[64,768]{1,0:T(8,128)(2,1)S(1)}, u32[]{:S(2)}, u32[]{:S(2)}) collective-permute-start(bf16[64,768]{1,0:T(8,128)(2,1)S(1)} %get-tuple-element.206), channel_id=1, source_target_pairs={{0,9},{1,8},{2,11},{3,10},{4,13},{5,12},{6,15},{7,14},{8,1},{9,0},... | collective-permute-start | bytes 294920 | tf_op jit(solution)/shard_map/ppermute | solution.py:26
  91.8 1.8 %collective-permute-done.40.got1_ref = bf16[64,768]{1,0:T(8,128)(2,1)S(1)} collective-permute-done((bf16[64,768]{1,0:T(8,128)(2,1)S(1)}, bf16[64,768]{1,0:T(8,128)(2,1)S(1)}, u32[]{:S(2)}, u32[]{:S(2)}) %collective-permute-start.40) | collective-permute-done | bytes 98336 | tf_op jit(solution)/shard_map/ppermute | solution.py:26
  94.4 1.4 collective-permute-done.42.got3_ref
  96.0 2.0 %collective-permute-start.45 = (bf16[64,768]{1,0:T(8,128)(2,1)S(1)}, bf16[64,768]{1,0:T(8,128)(2,1)S(1)}, u32[]{:S(2)}, u32[]{:S(2)}) collective-permute-start(bf16[64,768]{1,0:T(8,128)(2,1)S(1)} %get-tuple-element.210.own_ref), channel_id=1, source_target_pairs={{0,9},{1,8},{2,11},{3,10},{4,13},{5,12},{6,15},{7,14},{8,1},{9,0},... | collective-permute-start | bytes 294920 | tf_op jit(solution)/shard_map/ppermute | solution.py:26
  98.5 1.0 collective-permute-start.43
  99.5 2.2 %collective-permute-done.45.got3_ref = bf16[64,768]{1,0:T(8,128)(2,1)S(1)} collective-permute-done((bf16[64,768]{1,0:T(8,128)(2,1)S(1)}, bf16[64,768]{1,0:T(8,128)(2,1)S(1)}, u32[]{:S(2)}, u32[]{:S(2)}) %collective-permute-start.45) | collective-permute-done | bytes 98336 | tf_op jit(solution)/shard_map/ppermute | solution.py:26
  104.0 1.2 collective-permute-start.47
  105.3 1.7 %collective-permute-start.50 = (bf16[2,48,1536]{2,1,0:T(8,128)(2,1)S(1)}, bf16[2,48,1536]{2,1,0:T(8,128)(2,1)S(1)}, u32[]{:S(2)}, u32[]{:S(2)}) collective-permute-start(bf16[2,48,1536]{2,1,0:T(8,128)(2,1)S(1)} %get-tuple-element.222), channel_id=1, source_target_pairs={{0,16},{1,17},{2,18},{3,19},{4,20},{5,21},{6,22},{7,23},{8,24},{9,... | collective-permute-start | bytes 884744 | tf_op jit(solution)/shard_map/ppermute | solution.py:26
  107.0 2.6 %query_back.1 = (bf16[256,192]{1,0:T(8,128)(2,1)S(1)}, f32[1,192]{1,0:T(1,128)S(1)}) custom-call(s32[2]{0:T(128)S(1)} %copy-done, bf16[256,512]{1,0:T(8,128)(2,1)S(1)} %get-tuple-element.212.packet_ref.g0_ref, bf16[256,256]{1,0:T(8,128)(2,1)S(1)} %get-tuple-element.215.refs_0_.pair_ref, bf16[256,256]{1,0:T(8,128)(2,1)S(1)} %collective-permute-done.13.refs_1_, ...), custom_call_target="tpu_custom_call" | custom-call | flops 30000000 | bytes 30000 | tf_op jit(solution)/shard_map/query_back/pallas_call | solution.py:413
  109.5 0.9 collective-permute-done.47.g1_ref
  110.6 1.1 collective-permute-start.51
  112.0 3.0 %pair_back.1 = (f32[64,768]{1,0:T(8,128)S(1)}, bf16[64,768]{1,0:T(8,128)(2,1)S(1)}, bf16[64,768]{1,0:T(8,128)(2,1)S(1)}, bf16[64,768]{1,0:T(8,128)(2,1)S(1)}, bf16[256,576]{1,0:T(8,128)(2,1)S(1)}) custom-call(s32[2]{0:T(128)S(1)} %copy-done, bf16[256,256]{1,0:T(8,128)(2,1)S(1)} %get-tuple-element.215.refs_0_.pair_ref, ...), custom_call_target="tpu_custom_call" | custom-call | flops 40000000 | bytes 40000 | tf_op jit(solution)/shard_map/pair_back/pallas_call | solution.py:413
  115.0 4.0 %collective-permute-done.50.refs_1_ = bf16[2,48,1536]{2,1,0:T(8,128)(2,1)S(1)} collective-permute-done((bf16[2,48,1536]{2,1,0:T(8,128)(2,1)S(1)}, bf16[2,48,1536]{2,1,0:T(8,128)(2,1)S(1)}, u32[]{:S(2)}, u32[]{:S(2)}) %collective-permute-start.50) | collective-permute-done | bytes 294944 | tf_op jit(solution)/shard_map/ppermute | solution.py:26
  119.0 1.1 head_weights.1
  120.7 1.8 %collective-permute-done.52.refs_1_ = bf16[8,48,192]{2,1,0:T(8,128)(2,1)S(1)} collective-permute-done((bf16[8,48,192]{2,1,0:T(8,128)(2,1)S(1)}, bf16[8,48,192]{2,1,0:T(8,128)(2,1)S(1)}, u32[]{:S(2)}, u32[]{:S(2)}) %collective-permute-start.52) | collective-permute-done | bytes 147488 | tf_op jit(solution)/shard_map/ppermute | solution.py:26
  123.6 1.0 collective-permute-start.55
  124.6 2.5 %collective-permute-start.56 = (bf16[64,768]{1,0:T(8,128)(2,1)S(1)}, bf16[64,768]{1,0:T(8,128)(2,1)S(1)}, u32[]{:S(2)}, u32[]{:S(2)}) collective-permute-start(bf16[64,768]{1,0:T(8,128)(2,1)S(1)} %get-tuple-element.236), channel_id=1, source_target_pairs={{0,9},{1,8},{2,11},{3,10},{4,13},{5,12},{6,15},{7,14},{8,1},{9,0},... | collective-permute-start | bytes 294920 | tf_op jit(solution)/shard_map/ppermute | solution.py:26
  127.2 2.0 %collective-permute-done.54.got1_ref = bf16[64,768]{1,0:T(8,128)(2,1)S(1)} collective-permute-done((bf16[64,768]{1,0:T(8,128)(2,1)S(1)}, bf16[64,768]{1,0:T(8,128)(2,1)S(1)}, u32[]{:S(2)}, u32[]{:S(2)}) %collective-permute-start.54) | collective-permute-done | bytes 98336 | tf_op jit(solution)/shard_map/ppermute | solution.py:26
  129.2 2.5 %collective-permute-done.56.got3_ref = bf16[64,768]{1,0:T(8,128)(2,1)S(1)} collective-permute-done((bf16[64,768]{1,0:T(8,128)(2,1)S(1)}, bf16[64,768]{1,0:T(8,128)(2,1)S(1)}, u32[]{:S(2)}, u32[]{:S(2)}) %collective-permute-start.56) | collective-permute-done | bytes 98336 | tf_op jit(solution)/shard_map/ppermute | solution.py:26
  131.8 1.6 %collective-permute-start.57 = (bf16[32,1536]{1,0:T(8,128)(2,1)S(1)}, bf16[32,1536]{1,0:T(8,128)(2,1)S(1)}, u32[]{:S(2)}, u32[]{:S(2)}) collective-permute-start(bf16[32,1536]{1,0:T(8,128)(2,1)S(1)} %get-tuple-element.240), channel_id=1, source_target_pairs={{0,16},{1,17},{2,18},{3,19},{4,20},{5,21},{6,22},{7,23},{8,24},{9,... | collective-permute-start | bytes 294920 | tf_op jit(solution)/shard_map/ppermute | solution.py:26
  134.1 2.2 %collective-permute-start.60 = (bf16[48,896]{1,0:T(8,128)(2,1)S(1)}, bf16[48,896]{1,0:T(8,128)(2,1)S(1)}, u32[]{:S(2)}, u32[]{:S(2)}) collective-permute-start(bf16[48,896]{1,0:T(8,128)(2,1)S(1)} %get-tuple-element.246), channel_id=1, source_target_pairs={{0,16},{1,17},{2,18},{3,19},{4,20},{5,21},{6,22},{7,23},{8,24},{9,... | collective-permute-start | bytes 258056 | tf_op jit(solution)/shard_map/ppermute | solution.py:26
  136.3 1.6 %collective-permute-start.61 = (bf16[48,896]{1,0:T(8,128)(2,1)S(1)}, bf16[48,896]{1,0:T(8,128)(2,1)S(1)}, u32[]{:S(2)}, u32[]{:S(2)}) collective-permute-start(bf16[48,896]{1,0:T(8,128)(2,1)S(1)} %get-tuple-element.247), channel_id=1, source_target_pairs={{0,24},{1,25},{2,26},{3,27},{4,28},{5,29},{6,30},{7,31},{8,16},{9,... | collective-permute-start | bytes 258056 | tf_op jit(solution)/shard_map/ppermute | solution.py:26
  138.7 4.3 %collective-permute-done.57.got_ref = bf16[32,1536]{1,0:T(8,128)(2,1)S(1)} collective-permute-done((bf16[32,1536]{1,0:T(8,128)(2,1)S(1)}, bf16[32,1536]{1,0:T(8,128)(2,1)S(1)}, u32[]{:S(2)}, u32[]{:S(2)}) %collective-permute-start.57) | collective-permute-done | bytes 98336 | tf_op jit(solution)/shard_map/ppermute | solution.py:26
  (96 shorter events, 20.5 us)
Async XLA Ops:
  2.7 11.9 %collective-permute-start.4 = (bf16[160,768]{1,0:T(8,128)(2,1)S(1)}, bf16[160,768]{1,0:T(8,128)(2,1)S(1)}, u32[]{:S(2)}, u32[]{:S(2)}) collective-permute-start(bf16[160,768]{1,0:T(8,128)(2,1)S(1)} %get-tuple-element.148), channel_id=1, source_target_pairs={{0,8},{1,9},{2,10},{3,11},{4,12},{5,13},{6,14},{7,15},{8,0},{9,1},... | collective-permute-start | bytes 737288 | tf_op jit(solution)/shard_map/ppermute | solution.py:26
  5.8 8.5 %collective-permute-start = (bf16[64,768]{1,0:T(8,128)(2,1)S(1)}, bf16[64,768]{1,0:T(8,128)(2,1)S(1)}, u32[]{:S(2)}, u32[]{:S(2)}) collective-permute-start(bf16[64,768]{1,0:T(8,128)(2,1)S(1)} %get-tuple-element.144), channel_id=1, source_target_pairs={{0,16},{1,17},{2,18},{3,19},{4,20},{5,21},{6,22},{7,23},{8,24},{9,... | collective-permute-start | bytes 294920 | tf_op jit(solution)/shard_map/ppermute | solution.py:26
  8.4 12.1 %collective-permute-start.6 = (bf16[64,768]{1,0:T(8,128)(2,1)S(1)}, bf16[64,768]{1,0:T(8,128)(2,1)S(1)}, u32[]{:S(2)}, u32[]{:S(2)}) collective-permute-start(bf16[64,768]{1,0:T(8,128)(2,1)S(1)} %get-tuple-element.146), channel_id=1, source_target_pairs={{0,24},{1,25},{2,26},{3,27},{4,28},{5,29},{6,30},{7,31},{8,16},{9,... | collective-permute-start | bytes 294920 | tf_op jit(solution)/shard_map/ppermute | solution.py:26
  8.4 13.4 %collective-permute-start.5 = (bf16[64,768]{1,0:T(8,128)(2,1)S(1)}, bf16[64,768]{1,0:T(8,128)(2,1)S(1)}, u32[]{:S(2)}, u32[]{:S(2)}) collective-permute-start(bf16[64,768]{1,0:T(8,128)(2,1)S(1)} %get-tuple-element.145), channel_id=1, source_target_pairs={{0,16},{1,17},{2,18},{3,19},{4,20},{5,21},{6,22},{7,23},{8,24},{9,... | collective-permute-start | bytes 294920 | tf_op jit(solution)/shard_map/ppermute | solution.py:26
  14.7 7.2 %collective-permute-start.7 = (bf16[2,64,768]{2,1,0:T(8,128)(2,1)S(1)}, bf16[2,64,768]{2,1,0:T(8,128)(2,1)S(1)}, u32[]{:S(2)}, u32[]{:S(2)}) collective-permute-start(bf16[2,64,768]{2,1,0:T(8,128)(2,1)S(1)} %pad_maximum_fusion.1.refs_0_), channel_id=1, source_target_pairs={{0,4},{1,5},{2,6},{3,7},{4,0},{5,1},{6,2},{7,3},{8,12},{9,13},{10,... | collective-permute-start | bytes 589832 | tf_op jit(solution)/shard_map/ppermute | solution.py:26
  16.5 7.3 %collective-permute-start.3 = (bf16[64,768]{1,0:T(8,128)(2,1)S(1)}, bf16[64,768]{1,0:T(8,128)(2,1)S(1)}, u32[]{:S(2)}, u32[]{:S(2)}) collective-permute-start(bf16[64,768]{1,0:T(8,128)(2,1)S(1)} %pad_maximum_fusion.3), channel_id=1, source_target_pairs={{0,9},{1,8},{2,11},{3,10},{4,13},{5,12},{6,15},{7,14},{8,1},{9,0},... | collective-permute-start | bytes 294920 | tf_op jit(solution)/shard_map/ppermute | solution.py:26
  20.5 4.6 %collective-permute-start.2 = (bf16[64,768]{1,0:T(8,128)(2,1)S(1)}, bf16[64,768]{1,0:T(8,128)(2,1)S(1)}, u32[]{:S(2)}, u32[]{:S(2)}) collective-permute-start(bf16[64,768]{1,0:T(8,128)(2,1)S(1)} %pad_maximum_fusion.3), channel_id=1, source_target_pairs={{0,8},{1,9},{2,10},{3,11},{4,12},{5,13},{6,14},{7,15},{8,0},{9,1},... | collective-permute-start | bytes 294920 | tf_op jit(solution)/shard_map/ppermute | solution.py:26
  20.5 4.6 %collective-permute-start.1 = (bf16[64,768]{1,0:T(8,128)(2,1)S(1)}, bf16[64,768]{1,0:T(8,128)(2,1)S(1)}, u32[]{:S(2)}, u32[]{:S(2)}) collective-permute-start(bf16[64,768]{1,0:T(8,128)(2,1)S(1)} %pad_maximum_fusion.3), channel_id=1, source_target_pairs={{0,1},{1,0},{2,3},{3,2},{4,5},{5,4},{6,7},{7,6},{8,9},{9,8},{10,11... | collective-permute-start | bytes 294920 | tf_op jit(solution)/shard_map/ppermute | solution.py:26
  21.9 9.2 %collective-permute-start.9 = (bf16[2,64,768]{2,1,0:T(8,128)(2,1)S(1)}, bf16[2,64,768]{2,1,0:T(8,128)(2,1)S(1)}, u32[]{:S(2)}, u32[]{:S(2)}) collective-permute-start(bf16[2,64,768]{2,1,0:T(8,128)(2,1)S(1)} %pad_maximum_fusion.1.refs_0_), channel_id=1, source_target_pairs={{0,2},{1,3},{2,0},{3,1},{4,6},{5,7},{6,4},{7,5},{8,10},{9,11},{10,... | collective-permute-start | bytes 589832 | tf_op jit(solution)/shard_map/ppermute | solution.py:26
  22.0 7.3 %collective-permute-start.8 = (bf16[2,64,768]{2,1,0:T(8,128)(2,1)S(1)}, bf16[2,64,768]{2,1,0:T(8,128)(2,1)S(1)}, u32[]{:S(2)}, u32[]{:S(2)}) collective-permute-start(bf16[2,64,768]{2,1,0:T(8,128)(2,1)S(1)} %pad_maximum_fusion.2.refs_1_), channel_id=1, source_target_pairs={{0,4},{1,5},{2,6},{3,7},{4,0},{5,1},{6,2},{7,3},{8,12},{9,13},{10,... | collective-permute-start | bytes 589832 | tf_op jit(solution)/shard_map/ppermute | solution.py:26
  23.7 7.3 %collective-permute-start.10 = (bf16[2,64,768]{2,1,0:T(8,128)(2,1)S(1)}, bf16[2,64,768]{2,1,0:T(8,128)(2,1)S(1)}, u32[]{:S(2)}, u32[]{:S(2)}) collective-permute-start(bf16[2,64,768]{2,1,0:T(8,128)(2,1)S(1)} %pad_maximum_fusion.2.refs_1_), channel_id=1, source_target_pairs={{0,2},{1,3},{2,0},{3,1},{4,6},{5,7},{6,4},{7,5},{8,10},{9,11},{10,... | collective-permute-start | bytes 589832 | tf_op jit(solution)/shard_map/ppermute | solution.py:26
  25.1 5.9 %collective-permute-start.11 = (bf16[2,64,768]{2,1,0:T(8,128)(2,1)S(1)}, bf16[2,64,768]{2,1,0:T(8,128)(2,1)S(1)}, u32[]{:S(2)}, u32[]{:S(2)}) collective-permute-start(bf16[2,64,768]{2,1,0:T(8,128)(2,1)S(1)} %collective-permute-done.7.refs_2_), channel_id=1, source_target_pairs={{0,2},{1,3},{2,0},{3,1},{4,6},{5,7},{6,4},{7,5},{8,10},{9,11},{10,... | collective-permute-start | bytes 589832 | tf_op jit(solution)/shard_map/ppermute | solution.py:26
  29.3 1.8 %collective-permute-start.12 = (bf16[2,64,768]{2,1,0:T(8,128)(2,1)S(1)}, bf16[2,64,768]{2,1,0:T(8,128)(2,1)S(1)}, u32[]{:S(2)}, u32[]{:S(2)}) collective-permute-start(bf16[2,64,768]{2,1,0:T(8,128)(2,1)S(1)} %collective-permute-done.8.refs_3_), channel_id=1, source_target_pairs={{0,2},{1,3},{2,0},{3,1},{4,6},{5,7},{6,4},{7,5},{8,10},{9,11},{10,... | collective-permute-start | bytes 589832 | tf_op jit(solution)/shard_map/ppermute | solution.py:26
  29.3 16.6 %collective-permute-start.25 = (bf16[2,96,768]{2,1,0:T(8,128)(2,1)S(1)}, bf16[2,96,768]{2,1,0:T(8,128)(2,1)S(1)}, u32[]{:S(2)}, u32[]{:S(2)}) collective-permute-start(bf16[2,96,768]{2,1,0:T(8,128)(2,1)S(1)} %pad_maximum_fusion.refs_0_), channel_id=1, source_target_pairs={{0,16},{1,17},{2,18},{3,19},{4,20},{5,21},{6,22},{7,23},{8,24},{9,... | collective-permute-start | bytes 884744 | tf_op jit(solution)/shard_map/ppermute | solution.py:26
  31.7 9.4 %copy-start = (s32[2]{0:T(128)S(1)}, s32[2]{0:T(128)}, u32[]{:S(2)}) copy-start(s32[2]{0:T(128)} %lengths_ref.7) | copy-start | bytes 28
  31.7 6.4 %collective-permute-start.13 = (bf16[256,256]{1,0:T(8,128)(2,1)S(1)}, bf16[256,256]{1,0:T(8,128)(2,1)S(1)}, u32[]{:S(2)}, u32[]{:S(2)}) collective-permute-start(bf16[256,256]{1,0:T(8,128)(2,1)S(1)} %get-tuple-element.215.refs_0_.pair_ref), channel_id=1, source_target_pairs={{0,4},{1,5},{2,6},{3,7},{4,0},{5,1},{6,2},{7,3},{8,12},{9,13},{10,... | collective-permute-start | bytes 393224 | tf_op jit(solution)/shard_map/ppermute | solution.py:26
  33.3 7.8 %collective-permute-start.14 = (bf16[256,256]{1,0:T(8,128)(2,1)S(1)}, bf16[256,256]{1,0:T(8,128)(2,1)S(1)}, u32[]{:S(2)}, u32[]{:S(2)}) collective-permute-start(bf16[256,256]{1,0:T(8,128)(2,1)S(1)} %get-tuple-element.215.refs_0_.pair_ref), channel_id=1, source_target_pairs={{0,2},{1,3},{2,0},{3,1},{4,6},{5,7},{6,4},{7,5},{8,10},{9,11},{10,... | collective-permute-start | bytes 393224 | tf_op jit(solution)/shard_map/ppermute | solution.py:26
  33.3 5.5 %collective-permute-start.16 = (bf16[256,128]{1,0:T(8,128)(2,1)S(1)}, bf16[256,128]{1,0:T(8,128)(2,1)S(1)}, u32[]{:S(2)}, u32[]{:S(2)}) collective-permute-start(bf16[256,128]{1,0:T(8,128)(2,1)S(1)} %get-tuple-element.164.refs_4_.rest_ref), channel_id=1, source_target_pairs={{0,4},{1,5},{2,6},{3,7},{4,0},{5,1},{6,2},{7,3},{8,12},{9,13},{10,... | collective-permute-start | bytes 196616 | tf_op jit(solution)/shard_map/ppermute | solution.py:26
  38.1 2.9 %collective-permute-start.15 = (bf16[256,256]{1,0:T(8,128)(2,1)S(1)}, bf16[256,256]{1,0:T(8,128)(2,1)S(1)}, u32[]{:S(2)}, u32[]{:S(2)}) collective-permute-start(bf16[256,256]{1,0:T(8,128)(2,1)S(1)} %collective-permute-done.13.refs_1_), channel_id=1, source_target_pairs={{0,2},{1,3},{2,0},{3,1},{4,6},{5,7},{6,4},{7,5},{8,10},{9,11},{10,... | collective-permute-start | bytes 393224 | tf_op jit(solution)/shard_map/ppermute | solution.py:26
  38.1 1.4 collective-permute-start.17
  38.8 2.2 %collective-permute-start.18 = (bf16[256,128]{1,0:T(8,128)(2,1)S(1)}, bf16[256,128]{1,0:T(8,128)(2,1)S(1)}, u32[]{:S(2)}, u32[]{:S(2)}) collective-permute-start(bf16[256,128]{1,0:T(8,128)(2,1)S(1)} %collective-permute-done.16.refs_5_), channel_id=1, source_target_pairs={{0,2},{1,3},{2,0},{3,1},{4,6},{5,7},{6,4},{7,5},{8,10},{9,11},{10,... | collective-permute-start | bytes 196616 | tf_op jit(solution)/shard_map/ppermute | solution.py:26
  39.6 15.4 %collective-permute-start.26 = (bf16[2,96,768]{2,1,0:T(8,128)(2,1)S(1)}, bf16[2,96,768]{2,1,0:T(8,128)(2,1)S(1)}, u32[]{:S(2)}, u32[]{:S(2)}) collective-permute-start(bf16[2,96,768]{2,1,0:T(8,128)(2,1)S(1)} %pad_maximum_fusion.refs_0_), channel_id=1, source_target_pairs={{0,4},{1,5},{2,6},{3,7},{4,0},{5,1},{6,2},{7,3},{8,12},{9,13},{10,... | collective-permute-start | bytes 884744 | tf_op jit(solution)/shard_map/ppermute | solution.py:26
  45.9 9.2 %collective-permute-start.27 = (bf16[2,96,768]{2,1,0:T(8,128)(2,1)S(1)}, bf16[2,96,768]{2,1,0:T(8,128)(2,1)S(1)}, u32[]{:S(2)}, u32[]{:S(2)}) collective-permute-start(bf16[2,96,768]{2,1,0:T(8,128)(2,1)S(1)} %collective-permute-done.25.refs_1_), channel_id=1, source_target_pairs={{0,4},{1,5},{2,6},{3,7},{4,0},{5,1},{6,2},{7,3},{8,12},{9,13},{10,... | collective-permute-start | bytes 884744 | tf_op jit(solution)/shard_map/ppermute | solution.py:26
  47.1 5.6 %collective-permute-start.19 = (bf16[64,768]{1,0:T(8,128)(2,1)S(1)}, bf16[64,768]{1,0:T(8,128)(2,1)S(1)}, u32[]{:S(2)}, u32[]{:S(2)}) collective-permute-start(bf16[64,768]{1,0:T(8,128)(2,1)S(1)} %get-tuple-element.167), channel_id=1, source_target_pairs={{0,8},{1,9},{2,10},{3,11},{4,12},{5,13},{6,14},{7,15},{8,0},{9,1},... | collective-permute-start | bytes 294920 | tf_op jit(solution)/shard_map/ppermute | solution.py:26
  47.1 5.6 %collective-permute-start.20 = (bf16[64,768]{1,0:T(8,128)(2,1)S(1)}, bf16[64,768]{1,0:T(8,128)(2,1)S(1)}, u32[]{:S(2)}, u32[]{:S(2)}) collective-permute-start(bf16[64,768]{1,0:T(8,128)(2,1)S(1)} %get-tuple-element.168), channel_id=1, source_target_pairs={{0,1},{1,0},{2,3},{3,2},{4,5},{5,4},{6,7},{7,6},{8,9},{9,8},{10,11... | collective-permute-start | bytes 294920 | tf_op jit(solution)/shard_map/ppermute | solution.py:26
  48.6 6.2 %collective-permute-start.21 = (bf16[64,768]{1,0:T(8,128)(2,1)S(1)}, bf16[64,768]{1,0:T(8,128)(2,1)S(1)}, u32[]{:S(2)}, u32[]{:S(2)}) collective-permute-start(bf16[64,768]{1,0:T(8,128)(2,1)S(1)} %get-tuple-element.169), channel_id=1, source_target_pairs={{0,9},{1,8},{2,11},{3,10},{4,13},{5,12},{6,15},{7,14},{8,1},{9,0},... | collective-permute-start | bytes 294920 | tf_op jit(solution)/shard_map/ppermute | solution.py:26
  55.1 3.7 %collective-permute-start.28 = (bf16[2,96,768]{2,1,0:T(8,128)(2,1)S(1)}, bf16[2,96,768]{2,1,0:T(8,128)(2,1)S(1)}, u32[]{:S(2)}, u32[]{:S(2)}) collective-permute-start(bf16[2,96,768]{2,1,0:T(8,128)(2,1)S(1)} %pad_maximum_fusion.refs_0_), channel_id=1, source_target_pairs={{0,2},{1,3},{2,0},{3,1},{4,6},{5,7},{6,4},{7,5},{8,10},{9,11},{10,... | collective-permute-start | bytes 884744 | tf_op jit(solution)/shard_map/ppermute | solution.py:26
  55.1 3.7 %collective-permute-start.29 = (bf16[2,96,768]{2,1,0:T(8,128)(2,1)S(1)}, bf16[2,96,768]{2,1,0:T(8,128)(2,1)S(1)}, u32[]{:S(2)}, u32[]{:S(2)}) collective-permute-start(bf16[2,96,768]{2,1,0:T(8,128)(2,1)S(1)} %collective-permute-done.25.refs_1_), channel_id=1, source_target_pairs={{0,2},{1,3},{2,0},{3,1},{4,6},{5,7},{6,4},{7,5},{8,10},{9,11},{10,... | collective-permute-start | bytes 884744 | tf_op jit(solution)/shard_map/ppermute | solution.py:26
  55.6 4.4 %collective-permute-start.30 = (bf16[2,96,768]{2,1,0:T(8,128)(2,1)S(1)}, bf16[2,96,768]{2,1,0:T(8,128)(2,1)S(1)}, u32[]{:S(2)}, u32[]{:S(2)}) collective-permute-start(bf16[2,96,768]{2,1,0:T(8,128)(2,1)S(1)} %collective-permute-done.26.refs_2_), channel_id=1, source_target_pairs={{0,2},{1,3},{2,0},{3,1},{4,6},{5,7},{6,4},{7,5},{8,10},{9,11},{10,... | collective-permute-start | bytes 884744 | tf_op jit(solution)/shard_map/ppermute | solution.py:26
  55.7 4.3 %collective-permute-start.31 = (bf16[2,96,768]{2,1,0:T(8,128)(2,1)S(1)}, bf16[2,96,768]{2,1,0:T(8,128)(2,1)S(1)}, u32[]{:S(2)}, u32[]{:S(2)}) collective-permute-start(bf16[2,96,768]{2,1,0:T(8,128)(2,1)S(1)} %collective-permute-done.27.refs_3_), channel_id=1, source_target_pairs={{0,2},{1,3},{2,0},{3,1},{4,6},{5,7},{6,4},{7,5},{8,10},{9,11},{10,... | collective-permute-start | bytes 884744 | tf_op jit(solution)/shard_map/ppermute | solution.py:26
  56.1 6.4 %collective-permute-start.24 = (bf16[64,768]{1,0:T(8,128)(2,1)S(1)}, bf16[64,768]{1,0:T(8,128)(2,1)S(1)}, u32[]{:S(2)}, u32[]{:S(2)}) collective-permute-start(bf16[64,768]{1,0:T(8,128)(2,1)S(1)} %get-tuple-element.171.own_ref), channel_id=1, source_target_pairs={{0,9},{1,8},{2,11},{3,10},{4,13},{5,12},{6,15},{7,14},{8,1},{9,0},... | collective-permute-start | bytes 294920 | tf_op jit(solution)/shard_map/ppermute | solution.py:26
  58.9 4.8 %collective-permute-start.23 = (bf16[64,768]{1,0:T(8,128)(2,1)S(1)}, bf16[64,768]{1,0:T(8,128)(2,1)S(1)}, u32[]{:S(2)}, u32[]{:S(2)}) collective-permute-start(bf16[64,768]{1,0:T(8,128)(2,1)S(1)} %get-tuple-element.171.own_ref), channel_id=1, source_target_pairs={{0,8},{1,9},{2,10},{3,11},{4,12},{5,13},{6,14},{7,15},{8,0},{9,1},... | collective-permute-start | bytes 294920 | tf_op jit(solution)/shard_map/ppermute | solution.py:26
  58.9 5.2 %collective-permute-start.22 = (bf16[64,768]{1,0:T(8,128)(2,1)S(1)}, bf16[64,768]{1,0:T(8,128)(2,1)S(1)}, u32[]{:S(2)}, u32[]{:S(2)}) collective-permute-start(bf16[64,768]{1,0:T(8,128)(2,1)S(1)} %get-tuple-element.171.own_ref), channel_id=1, source_target_pairs={{0,1},{1,0},{2,3},{3,2},{4,5},{5,4},{6,7},{7,6},{8,9},{9,8},{10,11... | collective-permute-start | bytes 294920 | tf_op jit(solution)/shard_map/ppermute | solution.py:26
  65.7 4.7 %collective-permute-start.32 = (bf16[64,768]{1,0:T(8,128)(2,1)S(1)}, bf16[64,768]{1,0:T(8,128)(2,1)S(1)}, u32[]{:S(2)}, u32[]{:S(2)}) collective-permute-start(bf16[64,768]{1,0:T(8,128)(2,1)S(1)} %get-tuple-element.184), channel_id=1, source_target_pairs={{0,8},{1,9},{2,10},{3,11},{4,12},{5,13},{6,14},{7,15},{8,0},{9,1},... | collective-permute-start | bytes 294920 | tf_op jit(solution)/shard_map/ppermute | solution.py:26
  67.5 5.7 %collective-permute-start.33 = (bf16[64,768]{1,0:T(8,128)(2,1)S(1)}, bf16[64,768]{1,0:T(8,128)(2,1)S(1)}, u32[]{:S(2)}, u32[]{:S(2)}) collective-permute-start(bf16[64,768]{1,0:T(8,128)(2,1)S(1)} %get-tuple-element.185), channel_id=1, source_target_pairs={{0,1},{1,0},{2,3},{3,2},{4,5},{5,4},{6,7},{7,6},{8,9},{9,8},{10,11... | collective-permute-start | bytes 294920 | tf_op jit(solution)/shard_map/ppermute | solution.py:26
  68.9 5.5 %collective-permute-start.34 = (bf16[64,768]{1,0:T(8,128)(2,1)S(1)}, bf16[64,768]{1,0:T(8,128)(2,1)S(1)}, u32[]{:S(2)}, u32[]{:S(2)}) collective-permute-start(bf16[64,768]{1,0:T(8,128)(2,1)S(1)} %get-tuple-element.186), channel_id=1, source_target_pairs={{0,9},{1,8},{2,11},{3,10},{4,13},{5,12},{6,15},{7,14},{8,1},{9,0},... | collective-permute-start | bytes 294920 | tf_op jit(solution)/shard_map/ppermute | solution.py:26
  75.3 5.6 %collective-permute-start.37 = (bf16[64,768]{1,0:T(8,128)(2,1)S(1)}, bf16[64,768]{1,0:T(8,128)(2,1)S(1)}, u32[]{:S(2)}, u32[]{:S(2)}) collective-permute-start(bf16[64,768]{1,0:T(8,128)(2,1)S(1)} %get-tuple-element.189.own_ref), channel_id=1, source_target_pairs={{0,9},{1,8},{2,11},{3,10},{4,13},{5,12},{6,15},{7,14},{8,1},{9,0},... | collective-permute-start | bytes 294920 | tf_op jit(solution)/shard_map/ppermute | solution.py:26
  75.8 5.4 %collective-permute-start.36 = (bf16[64,768]{1,0:T(8,128)(2,1)S(1)}, bf16[64,768]{1,0:T(8,128)(2,1)S(1)}, u32[]{:S(2)}, u32[]{:S(2)}) collective-permute-start(bf16[64,768]{1,0:T(8,128)(2,1)S(1)} %get-tuple-element.189.own_ref), channel_id=1, source_target_pairs={{0,8},{1,9},{2,10},{3,11},{4,12},{5,13},{6,14},{7,15},{8,0},{9,1},... | collective-permute-start | bytes 294920 | tf_op jit(solution)/shard_map/ppermute | solution.py:26
  77.5 4.6 %collective-permute-start.35 = (bf16[64,768]{1,0:T(8,128)(2,1)S(1)}, bf16[64,768]{1,0:T(8,128)(2,1)S(1)}, u32[]{:S(2)}, u32[]{:S(2)}) collective-permute-start(bf16[64,768]{1,0:T(8,128)(2,1)S(1)} %get-tuple-element.189.own_ref), channel_id=1, source_target_pairs={{0,1},{1,0},{2,3},{3,2},{4,5},{5,4},{6,7},{7,6},{8,9},{9,8},{10,11... | collective-permute-start | bytes 294920 | tf_op jit(solution)/shard_map/ppermute | solution.py:26
  84.1 2.1 %collective-permute-start.38 = (bf16[8,48,768]{2,1,0:T(8,128)(2,1)S(1)}, bf16[8,48,768]{2,1,0:T(8,128)(2,1)S(1)}, u32[]{:S(2)}, u32[]{:S(2)}) collective-permute-start(bf16[8,48,768]{2,1,0:T(8,128)(2,1)S(1)} %get-tuple-element.196), channel_id=1, source_target_pairs={{0,2},{1,3},{2,0},{3,1},{4,6},{5,7},{6,4},{7,5},{8,10},{9,11},{10,... | collective-permute-start | bytes 1769480 | tf_op jit(solution)/shard_map/ppermute | solution.py:26
  84.2 2.8 %collective-permute-start.39 = (bf16[8,48,768]{2,1,0:T(8,128)(2,1)S(1)}, bf16[8,48,768]{2,1,0:T(8,128)(2,1)S(1)}, u32[]{:S(2)}, u32[]{:S(2)}) collective-permute-start(bf16[8,48,768]{2,1,0:T(8,128)(2,1)S(1)} %get-tuple-element.197), channel_id=1, source_target_pairs={{0,2},{1,3},{2,0},{3,1},{4,6},{5,7},{6,4},{7,5},{8,10},{9,11},{10,... | collective-permute-start | bytes 1769480 | tf_op jit(solution)/shard_map/ppermute | solution.py:26
  87.3 17.9 %collective-permute-start.46 = (bf16[4,48,1536]{2,1,0:T(8,128)(2,1)S(1)}, bf16[4,48,1536]{2,1,0:T(8,128)(2,1)S(1)}, u32[]{:S(2)}, u32[]{:S(2)}) collective-permute-start(bf16[4,48,1536]{2,1,0:T(8,128)(2,1)S(1)} %get-tuple-element.203), channel_id=1, source_target_pairs={{0,4},{1,5},{2,6},{3,7},{4,0},{5,1},{6,2},{7,3},{8,12},{9,13},{10,... | collective-permute-start | bytes 1769480 | tf_op jit(solution)/shard_map/ppermute | solution.py:26
  88.3 5.3 %collective-permute-start.40 = (bf16[64,768]{1,0:T(8,128)(2,1)S(1)}, bf16[64,768]{1,0:T(8,128)(2,1)S(1)}, u32[]{:S(2)}, u32[]{:S(2)}) collective-permute-start(bf16[64,768]{1,0:T(8,128)(2,1)S(1)} %get-tuple-element.204), channel_id=1, source_target_pairs={{0,8},{1,9},{2,10},{3,11},{4,12},{5,13},{6,14},{7,15},{8,0},{9,1},... | collective-permute-start | bytes 294920 | tf_op jit(solution)/shard_map/ppermute | solution.py:26
  89.0 5.3 %collective-permute-start.41 = (bf16[64,768]{1,0:T(8,128)(2,1)S(1)}, bf16[64,768]{1,0:T(8,128)(2,1)S(1)}, u32[]{:S(2)}, u32[]{:S(2)}) collective-permute-start(bf16[64,768]{1,0:T(8,128)(2,1)S(1)} %get-tuple-element.205), channel_id=1, source_target_pairs={{0,1},{1,0},{2,3},{3,2},{4,5},{5,4},{6,7},{7,6},{8,9},{9,8},{10,11... | collective-permute-start | bytes 294920 | tf_op jit(solution)/shard_map/ppermute | solution.py:26
  90.0 5.7 %collective-permute-start.42 = (bf16[64,768]{1,0:T(8,128)(2,1)S(1)}, bf16[64,768]{1,0:T(8,128)(2,1)S(1)}, u32[]{:S(2)}, u32[]{:S(2)}) collective-permute-start(bf16[64,768]{1,0:T(8,128)(2,1)S(1)} %get-tuple-element.206), channel_id=1, source_target_pairs={{0,9},{1,8},{2,11},{3,10},{4,13},{5,12},{6,15},{7,14},{8,1},{9,0},... | collective-permute-start | bytes 294920 | tf_op jit(solution)/shard_map/ppermute | solution.py:26
  96.0 5.7 %collective-permute-start.45 = (bf16[64,768]{1,0:T(8,128)(2,1)S(1)}, bf16[64,768]{1,0:T(8,128)(2,1)S(1)}, u32[]{:S(2)}, u32[]{:S(2)}) collective-permute-start(bf16[64,768]{1,0:T(8,128)(2,1)S(1)} %get-tuple-element.210.own_ref), channel_id=1, source_target_pairs={{0,9},{1,8},{2,11},{3,10},{4,13},{5,12},{6,15},{7,14},{8,1},{9,0},... | collective-permute-start | bytes 294920 | tf_op jit(solution)/shard_map/ppermute | solution.py:26
  98.0 4.6 %collective-permute-start.44 = (bf16[64,768]{1,0:T(8,128)(2,1)S(1)}, bf16[64,768]{1,0:T(8,128)(2,1)S(1)}, u32[]{:S(2)}, u32[]{:S(2)}) collective-permute-start(bf16[64,768]{1,0:T(8,128)(2,1)S(1)} %get-tuple-element.210.own_ref), channel_id=1, source_target_pairs={{0,8},{1,9},{2,10},{3,11},{4,12},{5,13},{6,14},{7,15},{8,0},{9,1},... | collective-permute-start | bytes 294920 | tf_op jit(solution)/shard_map/ppermute | solution.py:26
  98.5 4.6 %collective-permute-start.43 = (bf16[64,768]{1,0:T(8,128)(2,1)S(1)}, bf16[64,768]{1,0:T(8,128)(2,1)S(1)}, u32[]{:S(2)}, u32[]{:S(2)}) collective-permute-start(bf16[64,768]{1,0:T(8,128)(2,1)S(1)} %get-tuple-element.210.own_ref), channel_id=1, source_target_pairs={{0,1},{1,0},{2,3},{3,2},{4,5},{5,4},{6,7},{7,6},{8,9},{9,8},{10,11... | collective-permute-start | bytes 294920 | tf_op jit(solution)/shard_map/ppermute | solution.py:26
  104.0 6.4 %collective-permute-start.47 = (bf16[256,512]{1,0:T(8,128)(2,1)S(1)}, bf16[256,512]{1,0:T(8,128)(2,1)S(1)}, u32[]{:S(2)}, u32[]{:S(2)}) collective-permute-start(bf16[256,512]{1,0:T(8,128)(2,1)S(1)} %get-tuple-element.212.packet_ref.g0_ref), channel_id=1, source_target_pairs={{0,4},{1,5},{2,6},{3,7},{4,0},{5,1},{6,2},{7,3},{8,12},{9,13},{10,... | collective-permute-start | bytes 786440 | tf_op jit(solution)/shard_map/ppermute | solution.py:26
  105.3 13.7 %collective-permute-start.50 = (bf16[2,48,1536]{2,1,0:T(8,128)(2,1)S(1)}, bf16[2,48,1536]{2,1,0:T(8,128)(2,1)S(1)}, u32[]{:S(2)}, u32[]{:S(2)}) collective-permute-start(bf16[2,48,1536]{2,1,0:T(8,128)(2,1)S(1)} %get-tuple-element.222), channel_id=1, source_target_pairs={{0,16},{1,17},{2,18},{3,19},{4,20},{5,21},{6,22},{7,23},{8,24},{9,... | collective-permute-start | bytes 884744 | tf_op jit(solution)/shard_map/ppermute | solution.py:26
  107.0 4.7 %collective-permute-start.48 = (bf16[256,512]{1,0:T(8,128)(2,1)S(1)}, bf16[256,512]{1,0:T(8,128)(2,1)S(1)}, u32[]{:S(2)}, u32[]{:S(2)}) collective-permute-start(bf16[256,512]{1,0:T(8,128)(2,1)S(1)} %get-tuple-element.212.packet_ref.g0_ref), channel_id=1, source_target_pairs={{0,2},{1,3},{2,0},{3,1},{4,6},{5,7},{6,4},{7,5},{8,10},{9,11},{10,... | collective-permute-start | bytes 786440 | tf_op jit(solution)/shard_map/ppermute | solution.py:26
  110.5 1.5 %collective-permute-start.49 = (bf16[256,512]{1,0:T(8,128)(2,1)S(1)}, bf16[256,512]{1,0:T(8,128)(2,1)S(1)}, u32[]{:S(2)}, u32[]{:S(2)}) collective-permute-start(bf16[256,512]{1,0:T(8,128)(2,1)S(1)} %collective-permute-done.47.g1_ref), channel_id=1, source_target_pairs={{0,2},{1,3},{2,0},{3,1},{4,6},{5,7},{6,4},{7,5},{8,10},{9,11},{10,... | collective-permute-start | bytes 786440 | tf_op jit(solution)/shard_map/ppermute | solution.py:26
  110.6 8.4 %collective-permute-start.51 = (f32[16,768]{1,0:T(8,128)S(1)}, f32[16,768]{1,0:T(8,128)S(1)}, u32[]{:S(2)}, u32[]{:S(2)}) collective-permute-start(f32[16,768]{1,0:T(8,128)S(1)} %vectors.1.refs_4_), channel_id=1, source_target_pairs={{0,1},{1,0},{2,3},{3,2},{4,5},{5,4},{6,7},{7,6},{8,9},{9,8},{10,11... | collective-permute-start | bytes 147464 | tf_op jit(solution)/shard_map/ppermute | solution.py:26
  120.1 2.4 %collective-permute-start.53 = (bf16[8,48,704]{2,1,0:T(8,128)(2,1)S(1)}, bf16[8,48,704]{2,1,0:T(8,128)(2,1)S(1)}, u32[]{:S(2)}, u32[]{:S(2)}) collective-permute-start(bf16[8,48,704]{2,1,0:T(8,128)(2,1)S(1)} %get-tuple-element.231), channel_id=1, source_target_pairs={{0,2},{1,3},{2,0},{3,1},{4,6},{5,7},{6,4},{7,5},{8,10},{9,11},{10,... | collective-permute-start | bytes 1622024 | tf_op jit(solution)/shard_map/ppermute | solution.py:26
  120.2 2.3 %collective-permute-start.52 = (bf16[8,48,192]{2,1,0:T(8,128)(2,1)S(1)}, bf16[8,48,192]{2,1,0:T(8,128)(2,1)S(1)}, u32[]{:S(2)}, u32[]{:S(2)}) collective-permute-start(bf16[8,48,192]{2,1,0:T(8,128)(2,1)S(1)} %get-tuple-element.230), channel_id=1, source_target_pairs={{0,2},{1,3},{2,0},{3,1},{4,6},{5,7},{6,4},{7,5},{8,10},{9,11},{10,... | collective-permute-start | bytes 442376 | tf_op jit(solution)/shard_map/ppermute | solution.py:26
  122.7 10.6 %collective-permute-start.58 = (bf16[4,48,896]{2,1,0:T(8,128)(2,1)S(1)}, bf16[4,48,896]{2,1,0:T(8,128)(2,1)S(1)}, u32[]{:S(2)}, u32[]{:S(2)}) collective-permute-start(bf16[4,48,896]{2,1,0:T(8,128)(2,1)S(1)} %get-tuple-element.243), channel_id=1, source_target_pairs={{0,4},{1,5},{2,6},{3,7},{4,0},{5,1},{6,2},{7,3},{8,12},{9,13},{10,... | collective-permute-start | bytes 1032200 | tf_op jit(solution)/shard_map/ppermute | solution.py:26
  123.6 5.6 %collective-permute-start.54 = (bf16[64,768]{1,0:T(8,128)(2,1)S(1)}, bf16[64,768]{1,0:T(8,128)(2,1)S(1)}, u32[]{:S(2)}, u32[]{:S(2)}) collective-permute-start(bf16[64,768]{1,0:T(8,128)(2,1)S(1)} %get-tuple-element.234), channel_id=1, source_target_pairs={{0,8},{1,9},{2,10},{3,11},{4,12},{5,13},{6,14},{7,15},{8,0},{9,1},... | collective-permute-start | bytes 294920 | tf_op jit(solution)/shard_map/ppermute | solution.py:26
  123.6 5.6 %collective-permute-start.55 = (bf16[64,768]{1,0:T(8,128)(2,1)S(1)}, bf16[64,768]{1,0:T(8,128)(2,1)S(1)}, u32[]{:S(2)}, u32[]{:S(2)}) collective-permute-start(bf16[64,768]{1,0:T(8,128)(2,1)S(1)} %get-tuple-element.235), channel_id=1, source_target_pairs={{0,1},{1,0},{2,3},{3,2},{4,5},{5,4},{6,7},{7,6},{8,9},{9,8},{10,11... | collective-permute-start | bytes 294920 | tf_op jit(solution)/shard_map/ppermute | solution.py:26
  124.6 7.1 %collective-permute-start.56 = (bf16[64,768]{1,0:T(8,128)(2,1)S(1)}, bf16[64,768]{1,0:T(8,128)(2,1)S(1)}, u32[]{:S(2)}, u32[]{:S(2)}) collective-permute-start(bf16[64,768]{1,0:T(8,128)(2,1)S(1)} %get-tuple-element.236), channel_id=1, source_target_pairs={{0,9},{1,8},{2,11},{3,10},{4,13},{5,12},{6,15},{7,14},{8,1},{9,0},... | collective-permute-start | bytes 294920 | tf_op jit(solution)/shard_map/ppermute | solution.py:26
  127.1 10.8 %collective-permute-start.62 = (bf16[48,1536]{1,0:T(8,128)(2,1)S(1)}, bf16[48,1536]{1,0:T(8,128)(2,1)S(1)}, u32[]{:S(2)}, u32[]{:S(2)}) collective-permute-start(bf16[48,1536]{1,0:T(8,128)(2,1)S(1)} %get-tuple-element.249), channel_id=1, source_target_pairs={{0,8},{1,9},{2,10},{3,11},{4,12},{5,13},{6,14},{7,15},{8,0},{9,1},... | collective-permute-start | bytes 442376 | tf_op jit(solution)/shard_map/ppermute | solution.py:26
  131.8 11.3 %collective-permute-start.57 = (bf16[32,1536]{1,0:T(8,128)(2,1)S(1)}, bf16[32,1536]{1,0:T(8,128)(2,1)S(1)}, u32[]{:S(2)}, u32[]{:S(2)}) collective-permute-start(bf16[32,1536]{1,0:T(8,128)(2,1)S(1)} %get-tuple-element.240), channel_id=1, source_target_pairs={{0,16},{1,17},{2,18},{3,19},{4,20},{5,21},{6,22},{7,23},{8,24},{9,... | collective-permute-start | bytes 294920 | tf_op jit(solution)/shard_map/ppermute | solution.py:26
  133.4 10.4 %collective-permute-start.59 = (bf16[48,896]{1,0:T(8,128)(2,1)S(1)}, bf16[48,896]{1,0:T(8,128)(2,1)S(1)}, u32[]{:S(2)}, u32[]{:S(2)}) collective-permute-start(bf16[48,896]{1,0:T(8,128)(2,1)S(1)} %get-tuple-element.245), channel_id=1, source_target_pairs={{0,8},{1,9},{2,10},{3,11},{4,12},{5,13},{6,14},{7,15},{8,0},{9,1},... | collective-permute-start | bytes 258056 | tf_op jit(solution)/shard_map/ppermute | solution.py:26
  134.1 10.4 %collective-permute-start.60 = (bf16[48,896]{1,0:T(8,128)(2,1)S(1)}, bf16[48,896]{1,0:T(8,128)(2,1)S(1)}, u32[]{:S(2)}, u32[]{:S(2)}) collective-permute-start(bf16[48,896]{1,0:T(8,128)(2,1)S(1)} %get-tuple-element.246), channel_id=1, source_target_pairs={{0,16},{1,17},{2,18},{3,19},{4,20},{5,21},{6,22},{7,23},{8,24},{9,... | collective-permute-start | bytes 258056 | tf_op jit(solution)/shard_map/ppermute | solution.py:26
  136.3 8.2 %collective-permute-start.61 = (bf16[48,896]{1,0:T(8,128)(2,1)S(1)}, bf16[48,896]{1,0:T(8,128)(2,1)S(1)}, u32[]{:S(2)}, u32[]{:S(2)}) collective-permute-start(bf16[48,896]{1,0:T(8,128)(2,1)S(1)} %get-tuple-element.247), channel_id=1, source_target_pairs={{0,24},{1,25},{2,26},{3,27},{4,28},{5,29},{6,30},{7,31},{8,16},{9,... | collective-permute-start | bytes 258056 | tf_op jit(solution)/shard_map/ppermute | solution.py:26

commit v7 on v6

--- a/solution.py
+++ b/solution.py
@@ -700,7 +700,7 @@
 
 def hidden_kernel(
     own_ref, got1_ref, got2_ref, got3_ref, up_ref, down_ref, bias_ref,
-    keep_ref, send1_ref, send2_ref, send3_ref, active_ref, slope_ref, rows_ref,
+    keep_ref, send1_ref, send2_ref, send3_ref, active_ref, pre_ref, spread_ref, rows_ref,
 ):
     rows = jnp.concatenate([r[...] for r in (own_ref, got1_ref, got2_ref, got3_ref)], 0)
     rows_ref[...] = rows
@@ -708,8 +708,15 @@
     spread = spread_of(preact)
     active = (preact * spread).astype(low_type)
     active_ref[...] = active
-    slope_ref[...] = spread + preact * jnp.exp(-0.5 * preact * preact) * (2.0 * math.pi) ** (-0.5)
+    pre_ref[...] = preact
+    spread_ref[...] = spread
     give_out(mul(active, down_ref[...], 1, 1), keep_ref, (send1_ref, send2_ref, send3_ref))
+
+
+def slope_kernel(pre_ref, spread_ref, slope_ref):
+    preact = pre_ref[...]
+    density = jnp.exp(-0.5 * preact * preact) * (2.0 * math.pi) ** (-0.5)
+    slope_ref[...] = spread_ref[...] + preact * density
 
 
 def second_norm_kernel(
@@ -1070,6 +1077,7 @@
     )
     pair_parts, rest_parts = gather_parts(pair), gather_parts(rest)
     later_near_side = swap(tie(later_near, pair_parts[1]), BIT_SIDE)
+    near_core = swap(tie(later_near, pair_parts[1]), BIT_CORE)
     vectors, up_bias = run_kernel(
         lines_kernel,
         [((8, width), wide), ((1, unit_cols), wide)],
@@ -1088,6 +1096,7 @@
     )
     sends = send_team(sends)
     later_far_side = swap(tie(later_far, attended_low), BIT_SIDE)
+    far_core = swap(tie(later_far, sends[0]), BIT_CORE)
     first_out, first_low, normed, scale = run_kernel(
         first_norm_kernel,
         [(rows_shape, wide), (rows_shape, low_type), (rows_shape, wide), ((rows_here, 128), wide)],
@@ -1096,8 +1105,11 @@
         name="first_norm",
     )
     first_team = gather_team(first_low)
-    later_sides = tie((later_near, later_far, later_near_side, later_far_side), first_low)
-    later_pieces = later_sides + tuple(swap(part, BIT_CORE) for part in later_sides)
+    later_sides = later_near, later_far, later_near_side, later_far_side
+    waited = tie((later_near_side, later_far_side), first_low)
+    later_pieces = later_sides + (
+        near_core, far_core, swap(waited[0], BIT_CORE), swap(waited[1], BIT_CORE)
+    )
     up_weight, down_weight = run_kernel(
         full_kernel,
         [((width, unit_cols), low_type)] * 2,
@@ -1105,15 +1117,20 @@
         us=1.0,
         name="full_units",
     )
-    keep, s1, s2, s3, active, slope, first_rows = run_kernel(
+    keep, s1, s2, s3, active, preact, spread, first_rows = run_kernel(
         hidden_kernel,
         given
-        + [((group, unit_cols), low_type), ((group, unit_cols), wide), ((group, width), low_type)],
+        + [((group, unit_cols), low_type)]
+        + [((group, unit_cols), wide)] * 2
+        + [((group, width), low_type)],
         first_low, *first_team, up_weight, down_weight, up_bias,
         us=2.0,
         name="hidden",
     )
     sends = send_team((s1, s2, s3))
+    (slope,) = run_kernel(
+        slope_kernel, [((group, unit_cols), wide)], preact, spread, us=0.7, name="slope"
+    )
     output, second_grad, second_low, second_sums = run_kernel(
         second_norm_kernel,
         [(rows_shape, low_type), (rows_shape, wide), (rows_shape, low_type), ((8, width), wide)],

time: 146 us -> 145 us (level)
  waiting for transfers between devices: 60.9 us -> 59.2 us
    ppermute x63, waiting for transfers between devices: 60.9 us -> 59.2 us  [swap(): lax.ppermute(values, AXES, [(i, i ^ bit) for i in range(device_count())])]
    pallas_call x25 -> x26, Pallas kernels: 21.8 us -> 21.9 us  [run_kernel(): pl.pallas_call(body, out_shape=[jax.ShapeDtypeStruct(shape, kind) for sha...]
  transfers between devices with their start and end apart: 63 -> 63, of which waited for: 38 -> 37; matrix products, arithmetic and copies ran while one was open for 0% -> 0% of each run, Pallas kernels for 9% -> 9%
where the time goes in v7:
time: 145 us
  starting transfers between devices  62.6 us (43%)
  waiting for transfers between devices  59.2 us (41%)
  Pallas kernels  21.9 us (15%)
    ppermute x63, starting transfers between devices, swap(): lax.ppermute(values, AXES, [(i, i ^ bit) for i in range(device_count())])  62.6 us
    ppermute x63, waiting for transfers between devices, swap(): lax.ppermute(values, AXES, [(i, i ^ bit) for i in range(device_count())])  59.2 us
    pallas_call x26, Pallas kernels, run_kernel(): pl.pallas_call(body, out_shape=[jax.ShapeDtypeStruct(shape, kind) for sha...  21.9 us
  transfers between devices with their start and end apart: 63, of which 37 were waited for; matrix products, arithmetic and copies ran while one was open for 0% of the time, Pallas kernels for 9%

profile of v7, /device:TPU:0, one launch (start us, length us, event | category | flops | bytes accessed | tf_op | source)
XLA Modules:
  0.0 144.9 jit_solution(13500625472405766560)
XLA Ops:
  0.7 2.0 %pack.1 = (bf16[64,768]{1,0:T(8,128)(2,1)S(1)}, bf16[64,768]{1,0:T(8,128)(2,1)S(1)}, bf16[96,768]{1,0:T(8,128)(2,1)S(1)}, bf16[160,768]{1,0:T(8,128)(2,1)S(1)}, ...) custom-call(bf16[48,384]{1,0:T(8,128)(2,1)} %refs_0_.1, ...), custom_call_target="tpu_custom_call" | custom-call | flops 30000000 | bytes 30000 | tf_op jit(solution)/shard_map/pack/pallas_call | solution.py:413
  2.7 3.1 %collective-permute-start.4 = (bf16[160,768]{1,0:T(8,128)(2,1)S(1)}, bf16[160,768]{1,0:T(8,128)(2,1)S(1)}, u32[]{:S(2)}, u32[]{:S(2)}) collective-permute-start(bf16[160,768]{1,0:T(8,128)(2,1)S(1)} %get-tuple-element.148), channel_id=1, source_target_pairs={{0,8},{1,9},{2,10},{3,11},{4,12},{5,13},{6,14},{7,15},{8,0},{9,1},... | collective-permute-start | bytes 737288 | tf_op jit(solution)/shard_map/ppermute | solution.py:26
  5.8 2.6 %collective-permute-start = (bf16[64,768]{1,0:T(8,128)(2,1)S(1)}, bf16[64,768]{1,0:T(8,128)(2,1)S(1)}, u32[]{:S(2)}, u32[]{:S(2)}) collective-permute-start(bf16[64,768]{1,0:T(8,128)(2,1)S(1)} %get-tuple-element.144), channel_id=1, source_target_pairs={{0,16},{1,17},{2,18},{3,19},{4,20},{5,21},{6,22},{7,23},{8,24},{9,... | collective-permute-start | bytes 294920 | tf_op jit(solution)/shard_map/ppermute | solution.py:26
  8.4 1.9 %collective-permute-start.5 = (bf16[64,768]{1,0:T(8,128)(2,1)S(1)}, bf16[64,768]{1,0:T(8,128)(2,1)S(1)}, u32[]{:S(2)}, u32[]{:S(2)}) collective-permute-start(bf16[64,768]{1,0:T(8,128)(2,1)S(1)} %get-tuple-element.145), channel_id=1, source_target_pairs={{0,16},{1,17},{2,18},{3,19},{4,20},{5,21},{6,22},{7,23},{8,24},{9,... | collective-permute-start | bytes 294920 | tf_op jit(solution)/shard_map/ppermute | solution.py:26
  10.3 4.0 %collective-permute-done.got_ref.slot_ref = bf16[64,768]{1,0:T(8,128)(2,1)S(1)} collective-permute-done((bf16[64,768]{1,0:T(8,128)(2,1)S(1)}, bf16[64,768]{1,0:T(8,128)(2,1)S(1)}, u32[]{:S(2)}, u32[]{:S(2)}) %collective-permute-start) | collective-permute-done | bytes 98336 | tf_op jit(solution)/shard_map/ppermute | solution.py:26
  14.7 1.8 %collective-permute-start.7 = (bf16[2,64,768]{2,1,0:T(8,128)(2,1)S(1)}, bf16[2,64,768]{2,1,0:T(8,128)(2,1)S(1)}, u32[]{:S(2)}, u32[]{:S(2)}) collective-permute-start(bf16[2,64,768]{2,1,0:T(8,128)(2,1)S(1)} %pad_maximum_fusion.1.refs_0_), channel_id=1, source_target_pairs={{0,4},{1,5},{2,6},{3,7},{4,0},{5,1},{6,2},{7,3},{8,12},{9,13},{10,... | collective-permute-start | bytes 589832 | tf_op jit(solution)/shard_map/ppermute | solution.py:26
  16.5 4.0 %collective-permute-start.3 = (bf16[64,768]{1,0:T(8,128)(2,1)S(1)}, bf16[64,768]{1,0:T(8,128)(2,1)S(1)}, u32[]{:S(2)}, u32[]{:S(2)}) collective-permute-start(bf16[64,768]{1,0:T(8,128)(2,1)S(1)} %pad_maximum_fusion.3), channel_id=1, source_target_pairs={{0,9},{1,8},{2,11},{3,10},{4,13},{5,12},{6,15},{7,14},{8,1},{9,0},... | collective-permute-start | bytes 294920 | tf_op jit(solution)/shard_map/ppermute | solution.py:26
  22.0 1.5 %collective-permute-start.8 = (bf16[2,64,768]{2,1,0:T(8,128)(2,1)S(1)}, bf16[2,64,768]{2,1,0:T(8,128)(2,1)S(1)}, u32[]{:S(2)}, u32[]{:S(2)}) collective-permute-start(bf16[2,64,768]{2,1,0:T(8,128)(2,1)S(1)} %pad_maximum_fusion.2.refs_1_), channel_id=1, source_target_pairs={{0,4},{1,5},{2,6},{3,7},{4,0},{5,1},{6,2},{7,3},{8,12},{9,13},{10,... | collective-permute-start | bytes 589832 | tf_op jit(solution)/shard_map/ppermute | solution.py:26
  23.7 1.4 collective-permute-done.2.low_ref
  25.1 4.1 %collective-permute-done.8.refs_3_ = bf16[2,64,768]{2,1,0:T(8,128)(2,1)S(1)} collective-permute-done((bf16[2,64,768]{2,1,0:T(8,128)(2,1)S(1)}, bf16[2,64,768]{2,1,0:T(8,128)(2,1)S(1)}, u32[]{:S(2)}, u32[]{:S(2)}) %collective-permute-start.8) | collective-permute-done | bytes 196640 | tf_op jit(solution)/shard_map/ppermute | solution.py:26
  29.3 1.7 %collective-permute-start.25 = (bf16[2,96,768]{2,1,0:T(8,128)(2,1)S(1)}, bf16[2,96,768]{2,1,0:T(8,128)(2,1)S(1)}, u32[]{:S(2)}, u32[]{:S(2)}) collective-permute-start(bf16[2,96,768]{2,1,0:T(8,128)(2,1)S(1)} %pad_maximum_fusion.refs_0_), channel_id=1, source_target_pairs={{0,16},{1,17},{2,18},{3,19},{4,20},{5,21},{6,22},{7,23},{8,24},{9,... | collective-permute-start | bytes 884744 | tf_op jit(solution)/shard_map/ppermute | solution.py:26
  31.7 1.6 %collective-permute-start.13 = (bf16[256,256]{1,0:T(8,128)(2,1)S(1)}, bf16[256,256]{1,0:T(8,128)(2,1)S(1)}, u32[]{:S(2)}, u32[]{:S(2)}) collective-permute-start(bf16[256,256]{1,0:T(8,128)(2,1)S(1)} %get-tuple-element.215.refs_0_.pair_ref), channel_id=1, source_target_pairs={{0,4},{1,5},{2,6},{3,7},{4,0},{5,1},{6,2},{7,3},{8,12},{9,13},{10,... | collective-permute-start | bytes 393224 | tf_op jit(solution)/shard_map/ppermute | solution.py:26
  33.8 4.3 %collective-permute-done.13.refs_1_ = bf16[256,256]{1,0:T(8,128)(2,1)S(1)} collective-permute-done((bf16[256,256]{1,0:T(8,128)(2,1)S(1)}, bf16[256,256]{1,0:T(8,128)(2,1)S(1)}, u32[]{:S(2)}, u32[]{:S(2)}) %collective-permute-start.13) | collective-permute-done | bytes 131104 | tf_op jit(solution)/shard_map/ppermute | solution.py:26
  39.6 1.5 %collective-permute-start.26 = (bf16[2,96,768]{2,1,0:T(8,128)(2,1)S(1)}, bf16[2,96,768]{2,1,0:T(8,128)(2,1)S(1)}, u32[]{:S(2)}, u32[]{:S(2)}) collective-permute-start(bf16[2,96,768]{2,1,0:T(8,128)(2,1)S(1)} %pad_maximum_fusion.refs_0_), channel_id=1, source_target_pairs={{0,4},{1,5},{2,6},{3,7},{4,0},{5,1},{6,2},{7,3},{8,12},{9,13},{10,... | collective-permute-start | bytes 884744 | tf_op jit(solution)/shard_map/ppermute | solution.py:26
  41.1 2.8 %attend.1 = (bf16[256,192]{1,0:T(8,128)(2,1)S(1)}, f32[256,128]{1,0:T(8,128)S(1)}, f32[64,768]{1,0:T(8,128)S(1)}, bf16[64,768]{1,0:T(8,128)(2,1)S(1)}, bf16[64,7...) custom-call(s32[2]{0:T(128)S(1)} %copy-done, bf16[256,192]{1,0:T(8,128)(2,1)S(1)} %get-tuple-element.163.query_ref, ...), custom_call_target="tpu_custom_call" | custom-call | flops 30000000 | bytes 30000 | tf_op jit(solution)/shard_map/attend/pallas_call | solution.py:413
  43.9 2.0 %collective-permute-done.25.refs_1_ = bf16[2,96,768]{2,1,0:T(8,128)(2,1)S(1)} collective-permute-done((bf16[2,96,768]{2,1,0:T(8,128)(2,1)S(1)}, bf16[2,96,768]{2,1,0:T(8,128)(2,1)S(1)}, u32[]{:S(2)}, u32[]{:S(2)}) %collective-permute-start.25) | collective-permute-done | bytes 294944 | tf_op jit(solution)/shard_map/ppermute | solution.py:26
  45.9 1.2 collective-permute-start.27
  47.1 1.5 %collective-permute-start.20 = (bf16[64,768]{1,0:T(8,128)(2,1)S(1)}, bf16[64,768]{1,0:T(8,128)(2,1)S(1)}, u32[]{:S(2)}, u32[]{:S(2)}) collective-permute-start(bf16[64,768]{1,0:T(8,128)(2,1)S(1)} %get-tuple-element.168), channel_id=1, source_target_pairs={{0,1},{1,0},{2,3},{3,2},{4,5},{5,4},{6,7},{7,6},{8,9},{9,8},{10,11... | collective-permute-start | bytes 294920 | tf_op jit(solution)/shard_map/ppermute | solution.py:26
  48.6 2.0 %collective-permute-start.21 = (bf16[64,768]{1,0:T(8,128)(2,1)S(1)}, bf16[64,768]{1,0:T(8,128)(2,1)S(1)}, u32[]{:S(2)}, u32[]{:S(2)}) collective-permute-start(bf16[64,768]{1,0:T(8,128)(2,1)S(1)} %get-tuple-element.169), channel_id=1, source_target_pairs={{0,9},{1,8},{2,11},{3,10},{4,13},{5,12},{6,15},{7,14},{8,1},{9,0},... | collective-permute-start | bytes 294920 | tf_op jit(solution)/shard_map/ppermute | solution.py:26
  50.6 2.1 %collective-permute-done.19.got1_ref = bf16[64,768]{1,0:T(8,128)(2,1)S(1)} collective-permute-done((bf16[64,768]{1,0:T(8,128)(2,1)S(1)}, bf16[64,768]{1,0:T(8,128)(2,1)S(1)}, u32[]{:S(2)}, u32[]{:S(2)}) %collective-permute-start.19) | collective-permute-done | bytes 98336 | tf_op jit(solution)/shard_map/ppermute | solution.py:26
  53.2 1.6 %collective-permute-done.21.got3_ref = bf16[64,768]{1,0:T(8,128)(2,1)S(1)} collective-permute-done((bf16[64,768]{1,0:T(8,128)(2,1)S(1)}, bf16[64,768]{1,0:T(8,128)(2,1)S(1)}, u32[]{:S(2)}, u32[]{:S(2)}) %collective-permute-start.21) | collective-permute-done | bytes 98336 | tf_op jit(solution)/shard_map/ppermute | solution.py:26
  55.6 2.7 %collective-permute-start.24 = (bf16[64,768]{1,0:T(8,128)(2,1)S(1)}, bf16[64,768]{1,0:T(8,128)(2,1)S(1)}, u32[]{:S(2)}, u32[]{:S(2)}) collective-permute-start(bf16[64,768]{1,0:T(8,128)(2,1)S(1)} %get-tuple-element.171.own_ref), channel_id=1, source_target_pairs={{0,9},{1,8},{2,11},{3,10},{4,13},{5,12},{6,15},{7,14},{8,1},{9,0},... | collective-permute-start | bytes 294920 | tf_op jit(solution)/shard_map/ppermute | solution.py:26
  59.3 2.7 %collective-permute-done.24.got3_ref = bf16[64,768]{1,0:T(8,128)(2,1)S(1)} collective-permute-done((bf16[64,768]{1,0:T(8,128)(2,1)S(1)}, bf16[64,768]{1,0:T(8,128)(2,1)S(1)}, u32[]{:S(2)}, u32[]{:S(2)}) %collective-permute-start.24) | collective-permute-done | bytes 98336 | tf_op jit(solution)/shard_map/ppermute | solution.py:26
  62.1 1.1 collective-permute-done.23.got2_ref
  63.5 1.5 %hidden.1 = (f32[64,768]{1,0:T(8,128)S(1)}, bf16[64,768]{1,0:T(8,128)(2,1)S(1)}, bf16[64,768]{1,0:T(8,128)(2,1)S(1)}, bf16[64,768]{1,0:T(8,128)(2,1)S(1)}, bf16[...) custom-call(bf16[64,768]{1,0:T(8,128)(2,1)S(1)} %get-tuple-element.171., ...), custom_call_target="tpu_custom_call" | custom-call | flops 20000000 | bytes 20000 | tf_op jit(solution)/shard_map/hidden/pallas_call | solution.py:413
  65.0 1.9 %collective-permute-start.32 = (bf16[64,768]{1,0:T(8,128)(2,1)S(1)}, bf16[64,768]{1,0:T(8,128)(2,1)S(1)}, u32[]{:S(2)}, u32[]{:S(2)}) collective-permute-start(bf16[64,768]{1,0:T(8,128)(2,1)S(1)} %get-tuple-element.183), channel_id=1, source_target_pairs={{0,8},{1,9},{2,10},{3,11},{4,12},{5,13},{6,14},{7,15},{8,0},{9,1},... | collective-permute-start | bytes 294920 | tf_op jit(solution)/shard_map/ppermute | solution.py:26
  66.9 1.3 collective-permute-start.33
  68.6 1.2 collective-permute-done.32.got1_ref
  69.8 2.8 %collective-permute-done.33.got2_ref = bf16[64,768]{1,0:T(8,128)(2,1)S(1)} collective-permute-done((bf16[64,768]{1,0:T(8,128)(2,1)S(1)}, bf16[64,768]{1,0:T(8,128)(2,1)S(1)}, u32[]{:S(2)}, u32[]{:S(2)}) %collective-permute-start.33) | collective-permute-done | bytes 98336 | tf_op jit(solution)/shard_map/ppermute | solution.py:26
  72.6 1.2 collective-permute-done.34.got3_ref
  73.7 0.9 second_norm.1
  75.2 1.7 %collective-permute-start.36 = (bf16[64,768]{1,0:T(8,128)(2,1)S(1)}, bf16[64,768]{1,0:T(8,128)(2,1)S(1)}, u32[]{:S(2)}, u32[]{:S(2)}) collective-permute-start(bf16[64,768]{1,0:T(8,128)(2,1)S(1)} %get-tuple-element.188.own_ref), channel_id=1, source_target_pairs={{0,8},{1,9},{2,10},{3,11},{4,12},{5,13},{6,14},{7,15},{8,0},{9,1},... | collective-permute-start | bytes 294920 | tf_op jit(solution)/shard_map/ppermute | solution.py:26
  76.9 1.3 collective-permute-start.35
  78.4 1.8 %collective-permute-done.37.got3_ref = bf16[64,768]{1,0:T(8,128)(2,1)S(1)} collective-permute-done((bf16[64,768]{1,0:T(8,128)(2,1)S(1)}, bf16[64,768]{1,0:T(8,128)(2,1)S(1)}, u32[]{:S(2)}, u32[]{:S(2)}) %collective-permute-start.37) | collective-permute-done | bytes 98336 | tf_op jit(solution)/shard_map/ppermute | solution.py:26
  80.5 1.0 collective-permute-done.35.got1_ref
  81.5 0.9 hidden_back.1
  82.4 1.1 unit_weights.1
  84.1 1.5 %collective-permute-done.38.refs_1_ = bf16[8,48,768]{2,1,0:T(8,128)(2,1)S(1)} collective-permute-done((bf16[8,48,768]{2,1,0:T(8,128)(2,1)S(1)}, bf16[8,48,768]{2,1,0:T(8,128)(2,1)S(1)}, u32[]{:S(2)}, u32[]{:S(2)}) %collective-permute-start.38) | collective-permute-done | bytes 589856 | tf_op jit(solution)/shard_map/ppermute | solution.py:26
  86.7 1.0 collective-permute-start.46
  88.4 1.0 collective-permute-start.41
  89.4 1.8 %collective-permute-start.42 = (bf16[64,768]{1,0:T(8,128)(2,1)S(1)}, bf16[64,768]{1,0:T(8,128)(2,1)S(1)}, u32[]{:S(2)}, u32[]{:S(2)}) collective-permute-start(bf16[64,768]{1,0:T(8,128)(2,1)S(1)} %get-tuple-element.206), channel_id=1, source_target_pairs={{0,9},{1,8},{2,11},{3,10},{4,13},{5,12},{6,15},{7,14},{8,1},{9,0},... | collective-permute-start | bytes 294920 | tf_op jit(solution)/shard_map/ppermute | solution.py:26
  91.2 1.8 %collective-permute-done.40.got1_ref = bf16[64,768]{1,0:T(8,128)(2,1)S(1)} collective-permute-done((bf16[64,768]{1,0:T(8,128)(2,1)S(1)}, bf16[64,768]{1,0:T(8,128)(2,1)S(1)}, u32[]{:S(2)}, u32[]{:S(2)}) %collective-permute-start.40) | collective-permute-done | bytes 98336 | tf_op jit(solution)/shard_map/ppermute | solution.py:26
  93.7 1.3 collective-permute-done.42.got3_ref
  95.3 2.0 %collective-permute-start.45 = (bf16[64,768]{1,0:T(8,128)(2,1)S(1)}, bf16[64,768]{1,0:T(8,128)(2,1)S(1)}, u32[]{:S(2)}, u32[]{:S(2)}) collective-permute-start(bf16[64,768]{1,0:T(8,128)(2,1)S(1)} %get-tuple-element.210.own_ref), channel_id=1, source_target_pairs={{0,9},{1,8},{2,11},{3,10},{4,13},{5,12},{6,15},{7,14},{8,1},{9,0},... | collective-permute-start | bytes 294920 | tf_op jit(solution)/shard_map/ppermute | solution.py:26
  97.9 1.0 collective-permute-start.43
  98.9 2.2 %collective-permute-done.45.got3_ref = bf16[64,768]{1,0:T(8,128)(2,1)S(1)} collective-permute-done((bf16[64,768]{1,0:T(8,128)(2,1)S(1)}, bf16[64,768]{1,0:T(8,128)(2,1)S(1)}, u32[]{:S(2)}, u32[]{:S(2)}) %collective-permute-start.45) | collective-permute-done | bytes 98336 | tf_op jit(solution)/shard_map/ppermute | solution.py:26
  101.1 0.9 collective-permute-done.44.got2_ref
  102.5 0.9 attended_back.1
  103.4 1.2 collective-permute-start.47
  104.7 2.1 %collective-permute-start.50 = (bf16[2,48,1536]{2,1,0:T(8,128)(2,1)S(1)}, bf16[2,48,1536]{2,1,0:T(8,128)(2,1)S(1)}, u32[]{:S(2)}, u32[]{:S(2)}) collective-permute-start(bf16[2,48,1536]{2,1,0:T(8,128)(2,1)S(1)} %get-tuple-element.222), channel_id=1, source_target_pairs={{0,16},{1,17},{2,18},{3,19},{4,20},{5,21},{6,22},{7,23},{8,24},{9,... | collective-permute-start | bytes 884744 | tf_op jit(solution)/shard_map/ppermute | solution.py:26
  106.8 2.6 %query_back.1 = (bf16[256,192]{1,0:T(8,128)(2,1)S(1)}, f32[1,192]{1,0:T(1,128)S(1)}) custom-call(s32[2]{0:T(128)S(1)} %copy-done, bf16[256,512]{1,0:T(8,128)(2,1)S(1)} %get-tuple-element.212.packet_ref.g0_ref, bf16[256,256]{1,0:T(8,128)(2,1)S(1)} %get-tuple-element.215.refs_0_.pair_ref, bf16[256,256]{1,0:T(8,128)(2,1)S(1)} %collective-permute-done.13.refs_1_, ...), custom_call_target="tpu_custom_call" | custom-call | flops 30000000 | bytes 30000 | tf_op jit(solution)/shard_map/query_back/pallas_call | solution.py:413
  110.1 1.4 collective-permute-start.51
  111.5 3.0 %pair_back.1 = (f32[64,768]{1,0:T(8,128)S(1)}, bf16[64,768]{1,0:T(8,128)(2,1)S(1)}, bf16[64,768]{1,0:T(8,128)(2,1)S(1)}, bf16[64,768]{1,0:T(8,128)(2,1)S(1)}, bf16[256,576]{1,0:T(8,128)(2,1)S(1)}) custom-call(s32[2]{0:T(128)S(1)} %copy-done, bf16[256,256]{1,0:T(8,128)(2,1)S(1)} %get-tuple-element.215.refs_0_.pair_ref, ...), custom_call_target="tpu_custom_call" | custom-call | flops 40000000 | bytes 40000 | tf_op jit(solution)/shard_map/pair_back/pallas_call | solution.py:413
  114.5 3.8 %collective-permute-done.50.refs_1_ = bf16[2,48,1536]{2,1,0:T(8,128)(2,1)S(1)} collective-permute-done((bf16[2,48,1536]{2,1,0:T(8,128)(2,1)S(1)}, bf16[2,48,1536]{2,1,0:T(8,128)(2,1)S(1)}, u32[]{:S(2)}, u32[]{:S(2)}) %collective-permute-start.50) | collective-permute-done | bytes 294944 | tf_op jit(solution)/shard_map/ppermute | solution.py:26
  118.4 1.1 head_weights.1
  120.1 1.8 %collective-permute-done.52.refs_1_ = bf16[8,48,192]{2,1,0:T(8,128)(2,1)S(1)} collective-permute-done((bf16[8,48,192]{2,1,0:T(8,128)(2,1)S(1)}, bf16[8,48,192]{2,1,0:T(8,128)(2,1)S(1)}, u32[]{:S(2)}, u32[]{:S(2)}) %collective-permute-start.52) | collective-permute-done | bytes 147488 | tf_op jit(solution)/shard_map/ppermute | solution.py:26
  123.0 1.0 collective-permute-start.55
  124.0 2.5 %collective-permute-start.56 = (bf16[64,768]{1,0:T(8,128)(2,1)S(1)}, bf16[64,768]{1,0:T(8,128)(2,1)S(1)}, u32[]{:S(2)}, u32[]{:S(2)}) collective-permute-start(bf16[64,768]{1,0:T(8,128)(2,1)S(1)} %get-tuple-element.236), channel_id=1, source_target_pairs={{0,9},{1,8},{2,11},{3,10},{4,13},{5,12},{6,15},{7,14},{8,1},{9,0},... | collective-permute-start | bytes 294920 | tf_op jit(solution)/shard_map/ppermute | solution.py:26
  126.6 2.0 %collective-permute-done.54.got1_ref = bf16[64,768]{1,0:T(8,128)(2,1)S(1)} collective-permute-done((bf16[64,768]{1,0:T(8,128)(2,1)S(1)}, bf16[64,768]{1,0:T(8,128)(2,1)S(1)}, u32[]{:S(2)}, u32[]{:S(2)}) %collective-permute-start.54) | collective-permute-done | bytes 98336 | tf_op jit(solution)/shard_map/ppermute | solution.py:26
  128.6 2.5 %collective-permute-done.56.got3_ref = bf16[64,768]{1,0:T(8,128)(2,1)S(1)} collective-permute-done((bf16[64,768]{1,0:T(8,128)(2,1)S(1)}, bf16[64,768]{1,0:T(8,128)(2,1)S(1)}, u32[]{:S(2)}, u32[]{:S(2)}) %collective-permute-start.56) | collective-permute-done | bytes 98336 | tf_op jit(solution)/shard_map/ppermute | solution.py:26
  131.2 2.0 %collective-permute-start.57 = (bf16[32,1536]{1,0:T(8,128)(2,1)S(1)}, bf16[32,1536]{1,0:T(8,128)(2,1)S(1)}, u32[]{:S(2)}, u32[]{:S(2)}) collective-permute-start(bf16[32,1536]{1,0:T(8,128)(2,1)S(1)} %get-tuple-element.240), channel_id=1, source_target_pairs={{0,16},{1,17},{2,18},{3,19},{4,20},{5,21},{6,22},{7,23},{8,24},{9,... | collective-permute-start | bytes 294920 | tf_op jit(solution)/shard_map/ppermute | solution.py:26
  133.9 1.8 %collective-permute-start.60 = (bf16[48,896]{1,0:T(8,128)(2,1)S(1)}, bf16[48,896]{1,0:T(8,128)(2,1)S(1)}, u32[]{:S(2)}, u32[]{:S(2)}) collective-permute-start(bf16[48,896]{1,0:T(8,128)(2,1)S(1)} %get-tuple-element.246), channel_id=1, source_target_pairs={{0,16},{1,17},{2,18},{3,19},{4,20},{5,21},{6,22},{7,23},{8,24},{9,... | collective-permute-start | bytes 258056 | tf_op jit(solution)/shard_map/ppermute | solution.py:26
  135.7 2.0 %collective-permute-start.61 = (bf16[48,896]{1,0:T(8,128)(2,1)S(1)}, bf16[48,896]{1,0:T(8,128)(2,1)S(1)}, u32[]{:S(2)}, u32[]{:S(2)}) collective-permute-start(bf16[48,896]{1,0:T(8,128)(2,1)S(1)} %get-tuple-element.247), channel_id=1, source_target_pairs={{0,24},{1,25},{2,26},{3,27},{4,28},{5,29},{6,30},{7,31},{8,16},{9,... | collective-permute-start | bytes 258056 | tf_op jit(solution)/shard_map/ppermute | solution.py:26
  138.5 3.9 %collective-permute-done.57.got_ref = bf16[32,1536]{1,0:T(8,128)(2,1)S(1)} collective-permute-done((bf16[32,1536]{1,0:T(8,128)(2,1)S(1)}, bf16[32,1536]{1,0:T(8,128)(2,1)S(1)}, u32[]{:S(2)}, u32[]{:S(2)}) %collective-permute-start.57) | collective-permute-done | bytes 98336 | tf_op jit(solution)/shard_map/ppermute | solution.py:26
  (97 shorter events, 20.0 us)
Async XLA Ops:
  2.7 11.9 %collective-permute-start.4 = (bf16[160,768]{1,0:T(8,128)(2,1)S(1)}, bf16[160,768]{1,0:T(8,128)(2,1)S(1)}, u32[]{:S(2)}, u32[]{:S(2)}) collective-permute-start(bf16[160,768]{1,0:T(8,128)(2,1)S(1)} %get-tuple-element.148), channel_id=1, source_target_pairs={{0,8},{1,9},{2,10},{3,11},{4,12},{5,13},{6,14},{7,15},{8,0},{9,1},... | collective-permute-start | bytes 737288 | tf_op jit(solution)/shard_map/ppermute | solution.py:26
  5.8 8.5 %collective-permute-start = (bf16[64,768]{1,0:T(8,128)(2,1)S(1)}, bf16[64,768]{1,0:T(8,128)(2,1)S(1)}, u32[]{:S(2)}, u32[]{:S(2)}) collective-permute-start(bf16[64,768]{1,0:T(8,128)(2,1)S(1)} %get-tuple-element.144), channel_id=1, source_target_pairs={{0,16},{1,17},{2,18},{3,19},{4,20},{5,21},{6,22},{7,23},{8,24},{9,... | collective-permute-start | bytes 294920 | tf_op jit(solution)/shard_map/ppermute | solution.py:26
  8.4 12.1 %collective-permute-start.6 = (bf16[64,768]{1,0:T(8,128)(2,1)S(1)}, bf16[64,768]{1,0:T(8,128)(2,1)S(1)}, u32[]{:S(2)}, u32[]{:S(2)}) collective-permute-start(bf16[64,768]{1,0:T(8,128)(2,1)S(1)} %get-tuple-element.146), channel_id=1, source_target_pairs={{0,24},{1,25},{2,26},{3,27},{4,28},{5,29},{6,30},{7,31},{8,16},{9,... | collective-permute-start | bytes 294920 | tf_op jit(solution)/shard_map/ppermute | solution.py:26
  8.4 13.4 %collective-permute-start.5 = (bf16[64,768]{1,0:T(8,128)(2,1)S(1)}, bf16[64,768]{1,0:T(8,128)(2,1)S(1)}, u32[]{:S(2)}, u32[]{:S(2)}) collective-permute-start(bf16[64,768]{1,0:T(8,128)(2,1)S(1)} %get-tuple-element.145), channel_id=1, source_target_pairs={{0,16},{1,17},{2,18},{3,19},{4,20},{5,21},{6,22},{7,23},{8,24},{9,... | collective-permute-start | bytes 294920 | tf_op jit(solution)/shard_map/ppermute | solution.py:26
  14.7 7.2 %collective-permute-start.7 = (bf16[2,64,768]{2,1,0:T(8,128)(2,1)S(1)}, bf16[2,64,768]{2,1,0:T(8,128)(2,1)S(1)}, u32[]{:S(2)}, u32[]{:S(2)}) collective-permute-start(bf16[2,64,768]{2,1,0:T(8,128)(2,1)S(1)} %pad_maximum_fusion.1.refs_0_), channel_id=1, source_target_pairs={{0,4},{1,5},{2,6},{3,7},{4,0},{5,1},{6,2},{7,3},{8,12},{9,13},{10,... | collective-permute-start | bytes 589832 | tf_op jit(solution)/shard_map/ppermute | solution.py:26
  16.5 7.3 %collective-permute-start.3 = (bf16[64,768]{1,0:T(8,128)(2,1)S(1)}, bf16[64,768]{1,0:T(8,128)(2,1)S(1)}, u32[]{:S(2)}, u32[]{:S(2)}) collective-permute-start(bf16[64,768]{1,0:T(8,128)(2,1)S(1)} %pad_maximum_fusion.3), channel_id=1, source_target_pairs={{0,9},{1,8},{2,11},{3,10},{4,13},{5,12},{6,15},{7,14},{8,1},{9,0},... | collective-permute-start | bytes 294920 | tf_op jit(solution)/shard_map/ppermute | solution.py:26
  20.5 4.6 %collective-permute-start.2 = (bf16[64,768]{1,0:T(8,128)(2,1)S(1)}, bf16[64,768]{1,0:T(8,128)(2,1)S(1)}, u32[]{:S(2)}, u32[]{:S(2)}) collective-permute-start(bf16[64,768]{1,0:T(8,128)(2,1)S(1)} %pad_maximum_fusion.3), channel_id=1, source_target_pairs={{0,8},{1,9},{2,10},{3,11},{4,12},{5,13},{6,14},{7,15},{8,0},{9,1},... | collective-permute-start | bytes 294920 | tf_op jit(solution)/shard_map/ppermute | solution.py:26
  20.5 4.6 %collective-permute-start.1 = (bf16[64,768]{1,0:T(8,128)(2,1)S(1)}, bf16[64,768]{1,0:T(8,128)(2,1)S(1)}, u32[]{:S(2)}, u32[]{:S(2)}) collective-permute-start(bf16[64,768]{1,0:T(8,128)(2,1)S(1)} %pad_maximum_fusion.3), channel_id=1, source_target_pairs={{0,1},{1,0},{2,3},{3,2},{4,5},{5,4},{6,7},{7,6},{8,9},{9,8},{10,11... | collective-permute-start | bytes 294920 | tf_op jit(solution)/shard_map/ppermute | solution.py:26
  21.9 9.2 %collective-permute-start.9 = (bf16[2,64,768]{2,1,0:T(8,128)(2,1)S(1)}, bf16[2,64,768]{2,1,0:T(8,128)(2,1)S(1)}, u32[]{:S(2)}, u32[]{:S(2)}) collective-permute-start(bf16[2,64,768]{2,1,0:T(8,128)(2,1)S(1)} %pad_maximum_fusion.1.refs_0_), channel_id=1, source_target_pairs={{0,2},{1,3},{2,0},{3,1},{4,6},{5,7},{6,4},{7,5},{8,10},{9,11},{10,... | collective-permute-start | bytes 589832 | tf_op jit(solution)/shard_map/ppermute | solution.py:26
  22.0 7.3 %collective-permute-start.8 = (bf16[2,64,768]{2,1,0:T(8,128)(2,1)S(1)}, bf16[2,64,768]{2,1,0:T(8,128)(2,1)S(1)}, u32[]{:S(2)}, u32[]{:S(2)}) collective-permute-start(bf16[2,64,768]{2,1,0:T(8,128)(2,1)S(1)} %pad_maximum_fusion.2.refs_1_), channel_id=1, source_target_pairs={{0,4},{1,5},{2,6},{3,7},{4,0},{5,1},{6,2},{7,3},{8,12},{9,13},{10,... | collective-permute-start | bytes 589832 | tf_op jit(solution)/shard_map/ppermute | solution.py:26
  23.7 7.3 %collective-permute-start.10 = (bf16[2,64,768]{2,1,0:T(8,128)(2,1)S(1)}, bf16[2,64,768]{2,1,0:T(8,128)(2,1)S(1)}, u32[]{:S(2)}, u32[]{:S(2)}) collective-permute-start(bf16[2,64,768]{2,1,0:T(8,128)(2,1)S(1)} %pad_maximum_fusion.2.refs_1_), channel_id=1, source_target_pairs={{0,2},{1,3},{2,0},{3,1},{4,6},{5,7},{6,4},{7,5},{8,10},{9,11},{10,... | collective-permute-start | bytes 589832 | tf_op jit(solution)/shard_map/ppermute | solution.py:26
  25.1 5.9 %collective-permute-start.11 = (bf16[2,64,768]{2,1,0:T(8,128)(2,1)S(1)}, bf16[2,64,768]{2,1,0:T(8,128)(2,1)S(1)}, u32[]{:S(2)}, u32[]{:S(2)}) collective-permute-start(bf16[2,64,768]{2,1,0:T(8,128)(2,1)S(1)} %collective-permute-done.7.refs_2_), channel_id=1, source_target_pairs={{0,2},{1,3},{2,0},{3,1},{4,6},{5,7},{6,4},{7,5},{8,10},{9,11},{10,... | collective-permute-start | bytes 589832 | tf_op jit(solution)/shard_map/ppermute | solution.py:26
  29.3 1.8 %collective-permute-start.12 = (bf16[2,64,768]{2,1,0:T(8,128)(2,1)S(1)}, bf16[2,64,768]{2,1,0:T(8,128)(2,1)S(1)}, u32[]{:S(2)}, u32[]{:S(2)}) collective-permute-start(bf16[2,64,768]{2,1,0:T(8,128)(2,1)S(1)} %collective-permute-done.8.refs_3_), channel_id=1, source_target_pairs={{0,2},{1,3},{2,0},{3,1},{4,6},{5,7},{6,4},{7,5},{8,10},{9,11},{10,... | collective-permute-start | bytes 589832 | tf_op jit(solution)/shard_map/ppermute | solution.py:26
  29.3 16.6 %collective-permute-start.25 = (bf16[2,96,768]{2,1,0:T(8,128)(2,1)S(1)}, bf16[2,96,768]{2,1,0:T(8,128)(2,1)S(1)}, u32[]{:S(2)}, u32[]{:S(2)}) collective-permute-start(bf16[2,96,768]{2,1,0:T(8,128)(2,1)S(1)} %pad_maximum_fusion.refs_0_), channel_id=1, source_target_pairs={{0,16},{1,17},{2,18},{3,19},{4,20},{5,21},{6,22},{7,23},{8,24},{9,... | collective-permute-start | bytes 884744 | tf_op jit(solution)/shard_map/ppermute | solution.py:26
  31.7 9.4 %copy-start = (s32[2]{0:T(128)S(1)}, s32[2]{0:T(128)}, u32[]{:S(2)}) copy-start(s32[2]{0:T(128)} %lengths_ref.7) | copy-start | bytes 28
  31.7 6.4 %collective-permute-start.13 = (bf16[256,256]{1,0:T(8,128)(2,1)S(1)}, bf16[256,256]{1,0:T(8,128)(2,1)S(1)}, u32[]{:S(2)}, u32[]{:S(2)}) collective-permute-start(bf16[256,256]{1,0:T(8,128)(2,1)S(1)} %get-tuple-element.215.refs_0_.pair_ref), channel_id=1, source_target_pairs={{0,4},{1,5},{2,6},{3,7},{4,0},{5,1},{6,2},{7,3},{8,12},{9,13},{10,... | collective-permute-start | bytes 393224 | tf_op jit(solution)/shard_map/ppermute | solution.py:26
  33.3 7.8 %collective-permute-start.14 = (bf16[256,256]{1,0:T(8,128)(2,1)S(1)}, bf16[256,256]{1,0:T(8,128)(2,1)S(1)}, u32[]{:S(2)}, u32[]{:S(2)}) collective-permute-start(bf16[256,256]{1,0:T(8,128)(2,1)S(1)} %get-tuple-element.215.refs_0_.pair_ref), channel_id=1, source_target_pairs={{0,2},{1,3},{2,0},{3,1},{4,6},{5,7},{6,4},{7,5},{8,10},{9,11},{10,... | collective-permute-start | bytes 393224 | tf_op jit(solution)/shard_map/ppermute | solution.py:26
  33.3 5.5 %collective-permute-start.16 = (bf16[256,128]{1,0:T(8,128)(2,1)S(1)}, bf16[256,128]{1,0:T(8,128)(2,1)S(1)}, u32[]{:S(2)}, u32[]{:S(2)}) collective-permute-start(bf16[256,128]{1,0:T(8,128)(2,1)S(1)} %get-tuple-element.164.refs_4_.rest_ref), channel_id=1, source_target_pairs={{0,4},{1,5},{2,6},{3,7},{4,0},{5,1},{6,2},{7,3},{8,12},{9,13},{10,... | collective-permute-start | bytes 196616 | tf_op jit(solution)/shard_map/ppermute | solution.py:26
  38.1 2.9 %collective-permute-start.15 = (bf16[256,256]{1,0:T(8,128)(2,1)S(1)}, bf16[256,256]{1,0:T(8,128)(2,1)S(1)}, u32[]{:S(2)}, u32[]{:S(2)}) collective-permute-start(bf16[256,256]{1,0:T(8,128)(2,1)S(1)} %collective-permute-done.13.refs_1_), channel_id=1, source_target_pairs={{0,2},{1,3},{2,0},{3,1},{4,6},{5,7},{6,4},{7,5},{8,10},{9,11},{10,... | collective-permute-start | bytes 393224 | tf_op jit(solution)/shard_map/ppermute | solution.py:26
  38.1 1.4 collective-permute-start.17
  38.8 2.2 %collective-permute-start.18 = (bf16[256,128]{1,0:T(8,128)(2,1)S(1)}, bf16[256,128]{1,0:T(8,128)(2,1)S(1)}, u32[]{:S(2)}, u32[]{:S(2)}) collective-permute-start(bf16[256,128]{1,0:T(8,128)(2,1)S(1)} %collective-permute-done.16.refs_5_), channel_id=1, source_target_pairs={{0,2},{1,3},{2,0},{3,1},{4,6},{5,7},{6,4},{7,5},{8,10},{9,11},{10,... | collective-permute-start | bytes 196616 | tf_op jit(solution)/shard_map/ppermute | solution.py:26
  39.6 15.4 %collective-permute-start.26 = (bf16[2,96,768]{2,1,0:T(8,128)(2,1)S(1)}, bf16[2,96,768]{2,1,0:T(8,128)(2,1)S(1)}, u32[]{:S(2)}, u32[]{:S(2)}) collective-permute-start(bf16[2,96,768]{2,1,0:T(8,128)(2,1)S(1)} %pad_maximum_fusion.refs_0_), channel_id=1, source_target_pairs={{0,4},{1,5},{2,6},{3,7},{4,0},{5,1},{6,2},{7,3},{8,12},{9,13},{10,... | collective-permute-start | bytes 884744 | tf_op jit(solution)/shard_map/ppermute | solution.py:26
  45.9 9.2 %collective-permute-start.27 = (bf16[2,96,768]{2,1,0:T(8,128)(2,1)S(1)}, bf16[2,96,768]{2,1,0:T(8,128)(2,1)S(1)}, u32[]{:S(2)}, u32[]{:S(2)}) collective-permute-start(bf16[2,96,768]{2,1,0:T(8,128)(2,1)S(1)} %collective-permute-done.25.refs_1_), channel_id=1, source_target_pairs={{0,4},{1,5},{2,6},{3,7},{4,0},{5,1},{6,2},{7,3},{8,12},{9,13},{10,... | collective-permute-start | bytes 884744 | tf_op jit(solution)/shard_map/ppermute | solution.py:26
  47.1 5.6 %collective-permute-start.19 = (bf16[64,768]{1,0:T(8,128)(2,1)S(1)}, bf16[64,768]{1,0:T(8,128)(2,1)S(1)}, u32[]{:S(2)}, u32[]{:S(2)}) collective-permute-start(bf16[64,768]{1,0:T(8,128)(2,1)S(1)} %get-tuple-element.167), channel_id=1, source_target_pairs={{0,8},{1,9},{2,10},{3,11},{4,12},{5,13},{6,14},{7,15},{8,0},{9,1},... | collective-permute-start | bytes 294920 | tf_op jit(solution)/shard_map/ppermute | solution.py:26
  47.1 5.6 %collective-permute-start.20 = (bf16[64,768]{1,0:T(8,128)(2,1)S(1)}, bf16[64,768]{1,0:T(8,128)(2,1)S(1)}, u32[]{:S(2)}, u32[]{:S(2)}) collective-permute-start(bf16[64,768]{1,0:T(8,128)(2,1)S(1)} %get-tuple-element.168), channel_id=1, source_target_pairs={{0,1},{1,0},{2,3},{3,2},{4,5},{5,4},{6,7},{7,6},{8,9},{9,8},{10,11... | collective-permute-start | bytes 294920 | tf_op jit(solution)/shard_map/ppermute | solution.py:26
  48.6 6.2 %collective-permute-start.21 = (bf16[64,768]{1,0:T(8,128)(2,1)S(1)}, bf16[64,768]{1,0:T(8,128)(2,1)S(1)}, u32[]{:S(2)}, u32[]{:S(2)}) collective-permute-start(bf16[64,768]{1,0:T(8,128)(2,1)S(1)} %get-tuple-element.169), channel_id=1, source_target_pairs={{0,9},{1,8},{2,11},{3,10},{4,13},{5,12},{6,15},{7,14},{8,1},{9,0},... | collective-permute-start | bytes 294920 | tf_op jit(solution)/shard_map/ppermute | solution.py:26
  52.7 5.7 %collective-permute-start.28 = (bf16[2,96,768]{2,1,0:T(8,128)(2,1)S(1)}, bf16[2,96,768]{2,1,0:T(8,128)(2,1)S(1)}, u32[]{:S(2)}, u32[]{:S(2)}) collective-permute-start(bf16[2,96,768]{2,1,0:T(8,128)(2,1)S(1)} %pad_maximum_fusion.refs_0_), channel_id=1, source_target_pairs={{0,2},{1,3},{2,0},{3,1},{4,6},{5,7},{6,4},{7,5},{8,10},{9,11},{10,... | collective-permute-start | bytes 884744 | tf_op jit(solution)/shard_map/ppermute | solution.py:26
  52.7 5.7 %collective-permute-start.29 = (bf16[2,96,768]{2,1,0:T(8,128)(2,1)S(1)}, bf16[2,96,768]{2,1,0:T(8,128)(2,1)S(1)}, u32[]{:S(2)}, u32[]{:S(2)}) collective-permute-start(bf16[2,96,768]{2,1,0:T(8,128)(2,1)S(1)} %collective-permute-done.25.refs_1_), channel_id=1, source_target_pairs={{0,2},{1,3},{2,0},{3,1},{4,6},{5,7},{6,4},{7,5},{8,10},{9,11},{10,... | collective-permute-start | bytes 884744 | tf_op jit(solution)/shard_map/ppermute | solution.py:26
  55.1 4.0 %collective-permute-start.30 = (bf16[2,96,768]{2,1,0:T(8,128)(2,1)S(1)}, bf16[2,96,768]{2,1,0:T(8,128)(2,1)S(1)}, u32[]{:S(2)}, u32[]{:S(2)}) collective-permute-start(bf16[2,96,768]{2,1,0:T(8,128)(2,1)S(1)} %collective-permute-done.26.refs_2_), channel_id=1, source_target_pairs={{0,2},{1,3},{2,0},{3,1},{4,6},{5,7},{6,4},{7,5},{8,10},{9,11},{10,... | collective-permute-start | bytes 884744 | tf_op jit(solution)/shard_map/ppermute | solution.py:26
  55.1 4.0 %collective-permute-start.31 = (bf16[2,96,768]{2,1,0:T(8,128)(2,1)S(1)}, bf16[2,96,768]{2,1,0:T(8,128)(2,1)S(1)}, u32[]{:S(2)}, u32[]{:S(2)}) collective-permute-start(bf16[2,96,768]{2,1,0:T(8,128)(2,1)S(1)} %collective-permute-done.27.refs_3_), channel_id=1, source_target_pairs={{0,2},{1,3},{2,0},{3,1},{4,6},{5,7},{6,4},{7,5},{8,10},{9,11},{10,... | collective-permute-start | bytes 884744 | tf_op jit(solution)/shard_map/ppermute | solution.py:26
  55.6 6.4 %collective-permute-start.24 = (bf16[64,768]{1,0:T(8,128)(2,1)S(1)}, bf16[64,768]{1,0:T(8,128)(2,1)S(1)}, u32[]{:S(2)}, u32[]{:S(2)}) collective-permute-start(bf16[64,768]{1,0:T(8,128)(2,1)S(1)} %get-tuple-element.171.own_ref), channel_id=1, source_target_pairs={{0,9},{1,8},{2,11},{3,10},{4,13},{5,12},{6,15},{7,14},{8,1},{9,0},... | collective-permute-start | bytes 294920 | tf_op jit(solution)/shard_map/ppermute | solution.py:26
  58.4 4.8 %collective-permute-start.23 = (bf16[64,768]{1,0:T(8,128)(2,1)S(1)}, bf16[64,768]{1,0:T(8,128)(2,1)S(1)}, u32[]{:S(2)}, u32[]{:S(2)}) collective-permute-start(bf16[64,768]{1,0:T(8,128)(2,1)S(1)} %get-tuple-element.171.own_ref), channel_id=1, source_target_pairs={{0,8},{1,9},{2,10},{3,11},{4,12},{5,13},{6,14},{7,15},{8,0},{9,1},... | collective-permute-start | bytes 294920 | tf_op jit(solution)/shard_map/ppermute | solution.py:26
  58.4 5.2 %collective-permute-start.22 = (bf16[64,768]{1,0:T(8,128)(2,1)S(1)}, bf16[64,768]{1,0:T(8,128)(2,1)S(1)}, u32[]{:S(2)}, u32[]{:S(2)}) collective-permute-start(bf16[64,768]{1,0:T(8,128)(2,1)S(1)} %get-tuple-element.171.own_ref), channel_id=1, source_target_pairs={{0,1},{1,0},{2,3},{3,2},{4,5},{5,4},{6,7},{7,6},{8,9},{9,8},{10,11... | collective-permute-start | bytes 294920 | tf_op jit(solution)/shard_map/ppermute | solution.py:26
  65.0 4.7 %collective-permute-start.32 = (bf16[64,768]{1,0:T(8,128)(2,1)S(1)}, bf16[64,768]{1,0:T(8,128)(2,1)S(1)}, u32[]{:S(2)}, u32[]{:S(2)}) collective-permute-start(bf16[64,768]{1,0:T(8,128)(2,1)S(1)} %get-tuple-element.183), channel_id=1, source_target_pairs={{0,8},{1,9},{2,10},{3,11},{4,12},{5,13},{6,14},{7,15},{8,0},{9,1},... | collective-permute-start | bytes 294920 | tf_op jit(solution)/shard_map/ppermute | solution.py:26
  66.9 5.7 %collective-permute-start.33 = (bf16[64,768]{1,0:T(8,128)(2,1)S(1)}, bf16[64,768]{1,0:T(8,128)(2,1)S(1)}, u32[]{:S(2)}, u32[]{:S(2)}) collective-permute-start(bf16[64,768]{1,0:T(8,128)(2,1)S(1)} %get-tuple-element.184), channel_id=1, source_target_pairs={{0,1},{1,0},{2,3},{3,2},{4,5},{5,4},{6,7},{7,6},{8,9},{9,8},{10,11... | collective-permute-start | bytes 294920 | tf_op jit(solution)/shard_map/ppermute | solution.py:26
  68.2 5.5 %collective-permute-start.34 = (bf16[64,768]{1,0:T(8,128)(2,1)S(1)}, bf16[64,768]{1,0:T(8,128)(2,1)S(1)}, u32[]{:S(2)}, u32[]{:S(2)}) collective-permute-start(bf16[64,768]{1,0:T(8,128)(2,1)S(1)} %get-tuple-element.185), channel_id=1, source_target_pairs={{0,9},{1,8},{2,11},{3,10},{4,13},{5,12},{6,15},{7,14},{8,1},{9,0},... | collective-permute-start | bytes 294920 | tf_op jit(solution)/shard_map/ppermute | solution.py:26
  74.7 5.6 %collective-permute-start.37 = (bf16[64,768]{1,0:T(8,128)(2,1)S(1)}, bf16[64,768]{1,0:T(8,128)(2,1)S(1)}, u32[]{:S(2)}, u32[]{:S(2)}) collective-permute-start(bf16[64,768]{1,0:T(8,128)(2,1)S(1)} %get-tuple-element.188.own_ref), channel_id=1, source_target_pairs={{0,9},{1,8},{2,11},{3,10},{4,13},{5,12},{6,15},{7,14},{8,1},{9,0},... | collective-permute-start | bytes 294920 | tf_op jit(solution)/shard_map/ppermute | solution.py:26
  75.2 5.4 %collective-permute-start.36 = (bf16[64,768]{1,0:T(8,128)(2,1)S(1)}, bf16[64,768]{1,0:T(8,128)(2,1)S(1)}, u32[]{:S(2)}, u32[]{:S(2)}) collective-permute-start(bf16[64,768]{1,0:T(8,128)(2,1)S(1)} %get-tuple-element.188.own_ref), channel_id=1, source_target_pairs={{0,8},{1,9},{2,10},{3,11},{4,12},{5,13},{6,14},{7,15},{8,0},{9,1},... | collective-permute-start | bytes 294920 | tf_op jit(solution)/shard_map/ppermute | solution.py:26
  76.9 4.6 %collective-permute-start.35 = (bf16[64,768]{1,0:T(8,128)(2,1)S(1)}, bf16[64,768]{1,0:T(8,128)(2,1)S(1)}, u32[]{:S(2)}, u32[]{:S(2)}) collective-permute-start(bf16[64,768]{1,0:T(8,128)(2,1)S(1)} %get-tuple-element.188.own_ref), channel_id=1, source_target_pairs={{0,1},{1,0},{2,3},{3,2},{4,5},{5,4},{6,7},{7,6},{8,9},{9,8},{10,11... | collective-permute-start | bytes 294920 | tf_op jit(solution)/shard_map/ppermute | solution.py:26
  83.5 2.1 %collective-permute-start.38 = (bf16[8,48,768]{2,1,0:T(8,128)(2,1)S(1)}, bf16[8,48,768]{2,1,0:T(8,128)(2,1)S(1)}, u32[]{:S(2)}, u32[]{:S(2)}) collective-permute-start(bf16[8,48,768]{2,1,0:T(8,128)(2,1)S(1)} %get-tuple-element.196), channel_id=1, source_target_pairs={{0,2},{1,3},{2,0},{3,1},{4,6},{5,7},{6,4},{7,5},{8,10},{9,11},{10,... | collective-permute-start | bytes 1769480 | tf_op jit(solution)/shard_map/ppermute | solution.py:26
  83.6 2.8 %collective-permute-start.39 = (bf16[8,48,768]{2,1,0:T(8,128)(2,1)S(1)}, bf16[8,48,768]{2,1,0:T(8,128)(2,1)S(1)}, u32[]{:S(2)}, u32[]{:S(2)}) collective-permute-start(bf16[8,48,768]{2,1,0:T(8,128)(2,1)S(1)} %get-tuple-element.197), channel_id=1, source_target_pairs={{0,2},{1,3},{2,0},{3,1},{4,6},{5,7},{6,4},{7,5},{8,10},{9,11},{10,... | collective-permute-start | bytes 1769480 | tf_op jit(solution)/shard_map/ppermute | solution.py:26
  86.7 17.9 %collective-permute-start.46 = (bf16[4,48,1536]{2,1,0:T(8,128)(2,1)S(1)}, bf16[4,48,1536]{2,1,0:T(8,128)(2,1)S(1)}, u32[]{:S(2)}, u32[]{:S(2)}) collective-permute-start(bf16[4,48,1536]{2,1,0:T(8,128)(2,1)S(1)} %get-tuple-element.203), channel_id=1, source_target_pairs={{0,4},{1,5},{2,6},{3,7},{4,0},{5,1},{6,2},{7,3},{8,12},{9,13},{10,... | collective-permute-start | bytes 1769480 | tf_op jit(solution)/shard_map/ppermute | solution.py:26
  87.7 5.3 %collective-permute-start.40 = (bf16[64,768]{1,0:T(8,128)(2,1)S(1)}, bf16[64,768]{1,0:T(8,128)(2,1)S(1)}, u32[]{:S(2)}, u32[]{:S(2)}) collective-permute-start(bf16[64,768]{1,0:T(8,128)(2,1)S(1)} %get-tuple-element.204), channel_id=1, source_target_pairs={{0,8},{1,9},{2,10},{3,11},{4,12},{5,13},{6,14},{7,15},{8,0},{9,1},... | collective-permute-start | bytes 294920 | tf_op jit(solution)/shard_map/ppermute | solution.py:26
  88.4 5.4 %collective-permute-start.41 = (bf16[64,768]{1,0:T(8,128)(2,1)S(1)}, bf16[64,768]{1,0:T(8,128)(2,1)S(1)}, u32[]{:S(2)}, u32[]{:S(2)}) collective-permute-start(bf16[64,768]{1,0:T(8,128)(2,1)S(1)} %get-tuple-element.205), channel_id=1, source_target_pairs={{0,1},{1,0},{2,3},{3,2},{4,5},{5,4},{6,7},{7,6},{8,9},{9,8},{10,11... | collective-permute-start | bytes 294920 | tf_op jit(solution)/shard_map/ppermute | solution.py:26
  89.4 5.7 %collective-permute-start.42 = (bf16[64,768]{1,0:T(8,128)(2,1)S(1)}, bf16[64,768]{1,0:T(8,128)(2,1)S(1)}, u32[]{:S(2)}, u32[]{:S(2)}) collective-permute-start(bf16[64,768]{1,0:T(8,128)(2,1)S(1)} %get-tuple-element.206), channel_id=1, source_target_pairs={{0,9},{1,8},{2,11},{3,10},{4,13},{5,12},{6,15},{7,14},{8,1},{9,0},... | collective-permute-start | bytes 294920 | tf_op jit(solution)/shard_map/ppermute | solution.py:26
  95.3 5.8 %collective-permute-start.45 = (bf16[64,768]{1,0:T(8,128)(2,1)S(1)}, bf16[64,768]{1,0:T(8,128)(2,1)S(1)}, u32[]{:S(2)}, u32[]{:S(2)}) collective-permute-start(bf16[64,768]{1,0:T(8,128)(2,1)S(1)} %get-tuple-element.210.own_ref), channel_id=1, source_target_pairs={{0,9},{1,8},{2,11},{3,10},{4,13},{5,12},{6,15},{7,14},{8,1},{9,0},... | collective-permute-start | bytes 294920 | tf_op jit(solution)/shard_map/ppermute | solution.py:26
  97.3 4.6 %collective-permute-start.44 = (bf16[64,768]{1,0:T(8,128)(2,1)S(1)}, bf16[64,768]{1,0:T(8,128)(2,1)S(1)}, u32[]{:S(2)}, u32[]{:S(2)}) collective-permute-start(bf16[64,768]{1,0:T(8,128)(2,1)S(1)} %get-tuple-element.210.own_ref), channel_id=1, source_target_pairs={{0,8},{1,9},{2,10},{3,11},{4,12},{5,13},{6,14},{7,15},{8,0},{9,1},... | collective-permute-start | bytes 294920 | tf_op jit(solution)/shard_map/ppermute | solution.py:26
  97.9 4.6 %collective-permute-start.43 = (bf16[64,768]{1,0:T(8,128)(2,1)S(1)}, bf16[64,768]{1,0:T(8,128)(2,1)S(1)}, u32[]{:S(2)}, u32[]{:S(2)}) collective-permute-start(bf16[64,768]{1,0:T(8,128)(2,1)S(1)} %get-tuple-element.210.own_ref), channel_id=1, source_target_pairs={{0,1},{1,0},{2,3},{3,2},{4,5},{5,4},{6,7},{7,6},{8,9},{9,8},{10,11... | collective-permute-start | bytes 294920 | tf_op jit(solution)/shard_map/ppermute | solution.py:26
  103.4 6.4 %collective-permute-start.47 = (bf16[256,512]{1,0:T(8,128)(2,1)S(1)}, bf16[256,512]{1,0:T(8,128)(2,1)S(1)}, u32[]{:S(2)}, u32[]{:S(2)}) collective-permute-start(bf16[256,512]{1,0:T(8,128)(2,1)S(1)} %get-tuple-element.212.packet_ref.g0_ref), channel_id=1, source_target_pairs={{0,4},{1,5},{2,6},{3,7},{4,0},{5,1},{6,2},{7,3},{8,12},{9,13},{10,... | collective-permute-start | bytes 786440 | tf_op jit(solution)/shard_map/ppermute | solution.py:26
  104.7 13.7 %collective-permute-start.50 = (bf16[2,48,1536]{2,1,0:T(8,128)(2,1)S(1)}, bf16[2,48,1536]{2,1,0:T(8,128)(2,1)S(1)}, u32[]{:S(2)}, u32[]{:S(2)}) collective-permute-start(bf16[2,48,1536]{2,1,0:T(8,128)(2,1)S(1)} %get-tuple-element.222), channel_id=1, source_target_pairs={{0,16},{1,17},{2,18},{3,19},{4,20},{5,21},{6,22},{7,23},{8,24},{9,... | collective-permute-start | bytes 884744 | tf_op jit(solution)/shard_map/ppermute | solution.py:26
  106.8 4.7 %collective-permute-start.48 = (bf16[256,512]{1,0:T(8,128)(2,1)S(1)}, bf16[256,512]{1,0:T(8,128)(2,1)S(1)}, u32[]{:S(2)}, u32[]{:S(2)}) collective-permute-start(bf16[256,512]{1,0:T(8,128)(2,1)S(1)} %get-tuple-element.212.packet_ref.g0_ref), channel_id=1, source_target_pairs={{0,2},{1,3},{2,0},{3,1},{4,6},{5,7},{6,4},{7,5},{8,10},{9,11},{10,... | collective-permute-start | bytes 786440 | tf_op jit(solution)/shard_map/ppermute | solution.py:26
  109.8 1.7 %collective-permute-start.49 = (bf16[256,512]{1,0:T(8,128)(2,1)S(1)}, bf16[256,512]{1,0:T(8,128)(2,1)S(1)}, u32[]{:S(2)}, u32[]{:S(2)}) collective-permute-start(bf16[256,512]{1,0:T(8,128)(2,1)S(1)} %collective-permute-done.47.g1_ref), channel_id=1, source_target_pairs={{0,2},{1,3},{2,0},{3,1},{4,6},{5,7},{6,4},{7,5},{8,10},{9,11},{10,... | collective-permute-start | bytes 786440 | tf_op jit(solution)/shard_map/ppermute | solution.py:26
  110.1 8.3 %collective-permute-start.51 = (f32[16,768]{1,0:T(8,128)S(1)}, f32[16,768]{1,0:T(8,128)S(1)}, u32[]{:S(2)}, u32[]{:S(2)}) collective-permute-start(f32[16,768]{1,0:T(8,128)S(1)} %vectors.1.refs_4_), channel_id=1, source_target_pairs={{0,1},{1,0},{2,3},{3,2},{4,5},{5,4},{6,7},{7,6},{8,9},{9,8},{10,11... | collective-permute-start | bytes 147464 | tf_op jit(solution)/shard_map/ppermute | solution.py:26
  119.5 2.4 %collective-permute-start.53 = (bf16[8,48,704]{2,1,0:T(8,128)(2,1)S(1)}, bf16[8,48,704]{2,1,0:T(8,128)(2,1)S(1)}, u32[]{:S(2)}, u32[]{:S(2)}) collective-permute-start(bf16[8,48,704]{2,1,0:T(8,128)(2,1)S(1)} %get-tuple-element.231), channel_id=1, source_target_pairs={{0,2},{1,3},{2,0},{3,1},{4,6},{5,7},{6,4},{7,5},{8,10},{9,11},{10,... | collective-permute-start | bytes 1622024 | tf_op jit(solution)/shard_map/ppermute | solution.py:26
  119.6 2.3 %collective-permute-start.52 = (bf16[8,48,192]{2,1,0:T(8,128)(2,1)S(1)}, bf16[8,48,192]{2,1,0:T(8,128)(2,1)S(1)}, u32[]{:S(2)}, u32[]{:S(2)}) collective-permute-start(bf16[8,48,192]{2,1,0:T(8,128)(2,1)S(1)} %get-tuple-element.230), channel_id=1, source_target_pairs={{0,2},{1,3},{2,0},{3,1},{4,6},{5,7},{6,4},{7,5},{8,10},{9,11},{10,... | collective-permute-start | bytes 442376 | tf_op jit(solution)/shard_map/ppermute | solution.py:26
  122.2 11.0 %collective-permute-start.58 = (bf16[4,48,896]{2,1,0:T(8,128)(2,1)S(1)}, bf16[4,48,896]{2,1,0:T(8,128)(2,1)S(1)}, u32[]{:S(2)}, u32[]{:S(2)}) collective-permute-start(bf16[4,48,896]{2,1,0:T(8,128)(2,1)S(1)} %get-tuple-element.243), channel_id=1, source_target_pairs={{0,4},{1,5},{2,6},{3,7},{4,0},{5,1},{6,2},{7,3},{8,12},{9,13},{10,... | collective-permute-start | bytes 1032200 | tf_op jit(solution)/shard_map/ppermute | solution.py:26
  123.0 5.6 %collective-permute-start.54 = (bf16[64,768]{1,0:T(8,128)(2,1)S(1)}, bf16[64,768]{1,0:T(8,128)(2,1)S(1)}, u32[]{:S(2)}, u32[]{:S(2)}) collective-permute-start(bf16[64,768]{1,0:T(8,128)(2,1)S(1)} %get-tuple-element.234), channel_id=1, source_target_pairs={{0,8},{1,9},{2,10},{3,11},{4,12},{5,13},{6,14},{7,15},{8,0},{9,1},... | collective-permute-start | bytes 294920 | tf_op jit(solution)/shard_map/ppermute | solution.py:26
  123.0 5.6 %collective-permute-start.55 = (bf16[64,768]{1,0:T(8,128)(2,1)S(1)}, bf16[64,768]{1,0:T(8,128)(2,1)S(1)}, u32[]{:S(2)}, u32[]{:S(2)}) collective-permute-start(bf16[64,768]{1,0:T(8,128)(2,1)S(1)} %get-tuple-element.235), channel_id=1, source_target_pairs={{0,1},{1,0},{2,3},{3,2},{4,5},{5,4},{6,7},{7,6},{8,9},{9,8},{10,11... | collective-permute-start | bytes 294920 | tf_op jit(solution)/shard_map/ppermute | solution.py:26
  124.0 7.1 %collective-permute-start.56 = (bf16[64,768]{1,0:T(8,128)(2,1)S(1)}, bf16[64,768]{1,0:T(8,128)(2,1)S(1)}, u32[]{:S(2)}, u32[]{:S(2)}) collective-permute-start(bf16[64,768]{1,0:T(8,128)(2,1)S(1)} %get-tuple-element.236), channel_id=1, source_target_pairs={{0,9},{1,8},{2,11},{3,10},{4,13},{5,12},{6,15},{7,14},{8,1},{9,0},... | collective-permute-start | bytes 294920 | tf_op jit(solution)/shard_map/ppermute | solution.py:26
  126.5 11.1 %collective-permute-start.62 = (bf16[48,1536]{1,0:T(8,128)(2,1)S(1)}, bf16[48,1536]{1,0:T(8,128)(2,1)S(1)}, u32[]{:S(2)}, u32[]{:S(2)}) collective-permute-start(bf16[48,1536]{1,0:T(8,128)(2,1)S(1)} %get-tuple-element.249), channel_id=1, source_target_pairs={{0,8},{1,9},{2,10},{3,11},{4,12},{5,13},{6,14},{7,15},{8,0},{9,1},... | collective-permute-start | bytes 442376 | tf_op jit(solution)/shard_map/ppermute | solution.py:26
  131.2 11.3 %collective-permute-start.57 = (bf16[32,1536]{1,0:T(8,128)(2,1)S(1)}, bf16[32,1536]{1,0:T(8,128)(2,1)S(1)}, u32[]{:S(2)}, u32[]{:S(2)}) collective-permute-start(bf16[32,1536]{1,0:T(8,128)(2,1)S(1)} %get-tuple-element.240), channel_id=1, source_target_pairs={{0,16},{1,17},{2,18},{3,19},{4,20},{5,21},{6,22},{7,23},{8,24},{9,... | collective-permute-start | bytes 294920 | tf_op jit(solution)/shard_map/ppermute | solution.py:26
  133.2 10.0 %collective-permute-start.59 = (bf16[48,896]{1,0:T(8,128)(2,1)S(1)}, bf16[48,896]{1,0:T(8,128)(2,1)S(1)}, u32[]{:S(2)}, u32[]{:S(2)}) collective-permute-start(bf16[48,896]{1,0:T(8,128)(2,1)S(1)} %get-tuple-element.245), channel_id=1, source_target_pairs={{0,8},{1,9},{2,10},{3,11},{4,12},{5,13},{6,14},{7,15},{8,0},{9,1},... | collective-permute-start | bytes 258056 | tf_op jit(solution)/shard_map/ppermute | solution.py:26
  133.9 10.0 %collective-permute-start.60 = (bf16[48,896]{1,0:T(8,128)(2,1)S(1)}, bf16[48,896]{1,0:T(8,128)(2,1)S(1)}, u32[]{:S(2)}, u32[]{:S(2)}) collective-permute-start(bf16[48,896]{1,0:T(8,128)(2,1)S(1)} %get-tuple-element.246), channel_id=1, source_target_pairs={{0,16},{1,17},{2,18},{3,19},{4,20},{5,21},{6,22},{7,23},{8,24},{9,... | collective-permute-start | bytes 258056 | tf_op jit(solution)/shard_map/ppermute | solution.py:26
  135.7 8.2 %collective-permute-start.61 = (bf16[48,896]{1,0:T(8,128)(2,1)S(1)}, bf16[48,896]{1,0:T(8,128)(2,1)S(1)}, u32[]{:S(2)}, u32[]{:S(2)}) collective-permute-start(bf16[48,896]{1,0:T(8,128)(2,1)S(1)} %get-tuple-element.247), channel_id=1, source_target_pairs={{0,24},{1,25},{2,26},{3,27},{4,28},{5,29},{6,30},{7,31},{8,16},{9,... | collective-permute-start | bytes 258056 | tf_op jit(solution)/shard_map/ppermute | solution.py:26
